TPU v7x, 32 devices: a whole 2x2x4 slice. The times are simulated.
32 devices in a mesh: dp: 4 (over x, core), blk: 8 (over z, y).
Axes of the slice: x: 2, y: 2, z: 4, core: 2. Of those that a mesh axis runs over, the one named last changes fastest.
Arguments:
- hidden_in: bfloat16 [2048, 8, 1024], P('blk', 'dp'), may hold values from -6 to 6
- first_values: bfloat16 [2048, 8, 1024], P('blk', 'dp'), may hold values from -13 to 13
- doc_lengths: int32 [8, 8], P('dp'), may hold values from 1 to 1024, 2048 in all within a row
- w_query: bfloat16 [1024, 1024], replicated, may hold values from -0.25 to 0.25
- w_key: bfloat16 [1024, 1024], replicated, may hold values from -0.25 to 0.25
- w_value: bfloat16 [1024, 1024], replicated, may hold values from -0.1875 to 0.1875
- w_out: bfloat16 [1024, 1024], replicated, may hold values from -0.75 to 0.75
- w_gate: bfloat16 [1024, 2816], replicated, may hold values from -0.1875 to 0.1875
- w_up: bfloat16 [1024, 2816], replicated, may hold values from -0.1875 to 0.1875
- w_down: bfloat16 [2816, 1024], replicated, may hold values from -0.109375 to 0.109375
- attn_gain: float32 [1024], replicated, may hold values from 0.5 to 1.5
- ffn_gain: float32 [1024], replicated, may hold values from 0.5 to 1.5
- out_cotangent: bfloat16 [2048, 8, 1024], P('blk', 'dp'), may hold values from -6 to 6
Outputs:
- block_out: bfloat16 [2048, 8, 1024], P('blk', 'dp')
- grad_input: float32 [2048, 8, 1024], P('blk', 'dp')
- grad_first: float32 [2048, 8, 1024], P('blk', 'dp')
- grad_query: float32 [1024, 1024], P('dp', 'blk')
- grad_key: float32 [1024, 1024], P('dp', 'blk')
- grad_value: float32 [1024, 1024], P('dp', 'blk')
- grad_project: float32 [1024, 1024], P('dp', 'blk')
- grad_gate: float32 [1024, 2816], P('dp', 'blk')
- grad_up: float32 [1024, 2816], P('dp', 'blk')
- grad_down: float32 [2816, 1024], P('dp', 'blk')
- grad_attn_gain: float32 [1024], replicated
- grad_ffn_gain: float32 [1024], replicated
- first_msq: float32 [], replicated
- mixed_msq: float32 [], replicated
Inputs may be any that keep to these rules, and one draw needn't show every extreme that they name: `doc_lengths`: the 8 lengths of a row sum to 2048.
All inputs are finite; a program needn't handle non-finite values.
Results may differ from a plain program's by a relative error of at most 0.033.
Values may be sent and summed in bfloat16 or wider, within the bound.
A program may use at most 320 MiB of HBM per device.

v0:
```python
import jax
import jax.numpy as jnp
from jax import lax
from jax.sharding import PartitionSpec as P

HEADS = 16
HEAD_DIM = 64


epsilon = 1e-06


def documents(doc_lengths, row_length):
    doc_ends = jnp.cumsum(doc_lengths, axis=1)
    places = jnp.arange(row_length, dtype=jnp.int32)
    passed = (doc_ends[:, None, :] <= places[None, :, None]).astype(jnp.int32)
    segment = jnp.sum(passed, axis=2)
    doc_start = jnp.sum(passed * doc_lengths[:, None, :], axis=2)
    return (segment, places[None, :] - doc_start)


def project(acts, weight):
    flat = acts.reshape(-1, acts.shape[-1])
    result = jnp.dot(flat, weight, preferred_element_type=jnp.float32)
    return result.reshape(acts.shape[:-1] + (weight.shape[1],))


def project_back(grads_in, weight):
    flat = grads_in.reshape(-1, grads_in.shape[-1])
    result = lax.dot_general(
        flat, weight, (((1,), (1,)), ((), ())), preferred_element_type=jnp.float32
    )
    return result.reshape(grads_in.shape[:-1] + (weight.shape[0],))


def weight_grad(acts, grads_in):
    flat_acts = acts.reshape(-1, acts.shape[-1])
    flat_grads = grads_in.reshape(-1, grads_in.shape[-1])
    return lax.dot_general(
        flat_acts, flat_grads, (((0,), (0,)), ((), ())), preferred_element_type=jnp.float32
    )


def rms_parts(values):
    inverse_rms = lax.rsqrt(jnp.mean(values * values, axis=-1, keepdims=True) + epsilon)
    return (values * inverse_rms, inverse_rms)


def norm_back(d_normed, normed, inverse_rms):
    return inverse_rms * (d_normed - normed * jnp.mean(d_normed * normed, axis=-1, keepdims=True))


def rope_tables(positions):
    half_dim = HEAD_DIM // 2
    inverse_freq = jnp.power(10000.0, -jnp.arange(half_dim, dtype=jnp.float32) * 2.0 / HEAD_DIM)
    angles = jnp.transpose(positions).astype(jnp.float32)[:, :, None] * inverse_freq[None, None, :]
    return (jnp.cos(angles)[:, :, None, :], jnp.sin(angles)[:, :, None, :])


def rotate(values, cos_table, sin_table):
    half_dim = HEAD_DIM // 2
    shaped = values.reshape(values.shape[:-1] + (HEADS, HEAD_DIM))
    first_half = shaped[..., :half_dim]
    second_half = shaped[..., half_dim:]
    turned = jnp.concatenate(
        [
            first_half * cos_table - second_half * sin_table,
            second_half * cos_table + first_half * sin_table,
        ],
        axis=-1,
    )
    return turned.reshape(values.shape)


def body(
    hidden_in,
    first_values,
    doc_lengths,
    w_query,
    w_key,
    w_value,
    w_out,
    w_gate,
    w_up,
    w_down,
    attn_gain,
    ffn_gain,
    out_cotangent,
):
    local_len, seq_count, model_width = hidden_in.shape
    cycle_size = lax.axis_size("blk")
    row_length = local_len * cycle_size
    offset = lax.axis_index("blk") * local_len
    score_scale = HEAD_DIM ** (-0.5)
    segment_all, position_all = documents(doc_lengths, row_length)
    segment_own = lax.dynamic_slice_in_dim(segment_all, offset, local_len, 1)
    position_own = lax.dynamic_slice_in_dim(position_all, offset, local_len, 1)
    query_index = offset + jnp.arange(local_len, dtype=jnp.int32)
    cos_table, sin_table = rope_tables(position_own)
    resid_in = hidden_in.astype(jnp.float32)
    normed_one, inv_one = rms_parts(resid_in)
    normed_in = (normed_one * attn_gain).astype(jnp.bfloat16)
    queries = rotate(project(normed_in, w_query), cos_table, sin_table).astype(jnp.bfloat16)
    keys_rot = rotate(project(normed_in, w_key), cos_table, sin_table).astype(jnp.bfloat16)
    first_f = first_values.astype(jnp.float32)
    mixed = 0.5 * project(normed_in, w_value) + 0.5 * first_f
    mixed_low = mixed.astype(jnp.bfloat16)
    first_sq = jnp.sum(first_f * first_f)
    mixed_sq = jnp.sum(mixed * mixed)
    query_four = queries.reshape(local_len, seq_count, HEADS, HEAD_DIM)

    def allowed_pairs(start, n_keys):
        key_index = start + jnp.arange(n_keys, dtype=jnp.int32)
        segment_key = lax.dynamic_slice_in_dim(segment_all, start, n_keys, 1)
        allowed = (key_index[None, None, :] <= query_index[None, :, None]) & (
            segment_key[:, None, :] == segment_own[:, :, None]
        )
        return allowed[:, None]

    def piece_step(running, key_piece, value_piece, start):
        run_max, run_sum, run_acc = running
        n_keys = key_piece.shape[0]
        allowed = allowed_pairs(start, n_keys)
        key_four = key_piece.reshape(n_keys, seq_count, HEADS, HEAD_DIM)
        value_four = value_piece.reshape(n_keys, seq_count, HEADS, HEAD_DIM)
        scores = (
            jnp.einsum("qshd,kshd->shqk", query_four, key_four, preferred_element_type=jnp.float32)
            * score_scale
        )
        new_max = jnp.maximum(run_max, jnp.max(jnp.where(allowed, scores, -1e30), axis=-1))
        weights = jnp.where(allowed, jnp.exp(scores - new_max[..., None]), 0.0)
        factor = jnp.exp(run_max - new_max)
        run_sum = run_sum * factor + jnp.sum(weights, axis=-1)
        run_acc = run_acc * factor[..., None] + jnp.einsum(
            "shqk,kshd->shqd",
            weights.astype(jnp.bfloat16),
            value_four,
            preferred_element_type=jnp.float32,
        )
        return (new_max, run_sum, run_acc)

    start_state = (
        jnp.full((seq_count, HEADS, local_len), -1e30, jnp.float32),
        jnp.zeros((seq_count, HEADS, local_len), jnp.float32),
        jnp.zeros((seq_count, HEADS, local_len, HEAD_DIM), jnp.float32),
    )
    running = start_state
    key_piece = lax.all_gather(keys_rot, "blk", axis=0, tiled=True)
    value_piece = lax.all_gather(mixed_low, "blk", axis=0, tiled=True)
    n_keys = key_piece.shape[0]
    step_rows = min(512, n_keys)
    n_steps = n_keys // step_rows

    def inner_step(fold_state, block_item):
        return (piece_step(fold_state, block_item[0], block_item[1], block_item[2]), None)

    starts = jnp.arange(n_steps, dtype=jnp.int32) * step_rows
    running, unused = lax.scan(
        inner_step,
        running,
        (
            key_piece.reshape(n_steps, step_rows, seq_count, model_width),
            value_piece.reshape(n_steps, step_rows, seq_count, model_width),
            starts,
        ),
    )
    run_max, run_sum, run_acc = running
    attn_four = jnp.transpose(run_acc / run_sum[..., None], (2, 0, 1, 3))
    attn_f = attn_four.reshape(local_len, seq_count, model_width)
    log_total = run_max + jnp.log(run_sum)
    attn_low = attn_f.astype(jnp.bfloat16)
    resid_mid = resid_in + project(attn_low, w_out)
    normed_two, inv_two = rms_parts(resid_mid)
    normed_mid = (normed_two * ffn_gain).astype(jnp.bfloat16)
    gate_pre = project(normed_mid, w_gate)
    up_pre = project(normed_mid, w_up)
    gate_act = jax.nn.silu(gate_pre)
    inner_low = (gate_act * up_pre).astype(jnp.bfloat16)
    block_out = (resid_mid + project(inner_low, w_down)).astype(jnp.bfloat16)
    grad_down = weight_grad(inner_low, out_cotangent)
    d_inner = project_back(out_cotangent, w_down)
    sigmoid_gate = jax.nn.sigmoid(gate_pre)
    d_gate = (d_inner * up_pre * sigmoid_gate * (1.0 + gate_pre * (1.0 - sigmoid_gate))).astype(
        jnp.bfloat16
    )
    d_up = (d_inner * gate_act).astype(jnp.bfloat16)
    grad_gate = weight_grad(normed_mid, d_gate)
    grad_up = weight_grad(normed_mid, d_up)
    d_normed_mid = project_back(d_gate, w_gate) + project_back(d_up, w_up)
    gain_two_grad = jnp.sum((d_normed_mid * normed_two).reshape(-1, model_width), axis=0)
    d_resid_mid = out_cotangent.astype(jnp.float32) + norm_back(
        d_normed_mid * ffn_gain, normed_two, inv_two
    )
    d_branch = d_resid_mid.astype(jnp.bfloat16)
    grad_project = weight_grad(attn_low, d_branch)
    d_attn = project_back(d_branch, w_out).astype(jnp.bfloat16)
    d_attn_four = d_attn.reshape(local_len, seq_count, HEADS, HEAD_DIM)
    delta_rows = jnp.transpose(
        jnp.sum(d_attn_four.astype(jnp.float32) * attn_four, axis=-1), (1, 2, 0)
    )
    back_keys, back_values = (
        lax.all_gather(keys_rot, "blk", axis=0, tiled=True),
        lax.all_gather(mixed_low, "blk", axis=0, tiled=True),
    )
    block_rows = min(512, row_length)
    n_blocks = row_length // block_rows
    block_starts = jnp.arange(n_blocks, dtype=jnp.int32) * block_rows

    def block_scores(key_four, value_four, start):
        allowed = allowed_pairs(start, block_rows)
        scores = (
            jnp.einsum("qshd,kshd->shqk", query_four, key_four, preferred_element_type=jnp.float32)
            * score_scale
        )
        probs = jnp.where(allowed, jnp.exp(scores - log_total[..., None]), 0.0)
        d_probs = jnp.einsum(
            "qshd,kshd->shqk", d_attn_four, value_four, preferred_element_type=jnp.float32
        )
        d_scores = (probs * (d_probs - delta_rows[..., None])).astype(jnp.bfloat16)
        return (probs, d_scores)

    def back_step(d_query_acc, block_item):
        key_block, value_block, start = block_item
        key_four = key_block.reshape(block_rows, seq_count, HEADS, HEAD_DIM)
        value_four = value_block.reshape(block_rows, seq_count, HEADS, HEAD_DIM)
        probs, d_scores = block_scores(key_four, value_four, start)
        d_query_acc = (
            d_query_acc
            + jnp.einsum("shqk,kshd->qshd", d_scores, key_four, preferred_element_type=jnp.float32)
            * score_scale
        )
        d_keys = (
            jnp.einsum("shqk,qshd->kshd", d_scores, query_four, preferred_element_type=jnp.float32)
            * score_scale
        )
        d_vals = jnp.einsum(
            "shqk,qshd->kshd",
            probs.astype(jnp.bfloat16),
            d_attn_four,
            preferred_element_type=jnp.float32,
        )
        joined = jnp.concatenate(
            [
                d_keys.reshape(block_rows, seq_count, model_width),
                d_vals.reshape(block_rows, seq_count, model_width),
            ],
            axis=-1,
        )
        return (d_query_acc, joined)

    d_query_rot, terms = lax.scan(
        back_step,
        jnp.zeros((local_len, seq_count, HEADS, HEAD_DIM), jnp.float32),
        (
            back_keys.reshape(n_blocks, block_rows, seq_count, model_width),
            back_values.reshape(n_blocks, block_rows, seq_count, model_width),
            block_starts,
        ),
    )
    terms = terms.reshape(row_length, seq_count, 2 * model_width)
    kv_grad = lax.psum_scatter(
        terms.astype(jnp.bfloat16), "blk", scatter_dimension=0, tiled=True
    ).astype(jnp.float32)
    d_key_rot = kv_grad[..., :model_width]
    d_mixed = kv_grad[..., model_width:]
    d_query_low = rotate(
        d_query_rot.reshape(local_len, seq_count, model_width), cos_table, -sin_table
    ).astype(jnp.bfloat16)
    d_key_low = rotate(d_key_rot, cos_table, -sin_table).astype(jnp.bfloat16)
    d_value_low = (0.5 * d_mixed).astype(jnp.bfloat16)
    grad_first = 0.5 * d_mixed
    grad_query = weight_grad(normed_in, d_query_low)
    grad_key = weight_grad(normed_in, d_key_low)
    grad_value = weight_grad(normed_in, d_value_low)
    d_normed_in = (
        project_back(d_query_low, w_query)
        + project_back(d_key_low, w_key)
        + project_back(d_value_low, w_value)
    )
    gain_one_grad = jnp.sum((d_normed_in * normed_one).reshape(-1, model_width), axis=0)
    grad_input = d_resid_mid + norm_back(d_normed_in * attn_gain, normed_one, inv_one)
    weight_grads = (grad_query, grad_key, grad_value, grad_project, grad_gate, grad_up, grad_down)
    partial_grads = (
        lax.psum_scatter(
            weight_grads[0].astype(jnp.bfloat16), "dp", scatter_dimension=0, tiled=True
        ).astype(jnp.float32),
        lax.psum_scatter(
            weight_grads[1].astype(jnp.bfloat16), "dp", scatter_dimension=0, tiled=True
        ).astype(jnp.float32),
        lax.psum_scatter(
            weight_grads[2].astype(jnp.bfloat16), "dp", scatter_dimension=0, tiled=True
        ).astype(jnp.float32),
        lax.psum_scatter(
            weight_grads[3].astype(jnp.bfloat16), "dp", scatter_dimension=0, tiled=True
        ).astype(jnp.float32),
        lax.psum_scatter(
            weight_grads[4].astype(jnp.bfloat16), "dp", scatter_dimension=0, tiled=True
        ).astype(jnp.float32),
        lax.psum_scatter(
            weight_grads[5].astype(jnp.bfloat16), "dp", scatter_dimension=0, tiled=True
        ).astype(jnp.float32),
        lax.psum_scatter(
            weight_grads[6].astype(jnp.bfloat16), "dp", scatter_dimension=0, tiled=True
        ).astype(jnp.float32),
    )
    summed = (
        lax.psum_scatter(
            partial_grads[0].astype(jnp.bfloat16), "blk", scatter_dimension=1, tiled=True
        ).astype(jnp.float32),
        lax.psum_scatter(
            partial_grads[1].astype(jnp.bfloat16), "blk", scatter_dimension=1, tiled=True
        ).astype(jnp.float32),
        lax.psum_scatter(
            partial_grads[2].astype(jnp.bfloat16), "blk", scatter_dimension=1, tiled=True
        ).astype(jnp.float32),
        lax.psum_scatter(
            partial_grads[3].astype(jnp.bfloat16), "blk", scatter_dimension=1, tiled=True
        ).astype(jnp.float32),
        lax.psum_scatter(
            partial_grads[4].astype(jnp.bfloat16), "blk", scatter_dimension=1, tiled=True
        ).astype(jnp.float32),
        lax.psum_scatter(
            partial_grads[5].astype(jnp.bfloat16), "blk", scatter_dimension=1, tiled=True
        ).astype(jnp.float32),
        lax.psum_scatter(
            partial_grads[6].astype(jnp.bfloat16), "blk", scatter_dimension=1, tiled=True
        ).astype(jnp.float32),
    )
    totals = lax.psum((gain_one_grad, gain_two_grad, first_sq, mixed_sq), ("dp", "blk"))
    n_entries = row_length * seq_count * lax.axis_size("dp") * model_width
    return (
        block_out,
        grad_input,
        grad_first,
        summed[0],
        summed[1],
        summed[2],
        summed[3],
        summed[4],
        summed[5],
        summed[6],
        totals[0],
        totals[1],
        totals[2] / n_entries,
        totals[3] / n_entries,
    )


def solution(mesh):
    in_specs = (
        P("blk", "dp", None),
        P("blk", "dp", None),
        P("dp", None),
        P(),
        P(),
        P(),
        P(),
        P(),
        P(),
        P(),
        P(),
        P(),
        P("blk", "dp", None),
    )
    out_specs = (
        P("blk", "dp", None),
        P("blk", "dp", None),
        P("blk", "dp", None),
        P("dp", "blk"),
        P("dp", "blk"),
        P("dp", "blk"),
        P("dp", "blk"),
        P("dp", "blk"),
        P("dp", "blk"),
        P("dp", "blk"),
        P(),
        P(),
        P(),
        P(),
    )
    return jax.shard_map(body, mesh=mesh, in_specs=in_specs, out_specs=out_specs, check_vma=False)
```

profile of v0, /device:TPU:0, one launch (start us, length us, event | category | flops | bytes accessed | tf_op | source)
XLA Modules:
  0.0 1740.5 jit_solution(13050748668814698923)
XLA Ops:
  42.2 99.5 %all-gather.5.cloned.1.call-done = bf16[2048,2,1024]{2,0,1:T(8,128)(2,1)} async-done(((bf16[256,2,1024]{2,0,1:T(8,128)(2,1)}), bf16[2048,2,1024]{2,0,1:T(8,128)(2,1)}) %all-gather.5.cloned.1.call-update) | async-done | bytes 8388624 | tf_op jit(solution)/shard_map/all_gather | solution.py:149
  141.7 11.7 copy.140
  153.4 114.2 %all-gather.3.cloned.1.call-done = bf16[2048,2,1024]{2,0,1:T(8,128)(2,1)} async-done(((bf16[256,2,1024]{2,0,1:T(8,128)(2,1)}), bf16[2048,2,1024]{2,0,1:T(8,128)(2,1)}) %all-gather.3.cloned.1.call-update) | async-done | bytes 8388624 | tf_op jit(solution)/shard_map/all_gather | solution.py:148
  267.6 11.5 copy.139
  279.1 144.7 %while.28 = (s32[]{:T(128)}, f32[2,16,256]{2,1,0:T(8,128)S(1)}, f32[2,16,256]{2,1,0:T(8,128)S(1)}, f32[2,16,256,64]{2,3,1,0:T(8,128)}, s32[4]{0:T(128)S(1)}, /*i...) while((s32[]{:T(128)}, f32[2,16,256]{2,1,0:T(8,128)S(1)}, ...), condition=%wide.region_7.8_spmd.clone, body=%wide.region_4.0_spmd.clone.sunk | while | flops 1122149120 | bytes 70013144 | solution.py:158
  303.7 11.1 fusion.161
  339.4 11.7 fusion.161
  375.7 11.7 fusion.161
  412.0 11.7 fusion.161
  436.6 10.4 multiply_convert_fusion.1
  465.8 192.9 %while.29 = (s32[]{:T(128)}, f32[256,2,16,64]{0,3,2,1:T(8,128)}, bf16[4,512,2,2048]{1,3,2,0:T(8,128)(2,1)}, bf16[4,512,2,1024]{1,3,2,0:T(8,128)(2,1)}, s32[4]{0:...) while((s32[]{:T(128)}, f32[256,2,16,64]{0,3,2,1:T(8,128)}, ...), condition=%wide.region_12.13_spmd.clone, body=%wide.region_11.12_spmd.clone.sunk | while | flops 2739012352 | bytes 129093912 | solution.py:251
  483.7 10.6 fusion.174
  530.7 10.6 fusion.174
  579.3 10.6 fusion.174
  627.8 10.6 fusion.174
  658.7 21.6 %copy.148 = bf16[4,512,2,2048]{3,1,0,2:T(8,128)(2,1)} copy(bf16[4,512,2,2048]{1,3,2,0:T(8,128)(2,1)} %get-tuple-element.145) | data formatting | bytes 33554432 | tf_op jit(solution)/shard_map/convert_element_type | solution.py:262
  709.0 251.6 %reduce-scatter.30.cloned.1.call-done = bf16[256,2,2048]{2,0,1:T(8,128)(2,1)} async-done(((bf16[2048,2,2048]{2,0,1:T(8,128)(2,1)}), bf16[256,2,2048]{2,0,1:T(8,128)(2,1)}) %reduce-scatter.30.cloned.1.call-update) | async-done | bytes 2097168 | tf_op jit(solution)/shard_map/reduce_scatter | solution.py:261
  967.9 26.4 %reduce-scatter.38.cloned.1.call-done = bf16[256,1024]{1,0:T(8,128)(2,1)} async-done(((bf16[1024,1024]{1,0:T(8,128)(2,1)}), bf16[256,1024]{1,0:T(8,128)(2,1)}) %reduce-scatter.38.cloned.1.call-update) | async-done | bytes 524304 | tf_op jit(solution)/shard_map/reduce_scatter | solution.py:293
  996.4 55.2 %reduce-scatter.40.cloned.1.call-done = bf16[256,2816]{1,0:T(8,128)(2,1)} async-done(((bf16[1024,2816]{1,0:T(8,128)(2,1)}), bf16[256,2816]{1,0:T(8,128)(2,1)}) %reduce-scatter.40.cloned.1.call-update) | async-done | bytes 1441808 | tf_op jit(solution)/shard_map/reduce_scatter | solution.py:296
  1054.2 54.8 %reduce-scatter.42.cloned.1.call-done = bf16[256,2816]{1,0:T(8,128)(2,1)} async-done(((bf16[1024,2816]{1,0:T(8,128)(2,1)}), bf16[256,2816]{1,0:T(8,128)(2,1)}) %reduce-scatter.42.cloned.1.call-update) | async-done | bytes 1441808 | tf_op jit(solution)/shard_map/reduce_scatter | solution.py:299
  1111.7 54.8 %reduce-scatter.44.cloned.1.call-done = bf16[704,1024]{1,0:T(8,128)(2,1)} async-done(((bf16[2816,1024]{1,0:T(8,128)(2,1)}), bf16[704,1024]{1,0:T(8,128)(2,1)}) %reduce-scatter.44.cloned.1.call-update) | async-done | bytes 1441808 | tf_op jit(solution)/shard_map/reduce_scatter | solution.py:302
  1187.5 13.2 reduce-scatter.36.cloned.1.call-done
  1214.4 51.5 %reduce-scatter.52.cloned.1.call-done = bf16[128,256]{1,0:T(8,128)(2,1)} async-done(((bf16[1024,256]{1,0:T(8,128)(2,1)}), bf16[128,256]{1,0:T(8,128)(2,1)}) %reduce-scatter.52.cloned.1.call-update) | async-done | bytes 65552
  1267.6 66.0 %reduce-scatter.54.cloned.1.call-done = bf16[352,256]{1,0:T(8,128)(2,1)} async-done(((bf16[2816,256]{1,0:T(8,128)(2,1)}), bf16[352,256]{1,0:T(8,128)(2,1)}) %reduce-scatter.54.cloned.1.call-update) | async-done | bytes 180240
  1335.5 65.7 %reduce-scatter.56.cloned.1.call-done = bf16[352,256]{1,0:T(8,128)(2,1)} async-done(((bf16[2816,256]{1,0:T(8,128)(2,1)}), bf16[352,256]{1,0:T(8,128)(2,1)}) %reduce-scatter.56.cloned.1.call-update) | async-done | bytes 180240
  1403.2 65.4 %reduce-scatter.58.cloned.1.call-done = bf16[128,704]{1,0:T(8,128)(2,1)} async-done(((bf16[1024,704]{1,0:T(8,128)(2,1)}), bf16[128,704]{1,0:T(8,128)(2,1)}) %reduce-scatter.58.cloned.1.call-update) | async-done | bytes 180240
  1470.5 31.6 %reduce-scatter.34.cloned.1.call-done = bf16[256,1024]{1,0:T(8,128)(2,1)} async-done(((bf16[1024,1024]{1,0:T(8,128)(2,1)}), bf16[256,1024]{1,0:T(8,128)(2,1)}) %reduce-scatter.34.cloned.1.call-update) | async-done | bytes 524304 | tf_op jit(solution)/shard_map/reduce_scatter | solution.py:287
  1514.2 21.9 %reduce-scatter.32.cloned.1.call-done = bf16[256,1024]{1,0:T(8,128)(2,1)} async-done(((bf16[1024,1024]{1,0:T(8,128)(2,1)}), bf16[256,1024]{1,0:T(8,128)(2,1)}) %reduce-scatter.32.cloned.1.call-update) | async-done | bytes 524304 | tf_op jit(solution)/shard_map/reduce_scatter | solution.py:284
  1544.2 39.7 %all-reduce = (f32[1024]{0:T(1024)}, f32[1024]{0:T(1024)}, f32[]{:T(128)}, f32[]{:T(128)}) all-reduce(f32[1024]{0:T(1024)S(1)} %get-tuple-element.384, f32[1024]{0:T(1024)S(1)} %copy-done.32, f32[]{:T(128)} %fusion.47, f32[]{:T(128)} %get-tuple-element.459), channel_id=1, replica_groups=mesh['dp'=4,'blk'=8] {'dp','blk'}, use_global_device_ids=true, to_apply=%region_30.31 | all-reduce | flops 2050 | bytes 16400 | tf_op jit(solution)/shard_map/psum | solution.py:329
  1590.9 10.4 reduce-scatter.50.cloned.1.call-done
  1602.9 62.8 %reduce-scatter.48.cloned.1.call-done = bf16[128,256]{1,0:T(8,128)(2,1)} async-done(((bf16[1024,256]{1,0:T(8,128)(2,1)}), bf16[128,256]{1,0:T(8,128)(2,1)}) %reduce-scatter.48.cloned.1.call-update) | async-done | bytes 65552
  1667.3 62.6 %reduce-scatter.46.cloned.1.call-done = bf16[128,256]{1,0:T(8,128)(2,1)} async-done(((bf16[1024,256]{1,0:T(8,128)(2,1)}), bf16[128,256]{1,0:T(8,128)(2,1)}) %reduce-scatter.46.cloned.1.call-update) | async-done | bytes 65552
  (301 shorter events, 415.0 us)
Async XLA Ops:
  7.2 134.5 %all-gather.5.cloned.1.call-start = ((), (), s32[]{:S(2)}) async-start(), calls=%async_computation.16 | async-start | bytes 9437184 | tf_op jit(solution)/shard_map/all_gather | solution.py:149
  9.1 18.2 %copy-start.28 = (f32[256,2]{0,1:T(2,128)}, f32[256,2]{0,1:T(2,128)S(1)}, u32[]{:S(2)}) copy-start(f32[256,2]{0,1:T(2,128)S(1)} %add_rsqrt_fusion.1) | copy-start | bytes 6148
  13.9 253.7 %all-gather.3.cloned.1.call-start = ((), (), s32[]{:S(2)}) async-start(), calls=%async_computation.15 | async-start | bytes 9437184 | tf_op jit(solution)/shard_map/all_gather | solution.py:148
  31.8 928.8 %reduce-scatter.30.cloned.1.call-start = ((), (), s32[]{:S(2)}) async-start(), calls=%async_computation.17 | async-start | bytes 18874368 | tf_op jit(solution)/shard_map/reduce_scatter | solution.py:261
  426.4 10.2 slice-start.2
  427.8 29.2 %copy-start.3 = (f32[256,2,1024]{2,0,1:T(8,128)}, f32[256,2,1024]{2,0,1:T(8,128)S(1)}, u32[]{:S(2)}) copy-start(f32[256,2,1024]{2,0,1:T(8,128)S(1)} %get-tuple-element.470) | copy-start | bytes 6291460
  428.1 8.4 copy-start.15
  428.1 8.4 slice-start.3
  428.1 18.9 %slice-start = ((s8[5767168]{0:T(1024)(128)(4,1)}), s8[4194304]{0:T(1024)(128)(4,1)S(1)}, s32[]{:S(2)}) async-start(s8[5767168]{0:T(1024)(128)(4,1)} %bitcast.283), calls=%async_computation.32 | async-start | bytes 8388608
  436.6 10.4 slice-start.1
  447.0 6.0 copy-start.33
  494.2 9.4 copy-start.2
  541.3 9.4 copy-start.2
  589.9 9.4 copy-start.2
  638.4 9.4 copy-start.2
  680.4 313.9 %reduce-scatter.38.cloned.1.call-start = ((), (), s32[]{:S(2)}) async-start(), calls=%async_computation.21 | async-start | bytes 2621440 | tf_op jit(solution)/shard_map/reduce_scatter | solution.py:293
  685.8 365.8 %reduce-scatter.40.cloned.1.call-start = ((), (), s32[]{:S(2)}) async-start(), calls=%async_computation.22 | async-start | bytes 7208960 | tf_op jit(solution)/shard_map/reduce_scatter | solution.py:296
  693.9 415.1 %reduce-scatter.42.cloned.1.call-start = ((), (), s32[]{:S(2)}) async-start(), calls=%async_computation.23 | async-start | bytes 7208960 | tf_op jit(solution)/shard_map/reduce_scatter | solution.py:299
  700.8 465.7 %reduce-scatter.44.cloned.1.call-start = ((), (), s32[]{:S(2)}) async-start(), calls=%async_computation.24 | async-start | bytes 7208960 | tf_op jit(solution)/shard_map/reduce_scatter | solution.py:302
  709.0 255.9 %copy-start.7 = (bf16[256,2,1024]{2,1,0:T(2,128)(2,1)S(1)}, bf16[256,2,1024]{2,1,0:T(2,128)(2,1)}, u32[]{:S(2)}) copy-start(bf16[256,2,1024]{2,1,0:T(2,128)(2,1)} %param.17) | copy-start | bytes 3145732
  709.0 255.9 %copy-start.27 = (f32[1024]{0:T(1024)S(1)}, f32[1024]{0:T(1024)}, u32[]{:S(2)}) copy-start(f32[1024]{0:T(1024)} %param.27) | copy-start | bytes 12292
  709.0 255.9 %copy-start.29 = (f32[256,2]{0,1:T(2,128)S(1)}, f32[256,2]{0,1:T(2,128)}, u32[]{:S(2)}) copy-start(f32[256,2]{0,1:T(2,128)} %copy-done.28) | copy-start | bytes 6148
  709.0 491.7 %reduce-scatter.36.cloned.1.call-start = ((), (), s32[]{:S(2)}) async-start(), calls=%async_computation.20 | async-start | bytes 2621440 | tf_op jit(solution)/shard_map/reduce_scatter | solution.py:290
  967.8 298.1 %reduce-scatter.52.cloned.1.call-start = ((), (), s32[]{:S(2)}) async-start(), calls=%async_computation.28 | async-start | bytes 589824
  996.3 337.2 %reduce-scatter.54.cloned.1.call-start = ((), (), s32[]{:S(2)}) async-start(), calls=%async_computation.29 | async-start | bytes 1622016
  1054.2 347.0 %reduce-scatter.56.cloned.1.call-start = ((), (), s32[]{:S(2)}) async-start(), calls=%async_computation.30 | async-start | bytes 1622016
  1111.6 357.0 %reduce-scatter.58.cloned.1.call-start = ((), (), s32[]{:S(2)}) async-start(), calls=%async_computation.31 | async-start | bytes 1769472
  1169.1 333.0 %reduce-scatter.34.cloned.1.call-start = ((), (), s32[]{:S(2)}) async-start(), calls=%async_computation.19 | async-start | bytes 2621440 | tf_op jit(solution)/shard_map/reduce_scatter | solution.py:287
  1183.1 353.0 %reduce-scatter.32.cloned.1.call-start = ((), (), s32[]{:S(2)}) async-start(), calls=%async_computation.18 | async-start | bytes 2621440 | tf_op jit(solution)/shard_map/reduce_scatter | solution.py:284
  1187.4 413.8 %reduce-scatter.50.cloned.1.call-start = ((), (), s32[]{:S(2)}) async-start(), calls=%async_computation.27 | async-start | bytes 589824
  1202.7 463.0 %reduce-scatter.48.cloned.1.call-start = ((), (), s32[]{:S(2)}) async-start(), calls=%async_computation.26 | async-start | bytes 589824
  1504.1 225.8 %reduce-scatter.46.cloned.1.call-start = ((), (), s32[]{:S(2)}) async-start(), calls=%async_computation.25 | async-start | bytes 589824
  (29 other events, 77.4 us)
Sparse Core Ops, SparseCore 0:
  14.1 127.5 all-gather.4
  144.5 123.0 all-gather.2
  680.5 280.1 reduce-scatter.29
  963.8 30.4 reduce-scatter.37
  996.7 54.8 reduce-scatter.39
  1054.1 54.8 reduce-scatter.41
  1111.6 54.8 reduce-scatter.43
  1169.2 31.4 reduce-scatter.35
  1204.0 61.8 reduce-scatter.51
  1269.6 63.9 reduce-scatter.53
  1337.4 63.8 reduce-scatter.55
  1404.9 63.6 reduce-scatter.57
  1471.7 30.3 reduce-scatter.33
  1504.6 31.4 reduce-scatter.31
  1539.3 61.9 reduce-scatter.49
  1604.8 60.8 reduce-scatter.47
  1668.9 60.9 reduce-scatter.45
where the time goes:
time: 1750 us; the launch traced here: 1740 us
  waiting for transfers between devices  1110 us (63%)
  matrix products  317 us (18%)
  local copies, waits for them, and re-layouts  150 us (9%)
  other arithmetic  89.3 us (5%)
  blocking collectives  39.7 us (2%)
  between operations  18.2 us (1%)
    unnamed x24, waiting for transfers between devices  385 us
    reduce_scatter x1, waiting for transfers between devices, body(): lax.psum_scatter(terms.astype(jnp.bfloat16), 'blk', scatter_dimension=0,...  252 us
    all_gather x1, waiting for transfers between devices, body(): key_piece = lax.all_gather(keys_rot, 'blk', axis=0, tiled=True)  114 us
    all_gather x1, waiting for transfers between devices, body(): value_piece = lax.all_gather(mixed_low, 'blk', axis=0, tiled=True)  99.5 us
    unnamed x95, local copies, waits for them, and re-layouts  72 us
    reduce_scatter x1, waiting for transfers between devices, body(): lax.psum_scatter(weight_grads[4].astype(jnp.bfloat16), 'dp', scatter_dime...  55.2 us
    reduce_scatter x1, waiting for transfers between devices, body(): lax.psum_scatter(weight_grads[6].astype(jnp.bfloat16), 'dp', scatter_dime...  54.8 us
    reduce_scatter x1, waiting for transfers between devices, body(): lax.psum_scatter(weight_grads[5].astype(jnp.bfloat16), 'dp', scatter_dime...  54.8 us
  transfers between devices with their start and end apart: 17, of which 17 were waited for; matrix products, arithmetic and copies ran while one was open for 8% of the time, Pallas kernels for 0%

commit v1 on v0

v1 whole, which is shorter than its diff:
```python
import functools

import jax
import jax.numpy as jnp
from jax import lax
from jax.experimental import pallas as pl
from jax.experimental.pallas import tpu as pltpu
from jax.sharding import PartitionSpec as P

HEADS = 16
HEAD_DIM = 64
NEG = -1e30
EPS = 1e-06
F32 = jnp.float32
BF16 = jnp.bfloat16
VMEM_LIMIT = 56 * 2**20


def dot(a, b):
    return jnp.dot(a, b, preferred_element_type=F32)


def dot_nt(a, b):
    return lax.dot_general(a, b, (((1,), (1,)), ((), ())), preferred_element_type=F32)


def dot_tn(a, b):
    return lax.dot_general(a, b, (((0,), (0,)), ((), ())), preferred_element_type=F32)


def swap_halves(v):
    half = HEAD_DIM // 2
    width = v.shape[-1]
    lane = lax.broadcasted_iota(jnp.int32, v.shape, v.ndim - 1)
    left = pltpu.roll(v, width - half, v.ndim - 1)
    right = pltpu.roll(v, half, v.ndim - 1)
    return jnp.where(lane % HEAD_DIM < half, left, right)


def qkv_kernel(rows, length, width, normed_ref, first_ref, cos_ref, sin_ref, wq_ref, wk_ref, wv_ref, *outs):
    out_refs, sums_ref = outs[:rows], outs[rows]
    chunk = wq_ref.shape[1]
    first_sum = jnp.zeros((1, chunk), F32)
    mixed_sum = jnp.zeros((1, chunk), F32)
    for r in range(rows):
        at = pl.ds(r * length, length)
        normed = normed_ref[at, :]
        cos, sin = cos_ref[at, :], sin_ref[at, :]
        for which, w_ref in ((0, wq_ref), (1, wk_ref)):
            raw = dot(normed, w_ref[...])
            for c in range(chunk // 128):
                part = raw[:, c * 128 : (c + 1) * 128]
                turned = (part * cos + swap_halves(part) * sin).astype(BF16)
                for s in range(128 // width):
                    out_refs[r][c * (128 // width) + s, which] = turned[:, s * width : (s + 1) * width]
        first = first_ref[at, :].astype(F32)
        mixed = 0.5 * dot(normed, wv_ref[...]) + 0.5 * first
        first_sum = first_sum + jnp.sum(first * first, axis=0, keepdims=True)
        mixed_sum = mixed_sum + jnp.sum(mixed * mixed, axis=0, keepdims=True)
        low = mixed.astype(BF16)
        for s in range(chunk // width):
            out_refs[r][s, 2] = low[:, s * width : (s + 1) * width]
    sums_ref[0, 0:1] = first_sum
    sums_ref[0, 1:2] = mixed_sum


def project_qkv(normed, first, cos, sin, w_query, w_key, w_value, rows, n_blk):
    tokens, model = normed.shape
    length, width = tokens // rows, model // n_blk
    chunk = 256
    steps = model // chunk
    full = lambda cols: pl.BlockSpec((tokens, cols), lambda j: (0, 0))
    weight = pl.BlockSpec((model, chunk), lambda j: (0, j))
    return pl.pallas_call(
        functools.partial(qkv_kernel, rows, length, width),
        grid=(steps,),
        in_specs=[
            full(model),
            pl.BlockSpec((tokens, chunk), lambda j: (0, j)),
            full(128),
            full(128),
            weight,
            weight,
            weight,
        ],
        out_specs=[pl.BlockSpec((chunk // width, 3, length, width), lambda j: (j, 0, 0, 0))] * rows
        + [pl.BlockSpec((1, 2, chunk), lambda j: (j, 0, 0))],
        out_shape=[jax.ShapeDtypeStruct((n_blk, 3, length, width), BF16)] * rows
        + [jax.ShapeDtypeStruct((steps, 2, chunk), F32)],
        compiler_params=pltpu.CompilerParams(vmem_limit_bytes=VMEM_LIMIT),
        cost_estimate=pl.CostEstimate(
            flops=6 * tokens * model * model, bytes_accessed=6 * model * model + 10 * tokens * model, transcendentals=0
        ),
        name="qkv",
    )(normed, first, cos, sin, w_query, w_key, w_value)


def doc_ends(lens_ref, row, n_docs):
    ends, total = [], jnp.int32(0)
    for d in range(n_docs):
        total = total + lens_ref[row * n_docs + d]
        ends.append(total)
    return ends


def start_rows(ends, tile, length, heads):
    place = tile * length + lax.broadcasted_iota(jnp.int32, (1, length), 1)
    start = jnp.zeros((1, length), jnp.int32)
    for end in ends:
        start = jnp.where(end <= place, end, start)
    return jnp.concatenate([start] * heads, axis=1), jnp.concatenate([place] * heads, axis=1)


def head_masks(heads, width):
    lane = lax.broadcasted_iota(jnp.int32, (1, width), 1) // HEAD_DIM
    return [jnp.where(lane == h, 1.0, 0.0).astype(BF16) for h in range(heads)]


def by_head(values, masks):
    return jnp.concatenate([values * mask for mask in masks], axis=0)


def attn_fwd_kernel(row, n_docs, heads, lens_ref, qkv_ref, o_ref, low_ref, lse_ref, acc_ref):
    length, width = qkv_ref.shape[2:]
    i = pl.program_id(0)
    ends = doc_ends(lens_ref, row, n_docs)
    start, place = start_rows(ends, i, length, heads)
    lowest = jnp.int32(0)
    for end in ends:
        lowest = jnp.where(end <= i * length, end, lowest)
    lowest = lax.div(lowest, jnp.int32(length))
    masks = head_masks(heads, width)
    queries = by_head(qkv_ref[i, 0] * jnp.asarray(HEAD_DIM**-0.5, BF16), masks)

    def tile(step, carry):
        run_max, run_sum = carry
        j = i - step
        scores = dot_nt(qkv_ref[j, 1], queries)
        key = j * length + lax.broadcasted_iota(jnp.int32, scores.shape, 0)
        scores = jnp.where((key <= place) & (key >= start), scores, NEG)
        new_max = jnp.maximum(run_max, jnp.max(scores, axis=0, keepdims=True))
        weights = jnp.exp(scores - new_max)
        factor = jnp.exp(run_max - new_max)
        run_sum = run_sum * factor + jnp.sum(weights, axis=0, keepdims=True)
        acc_ref[...] = acc_ref[...] * factor + dot_tn(qkv_ref[j, 2], weights.astype(BF16))
        return new_max, run_sum

    acc_ref[...] = jnp.zeros_like(acc_ref)
    run_max, run_sum = lax.fori_loop(
        0,
        i - lowest + 1,
        tile,
        (jnp.full((1, heads * length), NEG, F32), jnp.zeros((1, heads * length), F32)),
    )
    result = acc_ref[...] / run_sum
    joined = jnp.concatenate(
        [
            result[h * HEAD_DIM : (h + 1) * HEAD_DIM, h * length : (h + 1) * length]
            for h in range(heads)
        ],
        axis=0,
    )
    attended = joined.T
    o_ref[0] = attended
    low_ref[0] = attended.astype(BF16)
    total = run_max + jnp.log(run_sum)
    for h in range(heads):
        lse_ref[0, h : h + 1, :] = total[:, h * length : (h + 1) * length]


def attn_fwd(lens, qkv, row, n_docs):
    n_blk, _, length, width = qkv.shape
    heads = width // HEAD_DIM
    tile = pl.BlockSpec((1, length, width), lambda i, lens: (i, 0, 0))
    return pl.pallas_call(
        functools.partial(attn_fwd_kernel, row, n_docs, heads),
        grid_spec=pltpu.PrefetchScalarGridSpec(
            num_scalar_prefetch=1,
            grid=(n_blk,),
            in_specs=[pl.BlockSpec(qkv.shape, lambda i, lens: (0, 0, 0, 0))],
            out_specs=[tile, tile, pl.BlockSpec((1, heads, length), lambda i, lens: (i, 0, 0))],
            scratch_shapes=[pltpu.VMEM((width, heads * length), F32)],
        ),
        out_shape=[
            jax.ShapeDtypeStruct((n_blk, length, width), F32),
            jax.ShapeDtypeStruct((n_blk, length, width), BF16),
            jax.ShapeDtypeStruct((n_blk, heads, length), F32),
        ],
        compiler_params=pltpu.CompilerParams(vmem_limit_bytes=VMEM_LIMIT),
        cost_estimate=pl.CostEstimate(flops=10**10, bytes_accessed=3 * 10**6, transcendentals=10**7),
        name="attn_fwd",
    )(lens, qkv)


def attn_bwd_kernel(row, n_docs, heads, lens_ref, qkv_ref, do_ref, o_ref, lse_ref, out_ref, dq_ref, delta_ref):
    n_blk, _, length, width = qkv_ref.shape
    j = pl.program_id(0)
    ends = doc_ends(lens_ref, row, n_docs)
    masks = head_masks(heads, width)
    scale = HEAD_DIM**-0.5

    @pl.when(j == 0)
    def _():
        def one(i, _):
            prod = (do_ref[i].astype(F32) * o_ref[i]).T
            for h in range(heads):
                delta_ref[i, h : h + 1, :] = jnp.sum(
                    prod[h * HEAD_DIM : (h + 1) * HEAD_DIM], axis=0, keepdims=True
                )
            dq_ref[i] = jnp.zeros((length, width), F32)
            return 0

        lax.fori_loop(0, n_blk, one, 0)

    last = jnp.int32(n_blk * length)
    final = (j + 1) * length - 1
    for end in reversed(ends):
        last = jnp.where(end > final, end, last)
    highest = lax.div(last - 1, jnp.int32(length))
    keys, values = qkv_ref[j, 1], qkv_ref[j, 2]
    key_heads = [keys * mask for mask in masks]

    def tile(i, carry):
        d_key, d_value = carry
        start, place = start_rows(ends, i, length, heads)
        queries = by_head(qkv_ref[i, 0] * jnp.asarray(scale, BF16), masks)
        d_out = by_head(do_ref[i], masks)
        lse = jnp.concatenate([lse_ref[i, h : h + 1, :] for h in range(heads)], axis=1)
        delta = jnp.concatenate([delta_ref[i, h : h + 1, :] for h in range(heads)], axis=1)
        scores = dot_nt(keys, queries)
        key = j * length + lax.broadcasted_iota(jnp.int32, scores.shape, 0)
        probs = jnp.exp(jnp.where((key <= place) & (key >= start), scores - lse, NEG))
        d_probs = dot_nt(values, d_out)
        d_scores = (probs * (d_probs - delta)).astype(BF16)
        d_value = d_value + dot(probs.astype(BF16), d_out)
        d_key = d_key + dot(d_scores, queries)
        d_query = dq_ref[i]
        for h in range(heads):
            d_query = d_query + dot_tn(d_scores[:, h * length : (h + 1) * length], key_heads[h])
        dq_ref[i] = d_query
        return d_key, d_value

    zero = jnp.zeros((length, width), F32)
    d_key, d_value = lax.fori_loop(j, highest + 1, tile, (zero, zero))
    out_ref[0, 0] = (dq_ref[j] * scale).astype(BF16)
    out_ref[0, 1] = d_key.astype(BF16)
    out_ref[0, 2] = d_value.astype(BF16)


def attn_bwd(lens, qkv, d_out, attended, lse, row, n_docs):
    n_blk, _, length, width = qkv.shape
    heads = width // HEAD_DIM
    whole = lambda a: pl.BlockSpec(a.shape, lambda j, lens: (0,) * a.ndim)
    return pl.pallas_call(
        functools.partial(attn_bwd_kernel, row, n_docs, heads),
        grid_spec=pltpu.PrefetchScalarGridSpec(
            num_scalar_prefetch=1,
            grid=(n_blk,),
            in_specs=[whole(qkv), whole(d_out), whole(attended), whole(lse)],
            out_specs=pl.BlockSpec((1, 3, length, width), lambda j, lens: (j, 0, 0, 0)),
            scratch_shapes=[
                pltpu.VMEM((n_blk, length, width), F32),
                pltpu.VMEM((n_blk, heads, length), F32),
            ],
        ),
        out_shape=jax.ShapeDtypeStruct((n_blk, 3, length, width), BF16),
        compiler_params=pltpu.CompilerParams(vmem_limit_bytes=VMEM_LIMIT),
        cost_estimate=pl.CostEstimate(flops=2 * 10**10, bytes_accessed=6 * 10**6, transcendentals=10**7),
        name="attn_bwd",
    )(lens, qkv, d_out, attended, lse)


def exchange(values):
    return lax.all_to_all(values, "blk", 0, 0, tiled=True)


def bits_of(axis):
    return lax.axis_size(axis).bit_length() - 1


def halve(current, axis, name, bit):
    size = lax.axis_size(name)
    mine = (lax.axis_index(name) >> bit) & 1
    half = current.shape[axis] // 2
    keep = lax.dynamic_slice_in_dim(current, mine * half, half, axis)
    send = lax.dynamic_slice_in_dim(current, (1 - mine) * half, half, axis)
    got = lax.ppermute(send, name, [(k, k ^ (1 << bit)) for k in range(size)])
    return (keep.astype(F32) + got.astype(F32)).astype(BF16)


def core_first(values):
    n_dp = lax.axis_size("dp")
    tokens, cols = values.shape
    return values.reshape(tokens, n_dp // 2, 2, cols // n_dp).transpose(0, 2, 1, 3).reshape(tokens, cols)


def y_first(values):
    n_blk = lax.axis_size("blk")
    tokens, cols = values.shape
    return values.reshape(tokens, n_blk // 2, 2, cols // n_blk).transpose(0, 2, 1, 3).reshape(tokens, cols)


def scatter_steps(y_early):
    dp_bits, blk_bits = bits_of("dp"), bits_of("blk")
    rest = [("dp", b) for b in reversed(range(1, dp_bits))]
    blk = [("blk", 0)] + [("blk", b) for b in reversed(range(1, blk_bits))]
    if y_early:
        return [("dp", 0)] + blk[:1] + rest + blk[1:]
    return [("dp", 0)] + rest + blk


def scatter(grad, rows_name, y_early):
    n_rows = lax.axis_size(rows_name)
    rows, cols = grad.shape
    current = grad.reshape((n_rows // 2, 2, rows // n_rows, cols))
    for name, bit in scatter_steps(y_early):
        if name != rows_name:
            current = halve(current, 3, name, bit)
        elif bit == 0:
            current = halve(current, 1, name, bit)
        else:
            current = halve(current, 0, name, bit)
    return current.reshape(rows // n_rows, current.shape[3])


def total(values):
    for name in ("dp", "blk"):
        size = lax.axis_size(name)
        for bit in range(bits_of(name)):
            values = values + lax.ppermute(values, name, [(k, k ^ (1 << bit)) for k in range(size)])
    return values


def rms_parts(values):
    inverse_rms = lax.rsqrt(jnp.mean(values * values, axis=-1, keepdims=True) + EPS)
    return values * inverse_rms, inverse_rms


def norm_back(d_normed, normed, inverse_rms):
    return inverse_rms * (d_normed - normed * jnp.mean(d_normed * normed, axis=-1, keepdims=True))


def rope_tables(doc_lengths, offset, length):
    half = HEAD_DIM // 2
    places = offset + jnp.arange(length, dtype=jnp.int32)
    ends = jnp.cumsum(doc_lengths, axis=1)
    start = jnp.max(jnp.where(ends[:, None, :] <= places[None, :, None], ends[:, None, :], 0), axis=2)
    position = (places[None, :] - start).astype(F32).reshape(-1, 1)
    lane = jnp.arange(128, dtype=jnp.int32)
    freq = jnp.power(10000.0, -(lane % half).astype(F32) * 2.0 / HEAD_DIM)
    angles = position * freq[None, :]
    sign = jnp.where(lane % HEAD_DIM < half, -1.0, 1.0)
    return jnp.cos(angles), jnp.sin(angles) * sign[None, :]


def rotate_back(values, cos, sin):
    half = HEAD_DIM // 2
    shaped = values.reshape(values.shape[:2] + (values.shape[2] // HEAD_DIM, 2, half))
    swapped = shaped[:, :, :, ::-1, :].reshape(values.shape)
    return values * cos - swapped * sin


def body(
    hidden_in,
    first_values,
    doc_lengths,
    w_query,
    w_key,
    w_value,
    w_out,
    w_gate,
    w_up,
    w_down,
    attn_gain,
    ffn_gain,
    out_cotangent,
):
    length, rows, model = hidden_in.shape
    n_docs = doc_lengths.shape[1]
    n_blk, n_dp = lax.axis_size("blk"), lax.axis_size("dp")
    width = model // n_blk
    tokens = rows * length
    flat = lambda a: jnp.transpose(a, (1, 0, 2)).reshape(tokens, model)
    unflat = lambda a: jnp.transpose(a.reshape(rows, length, model), (1, 0, 2))
    lens = doc_lengths.reshape(-1)

    resid_in = flat(hidden_in).astype(F32)
    normed_one, inv_one = rms_parts(resid_in)
    normed_in = (normed_one * attn_gain).astype(BF16)
    cos, sin = rope_tables(doc_lengths, lax.axis_index("blk") * length, length)
    *qkv_own, sums = project_qkv(normed_in, flat(first_values), cos, sin, w_query, w_key, w_value, rows, n_blk)
    cot = flat(out_cotangent)

    qkv, attended, lse, gathered = [], [], [], []
    for r in range(rows):
        qkv.append(exchange(qkv_own[r]))
    for r in range(rows):
        o_f, o_low, lse_r = attn_fwd(lens, qkv[r], r, n_docs)
        attended.append(o_f)
        lse.append(lse_r)
        gathered.append(exchange(o_low))
    attn_low = jnp.concatenate([jnp.transpose(g, (1, 0, 2)).reshape(length, model) for g in gathered], axis=0)

    resid_mid = resid_in + dot(attn_low, w_out)
    normed_two, inv_two = rms_parts(resid_mid)
    normed_mid = (normed_two * ffn_gain).astype(BF16)
    gate_pre = dot(normed_mid, w_gate)
    up_pre = dot(normed_mid, w_up)
    gate_act = jax.nn.silu(gate_pre)
    inner_low = (gate_act * up_pre).astype(BF16)
    block_out = (resid_mid + dot(inner_low, w_down)).astype(BF16)
    d_inner = dot_nt(cot, w_down)
    sigmoid_gate = jax.nn.sigmoid(gate_pre)
    d_gate = (d_inner * up_pre * sigmoid_gate * (1.0 + gate_pre * (1.0 - sigmoid_gate))).astype(BF16)
    d_up = (d_inner * gate_act).astype(BF16)
    d_normed_mid = dot_nt(d_gate, w_gate) + dot_nt(d_up, w_up)
    gain_two_grad = jnp.sum(d_normed_mid * normed_two, axis=0)
    d_resid_mid = cot.astype(F32) + norm_back(d_normed_mid * ffn_gain, normed_two, inv_two)
    d_branch = d_resid_mid.astype(BF16)
    d_attn = dot_nt(d_branch, w_out).astype(BF16)

    grads = []
    d_own = []
    for r in range(rows):
        piece = jnp.transpose(d_attn[r * length : (r + 1) * length].reshape(length, n_blk, width), (1, 0, 2))
        d_own.append(exchange(piece))
    mid_cf = core_first(normed_mid)
    grad_down = scatter(dot_tn(inner_low, y_first(cot)).astype(BF16), "dp", False)
    grad_gate = scatter(dot_tn(d_gate, mid_cf).astype(BF16), "blk", False)
    grad_up = scatter(dot_tn(d_up, mid_cf).astype(BF16), "blk", True)
    grad_project = scatter(dot_tn(d_branch, core_first(attn_low)).astype(BF16), "blk", True)

    back = []
    for r in range(rows):
        back.append(exchange(attn_bwd(lens, qkv[r], d_own[r], attended[r], lse[r], r, n_docs)))

    def owned(which, rotated):
        parts = []
        for r in range(rows):
            values = back[r][:, which].astype(F32)
            if rotated:
                at = slice(r * length, (r + 1) * length)
                values = rotate_back(values, cos[at, :width], sin[at, :width])
            parts.append(jnp.transpose(values, (1, 0, 2)).reshape(length, model))
        return jnp.concatenate(parts, axis=0)

    d_query = owned(0, True).astype(BF16)
    d_key = owned(1, True).astype(BF16)
    grad_first = 0.5 * owned(2, False)
    d_value = grad_first.astype(BF16)
    in_cf = core_first(normed_in)
    grad_query = scatter(dot_tn(d_query, in_cf).astype(BF16), "blk", True)
    grad_key = scatter(dot_tn(d_key, in_cf).astype(BF16), "blk", False)
    grad_value = scatter(dot_tn(d_value, in_cf).astype(BF16), "blk", True)
    d_normed_in = dot_nt(d_query, w_query) + dot_nt(d_key, w_key) + dot_nt(d_value, w_value)
    gain_one_grad = jnp.sum(d_normed_in * normed_one, axis=0)
    grad_input = d_resid_mid + norm_back(d_normed_in * attn_gain, normed_one, inv_one)

    squares = jnp.sum(sums, axis=(0, 2))
    squares = jnp.concatenate([squares, jnp.zeros((126,), F32)])
    early = total(jnp.concatenate([gain_two_grad, squares]))
    gain_one = total(gain_one_grad)
    n_entries = n_blk * length * rows * n_dp * model
    return (
        block_out_shape(unflat(block_out)),
        unflat(grad_input),
        unflat(grad_first),
        grad_query.T.astype(F32),
        grad_key.T.astype(F32),
        grad_value.T.astype(F32),
        grad_project.T.astype(F32),
        grad_gate.T.astype(F32),
        grad_up.T.astype(F32),
        grad_down.astype(F32),
        gain_one,
        early[:model],
        early[model] / n_entries,
        early[model + 1] / n_entries,
    )


def block_out_shape(values):
    return values


def solution(mesh):
    tokens = P("blk", "dp", None)
    return jax.shard_map(
        body,
        mesh=mesh,
        in_specs=(tokens, tokens, P("dp", None)) + (P(),) * 9 + (tokens,),
        out_specs=(tokens,) * 3 + (P("dp", "blk"),) * 7 + (P(),) * 4,
        check_vma=False,
    )
```

time: 1750 us -> 568 us (0.32)
  waiting for transfers between devices: 1110 us -> 121 us
  matrix products: 317 us -> 80 us
  Pallas kernels: 0 us -> 72.8 us
  starting transfers between devices: 1.81 us -> 74.3 us
  local copies, waits for them, and re-layouts: 150 us -> 108 us
  other arithmetic: 89.3 us -> 54.9 us
    reduce_scatter x8 -> x0, waiting for transfers between devices: 510 us -> none  [the longest x1 252 us: body(): lax.psum_scatter(terms.astype(jnp.bfloat16), 'blk', scatter_dimension=0,...]
    unnamed x24 -> x0, waiting for transfers between devices: 385 us -> none
    dot_general x49 -> x18, matrix products: 317 us -> 80 us  [the longest x7 30.5 us: dot_nt(): lax.dot_general(a, b, (((1,), (1,)), ((), ())), preferred_element_type=F32)]
    all_gather x2 -> x0, waiting for transfers between devices: 214 us -> none  [the longest x1 114 us: body(): key_piece = lax.all_gather(keys_rot, 'blk', axis=0, tiled=True)]
    ppermute x0 -> x45, waiting for transfers between devices: none -> 86.8 us  [the longest x35 82 us: halve(): got = lax.ppermute(send, name, [(k, k ^ 1 << bit) for k in range(size)])]
    pallas_call x0 -> x5, Pallas kernels: none -> 72.8 us  [the longest x2 35.4 us: attn_bwd(): pl.pallas_call(functools.partial(attn_bwd_kernel, row, n_docs, heads), gr...]
    unnamed x95 -> x132, local copies, waits for them, and re-layouts: 72 us -> 17.1 us
    all_to_all x0 -> x1, blocking collectives: none -> 44.4 us  [exchange(): return lax.all_to_all(values, 'blk', 0, 0, tiled=True)]
  transfers between devices with their start and end apart: 17 -> 52, of which waited for: 17 -> 20; matrix products, arithmetic and copies ran while one was open for 8% -> 28% of each run, Pallas kernels for 0% -> 12%
where the time goes in v1:
time: 568 us; the launch traced here: 561 us
  waiting for transfers between devices  121 us (21%)
  local copies, waits for them, and re-layouts  108 us (19%)
  matrix products  80 us (14%)
  starting transfers between devices  74.3 us (13%)
  Pallas kernels  72.8 us (13%)
  other arithmetic  54.9 us (10%)
  blocking collectives  44.4 us (8%)
  between operations  5.71 us (1%)
    ppermute x35, waiting for transfers between devices, halve(): got = lax.ppermute(send, name, [(k, k ^ 1 << bit) for k in range(size)])  82 us
    all_to_all x1, blocking collectives, exchange(): return lax.all_to_all(values, 'blk', 0, 0, tiled=True)  44.4 us
    pallas_call x2, Pallas kernels, attn_bwd(): pl.pallas_call(functools.partial(attn_bwd_kernel, row, n_docs, heads), gr...  35.4 us
    all_to_all x7, starting transfers between devices, exchange(): return lax.all_to_all(values, 'blk', 0, 0, tiled=True)  35.2 us
    all_to_all x7, waiting for transfers between devices, exchange(): return lax.all_to_all(values, 'blk', 0, 0, tiled=True)  34.4 us
    dot_general x7, matrix products, dot_nt(): lax.dot_general(a, b, (((1,), (1,)), ((), ())), preferred_element_type=F32)  30.5 us
    pallas_call x2, Pallas kernels, attn_fwd(): pl.pallas_call(functools.partial(attn_fwd_kernel, row, n_docs, heads), gr...  29.4 us
    dot_general x4, matrix products, dot(): return jnp.dot(a, b, preferred_element_type=F32)  25.8 us
  transfers between devices with their start and end apart: 52, of which 20 were waited for; matrix products, arithmetic and copies ran while one was open for 28% of the time, Pallas kernels for 12%

profile of v1, /device:TPU:0, one launch (start us, length us, event | category | flops | bytes accessed | tf_op | source)
XLA Modules:
  0.0 560.7 jit_solution(12440246619504159890)
XLA Ops:
  12.2 8.0 %qkv.1 = (bf16[8,3,256,128]{3,2,1,0:T(8,128)(2,1)}, bf16[8,3,256,128]{3,2,1,0:T(8,128)(2,1)}, f32[4,2,256]{2,1,0:T(2,128)}) custom-call(bf16[512,1024]{1,0:T(8,128)(2,1)} %multiply_convert_fusion.5.normed_ref, bf16[512,1024]{1,0:T(8,128)(2,1)} %bitcast.258, f32[512,128]{1,0:T(8,128)} %get-tuple-element.122.cos_ref, f32[512,128]{1,0:T(8,128)} %get-tuple-element.121.sin_ref, ...), custom_call_target="tpu_custom_call" | custom-call | flops 3221225472 | bytes 11534336 | tf_op jit(solution)/shard_map/qkv/pallas_call | solution.py:74
  20.2 44.4 %all_to_all.40.qkv_ref = bf16[8,3,256,128]{3,2,1,0:T(8,128)(2,1)} all-to-all(bf16[8,3,256,128]{3,2,1,0:T(8,128)(2,1)} %get-tuple-element.25), channel_id=1, replica_groups=mesh['dp'=4,'blk'=8] {'blk'}, dimensions={0} | all-to-all | bytes 3145728 | tf_op jit(solution)/shard_map/all_to_all | solution.py:274
  69.5 14.4 %attn_fwd.3 = (f32[8,256,128]{2,1,0:T(8,128)}, bf16[8,256,128]{2,1,0:T(8,128)(2,1)}, f32[8,2,256]{2,1,0:T(2,128)}) custom-call(s32[16]{0:T(128)} %reshape.294.lens_ref, bf16[8,3,256,128]{3,2,1,0:T(8,128)(2,1)} %all_to_all.40.qkv_ref), custom_call_target="tpu_custom_call" | custom-call | flops 10000000000 | bytes 3000000 | tf_op jit(solution)/shard_map/attn_fwd/pallas_call | solution.py:175
  83.9 21.2 %all-to-all-done.qkv_ref = bf16[8,3,256,128]{3,2,1,0:T(8,128)(2,1)} async-done(((bf16[8,3,256,128]{3,2,1,0:T(8,128)(2,1)}), bf16[8,3,256,128]{3,2,1,0:T(8,128)(2,1)}, u32[]{:S(2)}, u32[]{:S(2)}) %all-to-all-start) | async-done | bytes 1572896 | tf_op jit(solution)/shard_map/all_to_all | solution.py:274
  108.6 14.9 %attn_fwd.2 = (f32[8,256,128]{2,1,0:T(8,128)}, bf16[8,256,128]{2,1,0:T(8,128)(2,1)}, f32[8,2,256]{2,1,0:T(2,128)}) custom-call(s32[16]{0:T(128)} %reshape.294.lens_ref, bf16[8,3,256,128]{3,2,1,0:T(8,128)(2,1)} %all-to-all-done.qkv_ref), custom_call_target="tpu_custom_call" | custom-call | flops 10000000000 | bytes 3000000 | tf_op jit(solution)/shard_map/attn_fwd/pallas_call | solution.py:175
  123.5 6.4 %all-to-all-start.1 = ((bf16[8,256,128]{2,1,0:T(8,128)(2,1)}), bf16[8,256,128]{2,1,0:T(8,128)(2,1)}, u32[]{:S(2)}, u32[]{:S(2)}) async-start(bf16[8,256,128]{2,1,0:T(8,128)(2,1)} %get-tuple-element.24), calls=%async_computation.1 | async-start | bytes 1048576 | tf_op jit(solution)/shard_map/all_to_all | solution.py:274
  153.6 4.5 multiply_reduce_fusion.4
  163.6 6.2 %fusion.52 = f32[512,2816]{1,0:T(8,128)S(1)} fusion(bf16[512,1024]{1,0:T(8,128)(2,1)} %multiply_convert_fusion.4, bf16[1024,2816]{1,0:T(8,128)(2,1)} %param.20), kind=kOutput, calls=%fused_computation.189 | convolution fusion | flops 2952790016 | bytes 12582912 | tf_op jit(solution)/shard_map/dot_general | solution.py:20
  169.9 7.8 %fusion.53 = f32[512,2816]{1,0:T(8,128)} fusion(bf16[512,1024]{1,0:T(8,128)(2,1)S(1)} %copy-done.19, bf16[1024,2816]{1,0:T(8,128)(2,1)} %param.21), kind=kOutput, calls=%fused_computation.190 | convolution fusion | flops 2952790016 | bytes 12582912 | tf_op jit(solution)/shard_map/dot_general | solution.py:20
  177.7 10.3 %multiply_convert_fusion = (bf16[512,2816]{1,0:T(8,128)(2,1)}, bf16[512,2816]{1,0:T(8,128)(2,1)}, bf16[512,2816]{1,0:T(8,128)(2,1)}) fusion(f32[512,2816]{1,0:T(8,128)S(1)} %fusion.52, f32[512,2816]{1,0:T(8,128)} %fusion.53, bf16[512,1024]{1,0:T(8,128)(2,1)S(1)} %bitcast.213, bf16[2816,1024]{1,0:T(8,128)(2,1)S(1)} %bitcast.282), kind=kOutput, calls=%fused_computation.3 | convolution fusion | flops 2974416896 | bytes 27000832 | tf_op jit(solution)/shard_map/dot_general | solution.py:24
  188.0 6.3 %fusion.54 = f32[512,1024]{1,0:T(8,128)} fusion(bf16[512,2816]{1,0:T(8,128)(2,1)} %get-tuple-element.93, bf16[1024,2816]{1,0:T(8,128)(2,1)S(1)} %bitcast.278), kind=kOutput, calls=%fused_computation.191 | convolution fusion | flops 2952790016 | bytes 10747904 | tf_op jit(solution)/shard_map/dot_general | solution.py:24
  198.0 8.0 %convolution_convert_fusion.2 = bf16[2816,1024]{1,0:T(8,128)(2,1)} fusion(bf16[512,2816]{1,0:T(8,128)(2,1)} %get-tuple-element.93, bf16[512,1024]{0,1:T(8,128)(2,1)} %bitcast.259), kind=kOutput, calls=%fused_computation.10 | convolution fusion | flops 2955673600 | bytes 9699328 | tf_op jit(solution)/shard_map/dot_general | solution.py:28
  206.0 5.3 convolution_convert_fusion.1
  211.4 5.1 multiply_reduce_fusion
  226.5 6.0 %all-to-all-start.6 = ((bf16[8,256,128]{2,1,0:T(8,128)(2,1)}), bf16[8,256,128]{2,1,0:T(8,128)(2,1)}, u32[]{:S(2)}, u32[]{:S(2)}) async-start(bf16[8,256,128]{2,1,0:T(8,128)(2,1)} %bitcast.21), calls=%async_computation.6 | async-start | bytes 1048576 | tf_op jit(solution)/shard_map/all_to_all | solution.py:274
  244.1 5.2 convolution_convert_fusion
  253.7 4.5 all-to-all-start.4
  258.2 17.4 %attn_bwd.3 = bf16[8,3,256,128]{3,2,1,0:T(8,128)(2,1)} custom-call(s32[16]{0:T(128)} %reshape.294.lens_ref, bf16[8,3,256,128]{3,2,1,0:T(8,128)(2,1)} %all_to_all.40.qkv_ref, bf16[8,256,128]{2,1,0:T(8,128)(2,1)} %all-to-all-done.6.do_ref, f32[8,256,128]{2,1,0:T(8,128)} %get-tuple-element.29.o_ref, f32[8,2,256]{2,1,0:T(2,128)} %get-tuple-element.30.lse_ref), custom_call_target="tpu_custom_call" | custom-call | flops 20000000000 | bytes 6000000 | tf_op jit(solution)/shard_map/attn_bwd/pallas_call | solution.py:254
  276.4 6.0 %all-to-all-start.7 = ((bf16[8,3,256,128]{3,2,1,0:T(8,128)(2,1)}), bf16[8,3,256,128]{3,2,1,0:T(8,128)(2,1)S(1)}, u32[]{:S(2)}, u32[]{:S(2)}) async-start(bf16[8,3,256,128]{3,2,1,0:T(8,128)(2,1)} %attn_bwd.3), calls=%async_computation.7 | async-start | bytes 3145728 | tf_op jit(solution)/shard_map/all_to_all | solution.py:274
  292.3 18.0 %attn_bwd.2 = bf16[8,3,256,128]{3,2,1,0:T(8,128)(2,1)} custom-call(s32[16]{0:T(128)} %reshape.294.lens_ref, bf16[8,3,256,128]{3,2,1,0:T(8,128)(2,1)} %all-to-all-done.qkv_ref, bf16[8,256,128]{2,1,0:T(8,128)(2,1)} %copy-done.30, f32[8,256,128]{2,1,0:T(8,128)} %get-tuple-element.27.o_ref, f32[8,2,256]{2,1,0:T(2,128)} %get-tuple-element.28.lse_ref), custom_call_target="tpu_custom_call" | custom-call | flops 20000000000 | bytes 6000000 | tf_op jit(solution)/shard_map/attn_bwd/pallas_call | solution.py:254
  310.5 13.2 %all-to-all-done.7 = bf16[8,3,256,128]{3,2,1,0:T(8,128)(2,1)S(1)} async-done(((bf16[8,3,256,128]{3,2,1,0:T(8,128)(2,1)}), bf16[8,3,256,128]{3,2,1,0:T(8,128)(2,1)S(1)}, u32[]{:S(2)}, u32[]{:S(2)}) %all-to-all-start.7) | async-done | bytes 1572896 | tf_op jit(solution)/shard_map/all_to_all | solution.py:274
  323.7 4.5 all-to-all-start.5
  328.2 7.2 %add_convert_fusion.10 = bf16[512,1024]{1,0:T(8,128)(2,1)S(1)} fusion(f32[512,1024]{1,0:T(8,128)} %get-tuple-element.124, bf16[512,2816]{1,0:T(8,128)(2,1)} %get-tuple-element.94, bf16[2816,1024]{1,0:T(8,128)(2,1)} %param.22), kind=kOutput, calls=%fused_computation.33 | convolution fusion | flops 2953838592 | bytes 11796480 | tf_op jit(solution)/shard_map/dot_general | solution.py:20
  342.0 11.0 %collective-permute-done.19 = bf16[1,1,128,256]{2,3,1,0:T(8,128)(2,1)S(1)} collective-permute-done((bf16[1,1,128,256]{2,3,1,0:T(8,128)(2,1)S(1)}, bf16[1,1,128,256]{2,3,1,0:T(8,128)(2,1)S(1)}, u32[]{:S(2)}, u32[]{:S(2)}) %collective-permute-start.19) | collective-permute-done | bytes 65568 | tf_op jit(solution)/shard_map/ppermute | solution.py:287
  444.8 4.6 copy.224
  471.6 7.7 %collective-permute-done.22 = bf16[4,1,352,256]{3,2,1,0:T(8,128)(2,1)S(1)} collective-permute-done((bf16[4,1,352,256]{3,2,1,0:T(8,128)(2,1)S(1)}, bf16[4,1,352,256]{3,2,1,0:T(8,128)(2,1)S(1)}, u32[]{:S(2)}, u32[]{:S(2)}) %collective-permute-start.22) | collective-permute-done | bytes 720928 | tf_op jit(solution)/shard_map/ppermute | solution.py:287
  482.2 12.5 %collective-permute-done.32 = bf16[1,1,704,512]{3,2,1,0:T(8,128)(2,1)S(1)} collective-permute-done((bf16[1,1,704,512]{3,2,1,0:T(8,128)(2,1)S(1)}, bf16[1,1,704,512]{3,2,1,0:T(8,128)(2,1)S(1)}, u32[]{:S(2)}, u32[]{:S(2)}) %collective-permute-start.32) | collective-permute-done | bytes 720928 | tf_op jit(solution)/shard_map/ppermute | solution.py:287
  495.0 10.9 %collective-permute-done.1 = bf16[4,1,128,512]{2,3,1,0:T(8,128)(2,1)S(1)} collective-permute-done((bf16[4,1,128,512]{2,3,1,0:T(8,128)(2,1)S(1)}, bf16[4,1,128,512]{2,3,1,0:T(8,128)(2,1)S(1)}, u32[]{:S(2)}, u32[]{:S(2)}) %collective-permute-start.1) | collective-permute-done | bytes 524320 | tf_op jit(solution)/shard_map/ppermute | solution.py:287
  507.0 9.9 %collective-permute-done.11 = bf16[4,1,128,512]{2,3,1,0:T(8,128)(2,1)S(1)} collective-permute-done((bf16[4,1,128,512]{2,3,1,0:T(8,128)(2,1)S(1)}, bf16[4,1,128,512]{2,3,1,0:T(8,128)(2,1)S(1)}, u32[]{:S(2)}, u32[]{:S(2)}) %collective-permute-start.11) | collective-permute-done | bytes 524320 | tf_op jit(solution)/shard_map/ppermute | solution.py:287
  518.7 4.5 collective-permute-done.28
  523.3 7.6 %collective-permute-done.33 = bf16[1,1,704,256]{3,2,1,0:T(8,128)(2,1)S(1)} collective-permute-done((bf16[1,1,704,256]{3,2,1,0:T(8,128)(2,1)S(1)}, bf16[1,1,704,256]{3,2,1,0:T(8,128)(2,1)S(1)}, u32[]{:S(2)}, u32[]{:S(2)}) %collective-permute-start.33) | collective-permute-done | bytes 360480 | tf_op jit(solution)/shard_map/ppermute | solution.py:287
  537.4 5.2 collective-permute-done.29
  (382 shorter events, 236.2 us)
Async XLA Ops:
  64.6 40.5 %all-to-all-start = ((bf16[8,3,256,128]{3,2,1,0:T(8,128)(2,1)}), bf16[8,3,256,128]{3,2,1,0:T(8,128)(2,1)}, u32[]{:S(2)}, u32[]{:S(2)}) async-start(bf16[8,3,256,128]{3,2,1,0:T(8,128)(2,1)} %get-tuple-element.23), calls=%async_computation | async-start | bytes 3145728 | tf_op jit(solution)/shard_map/all_to_all | solution.py:274
  105.1 18.5 %all-to-all-start.3 = ((bf16[8,256,128]{2,1,0:T(8,128)(2,1)}), bf16[8,256,128]{2,1,0:T(8,128)(2,1)S(1)}, u32[]{:S(2)}, u32[]{:S(2)}) async-start(bf16[8,256,128]{2,1,0:T(8,128)(2,1)} %get-tuple-element.26), calls=%async_computation.3 | async-start | bytes 1048576 | tf_op jit(solution)/shard_map/all_to_all | solution.py:274
  123.5 28.0 %all-to-all-start.1 = ((bf16[8,256,128]{2,1,0:T(8,128)(2,1)}), bf16[8,256,128]{2,1,0:T(8,128)(2,1)}, u32[]{:S(2)}, u32[]{:S(2)}) async-start(bf16[8,256,128]{2,1,0:T(8,128)(2,1)} %get-tuple-element.24), calls=%async_computation.1 | async-start | bytes 1048576 | tf_op jit(solution)/shard_map/all_to_all | solution.py:274
  224.1 27.4 %collective-permute-start.15 = (bf16[4,2,128,512]{2,3,1,0:T(8,128)(2,1)}, bf16[4,2,128,512]{2,3,1,0:T(8,128)(2,1)}, u32[]{:S(2)}, u32[]{:S(2)}) collective-permute-start(bf16[4,2,128,512]{2,3,1,0:T(8,128)(2,1)} %copy.234), channel_id=1, source_target_pairs={{0,8},{8,0},{16,24},{24,16},{1,9},{9,1},{17,25},{25,17},{2,10},{10... | collective-permute-start | bytes 3145736 | tf_op jit(solution)/shard_map/ppermute | solution.py:287
  226.5 27.1 %all-to-all-start.6 = ((bf16[8,256,128]{2,1,0:T(8,128)(2,1)}), bf16[8,256,128]{2,1,0:T(8,128)(2,1)}, u32[]{:S(2)}, u32[]{:S(2)}) async-start(bf16[8,256,128]{2,1,0:T(8,128)(2,1)} %bitcast.21), calls=%async_computation.6 | async-start | bytes 1048576 | tf_op jit(solution)/shard_map/all_to_all | solution.py:274
  237.8 115.9 %collective-permute-start.20 = (bf16[4,2,352,512]{3,2,1,0:T(8,128)(2,1)}, bf16[4,2,352,512]{3,2,1,0:T(8,128)(2,1)}, u32[]{:S(2)}, u32[]{:S(2)}) collective-permute-start(bf16[4,2,352,512]{3,2,1,0:T(8,128)(2,1)} %constant_dynamic-slice_fusion.14), channel_id=1, source_target_pairs={{0,8},{8,0},{16,24},{24,16},{1,9},{9,1},{17,25},{25,17},{2,10},{10... | collective-permute-start | bytes 8650760 | tf_op jit(solution)/shard_map/ppermute | solution.py:287
  242.0 118.5 %collective-permute-start.25 = (bf16[4,2,352,512]{3,2,1,0:T(8,128)(2,1)}, bf16[4,2,352,512]{3,2,1,0:T(8,128)(2,1)}, u32[]{:S(2)}, u32[]{:S(2)}) collective-permute-start(bf16[4,2,352,512]{3,2,1,0:T(8,128)(2,1)} %constant_dynamic-slice_fusion.9), channel_id=1, source_target_pairs={{0,8},{8,0},{16,24},{24,16},{1,9},{9,1},{17,25},{25,17},{2,10},{10... | collective-permute-start | bytes 8650760 | tf_op jit(solution)/shard_map/ppermute | solution.py:287
  249.9 36.1 %collective-permute-start.43 = (f32[1152]{0:T(1024)S(1)}, f32[1152]{0:T(1024)S(1)}, u32[]{:S(2)}, u32[]{:S(2)}) collective-permute-start(f32[1152]{0:T(1024)S(1)} %add.404), channel_id=1, source_target_pairs={{0,2},{1,3},{2,0},{3,1},{4,6},{5,7},{6,4},{7,5},{8,10},{9,11},{10,... | collective-permute-start | bytes 13832 | tf_op jit(solution)/shard_map/ppermute | solution.py:330
  253.0 36.0 %collective-permute-start.16 = (bf16[4,1,128,512]{2,3,1,0:T(8,128)(2,1)S(1)}, bf16[4,1,128,512]{2,3,1,0:T(8,128)(2,1)}, u32[]{:S(2)}, u32[]{:S(2)}) collective-permute-start(bf16[4,1,128,512]{2,3,1,0:T(8,128)(2,1)S(1)} %constant_dynamic-slice_fusion.18), channel_id=1, source_target_pairs={{0,1},{1,0},{2,3},{3,2},{4,5},{5,4},{6,7},{7,6},{8,9},{9,8},{10,11... | collective-permute-start | bytes 1572872 | tf_op jit(solution)/shard_map/ppermute | solution.py:287
  253.7 21.9 %all-to-all-start.4 = ((bf16[8,256,128]{2,1,0:T(8,128)(2,1)}), bf16[8,256,128]{2,1,0:T(8,128)(2,1)S(1)}, u32[]{:S(2)}, u32[]{:S(2)}) async-start(bf16[8,256,128]{2,1,0:T(8,128)(2,1)} %bitcast.14), calls=%async_computation.4 | async-start | bytes 1048576 | tf_op jit(solution)/shard_map/all_to_all | solution.py:274
  276.4 47.3 %all-to-all-start.7 = ((bf16[8,3,256,128]{3,2,1,0:T(8,128)(2,1)}), bf16[8,3,256,128]{3,2,1,0:T(8,128)(2,1)S(1)}, u32[]{:S(2)}, u32[]{:S(2)}) async-start(bf16[8,3,256,128]{3,2,1,0:T(8,128)(2,1)} %attn_bwd.3), calls=%async_computation.7 | async-start | bytes 3145728 | tf_op jit(solution)/shard_map/all_to_all | solution.py:274
  286.0 81.1 %collective-permute-start.30 = (bf16[2,1,704,1024]{3,2,1,0:T(8,128)(2,1)}, bf16[2,1,704,1024]{3,2,1,0:T(8,128)(2,1)}, u32[]{:S(2)}, u32[]{:S(2)}) collective-permute-start(bf16[2,1,704,1024]{3,2,1,0:T(8,128)(2,1)} %constant_dynamic-slice_fusion.4), channel_id=1, source_target_pairs={{0,8},{8,0},{16,24},{24,16},{1,9},{9,1},{17,25},{25,17},{2,10},{10... | collective-permute-start | bytes 8650760 | tf_op jit(solution)/shard_map/ppermute | solution.py:287
  286.0 51.5 %collective-permute-start.44 = (f32[1152]{0:T(1024)S(1)}, f32[1152]{0:T(1024)S(1)}, u32[]{:S(2)}, u32[]{:S(2)}) collective-permute-start(f32[1152]{0:T(1024)S(1)} %add.405), channel_id=1, source_target_pairs={{0,4},{1,5},{2,6},{3,7},{4,0},{5,1},{6,2},{7,3},{8,12},{9,13},{10,... | collective-permute-start | bytes 13832 | tf_op jit(solution)/shard_map/ppermute | solution.py:330
  290.2 20.1 %collective-permute-start.17 = (bf16[4,1,128,256]{2,3,1,0:T(8,128)(2,1)S(1)}, bf16[4,1,128,256]{2,3,1,0:T(8,128)(2,1)S(1)}, u32[]{:S(2)}, u32[]{:S(2)}) collective-permute-start(bf16[4,1,128,256]{2,3,1,0:T(8,128)(2,1)S(1)} %constant_dynamic-slice_fusion.17), channel_id=1, source_target_pairs={{0,16},{8,24},{16,0},{24,8},{1,17},{9,25},{17,1},{25,9},{2,18},{10... | collective-permute-start | bytes 786440 | tf_op jit(solution)/shard_map/ppermute | solution.py:287
  310.4 27.7 %collective-permute-start.18 = (bf16[2,1,128,256]{2,3,1,0:T(8,128)(2,1)S(1)}, bf16[2,1,128,256]{2,3,1,0:T(8,128)(2,1)S(1)}, u32[]{:S(2)}, u32[]{:S(2)}) collective-permute-start(bf16[2,1,128,256]{2,3,1,0:T(8,128)(2,1)S(1)} %constant_dynamic-slice_fusion.16), channel_id=1, source_target_pairs={{0,4},{1,5},{2,6},{3,7},{4,0},{5,1},{6,2},{7,3},{8,12},{9,13},{10,... | collective-permute-start | bytes 393224 | tf_op jit(solution)/shard_map/ppermute | solution.py:287
  323.7 51.2 %all-to-all-start.5 = ((bf16[8,3,256,128]{3,2,1,0:T(8,128)(2,1)}), bf16[8,3,256,128]{3,2,1,0:T(8,128)(2,1)}, u32[]{:S(2)}, u32[]{:S(2)}) async-start(bf16[8,3,256,128]{3,2,1,0:T(8,128)(2,1)} %attn_bwd.2), calls=%async_computation.5 | async-start | bytes 3145728 | tf_op jit(solution)/shard_map/all_to_all | solution.py:274
  358.5 99.5 %collective-permute-start.21 = (bf16[4,2,352,256]{3,2,1,0:T(8,128)(2,1)}, bf16[4,2,352,256]{3,2,1,0:T(8,128)(2,1)}, u32[]{:S(2)}, u32[]{:S(2)}) collective-permute-start(bf16[4,2,352,256]{3,2,1,0:T(8,128)(2,1)} %constant_dynamic-slice_fusion.13), channel_id=1, source_target_pairs={{0,16},{8,24},{16,0},{24,8},{1,17},{9,25},{17,1},{25,9},{2,18},{10... | collective-permute-start | bytes 4325384 | tf_op jit(solution)/shard_map/ppermute | solution.py:287
  365.4 94.9 %collective-permute-start.26 = (bf16[4,1,352,512]{3,2,1,0:T(8,128)(2,1)}, bf16[4,1,352,512]{3,2,1,0:T(8,128)(2,1)}, u32[]{:S(2)}, u32[]{:S(2)}) collective-permute-start(bf16[4,1,352,512]{3,2,1,0:T(8,128)(2,1)} %constant_dynamic-slice_fusion.8), channel_id=1, source_target_pairs={{0,1},{1,0},{2,3},{3,2},{4,5},{5,4},{6,7},{7,6},{8,9},{9,8},{10,11... | collective-permute-start | bytes 4325384 | tf_op jit(solution)/shard_map/ppermute | solution.py:287
  371.7 91.3 %collective-permute-start.31 = (bf16[1,1,704,1024]{3,2,1,0:T(8,128)(2,1)}, bf16[1,1,704,1024]{3,2,1,0:T(8,128)(2,1)}, u32[]{:S(2)}, u32[]{:S(2)}) collective-permute-start(bf16[1,1,704,1024]{3,2,1,0:T(8,128)(2,1)} %constant_dynamic-slice_fusion.3), channel_id=1, source_target_pairs={{0,16},{8,24},{16,0},{24,8},{1,17},{9,25},{17,1},{25,9},{2,18},{10... | collective-permute-start | bytes 4325384 | tf_op jit(solution)/shard_map/ppermute | solution.py:287
  434.5 22.2 %collective-permute-start.39 = (f32[1024]{0:T(1024)S(1)}, f32[1024]{0:T(1024)S(1)}, u32[]{:S(2)}, u32[]{:S(2)}) collective-permute-start(f32[1024]{0:T(1024)S(1)} %add.400), channel_id=1, source_target_pairs={{0,4},{1,5},{2,6},{3,7},{4,0},{5,1},{6,2},{7,3},{8,12},{9,13},{10,... | collective-permute-start | bytes 12296 | tf_op jit(solution)/shard_map/ppermute | solution.py:330
  460.3 19.0 %collective-permute-start.22 = (bf16[4,1,352,256]{3,2,1,0:T(8,128)(2,1)S(1)}, bf16[4,1,352,256]{3,2,1,0:T(8,128)(2,1)S(1)}, u32[]{:S(2)}, u32[]{:S(2)}) collective-permute-start(bf16[4,1,352,256]{3,2,1,0:T(8,128)(2,1)S(1)} %constant_dynamic-slice_fusion.12), channel_id=1, source_target_pairs={{0,1},{1,0},{2,3},{3,2},{4,5},{5,4},{6,7},{7,6},{8,9},{9,8},{10,11... | collective-permute-start | bytes 2162696 | tf_op jit(solution)/shard_map/ppermute | solution.py:287
  463.0 19.0 %collective-permute-start.27 = (bf16[4,1,352,256]{3,2,1,0:T(8,128)(2,1)S(1)}, bf16[4,1,352,256]{3,2,1,0:T(8,128)(2,1)S(1)}, u32[]{:S(2)}, u32[]{:S(2)}) collective-permute-start(bf16[4,1,352,256]{3,2,1,0:T(8,128)(2,1)S(1)} %constant_dynamic-slice_fusion.7), channel_id=1, source_target_pairs={{0,16},{8,24},{16,0},{24,8},{1,17},{9,25},{17,1},{25,9},{2,18},{10... | collective-permute-start | bytes 2162696 | tf_op jit(solution)/shard_map/ppermute | solution.py:287
  465.7 29.0 %collective-permute-start.32 = (bf16[1,1,704,512]{3,2,1,0:T(8,128)(2,1)S(1)}, bf16[1,1,704,512]{3,2,1,0:T(8,128)(2,1)S(1)}, u32[]{:S(2)}, u32[]{:S(2)}) collective-permute-start(bf16[1,1,704,512]{3,2,1,0:T(8,128)(2,1)S(1)} %constant_dynamic-slice_fusion.2), channel_id=1, source_target_pairs={{0,1},{1,0},{2,3},{3,2},{4,5},{5,4},{6,7},{7,6},{8,9},{9,8},{10,11... | collective-permute-start | bytes 2162696 | tf_op jit(solution)/shard_map/ppermute | solution.py:287
  468.6 37.3 %collective-permute-start.1 = (bf16[4,1,128,512]{2,3,1,0:T(8,128)(2,1)S(1)}, bf16[4,1,128,512]{2,3,1,0:T(8,128)(2,1)S(1)}, u32[]{:S(2)}, u32[]{:S(2)}) collective-permute-start(bf16[4,1,128,512]{2,3,1,0:T(8,128)(2,1)S(1)} %constant_dynamic-slice_fusion.36), channel_id=1, source_target_pairs={{0,1},{1,0},{2,3},{3,2},{4,5},{5,4},{6,7},{7,6},{8,9},{9,8},{10,11... | collective-permute-start | bytes 1572872 | tf_op jit(solution)/shard_map/ppermute | solution.py:287
  469.8 36.3 %collective-permute-start.6 = (bf16[4,2,128,256]{2,3,1,0:T(8,128)(2,1)S(1)}, bf16[4,2,128,256]{2,3,1,0:T(8,128)(2,1)S(1)}, u32[]{:S(2)}, u32[]{:S(2)}) collective-permute-start(bf16[4,2,128,256]{2,3,1,0:T(8,128)(2,1)S(1)} %constant_dynamic-slice_fusion.30), channel_id=1, source_target_pairs={{0,16},{8,24},{16,0},{24,8},{1,17},{9,25},{17,1},{25,9},{2,18},{10... | collective-permute-start | bytes 1572872 | tf_op jit(solution)/shard_map/ppermute | solution.py:287
  479.3 37.6 %collective-permute-start.11 = (bf16[4,1,128,512]{2,3,1,0:T(8,128)(2,1)S(1)}, bf16[4,1,128,512]{2,3,1,0:T(8,128)(2,1)S(1)}, u32[]{:S(2)}, u32[]{:S(2)}) collective-permute-start(bf16[4,1,128,512]{2,3,1,0:T(8,128)(2,1)S(1)} %constant_dynamic-slice_fusion.24), channel_id=1, source_target_pairs={{0,1},{1,0},{2,3},{3,2},{4,5},{5,4},{6,7},{7,6},{8,9},{9,8},{10,11... | collective-permute-start | bytes 1572872 | tf_op jit(solution)/shard_map/ppermute | solution.py:287
  482.0 35.9 %collective-permute-start.23 = (bf16[2,1,352,256]{3,2,1,0:T(8,128)(2,1)S(1)}, bf16[2,1,352,256]{3,2,1,0:T(8,128)(2,1)S(1)}, u32[]{:S(2)}, u32[]{:S(2)}) collective-permute-start(bf16[2,1,352,256]{3,2,1,0:T(8,128)(2,1)S(1)} %constant_dynamic-slice_fusion.11), channel_id=1, source_target_pairs={{0,4},{1,5},{2,6},{3,7},{4,0},{5,1},{6,2},{7,3},{8,12},{9,13},{10,... | collective-permute-start | bytes 1081352 | tf_op jit(solution)/shard_map/ppermute | solution.py:287
  494.7 28.4 %collective-permute-start.28 = (bf16[2,1,352,256]{3,2,1,0:T(8,128)(2,1)S(1)}, bf16[2,1,352,256]{3,2,1,0:T(8,128)(2,1)S(1)}, u32[]{:S(2)}, u32[]{:S(2)}) collective-permute-start(bf16[2,1,352,256]{3,2,1,0:T(8,128)(2,1)S(1)} %constant_dynamic-slice_fusion.6), channel_id=1, source_target_pairs={{0,4},{1,5},{2,6},{3,7},{4,0},{5,1},{6,2},{7,3},{8,12},{9,13},{10,... | collective-permute-start | bytes 1081352 | tf_op jit(solution)/shard_map/ppermute | solution.py:287
  506.0 24.9 %collective-permute-start.33 = (bf16[1,1,704,256]{3,2,1,0:T(8,128)(2,1)S(1)}, bf16[1,1,704,256]{3,2,1,0:T(8,128)(2,1)S(1)}, u32[]{:S(2)}, u32[]{:S(2)}) collective-permute-start(bf16[1,1,704,256]{3,2,1,0:T(8,128)(2,1)S(1)} %constant_dynamic-slice_fusion.1), channel_id=1, source_target_pairs={{0,4},{1,5},{2,6},{3,7},{4,0},{5,1},{6,2},{7,3},{8,12},{9,13},{10,... | collective-permute-start | bytes 1081352 | tf_op jit(solution)/shard_map/ppermute | solution.py:287
  506.2 24.9 %collective-permute-start.2 = (bf16[4,1,128,256]{2,3,1,0:T(8,128)(2,1)S(1)}, bf16[4,1,128,256]{2,3,1,0:T(8,128)(2,1)S(1)}, u32[]{:S(2)}, u32[]{:S(2)}) collective-permute-start(bf16[4,1,128,256]{2,3,1,0:T(8,128)(2,1)S(1)} %constant_dynamic-slice_fusion.35), channel_id=1, source_target_pairs={{0,16},{8,24},{16,0},{24,8},{1,17},{9,25},{17,1},{25,9},{2,18},{10... | collective-permute-start | bytes 786440 | tf_op jit(solution)/shard_map/ppermute | solution.py:287
  533.5 18.3 %collective-permute-start.8 = (bf16[2,1,128,256]{2,3,1,0:T(8,128)(2,1)S(1)}, bf16[2,1,128,256]{2,3,1,0:T(8,128)(2,1)S(1)}, u32[]{:S(2)}, u32[]{:S(2)}) collective-permute-start(bf16[2,1,128,256]{2,3,1,0:T(8,128)(2,1)S(1)} %constant_dynamic-slice_fusion.28), channel_id=1, source_target_pairs={{0,4},{1,5},{2,6},{3,7},{4,0},{5,1},{6,2},{7,3},{8,12},{9,13},{10,... | collective-permute-start | bytes 393224 | tf_op jit(solution)/shard_map/ppermute | solution.py:287
  536.6 16.7 %collective-permute-start.13 = (bf16[2,1,128,256]{2,3,1,0:T(8,128)(2,1)S(1)}, bf16[2,1,128,256]{2,3,1,0:T(8,128)(2,1)S(1)}, u32[]{:S(2)}, u32[]{:S(2)}) collective-permute-start(bf16[2,1,128,256]{2,3,1,0:T(8,128)(2,1)S(1)} %constant_dynamic-slice_fusion.22), channel_id=1, source_target_pairs={{0,4},{1,5},{2,6},{3,7},{4,0},{5,1},{6,2},{7,3},{8,12},{9,13},{10,... | collective-permute-start | bytes 393224 | tf_op jit(solution)/shard_map/ppermute | solution.py:287
  (80 other events, 768.1 us)

commit v2 on v1

--- a/solution.py
+++ b/solution.py
@@ -14,6 +14,7 @@
 F32 = jnp.float32
 BF16 = jnp.bfloat16
 VMEM_LIMIT = 56 * 2**20
+MESH = pl.DeviceIdType.MESH
 
 
 def dot(a, b):
@@ -37,9 +38,17 @@
     return jnp.where(lane % HEAD_DIM < half, left, right)
 
 
-def qkv_kernel(rows, length, width, normed_ref, first_ref, cos_ref, sin_ref, wq_ref, wk_ref, wv_ref, *outs):
-    out_refs, sums_ref = outs[:rows], outs[rows]
+def qkv_kernel(rows, length, width, hidden_ref, first_ref, cos_ref, sin_ref, gain_ref, wq_ref, wk_ref, wv_ref, *outs):
+    out_refs, (normed_ref, sums_ref) = outs[:rows], outs[rows:]
     chunk = wq_ref.shape[1]
+
+    @pl.when(pl.program_id(0) == 0)
+    def _():
+        for r in range(rows):
+            at = pl.ds(r * length, length)
+            normed, _ = rms_parts(hidden_ref[at, :].astype(F32))
+            normed_ref[at, :] = (normed * gain_ref[...]).astype(BF16)
+
     first_sum = jnp.zeros((1, chunk), F32)
     mixed_sum = jnp.zeros((1, chunk), F32)
     for r in range(rows):
@@ -64,35 +73,36 @@
     sums_ref[0, 1:2] = mixed_sum
 
 
-def project_qkv(normed, first, cos, sin, w_query, w_key, w_value, rows, n_blk):
-    tokens, model = normed.shape
+def project_qkv(hidden, first, cos, sin, gain, w_query, w_key, w_value, rows, n_blk):
+    tokens, model = hidden.shape
     length, width = tokens // rows, model // n_blk
     chunk = 256
     steps = model // chunk
-    full = lambda cols: pl.BlockSpec((tokens, cols), lambda j: (0, 0))
+    full = lambda rows, cols: pl.BlockSpec((rows, cols), lambda j: (0, 0))
     weight = pl.BlockSpec((model, chunk), lambda j: (0, j))
     return pl.pallas_call(
         functools.partial(qkv_kernel, rows, length, width),
         grid=(steps,),
         in_specs=[
-            full(model),
+            full(tokens, model),
             pl.BlockSpec((tokens, chunk), lambda j: (0, j)),
-            full(128),
-            full(128),
+            full(tokens, 128),
+            full(tokens, 128),
+            full(1, model),
             weight,
             weight,
             weight,
         ],
         out_specs=[pl.BlockSpec((chunk // width, 3, length, width), lambda j: (j, 0, 0, 0))] * rows
-        + [pl.BlockSpec((1, 2, chunk), lambda j: (j, 0, 0))],
+        + [full(tokens, model), pl.BlockSpec((1, 2, chunk), lambda j: (j, 0, 0))],
         out_shape=[jax.ShapeDtypeStruct((n_blk, 3, length, width), BF16)] * rows
-        + [jax.ShapeDtypeStruct((steps, 2, chunk), F32)],
+        + [jax.ShapeDtypeStruct((tokens, model), BF16), jax.ShapeDtypeStruct((steps, 2, chunk), F32)],
         compiler_params=pltpu.CompilerParams(vmem_limit_bytes=VMEM_LIMIT),
         cost_estimate=pl.CostEstimate(
             flops=6 * tokens * model * model, bytes_accessed=6 * model * model + 10 * tokens * model, transcendentals=0
         ),
         name="qkv",
-    )(normed, first, cos, sin, w_query, w_key, w_value)
+    )(hidden, first, cos, sin, gain, w_query, w_key, w_value)
 
 
 def doc_ends(lens_ref, row, n_docs):
@@ -331,6 +341,375 @@
     return values
 
 
+def place_of(order, dp, blk):
+    place = 0
+    for name, bit in order:
+        place = 2 * place + (((dp if name == "dp" else blk) >> bit) & 1)
+    return place
+
+
+def chunks_of(block_rows, block_cols):
+    cols = block_cols // 128
+    return 4 // cols, cols, block_rows // (4 // cols)
+
+
+def wgrad_kernel(orders, n_left, n_right, left_is_dp, n_out, left_ref, *refs):
+    right_refs, out_refs, turned_ref = refs[:n_out], refs[n_out : 2 * n_out], refs[2 * n_out]
+    left_rows, right_cols = left_ref.shape[1] // n_left, right_refs[0].shape[1] // n_right
+    row_parts, col_parts, size = chunks_of(left_rows, right_cols)
+    q = pl.program_id(0)
+
+    @pl.when(q == 0)
+    def _():
+        turned_ref[...] = left_ref[...].T
+
+    row_part, col_part = q // col_parts, q % col_parts
+    left = jnp.concatenate(
+        [
+            turned_ref[pl.ds(pl.multiple_of(k * left_rows + row_part * size, 16), size), :]
+            for k in range(n_left)
+        ],
+        axis=0,
+    )
+    for order, right_ref, out_ref in zip(orders, right_refs, out_refs):
+        if col_parts == 1:
+            right = right_ref[...]
+        else:
+            right = jnp.concatenate(
+                [
+                    right_ref[:, pl.ds(pl.multiple_of(k * right_cols + col_part * 128, 128), 128)]
+                    for k in range(n_right)
+                ],
+                axis=1,
+            )
+        result = dot(left, right).astype(BF16)
+        for k in range(n_left):
+            for m in range(n_right):
+                dp, blk = (k, m) if left_is_dp else (m, k)
+                out_ref[0, place_of(order, dp, blk)] = result[k * size : (k + 1) * size, m * 128 : (m + 1) * 128]
+
+
+def wgrad(orders, left, rights, left_is_dp):
+    n_dp, n_blk = lax.axis_size("dp"), lax.axis_size("blk")
+    n_left, n_right = (n_dp, n_blk) if left_is_dp else (n_blk, n_dp)
+    tokens, left_cols = left.shape
+    right_cols = rights[0].shape[1]
+    row_parts, col_parts, size = chunks_of(left_cols // n_left, right_cols // n_right)
+    full = lambda a: pl.BlockSpec(a.shape, lambda q: (0, 0))
+    n_out = len(rights)
+    return pl.pallas_call(
+        functools.partial(wgrad_kernel, orders, n_left, n_right, left_is_dp, n_out),
+        grid=(4,),
+        in_specs=[full(left)] + [full(a) for a in rights],
+        out_specs=[pl.BlockSpec((1, n_dp * n_blk, size, 128), lambda q: (q, 0, 0, 0))] * n_out,
+        out_shape=[jax.ShapeDtypeStruct((4, n_dp * n_blk, size, 128), BF16)] * n_out,
+        scratch_shapes=[pltpu.VMEM((left_cols, tokens), BF16)],
+        compiler_params=pltpu.CompilerParams(vmem_limit_bytes=VMEM_LIMIT),
+        cost_estimate=pl.CostEstimate(
+            flops=2 * n_out * tokens * left_cols * right_cols,
+            bytes_accessed=2 * tokens * (left_cols + n_out * right_cols) + 2 * n_out * left_cols * right_cols,
+            transcendentals=0,
+        ),
+        name="wgrad",
+    )(left, *rights)
+
+
+def partner(name, bit):
+    here = {"dp": lax.axis_index("dp"), "blk": lax.axis_index("blk")}
+    mine = (here[name] // (1 << bit)) % 2
+    other = dict(here)
+    other[name] = here[name] + (1 - 2 * mine) * (1 << bit)
+    return mine, (other["dp"], other["blk"])
+
+
+def scatter_kernel(orders, *refs):
+    n_streams, n_stages = len(orders), len(orders[0])
+    take = lambda n: [next(source) for _ in range(n)]
+    source = iter(refs)
+    grads, outs, works = take(n_streams), take(n_streams), take(n_streams)
+    landed = [take(n_stages) for _ in range(n_streams)]
+    local_sem, send_sem, recv_sem = take(3)
+    n_chunks = grads[0].shape[0]
+    blocks = grads[0].shape[1]
+
+    barrier = pltpu.get_barrier_semaphore()
+    for name, bit in orders[0]:
+        pl.semaphore_signal(barrier, inc=1, device_id=partner(name, bit)[1], device_id_type=MESH)
+    pl.semaphore_wait(barrier, n_stages)
+
+    def base_of(k, stage):
+        base = 0
+        for earlier in range(1, stage):
+            base = base + partner(*orders[k][earlier])[0] * (blocks >> (earlier + 1))
+        return base
+
+    def local(k, c):
+        mine = partner(*orders[k][0])[0]
+        half = blocks // 2
+        return pltpu.make_async_copy(grads[k].at[c, pl.ds(mine * half, half)], works[k].at[c], local_sem.at[k, c])
+
+    def remote(k, stage, c):
+        mine, device = partner(*orders[k][stage])
+        half = blocks >> (stage + 1)
+        if stage == 0:
+            sent = grads[k].at[c, pl.ds((1 - mine) * half, half)]
+        else:
+            sent = works[k].at[c, pl.ds(base_of(k, stage) + (1 - mine) * half, half)]
+        return pltpu.make_async_remote_copy(
+            src_ref=sent,
+            dst_ref=landed[k][stage].at[c],
+            send_sem=send_sem.at[k, stage, c],
+            recv_sem=recv_sem.at[k, stage, c],
+            device_id=device,
+            device_id_type=MESH,
+        )
+
+    def add(k, stage, c):
+        count = blocks >> (stage + 1)
+        base = base_of(k, stage + 1)
+        if stage == n_stages - 1:
+            outs[k][c] = works[k][c, base].astype(F32) + landed[k][stage][c, 0].astype(F32)
+            return
+
+        def one(d, _):
+            kept = works[k][c, base + d].astype(F32) + landed[k][stage][c, d].astype(F32)
+            works[k][c, base + d] = kept.astype(BF16)
+            return 0
+
+        lax.fori_loop(0, count, one, 0)
+
+    def step(t, _):
+        for stage in range(n_stages + 1):
+            c = t - stage
+
+            @pl.when((c >= 0) & (c < n_chunks))
+            def _():
+                for k in range(n_streams):
+                    if stage == 0:
+                        local(k, c).start()
+                    else:
+                        if stage == 1:
+                            local(k, c).wait()
+                        remote(k, stage - 1, c).wait_recv()
+                        add(k, stage - 1, c)
+                    if stage < n_stages:
+                        remote(k, stage, c).start()
+
+        return 0
+
+    lax.fori_loop(0, n_chunks + n_stages, step, 0)
+
+    def finish(c, _):
+        for k in range(n_streams):
+            for stage in range(n_stages):
+                remote(k, stage, c).wait_send()
+        return 0
+
+    lax.fori_loop(0, n_chunks, finish, 0)
+
+
+def scatter_sum(grads, orders, collective_id):
+    n_streams, n_stages = len(grads), len(orders[0])
+    n_chunks, blocks = grads[0].shape[:2]
+    size = sum(a.size for a in grads)
+    return pl.pallas_call(
+        functools.partial(scatter_kernel, orders),
+        in_specs=[pl.BlockSpec(memory_space=pl.ANY)] * n_streams,
+        out_specs=[pl.BlockSpec(memory_space=pltpu.VMEM)] * n_streams,
+        out_shape=[jax.ShapeDtypeStruct((n_chunks,) + a.shape[2:], F32) for a in grads],
+        scratch_shapes=[pltpu.VMEM((n_chunks, blocks // 2) + a.shape[2:], BF16) for a in grads]
+        + [
+            pltpu.VMEM((n_chunks, blocks >> (stage + 1)) + a.shape[2:], BF16)
+            for a in grads
+            for stage in range(n_stages)
+        ]
+        + [
+            pltpu.SemaphoreType.DMA((n_streams, n_chunks)),
+            pltpu.SemaphoreType.DMA((n_streams, n_stages, n_chunks)),
+            pltpu.SemaphoreType.DMA((n_streams, n_stages, n_chunks)),
+        ],
+        compiler_params=pltpu.CompilerParams(
+            collective_id=collective_id, has_side_effects=True, vmem_limit_bytes=VMEM_LIMIT
+        ),
+        cost_estimate=pl.CostEstimate(flops=size, bytes_accessed=8 * size, transcendentals=0),
+        name="scatter_sum",
+    )(*grads)
+
+
+def whole_block(pieces, block_rows, block_cols):
+    row_parts, col_parts, size = chunks_of(block_rows, block_cols)
+    shaped = pieces.reshape(row_parts, col_parts, size, 128)
+    return jnp.transpose(shaped, (0, 2, 1, 3)).reshape(block_rows, block_cols)
+
+
+def ffn_kernel(rows, n_blk, *refs):
+    source = iter(refs)
+    take = lambda n: [next(source) for _ in range(n)]
+    gathered = take(rows)
+    hidden_ref, cot_ref, gain_ref, wo_ref, wg_ref, wu_ref, wd_ref = take(7)
+    low_ref, mid_ref, inner_ref, dgate_ref, dup_ref, out_ref, dres_ref, dbranch_ref, dgain_ref = take(9)
+    d_attn = take(rows)
+    resid_ref, acc_ref, dmid_ref = take(3)
+    length, width = gathered[0].shape[1:]
+    step = pl.program_id(0)
+
+    @pl.when(step == 0)
+    def _():
+        for r in range(rows):
+            at = pl.ds(r * length, length)
+            for s in range(n_blk):
+                low_ref[at, s * width : (s + 1) * width] = gathered[r][s]
+            resid = hidden_ref[at, :].astype(F32) + dot(low_ref[at, :], wo_ref[...])
+            resid_ref[at, :] = resid
+            normed, _ = rms_parts(resid)
+            mid_ref[at, :] = (normed * gain_ref[...]).astype(BF16)
+        acc_ref[...] = jnp.zeros_like(acc_ref)
+        dmid_ref[...] = jnp.zeros_like(dmid_ref)
+
+    for r in range(rows):
+        at = pl.ds(r * length, length)
+        gate = dot(mid_ref[at, :], wg_ref[...])
+        up = dot(mid_ref[at, :], wu_ref[...])
+        d_inner = dot_nt(cot_ref[at, :], wd_ref[...])
+        sigma = 1.0 / (1.0 + jnp.exp(-gate))
+        act = gate * sigma
+        inner = (act * up).astype(BF16)
+        d_gate = (d_inner * up * (sigma * (1.0 + gate * (1.0 - sigma)))).astype(BF16)
+        d_up = (d_inner * act).astype(BF16)
+        inner_ref[at, :] = inner
+        dgate_ref[at, :] = d_gate
+        dup_ref[at, :] = d_up
+        acc_ref[at, :] += dot(inner, wd_ref[...])
+        dmid_ref[at, :] += dot_nt(d_gate, wg_ref[...]) + dot_nt(d_up, wu_ref[...])
+
+    @pl.when(step == pl.num_programs(0) - 1)
+    def _():
+        d_gain = jnp.zeros(dgain_ref.shape, F32)
+        for r in range(rows):
+            at = pl.ds(r * length, length)
+            resid = resid_ref[at, :]
+            out_ref[at, :] = (resid + acc_ref[at, :]).astype(BF16)
+            normed, inverse = rms_parts(resid)
+            d_mid = dmid_ref[at, :]
+            d_gain = d_gain + jnp.sum(d_mid * normed, axis=0, keepdims=True)
+            d_resid = cot_ref[at, :].astype(F32) + norm_back(d_mid * gain_ref[...], normed, inverse)
+            dres_ref[at, :] = d_resid
+            d_branch = d_resid.astype(BF16)
+            dbranch_ref[at, :] = d_branch
+            back = dot_nt(d_branch, wo_ref[...]).astype(BF16)
+            for s in range(n_blk):
+                d_attn[r][s] = back[:, s * width : (s + 1) * width]
+        dgain_ref[...] = d_gain
+
+
+def feed_forward(gathered, hidden, cot, gain, w_out, w_gate, w_up, w_down):
+    rows = len(gathered)
+    n_blk, length, width = gathered[0].shape
+    tokens, model = hidden.shape
+    inner = w_gate.shape[1]
+    chunk = 256
+    full = lambda a: pl.BlockSpec(a.shape, lambda j: (0,) * len(a.shape))
+    once = lambda a: pl.BlockSpec(a.shape, lambda j: (0,) * len(a.shape), pipeline_mode=pl.Buffered(1))
+    cols = pl.BlockSpec((model, chunk), lambda j: (0, j))
+    shape = jax.ShapeDtypeStruct
+    token_cols = pl.BlockSpec((tokens, chunk), lambda j: (0, j))
+    outs = (
+        [shape((tokens, model), BF16)] * 2
+        + [shape((tokens, inner), BF16)] * 3
+        + [shape((tokens, model), BF16), shape((tokens, model), F32), shape((tokens, model), BF16)]
+        + [shape((1, model), F32)]
+        + [shape((n_blk, length, width), BF16)] * rows
+    )
+    return pl.pallas_call(
+        functools.partial(ffn_kernel, rows, n_blk),
+        grid=(inner // chunk,),
+        in_specs=[once(a) for a in gathered]
+        + [once(hidden), once(cot), once(gain), once(w_out), cols, cols, pl.BlockSpec((chunk, model), lambda j: (j, 0))],
+        out_specs=[full(outs[0])] * 2 + [token_cols] * 3 + [full(a) for a in outs[5:]],
+        out_shape=outs,
+        scratch_shapes=[pltpu.VMEM((tokens, model), F32)] * 3,
+        compiler_params=pltpu.CompilerParams(vmem_limit_bytes=VMEM_LIMIT),
+        cost_estimate=pl.CostEstimate(
+            flops=12 * tokens * model * inner + 4 * tokens * model * model,
+            bytes_accessed=6 * model * inner + 6 * tokens * inner + 20 * tokens * model,
+            transcendentals=tokens * inner,
+        ),
+        name="ffn",
+    )(*gathered, hidden, cot, gain, w_out, w_gate, w_up, w_down)
+
+
+def turn_back_kernel(rows, cos_ref, sin_ref, *refs):
+    backs, (low_ref, first_ref) = refs[:rows], refs[rows:]
+    n_blk, _, length, width = backs[0].shape
+    which = pl.program_id(0)
+    for r in range(rows):
+        at = pl.ds(r * length, length)
+        for s in range(n_blk):
+            cols = slice(s * width, (s + 1) * width)
+            values = backs[r][s, 0].astype(F32)
+
+            @pl.when(which < 2)
+            def _():
+                cos, sin = cos_ref[at, :width], sin_ref[at, :width]
+                wide = values if width == 128 else jnp.concatenate([values, values], axis=1)
+                swapped = swap_halves(wide)[:, :width]
+                low_ref[0, at, cols] = (values * cos - swapped * sin).astype(BF16)
+
+            @pl.when(which == 2)
+            def _():
+                first_ref[at, cols] = 0.5 * values
+                low_ref[0, at, cols] = (0.5 * values).astype(BF16)
+
+
+def turn_back(backs, cos, sin):
+    rows = len(backs)
+    n_blk, _, length, width = backs[0].shape
+    tokens, model = rows * length, n_blk * width
+    full = lambda a: pl.BlockSpec(a.shape, lambda w: (0, 0))
+    return pl.pallas_call(
+        functools.partial(turn_back_kernel, rows),
+        grid=(3,),
+        in_specs=[full(cos), full(sin)] + [pl.BlockSpec((n_blk, 1, length, width), lambda w: (0, w, 0, 0))] * rows,
+        out_specs=[
+            pl.BlockSpec((1, tokens, model), lambda w: (w, 0, 0)),
+            pl.BlockSpec((tokens, model), lambda w: (0, 0)),
+        ],
+        out_shape=[jax.ShapeDtypeStruct((3, tokens, model), BF16), jax.ShapeDtypeStruct((tokens, model), F32)],
+        compiler_params=pltpu.CompilerParams(vmem_limit_bytes=VMEM_LIMIT),
+        name="turn_back",
+    )(cos, sin, *backs)
+
+
+def input_grad_kernel(hidden_ref, dres_ref, gain_ref, low_ref, wq_ref, wk_ref, wv_ref, out_ref, dgain_ref):
+    tokens = hidden_ref.shape[0]
+    half = tokens // 2
+    d_gain = jnp.zeros(dgain_ref.shape, F32)
+    for r in range(2):
+        at = pl.ds(r * half, half)
+        d_normed = (
+            dot_nt(low_ref[0, at, :], wq_ref[...])
+            + dot_nt(low_ref[1, at, :], wk_ref[...])
+            + dot_nt(low_ref[2, at, :], wv_ref[...])
+        )
+        normed, inverse = rms_parts(hidden_ref[at, :].astype(F32))
+        d_gain = d_gain + jnp.sum(d_normed * normed, axis=0, keepdims=True)
+        out_ref[at, :] = dres_ref[at, :] + norm_back(d_normed * gain_ref[...], normed, inverse)
+    dgain_ref[...] = d_gain
+
+
+def input_grad(hidden, d_resid, gain, low, w_query, w_key, w_value):
+    tokens, model = hidden.shape
+    return pl.pallas_call(
+        input_grad_kernel,
+        out_shape=[jax.ShapeDtypeStruct((tokens, model), F32), jax.ShapeDtypeStruct((1, model), F32)],
+        compiler_params=pltpu.CompilerParams(vmem_limit_bytes=VMEM_LIMIT),
+        cost_estimate=pl.CostEstimate(
+            flops=6 * tokens * model * model, bytes_accessed=6 * model * model + 16 * tokens * model, transcendentals=0
+        ),
+        name="input_grad",
+    )(hidden, d_resid, gain, low, w_query, w_key, w_value)
+
+
 def rms_parts(values):
     inverse_rms = lax.rsqrt(jnp.mean(values * values, axis=-1, keepdims=True) + EPS)
     return values * inverse_rms, inverse_rms
@@ -351,13 +730,6 @@
     angles = position * freq[None, :]
     sign = jnp.where(lane % HEAD_DIM < half, -1.0, 1.0)
     return jnp.cos(angles), jnp.sin(angles) * sign[None, :]
-
-
-def rotate_back(values, cos, sin):
-    half = HEAD_DIM // 2
-    shaped = values.reshape(values.shape[:2] + (values.shape[2] // HEAD_DIM, 2, half))
-    swapped = shaped[:, :, :, ::-1, :].reshape(values.shape)
-    return values * cos - swapped * sin
 
 
 def body(
@@ -384,13 +756,13 @@
     unflat = lambda a: jnp.transpose(a.reshape(rows, length, model), (1, 0, 2))
     lens = doc_lengths.reshape(-1)
 
-    resid_in = flat(hidden_in).astype(F32)
-    normed_one, inv_one = rms_parts(resid_in)
-    normed_in = (normed_one * attn_gain).astype(BF16)
+    hidden, cot, first = flat(hidden_in), flat(out_cotangent), flat(first_values)
+    row_gain = lambda gain: gain.reshape(1, model)
+
     cos, sin = rope_tables(doc_lengths, lax.axis_index("blk") * length, length)
-    *qkv_own, sums = project_qkv(normed_in, flat(first_values), cos, sin, w_query, w_key, w_value, rows, n_blk)
-    cot = flat(out_cotangent)
-
+    *qkv_own, normed_in, sums = project_qkv(
+        hidden, first, cos, sin, row_gain(attn_gain), w_query, w_key, w_value, rows, n_blk
+    )
     qkv, attended, lse, gathered = [], [], [], []
     for r in range(rows):
         qkv.append(exchange(qkv_own[r]))
@@ -399,88 +771,70 @@
         attended.append(o_f)
         lse.append(lse_r)
         gathered.append(exchange(o_low))
-    attn_low = jnp.concatenate([jnp.transpose(g, (1, 0, 2)).reshape(length, model) for g in gathered], axis=0)
-
-    resid_mid = resid_in + dot(attn_low, w_out)
-    normed_two, inv_two = rms_parts(resid_mid)
-    normed_mid = (normed_two * ffn_gain).astype(BF16)
-    gate_pre = dot(normed_mid, w_gate)
-    up_pre = dot(normed_mid, w_up)
-    gate_act = jax.nn.silu(gate_pre)
-    inner_low = (gate_act * up_pre).astype(BF16)
-    block_out = (resid_mid + dot(inner_low, w_down)).astype(BF16)
-    d_inner = dot_nt(cot, w_down)
-    sigmoid_gate = jax.nn.sigmoid(gate_pre)
-    d_gate = (d_inner * up_pre * sigmoid_gate * (1.0 + gate_pre * (1.0 - sigmoid_gate))).astype(BF16)
-    d_up = (d_inner * gate_act).astype(BF16)
-    d_normed_mid = dot_nt(d_gate, w_gate) + dot_nt(d_up, w_up)
-    gain_two_grad = jnp.sum(d_normed_mid * normed_two, axis=0)
-    d_resid_mid = cot.astype(F32) + norm_back(d_normed_mid * ffn_gain, normed_two, inv_two)
-    d_branch = d_resid_mid.astype(BF16)
-    d_attn = dot_nt(d_branch, w_out).astype(BF16)
-
-    grads = []
-    d_own = []
-    for r in range(rows):
-        piece = jnp.transpose(d_attn[r * length : (r + 1) * length].reshape(length, n_blk, width), (1, 0, 2))
-        d_own.append(exchange(piece))
-    mid_cf = core_first(normed_mid)
-    grad_down = scatter(dot_tn(inner_low, y_first(cot)).astype(BF16), "dp", False)
-    grad_gate = scatter(dot_tn(d_gate, mid_cf).astype(BF16), "blk", False)
-    grad_up = scatter(dot_tn(d_up, mid_cf).astype(BF16), "blk", True)
-    grad_project = scatter(dot_tn(d_branch, core_first(attn_low)).astype(BF16), "blk", True)
-
-    back = []
-    for r in range(rows):
-        back.append(exchange(attn_bwd(lens, qkv[r], d_own[r], attended[r], lse[r], r, n_docs)))
-
-    def owned(which, rotated):
-        parts = []
-        for r in range(rows):
-            values = back[r][:, which].astype(F32)
-            if rotated:
-                at = slice(r * length, (r + 1) * length)
-                values = rotate_back(values, cos[at, :width], sin[at, :width])
-            parts.append(jnp.transpose(values, (1, 0, 2)).reshape(length, model))
-        return jnp.concatenate(parts, axis=0)
-
-    d_query = owned(0, True).astype(BF16)
-    d_key = owned(1, True).astype(BF16)
-    grad_first = 0.5 * owned(2, False)
-    d_value = grad_first.astype(BF16)
-    in_cf = core_first(normed_in)
-    grad_query = scatter(dot_tn(d_query, in_cf).astype(BF16), "blk", True)
-    grad_key = scatter(dot_tn(d_key, in_cf).astype(BF16), "blk", False)
-    grad_value = scatter(dot_tn(d_value, in_cf).astype(BF16), "blk", True)
-    d_normed_in = dot_nt(d_query, w_query) + dot_nt(d_key, w_key) + dot_nt(d_value, w_value)
-    gain_one_grad = jnp.sum(d_normed_in * normed_one, axis=0)
-    grad_input = d_resid_mid + norm_back(d_normed_in * attn_gain, normed_one, inv_one)
+    attn_low, normed_mid, inner_low, d_gate, d_up, block_out, d_resid_mid, d_branch, d_gain_two, *d_attn = feed_forward(
+        gathered, hidden, cot, row_gain(ffn_gain), w_out, w_gate, w_up, w_down
+    )
+    d_own = [exchange(d_attn[r]) for r in range(rows)]
+
+    inner = w_gate.shape[1]
+    by_blocks = (model // n_dp) % 128 == 0 and width == 128 and (inner // n_blk) % 32 == 0
+    early, late = scatter_steps(False), scatter_steps(True)
+    if by_blocks:
+        (gate_blocks,) = wgrad([early], d_gate, [normed_mid], False)
+        (up_blocks,) = wgrad([early], d_up, [normed_mid], False)
+        (down_blocks,) = wgrad([late], inner_low, [cot], True)
+        (project_blocks,) = wgrad([early], attn_low, [d_branch], True)
+        ffn_blocks = (gate_blocks, up_blocks, down_blocks, project_blocks)
+
+    back_own = [attn_bwd(lens, qkv[r], d_own[r], attended[r], lse[r], r, n_docs) for r in range(rows)]
+    if by_blocks:
+        back_own[-1], ffn_blocks = lax.optimization_barrier((back_own[-1], ffn_blocks))
+    back = [exchange(b) for b in back_own]
+    if by_blocks:
+        sums_ffn = scatter_sum(ffn_blocks, (early, early, late, early), 0)
+        back, sums_ffn = lax.optimization_barrier((back, sums_ffn))
+    low, grad_first = turn_back(back, cos, sin)
+
+    if by_blocks:
+        qkv_blocks = wgrad([early, late, early], normed_in, [low[0], low[1], low[2]], True)
+        sums_qkv = scatter_sum(qkv_blocks, (early, late, early), 1)
+        block = lambda pieces, r, c: whole_block(pieces, r, c)
+        grad_gate = block(sums_ffn[0], inner // n_blk, model // n_dp).T
+        grad_up = block(sums_ffn[1], inner // n_blk, model // n_dp).T
+        grad_down = block(sums_ffn[2], inner // n_dp, model // n_blk)
+        grad_project = block(sums_ffn[3], model // n_dp, model // n_blk)
+        grad_query, grad_key, grad_value = [block(a, model // n_dp, model // n_blk) for a in sums_qkv]
+    else:
+        mid_cf, in_cf = core_first(normed_mid), core_first(normed_in)
+        sent = lambda a, b, name, y: scatter(dot_tn(a, b).astype(BF16), name, y).astype(F32)
+        grad_down = sent(inner_low, y_first(cot), "dp", False)
+        grad_gate = sent(d_gate, mid_cf, "blk", False).T
+        grad_up = sent(d_up, mid_cf, "blk", True).T
+        grad_project = sent(d_branch, core_first(attn_low), "blk", True).T
+        grad_query, grad_key, grad_value = [sent(low[k], in_cf, "blk", True).T for k in range(3)]
+    grad_input, d_gain_one = input_grad(hidden, d_resid_mid, row_gain(attn_gain), low, w_query, w_key, w_value)
 
     squares = jnp.sum(sums, axis=(0, 2))
     squares = jnp.concatenate([squares, jnp.zeros((126,), F32)])
-    early = total(jnp.concatenate([gain_two_grad, squares]))
-    gain_one = total(gain_one_grad)
+    early_sums = total(jnp.concatenate([d_gain_two.reshape(model), squares]))
+    gain_one = total(d_gain_one.reshape(model))
     n_entries = n_blk * length * rows * n_dp * model
     return (
-        block_out_shape(unflat(block_out)),
+        unflat(block_out),
         unflat(grad_input),
         unflat(grad_first),
-        grad_query.T.astype(F32),
-        grad_key.T.astype(F32),
-        grad_value.T.astype(F32),
-        grad_project.T.astype(F32),
-        grad_gate.T.astype(F32),
-        grad_up.T.astype(F32),
-        grad_down.astype(F32),
+        grad_query,
+        grad_key,
+        grad_value,
+        grad_project,
+        grad_gate,
+        grad_up,
+        grad_down,
         gain_one,
-        early[:model],
-        early[model] / n_entries,
-        early[model + 1] / n_entries,
+        early_sums[:model],
+        early_sums[model] / n_entries,
+        early_sums[model + 1] / n_entries,
     )
-
-
-def block_out_shape(values):
-    return values
 
 
 def solution(mesh):

time: 568 us -> 509 us (0.90)
  Pallas kernels: 72.8 us -> 324 us
  local copies, waits for them, and re-layouts: 108 us -> 26.5 us
  matrix products: 80 us -> 0 us
  waiting for transfers between devices: 121 us -> 42.7 us
  other arithmetic: 54.9 us -> 4.28 us
  starting transfers between devices: 74.3 us -> 42.5 us
  blocking collectives: 44.4 us -> 61.5 us
    pallas_call x0 -> x10, Pallas kernels: none -> 256 us  [the longest x2 168 us: scatter_sum(): pl.pallas_call(functools.partial(scatter_kernel, orders), in_specs=[pl.Bl...]
    ppermute x35 -> x0, waiting for transfers between devices: 82 us -> none  [halve(): got = lax.ppermute(send, name, [(k, k ^ 1 << bit) for k in range(size)])]
    dot_general x18 -> x0, matrix products: 80 us -> none  [the longest x7 30.5 us: dot_nt(): lax.dot_general(a, b, (((1,), (1,)), ((), ())), preferred_element_type=F32)]
    convert_element_type x38 -> x0, other arithmetic: 35.7 us -> none  [the longest x28 23 us: halve(): return (keep.astype(F32) + got.astype(F32)).astype(BF16)]
    ppermute x35 -> x0, starting transfers between devices: 25.2 us -> none  [halve(): got = lax.ppermute(send, name, [(k, k ^ 1 << bit) for k in range(size)])]
    dynamic_slice x35 -> x0, local copies, waits for them, and re-layouts: 20.4 us -> none  [the longest x31 15.8 us: halve(): send = lax.dynamic_slice_in_dim(current, (1 - mine) * half, half, axis)]
    all_to_all x1 -> x2, blocking collectives: 44.4 us -> 61.5 us  [exchange(): return lax.all_to_all(values, 'blk', 0, 0, tiled=True)]
    transpose x11 -> x2, local copies, waits for them, and re-layouts: 17.5 us -> 0.37 us  [whole_block(): return jnp.transpose(shaped, (0, 2, 1, 3)).reshape(block_rows, block_cols)]
  transfers between devices with their start and end apart: 52 -> 16, of which waited for: 20 -> 9; matrix products, arithmetic and copies ran while one was open for 28% -> 3% of each run, Pallas kernels for 12% -> 56%
where the time goes in v2:
time: 509 us; the launch traced here: 506 us
  Pallas kernels  324 us (64%)
  blocking collectives  61.5 us (12%)
  waiting for transfers between devices  42.7 us (8%)
  starting transfers between devices  42.5 us (8%)
  local copies, waits for them, and re-layouts  26.5 us (5%)
    pallas_call x2, Pallas kernels, scatter_sum(): pl.pallas_call(functools.partial(scatter_kernel, orders), in_specs=[pl.Bl...  168 us
    all_to_all x2, blocking collectives, exchange(): return lax.all_to_all(values, 'blk', 0, 0, tiled=True)  61.5 us
    pallas_call x5, Pallas kernels, wgrad(): pl.pallas_call(functools.partial(wgrad_kernel, orders, n_left, n_right, l...  36.5 us
    all_to_all x6, waiting for transfers between devices, exchange(): return lax.all_to_all(values, 'blk', 0, 0, tiled=True)  34.8 us
    pallas_call x1, Pallas kernels, feed_forward(): pl.pallas_call(functools.partial(ffn_kernel, rows, n_blk), grid=(inner //...  32.9 us
    pallas_call x2, Pallas kernels, attn_bwd(): pl.pallas_call(functools.partial(attn_bwd_kernel, row, n_docs, heads), gr...  32.5 us
    all_to_all x6, starting transfers between devices, exchange(): return lax.all_to_all(values, 'blk', 0, 0, tiled=True)  28.9 us
    pallas_call x2, Pallas kernels, attn_fwd(): pl.pallas_call(functools.partial(attn_fwd_kernel, row, n_docs, heads), gr...  27 us
  transfers between devices with their start and end apart: 16, of which 9 were waited for; matrix products, arithmetic and copies ran while one was open for 3% of the time, Pallas kernels for 56%

profile of v2, /device:TPU:0, one launch (start us, length us, event | category | flops | bytes accessed | tf_op | source)
XLA Modules:
  0.0 505.7 jit_solution(8843817081408366765)
XLA Ops:
  1.7 2.5 copy.35
  7.3 8.6 %qkv.1 = (bf16[8,3,256,128]{3,2,1,0:T(8,128)(2,1)}, bf16[8,3,256,128]{3,2,1,0:T(8,128)(2,1)}, bf16[512,1024]{1,0:T(8,128)(2,1)}, f32[4,2,256]{2,1,0:T(2,128)}) custom-call(bf16[512,1024]{1,0:T(8,128)(2,1)} %bitcast.60, bf16[512,1024]{1,0:T(8,128)(2,1)} %bitcast.76, f32[512,128]{1,0:T(8,128)} %get-tuple-element.112.cos_ref, ...), custom_call_target="tpu_custom_call" | custom-call | flops 3221225472 | bytes 11534336 | tf_op jit(solution)/shard_map/qkv/pallas_call | solution.py:83
  15.8 44.4 %all_to_all.40.qkv_ref = bf16[8,3,256,128]{3,2,1,0:T(8,128)(2,1)} all-to-all(bf16[8,3,256,128]{3,2,1,0:T(8,128)(2,1)} %get-tuple-element.62), channel_id=1, replica_groups=mesh['dp'=4,'blk'=8] {'blk'}, dimensions={0} | all-to-all | bytes 3145728 | tf_op jit(solution)/shard_map/all_to_all | solution.py:284
  60.2 3.7 all-to-all-start
  64.6 12.5 %attn_fwd.3 = (f32[8,256,128]{2,1,0:T(8,128)}, bf16[8,256,128]{2,1,0:T(8,128)(2,1)}, f32[8,2,256]{2,1,0:T(2,128)}) custom-call(s32[16]{0:T(128)} %reshape.128.lens_ref, bf16[8,3,256,128]{3,2,1,0:T(8,128)(2,1)} %all_to_all.40.qkv_ref), custom_call_target="tpu_custom_call" | custom-call | flops 10000000000 | bytes 3000000 | tf_op jit(solution)/shard_map/attn_fwd/pallas_call | solution.py:185
  77.0 23.6 %all-to-all-done.qkv_ref = bf16[8,3,256,128]{3,2,1,0:T(8,128)(2,1)S(1)} async-done(((bf16[8,3,256,128]{3,2,1,0:T(8,128)(2,1)}), bf16[8,3,256,128]{3,2,1,0:T(8,128)(2,1)S(1)}, u32[]{:S(2)}, u32[]{:S(2)}) %all-to-all-start) | async-done | bytes 1572896 | tf_op jit(solution)/shard_map/all_to_all | solution.py:284
  100.6 3.6 all-to-all-start.3
  104.3 14.6 %attn_fwd.2 = (f32[8,256,128]{2,1,0:T(8,128)}, bf16[8,256,128]{2,1,0:T(8,128)(2,1)}, f32[8,2,256]{2,1,0:T(2,128)}) custom-call(s32[16]{0:T(128)} %reshape.128.lens_ref, bf16[8,3,256,128]{3,2,1,0:T(8,128)(2,1)} %copy-done.5), custom_call_target="tpu_custom_call" | custom-call | flops 10000000000 | bytes 3000000 | tf_op jit(solution)/shard_map/attn_fwd/pallas_call | solution.py:185
  118.9 5.9 %all-to-all-start.1 = ((bf16[8,256,128]{2,1,0:T(8,128)(2,1)}), bf16[8,256,128]{2,1,0:T(8,128)(2,1)S(1)}, u32[]{:S(2)}, u32[]{:S(2)}) async-start(bf16[8,256,128]{2,1,0:T(8,128)(2,1)} %get-tuple-element.61), calls=%async_computation.1 | async-start | bytes 1048576 | tf_op jit(solution)/shard_map/all_to_all | solution.py:284
  126.1 11.1 %all-to-all-done.1.refs_0_ = bf16[8,256,128]{2,1,0:T(8,128)(2,1)S(1)} async-done(((bf16[8,256,128]{2,1,0:T(8,128)(2,1)}), bf16[8,256,128]{2,1,0:T(8,128)(2,1)S(1)}, u32[]{:S(2)}, u32[]{:S(2)}) %all-to-all-start.1) | async-done | bytes 524320 | tf_op jit(solution)/shard_map/all_to_all | solution.py:284
  138.1 32.9 %ffn.1 = (bf16[512,1024]{1,0:T(8,128)(2,1)}, bf16[512,1024]{1,0:T(8,128)(2,1)}, bf16[512,2816]{1,0:T(8,128)(2,1)}, bf16[512,2816]{1,0:T(8,128)(2,1)}, bf16[512,2...) custom-call(bf16[8,256,128]{2,1,0:T(8,128)(2,1)} %copy-done.11, ...), custom_call_target="tpu_custom_call" | custom-call | flops 19864223744 | bytes 36438016 | tf_op jit(solution)/shard_map/ffn/pallas_call | solution.py:623
  170.9 17.1 %all_to_all.41.do_ref = bf16[8,256,128]{2,1,0:T(8,128)(2,1)} all-to-all(bf16[8,256,128]{2,1,0:T(8,128)(2,1)} %get-tuple-element.66), channel_id=1, replica_groups=mesh['dp'=4,'blk'=8] {'blk'}, dimensions={0} | all-to-all | bytes 1048576 | tf_op jit(solution)/shard_map/all_to_all | solution.py:284
  188.1 3.6 all-to-all-start.6
  191.7 17.4 %attn_bwd.2 = bf16[8,3,256,128]{3,2,1,0:T(8,128)(2,1)} custom-call(s32[16]{0:T(128)} %reshape.128.lens_ref, bf16[8,3,256,128]{3,2,1,0:T(8,128)(2,1)} %copy-done.5, bf16[8,256,128]{2,1,0:T(8,128)(2,1)} %all_to_all.41.do_ref, f32[8,256,128]{2,1,0:T(8,128)} %get-tuple-element.67.o_ref, f32[8,2,256]{2,1,0:T(2,128)} %get-tuple-element.68.lse_ref), custom_call_target="tpu_custom_call" | custom-call | flops 20000000000 | bytes 6000000 | tf_op jit(solution)/shard_map/attn_bwd/pallas_call | solution.py:264
  209.1 6.0 %all-to-all-start.5 = ((bf16[8,3,256,128]{3,2,1,0:T(8,128)(2,1)}), bf16[8,3,256,128]{3,2,1,0:T(8,128)(2,1)S(1)}, u32[]{:S(2)}, u32[]{:S(2)}) async-start(bf16[8,3,256,128]{3,2,1,0:T(8,128)(2,1)} %attn_bwd.2), calls=%async_computation.5 | async-start | bytes 3145728 | tf_op jit(solution)/shard_map/all_to_all | solution.py:284
  215.1 4.8 wgrad.8.refs_3_
  220.0 7.9 %wgrad.7.refs_2_ = bf16[4,32,176,128]{3,2,1,0:T(8,128)(2,1)} custom-call(bf16[512,2816]{1,0:T(8,128)(2,1)} %get-tuple-element.75.left_ref, bf16[512,1024]{1,0:T(8,128)(2,1)} %bitcast.75), custom_call_target="tpu_custom_call" | custom-call | flops 2952790016 | bytes 9699328 | tf_op jit(solution)/shard_map/wgrad/pallas_call | solution.py:400
  227.9 8.1 %wgrad.5.refs_0_ = bf16[4,32,176,128]{3,2,1,0:T(8,128)(2,1)} custom-call(bf16[512,2816]{1,0:T(8,128)(2,1)} %get-tuple-element.72.left_ref, bf16[512,1024]{1,0:T(8,128)(2,1)} %get-tuple-element.73.refs_0_), custom_call_target="tpu_custom_call" | custom-call | flops 2952790016 | bytes 9699328 | tf_op jit(solution)/shard_map/wgrad/pallas_call | solution.py:400
  236.0 8.0 %wgrad.6.refs_1_ = bf16[4,32,176,128]{3,2,1,0:T(8,128)(2,1)} custom-call(bf16[512,2816]{1,0:T(8,128)(2,1)} %get-tuple-element.74.left_ref, bf16[512,1024]{1,0:T(8,128)(2,1)} %get-tuple-element.73.refs_0_), custom_call_target="tpu_custom_call" | custom-call | flops 2952790016 | bytes 9699328 | tf_op jit(solution)/shard_map/wgrad/pallas_call | solution.py:400
  244.0 15.0 %attn_bwd.3 = bf16[8,3,256,128]{3,2,1,0:T(8,128)(2,1)} custom-call(s32[16]{0:T(128)} %reshape.128.lens_ref, bf16[8,3,256,128]{3,2,1,0:T(8,128)(2,1)} %all_to_all.40.qkv_ref, bf16[8,256,128]{2,1,0:T(8,128)(2,1)} %copy-done.9, f32[8,256,128]{2,1,0:T(8,128)} %get-tuple-element.70.o_ref, f32[8,2,256]{2,1,0:T(2,128)} %get-tuple-element.71.lse_ref), custom_call_target="tpu_custom_call" | custom-call | flops 20000000000 | bytes 6000000 | tf_op jit(solution)/shard_map/attn_bwd/pallas_call | solution.py:264
  259.1 6.0 %all-to-all-start.7 = ((bf16[8,3,256,128]{3,2,1,0:T(8,128)(2,1)}), bf16[8,3,256,128]{3,2,1,0:T(8,128)(2,1)S(1)}, u32[]{:S(2)}, u32[]{:S(2)}) async-start(bf16[8,3,256,128]{3,2,1,0:T(8,128)(2,1)} %attn_bwd.3), calls=%async_computation.7 | async-start | bytes 3145728 | tf_op jit(solution)/shard_map/all_to_all | solution.py:284
  266.4 2.7 collective-permute-start.6
  272.8 2.7 collective-permute-done.7
  275.5 2.6 collective-permute-start.8
  278.1 123.3 %scatter_sum.2 = (f32[4,176,128]{2,1,0:T(8,128)}, f32[4,176,128]{2,1,0:T(8,128)}, f32[4,176,128]{2,1,0:T(8,128)}, f32[4,64,128]{2,1,0:T(8,128)}) custom-call(bf16[4,32,176,128]{3,2,1,0:T(8,128)(2,1)} %wgrad.5.refs_0_, bf16[4,32,176,128]{3,2,1,0:T(8,128)(2,1)} %wgrad.6.refs_1_, bf16[4,32,176,128]{3,2,1,0:T(8,128)(2,1)} %wgrad.7.refs_2_, ...), custom_call_target="tpu_custom_call" | custom-call | flops 9699328 | bytes 77594624 | tf_op jit(solution)/shard_map/scatter_sum/pallas_call | solution.py:515
  402.6 7.8 %turn_back.1 = (bf16[3,512,1024]{2,1,0:T(8,128)(2,1)}, f32[512,1024]{1,0:T(8,128)}) custom-call(f32[512,128]{1,0:T(8,128)} %get-tuple-element.112.cos_ref, f32[512,128]{1,0:T(8,128)} %get-tuple-element.111.sin_ref, bf16[8,3,256,128]{3,2,1,0:T(8,128)(2,1)} %copy-done.1, bf16[8,3,256,128]{3,2,1,0:T(8,128)(2,1)} %copy-done.2), custom_call_target="tpu_custom_call" | custom-call | tf_op jit(solution)/shard_map/turn_back/pallas_call | solution.py:669
  410.4 10.2 %input_grad.1 = (f32[512,1024]{1,0:T(8,128)}, f32[1,1024]{1,0:T(1,128)}) custom-call(bf16[512,1024]{1,0:T(8,128)(2,1)} %bitcast.62, f32[512,1024]{1,0:T(8,128)} %get-tuple-element.65.dres_ref, f32[1,1024]{1,0:T(1,128)} %bitcast.88, bf16[3,512,1024]{2,1,0:T(8,128)(2,1)} %get-tuple-element.89.low_ref, bf16[1024,1024]{1,0:T(8,128)(2,1)} %wq_ref.3, ...), custom_call_target="tpu_custom_call" | custom-call | flops 3221225472 | bytes 14680064 | tf_op jit(solution)/shard_map/input_grad/pallas_call | solution.py:702
  426.5 2.4 collective-permute-start.2
  436.3 7.6 %wgrad.9 = (bf16[4,32,64,128]{3,2,1,0:T(8,128)(2,1)}, bf16[4,32,64,128]{3,2,1,0:T(8,128)(2,1)}, bf16[4,32,64,128]{3,2,1,0:T(8,128)(2,1)}) custom-call(bf16[512,1024]{1,0:T(8,128)(2,1)} %get-tuple-element.92.left_ref, bf16[512,1024]{1,0:T(8,128)(2,1)} %get-tuple-element.108.refs_0_, bf16[512,1024]{1,0:T(8,128)(2,1)} %get-tuple-element.107.refs_1_, ...), custom_call_target="tpu_custom_call" | custom-call | flops 3221225472 | bytes 10485760 | tf_op jit(solution)/shard_map/wgrad/pallas_call | solution.py:400
  445.9 2.9 copy.51
  448.8 2.9 copy.52
  451.7 45.0 %scatter_sum.3 = (f32[4,64,128]{2,1,0:T(8,128)}, f32[4,64,128]{2,1,0:T(8,128)}, f32[4,64,128]{2,1,0:T(8,128)}) custom-call(bf16[4,32,64,128]{3,2,1,0:T(8,128)(2,1)} %get-tuple-element.93.refs_0_, bf16[4,32,64,128]{3,2,1,0:T(8,128)(2,1)} %get-tuple-element.94.refs_1_, bf16[4,32,64,128]{3,2,1,0:T(8,128)(2,1)} %get-tuple-element.95.refs_2_), custom_call_target="tpu_custom_call" | custom-call | flops 3145728 | bytes 25165824 | tf_op jit(solution)/shard_map/scatter_sum/pallas_call | solution.py:515
  (94 shorter events, 33.6 us)
Async XLA Ops:
  0.6 3.6 copy-start.6
  60.2 3.7 copy-start.18
  60.2 40.4 %all-to-all-start = ((bf16[8,3,256,128]{3,2,1,0:T(8,128)(2,1)}), bf16[8,3,256,128]{3,2,1,0:T(8,128)(2,1)S(1)}, u32[]{:S(2)}, u32[]{:S(2)}) async-start(bf16[8,3,256,128]{3,2,1,0:T(8,128)(2,1)} %get-tuple-element.60), calls=%async_computation | async-start | bytes 3145728 | tf_op jit(solution)/shard_map/all_to_all | solution.py:284
  100.6 3.6 copy-start.5
  100.6 18.3 %all-to-all-start.3 = ((bf16[8,256,128]{2,1,0:T(8,128)(2,1)}), bf16[8,256,128]{2,1,0:T(8,128)(2,1)S(1)}, u32[]{:S(2)}, u32[]{:S(2)}) async-start(bf16[8,256,128]{2,1,0:T(8,128)(2,1)} %get-tuple-element.63), calls=%async_computation.3 | async-start | bytes 1048576 | tf_op jit(solution)/shard_map/all_to_all | solution.py:284
  104.3 20.6 %copy-start.7 = (bf16[256,2,1024]{2,1,0:T(2,128)(2,1)S(1)}, bf16[256,2,1024]{2,1,0:T(2,128)(2,1)}, u32[]{:S(2)}) copy-start(bf16[256,2,1024]{2,1,0:T(2,128)(2,1)} %param.25) | copy-start | bytes 3145732
  118.9 18.3 %copy-start.10 = (bf16[8,256,128]{2,1,0:T(8,128)(2,1)}, bf16[8,256,128]{2,1,0:T(8,128)(2,1)S(1)}, u32[]{:S(2)}) copy-start(bf16[8,256,128]{2,1,0:T(8,128)(2,1)S(1)} %all-to-all-done.3.refs_1_) | copy-start | bytes 1572868
  118.9 18.3 %all-to-all-start.1 = ((bf16[8,256,128]{2,1,0:T(8,128)(2,1)}), bf16[8,256,128]{2,1,0:T(8,128)(2,1)S(1)}, u32[]{:S(2)}, u32[]{:S(2)}) async-start(bf16[8,256,128]{2,1,0:T(8,128)(2,1)} %get-tuple-element.61), calls=%async_computation.1 | async-start | bytes 1048576 | tf_op jit(solution)/shard_map/all_to_all | solution.py:284
  188.1 21.1 %all-to-all-start.6 = ((bf16[8,256,128]{2,1,0:T(8,128)(2,1)}), bf16[8,256,128]{2,1,0:T(8,128)(2,1)S(1)}, u32[]{:S(2)}, u32[]{:S(2)}) async-start(bf16[8,256,128]{2,1,0:T(8,128)(2,1)} %get-tuple-element.69), calls=%async_computation.6 | async-start | bytes 1048576 | tf_op jit(solution)/shard_map/all_to_all | solution.py:284
  209.1 10.8 %copy-start.9 = (bf16[8,256,128]{2,1,0:T(8,128)(2,1)}, bf16[8,256,128]{2,1,0:T(8,128)(2,1)S(1)}, u32[]{:S(2)}) copy-start(bf16[8,256,128]{2,1,0:T(8,128)(2,1)S(1)} %all-to-all-done.6.do_ref) | copy-start | bytes 1572868
  209.1 49.9 %all-to-all-start.5 = ((bf16[8,3,256,128]{3,2,1,0:T(8,128)(2,1)}), bf16[8,3,256,128]{3,2,1,0:T(8,128)(2,1)S(1)}, u32[]{:S(2)}, u32[]{:S(2)}) async-start(bf16[8,3,256,128]{3,2,1,0:T(8,128)(2,1)} %attn_bwd.2), calls=%async_computation.5 | async-start | bytes 3145728 | tf_op jit(solution)/shard_map/all_to_all | solution.py:284
  259.0 6.0 %copy-start.16 = (f32[4,2,256]{2,1,0:T(2,128)S(1)}, f32[4,2,256]{2,1,0:T(2,128)}, u32[]{:S(2)}) copy-start(f32[4,2,256]{2,1,0:T(2,128)} %get-tuple-element.105) | copy-start | bytes 24580
  259.0 6.1 %copy-start.17 = (f32[1,1024]{1,0:T(1,128)S(1)}, f32[1,1024]{1,0:T(1,128)}, u32[]{:S(2)}) copy-start(f32[1,1024]{1,0:T(1,128)} %get-tuple-element.104) | copy-start | bytes 12292
  259.0 142.4 %copy-start.1 = (bf16[8,3,256,128]{3,2,1,0:T(8,128)(2,1)}, bf16[8,3,256,128]{3,2,1,0:T(8,128)(2,1)S(1)}, u32[]{:S(2)}) copy-start(bf16[8,3,256,128]{3,2,1,0:T(8,128)(2,1)S(1)} %all-to-all-done.5.refs_0_) | copy-start | bytes 4718596
  259.1 142.4 %all-to-all-start.7 = ((bf16[8,3,256,128]{3,2,1,0:T(8,128)(2,1)}), bf16[8,3,256,128]{3,2,1,0:T(8,128)(2,1)S(1)}, u32[]{:S(2)}, u32[]{:S(2)}) async-start(bf16[8,3,256,128]{3,2,1,0:T(8,128)(2,1)} %attn_bwd.3), calls=%async_computation.7 | async-start | bytes 3145728 | tf_op jit(solution)/shard_map/all_to_all | solution.py:284
  265.3 1.2 collective-permute-start.5
  266.4 4.3 collective-permute-start.6
  270.8 4.7 collective-permute-start.7
  275.5 145.2 %collective-permute-start.8 = (f32[1152]{0:T(1024)S(1)}, f32[1152]{0:T(1024)S(1)}, u32[]{:S(2)}, u32[]{:S(2)}) collective-permute-start(f32[1152]{0:T(1024)S(1)} %add.73), channel_id=1, source_target_pairs={{0,2},{1,3},{2,0},{3,1},{4,6},{5,7},{6,4},{7,5},{8,10},{9,11},{10,... | collective-permute-start | bytes 13832 | tf_op jit(solution)/shard_map/ppermute | solution.py:340
  410.4 12.4 %copy-start.8 = (bf16[512,1024]{1,0:T(8,128)(2,1)S(1)}, bf16[512,1024]{1,0:T(8,128)(2,1)}, u32[]{:S(2)}) copy-start(bf16[512,1024]{1,0:T(8,128)(2,1)} %get-tuple-element.64) | copy-start | bytes 3145732
  410.4 22.1 %copy-start = (bf16[3,512,1024]{2,1,0:T(8,128)(2,1)S(1)}, bf16[3,512,1024]{2,1,0:T(8,128)(2,1)}, u32[]{:S(2)}) copy-start(bf16[3,512,1024]{2,1,0:T(8,128)(2,1)} %get-tuple-element.89.low_ref) | copy-start | bytes 9437188
  420.7 1.5 collective-permute-start
  420.7 4.6 collective-permute-start.9
  422.9 3.6 collective-permute-start.1
  426.5 4.9 collective-permute-start.2
  431.4 3.7 collective-permute-start.3
  435.1 61.7 %collective-permute-start.4 = (f32[1024]{0:T(1024)S(1)}, f32[1024]{0:T(1024)S(1)}, u32[]{:S(2)}, u32[]{:S(2)}) collective-permute-start(f32[1024]{0:T(1024)S(1)} %add.69), channel_id=1, source_target_pairs={{0,4},{1,5},{2,6},{3,7},{4,0},{5,1},{6,2},{7,3},{8,12},{9,13},{10,... | collective-permute-start | bytes 12296 | tf_op jit(solution)/shard_map/ppermute | solution.py:340
  436.3 7.6 %copy-start.14 = (f32[4,176,128]{2,1,0:T(8,128)S(1)}, f32[4,176,128]{2,1,0:T(8,128)}, u32[]{:S(2)}) copy-start(f32[4,176,128]{2,1,0:T(8,128)} %get-tuple-element.100) | copy-start | bytes 1081348
  436.3 8.6 %copy-start.13 = (f32[4,176,128]{2,1,0:T(8,128)S(1)}, f32[4,176,128]{2,1,0:T(8,128)}, u32[]{:S(2)}) copy-start(f32[4,176,128]{2,1,0:T(8,128)} %get-tuple-element.101) | copy-start | bytes 1081348
  445.8 2.9 copy-start.4
  451.7 50.3 %copy-start.15 = (f32[4,64,128]{2,1,0:T(8,128)S(1)}, f32[4,64,128]{2,1,0:T(8,128)}, u32[]{:S(2)}) copy-start(f32[4,64,128]{2,1,0:T(8,128)} %get-tuple-element.99) | copy-start | bytes 393220
  451.7 51.0 %copy-start.12 = (f32[4,176,128]{2,1,0:T(8,128)S(1)}, f32[4,176,128]{2,1,0:T(8,128)}, u32[]{:S(2)}) copy-start(f32[4,176,128]{2,1,0:T(8,128)} %get-tuple-element.102) | copy-start | bytes 1081348
  (3 other events, 3.9 us)

commit v3 on v2

--- a/solution.py
+++ b/solution.py
@@ -202,9 +202,18 @@
     )(lens, qkv)
 
 
-def attn_bwd_kernel(row, n_docs, heads, lens_ref, qkv_ref, do_ref, o_ref, lse_ref, out_ref, dq_ref, delta_ref):
+def attn_bwd_kernel(rows, n_docs, heads, lens_ref, *refs):
+    scratch = refs[4 * rows :]
+    for row in range(rows):
+
+        @pl.when(pl.program_id(0) == row)
+        def _():
+            attn_bwd_row(row, n_docs, heads, lens_ref, *refs[4 * row : 4 * row + 4], *scratch)
+
+
+def attn_bwd_row(row, n_docs, heads, lens_ref, qkv_ref, do_ref, o_ref, lse_ref, out_ref, dq_ref, delta_ref):
     n_blk, _, length, width = qkv_ref.shape
-    j = pl.program_id(0)
+    j = pl.program_id(1)
     ends = doc_ends(lens_ref, row, n_docs)
     masks = head_masks(heads, width)
     scale = HEAD_DIM**-0.5
@@ -252,32 +261,34 @@
 
     zero = jnp.zeros((length, width), F32)
     d_key, d_value = lax.fori_loop(j, highest + 1, tile, (zero, zero))
-    out_ref[0, 0] = (dq_ref[j] * scale).astype(BF16)
-    out_ref[0, 1] = d_key.astype(BF16)
-    out_ref[0, 2] = d_value.astype(BF16)
-
-
-def attn_bwd(lens, qkv, d_out, attended, lse, row, n_docs):
-    n_blk, _, length, width = qkv.shape
+    out_ref[0, 0, 0] = (dq_ref[j] * scale).astype(BF16)
+    out_ref[0, 0, 1] = d_key.astype(BF16)
+    out_ref[0, 0, 2] = d_value.astype(BF16)
+
+
+def attn_bwd(lens, qkv, d_out, attended, lse, n_docs):
+    rows = len(qkv)
+    n_blk, _, length, width = qkv[0].shape
     heads = width // HEAD_DIM
-    whole = lambda a: pl.BlockSpec(a.shape, lambda j, lens: (0,) * a.ndim)
+    whole = lambda a: pl.BlockSpec(a.shape, lambda r, j, lens: (0,) * a.ndim)
+    arrays = [a for per_row in zip(qkv, d_out, attended, lse) for a in per_row]
     return pl.pallas_call(
-        functools.partial(attn_bwd_kernel, row, n_docs, heads),
+        functools.partial(attn_bwd_kernel, rows, n_docs, heads),
         grid_spec=pltpu.PrefetchScalarGridSpec(
             num_scalar_prefetch=1,
-            grid=(n_blk,),
-            in_specs=[whole(qkv), whole(d_out), whole(attended), whole(lse)],
-            out_specs=pl.BlockSpec((1, 3, length, width), lambda j, lens: (j, 0, 0, 0)),
+            grid=(rows, n_blk),
+            in_specs=[whole(a) for a in arrays],
+            out_specs=pl.BlockSpec((1, 1, 3, length, width), lambda r, j, lens: (j, r, 0, 0, 0)),
             scratch_shapes=[
                 pltpu.VMEM((n_blk, length, width), F32),
                 pltpu.VMEM((n_blk, heads, length), F32),
             ],
         ),
-        out_shape=jax.ShapeDtypeStruct((n_blk, 3, length, width), BF16),
+        out_shape=jax.ShapeDtypeStruct((n_blk, rows, 3, length, width), BF16),
         compiler_params=pltpu.CompilerParams(vmem_limit_bytes=VMEM_LIMIT),
-        cost_estimate=pl.CostEstimate(flops=2 * 10**10, bytes_accessed=6 * 10**6, transcendentals=10**7),
+        cost_estimate=pl.CostEstimate(flops=4 * 10**9, bytes_accessed=12 * 10**6, transcendentals=10**7),
         name="attn_bwd",
-    )(lens, qkv, d_out, attended, lse)
+    )(lens, *arrays)
 
 
 def exchange(values):
@@ -341,52 +352,60 @@
     return values
 
 
-def place_of(order, dp, blk):
-    place = 0
-    for name, bit in order:
-        place = 2 * place + (((dp if name == "dp" else blk) >> bit) & 1)
-    return place
-
-
 def chunks_of(block_rows, block_cols):
     cols = block_cols // 128
     return 4 // cols, cols, block_rows // (4 // cols)
 
 
+def place_of(order, dp, blk):
+    place = 0
+    for name, bit in order[1:]:
+        place = 2 * place + (((dp if name == "dp" else blk) >> bit) & 1)
+    return place
+
+
 def wgrad_kernel(orders, n_left, n_right, left_is_dp, n_out, left_ref, *refs):
-    right_refs, out_refs, turned_ref = refs[:n_out], refs[n_out : 2 * n_out], refs[2 * n_out]
+    right_refs, out_refs, turned_ref = refs[:n_out], refs[n_out : 3 * n_out], refs[3 * n_out]
     left_rows, right_cols = left_ref.shape[1] // n_left, right_refs[0].shape[1] // n_right
     row_parts, col_parts, size = chunks_of(left_rows, right_cols)
     q = pl.program_id(0)
+    core = lax.axis_index("dp") % 2
 
     @pl.when(q == 0)
     def _():
         turned_ref[...] = left_ref[...].T
 
     row_part, col_part = q // col_parts, q % col_parts
-    left = jnp.concatenate(
-        [
-            turned_ref[pl.ds(pl.multiple_of(k * left_rows + row_part * size, 16), size), :]
-            for k in range(n_left)
-        ],
-        axis=0,
-    )
-    for order, right_ref, out_ref in zip(orders, right_refs, out_refs):
-        if col_parts == 1:
-            right = right_ref[...]
-        else:
-            right = jnp.concatenate(
-                [
-                    right_ref[:, pl.ds(pl.multiple_of(k * right_cols + col_part * 128, 128), 128)]
-                    for k in range(n_right)
-                ],
-                axis=1,
-            )
-        result = dot(left, right).astype(BF16)
-        for k in range(n_left):
-            for m in range(n_right):
-                dp, blk = (k, m) if left_is_dp else (m, k)
-                out_ref[0, place_of(order, dp, blk)] = result[k * size : (k + 1) * size, m * 128 : (m + 1) * 128]
+    for half in range(2):
+        side = core if half == 0 else 1 - core
+        left_places = [2 * k + side for k in range(n_left // 2)] if left_is_dp else list(range(n_left))
+        right_places = list(range(n_right)) if left_is_dp else [2 * k + side for k in range(n_right // 2)]
+        left = jnp.concatenate(
+            [
+                turned_ref[pl.ds(pl.multiple_of(k * left_rows + row_part * size, 16), size), :]
+                for k in left_places
+            ],
+            axis=0,
+        )
+        for n, right_ref in enumerate(right_refs):
+            if left_is_dp:
+                right = right_ref[...]
+            else:
+                right = jnp.concatenate(
+                    [
+                        right_ref[:, pl.ds(pl.multiple_of(k * right_cols + col_part * 128, 128), 128)]
+                        for k in right_places
+                    ],
+                    axis=1,
+                )
+            result = dot(left, right).astype(BF16)
+            out_ref = out_refs[2 * n + half]
+            for k in range(len(left_places)):
+                for m in range(len(right_places)):
+                    dp, blk = (2 * k, m) if left_is_dp else (2 * m, k)
+                    out_ref[0, place_of(orders[n], dp, blk)] = result[
+                        k * size : (k + 1) * size, m * 128 : (m + 1) * 128
+                    ]
 
 
 def wgrad(orders, left, rights, left_is_dp):
@@ -397,12 +416,13 @@
     row_parts, col_parts, size = chunks_of(left_cols // n_left, right_cols // n_right)
     full = lambda a: pl.BlockSpec(a.shape, lambda q: (0, 0))
     n_out = len(rights)
-    return pl.pallas_call(
+    blocks = n_dp * n_blk // 2
+    flat = pl.pallas_call(
         functools.partial(wgrad_kernel, orders, n_left, n_right, left_is_dp, n_out),
         grid=(4,),
         in_specs=[full(left)] + [full(a) for a in rights],
-        out_specs=[pl.BlockSpec((1, n_dp * n_blk, size, 128), lambda q: (q, 0, 0, 0))] * n_out,
-        out_shape=[jax.ShapeDtypeStruct((4, n_dp * n_blk, size, 128), BF16)] * n_out,
+        out_specs=[pl.BlockSpec((1, blocks, size, 128), lambda q: (q, 0, 0, 0))] * (2 * n_out),
+        out_shape=[jax.ShapeDtypeStruct((4, blocks, size, 128), BF16)] * (2 * n_out),
         scratch_shapes=[pltpu.VMEM((left_cols, tokens), BF16)],
         compiler_params=pltpu.CompilerParams(vmem_limit_bytes=VMEM_LIMIT),
         cost_estimate=pl.CostEstimate(
@@ -412,6 +432,166 @@
         ),
         name="wgrad",
     )(left, *rights)
+    return [tuple(flat[2 * n : 2 * n + 2]) for n in range(n_out)]
+
+
+def blocks_dot(left_ref, right_ref, left_is_dp, side, col, order, n_dp, n_blk, out_ref, *at):
+    size = left_ref.shape[2]
+    tokens = left_ref.shape[3]
+    if left_is_dp:
+        left = jnp.concatenate([left_ref[2 * k + side, 0] for k in range(n_dp // 2)], axis=0)
+        right = right_ref[...]
+    else:
+        cols = right_ref.shape[1] // n_dp
+        left = left_ref[:, 0].reshape(n_blk * size, tokens)
+        right = jnp.concatenate(
+            [
+                right_ref[:, pl.ds(pl.multiple_of((2 * k + side) * cols + col * 128, 128), 128)]
+                for k in range(n_dp // 2)
+            ],
+            axis=1,
+        )
+    result = dot(left, right).astype(BF16)
+    for d in range(n_dp // 2):
+        for e in range(n_blk):
+            k, m = (d, e) if left_is_dp else (e, d)
+            out_ref[(*at, place_of(order, 2 * d, e))] = result[k * size : (k + 1) * size, m * 128 : (m + 1) * 128]
+
+
+def ffn_wgrad_kernel(plans, n_dp, n_blk, rows, *refs):
+    source = iter(refs)
+    take = lambda n: [next(source) for _ in range(n)]
+    n = len(plans)
+    lefts, rights, moved, outs, arrived = take(n), take(n), take(rows), take(2 * n), take(rows)
+    sents, landed, keeps = take(n), take(n), take(n)
+    send_sem, recv_sem, own_sem, out_sem, in_sem = take(5)
+    step = pl.program_id(0)
+    core, device = partner("dp", 0)
+    here = lax.axis_index("blk")
+
+    def own(r):
+        return pltpu.make_async_copy(moved[r].at[here], arrived[r].at[here], own_sem.at[r])
+
+    def across(r, m):
+        there = (here + m) % n_blk
+        return pltpu.make_async_remote_copy(
+            src_ref=moved[r].at[there],
+            dst_ref=arrived[r].at[here],
+            send_sem=out_sem.at[r, m],
+            recv_sem=in_sem.at[r, m],
+            device_id=(lax.axis_index("dp"), there),
+            device_id_type=MESH,
+        )
+
+    @pl.when(step == 0)
+    def _():
+        barrier = pltpu.get_barrier_semaphore()
+        pl.semaphore_signal(barrier, inc=1, device_id=device, device_id_type=MESH)
+        for m in range(1, n_blk):
+            there = (lax.axis_index("dp"), (here + m) % n_blk)
+            pl.semaphore_signal(barrier, inc=1, device_id=there, device_id_type=MESH)
+        pl.semaphore_wait(barrier, n_blk)
+        for r in range(rows):
+            own(r).start()
+            for m in range(1, n_blk):
+                across(r, m).start()
+
+    def remote(n, c):
+        return pltpu.make_async_remote_copy(
+            src_ref=sents[n].at[c],
+            dst_ref=landed[n].at[c],
+            send_sem=send_sem.at[n, c],
+            recv_sem=recv_sem.at[n, c],
+            device_id=device,
+            device_id_type=MESH,
+        )
+
+    for k, (order, left_is_dp, col_parts) in enumerate(plans):
+        c = step - 4 * k
+
+        @pl.when((c >= 0) & (c < 4))
+        def _():
+            make = lambda side, *out: blocks_dot(
+                lefts[k], rights[k], left_is_dp, side, c % col_parts, order, n_dp, n_blk, *out
+            )
+            make(1 - core, sents[k], c)
+            remote(k, c).start()
+            make(core, keeps[k], c % 2)
+
+        @pl.when((c >= 1) & (c < 5))
+        def _():
+            remote(k, c - 1).wait_recv()
+            mine, _ = partner(*order[1])
+            half = keeps[k].shape[1] // 2
+            for out_ref, side in ((outs[2 * k], mine), (outs[2 * k + 1], 1 - mine)):
+
+                def one(d, _):
+                    at = side * half + d
+                    out_ref[0, d] = keeps[k][(c - 1) % 2, at] + landed[k][c - 1, at]
+                    return 0
+
+                lax.fori_loop(0, half, one, 0)
+
+    @pl.when(step == 4 * n)
+    def _():
+        for k in range(n):
+            for c in range(4):
+                remote(k, c).wait_send()
+        for r in range(rows):
+            own(r).wait()
+            for m in range(1, n_blk):
+                across(r, m).wait()
+
+
+def ffn_wgrad(items, moved, collective_id):
+    n_dp, n_blk = lax.axis_size("dp"), lax.axis_size("blk")
+    lefts, rights, plans, left_specs, right_specs, out_specs, outs, scratch = [], [], [], [], [], [], [], []
+    held = n_dp * n_blk // 2
+    flops = 0
+    for k, (order, left_is_dp, left, right) in enumerate(items):
+        n_left, n_right = (n_dp, n_blk) if left_is_dp else (n_blk, n_dp)
+        cols, tokens = left.shape
+        row_parts, col_parts, size = chunks_of(cols // n_left, right.shape[1] // n_right)
+        lefts.append(left.reshape(n_left, row_parts, size, tokens))
+        rights.append(right)
+        plans.append((order, left_is_dp, col_parts))
+        flops += 2 * left.size * right.shape[1]
+        left_specs.append(
+            pl.BlockSpec(
+                (n_left, 1, size, tokens),
+                lambda p, k=k, col_parts=col_parts: (0, jnp.clip(p - 4 * k, 0, 3) // col_parts, 0, 0),
+            )
+        )
+        right_specs.append(pl.BlockSpec(right.shape, lambda p: (0, 0), pipeline_mode=pl.Buffered(1)))
+        out_specs += [
+            pl.BlockSpec((1, held // 2, size, 128), lambda p, k=k: (jnp.clip(p - 1 - 4 * k, 0, 3), 0, 0, 0))
+        ] * 2
+        outs += [jax.ShapeDtypeStruct((4, held // 2, size, 128), BF16)] * 2
+        scratch.append((held, size, 128))
+    n = len(items)
+    flat = pl.pallas_call(
+        functools.partial(ffn_wgrad_kernel, plans, n_dp, n_blk, len(moved)),
+        grid=(4 * n + 1,),
+        in_specs=left_specs + right_specs + [pl.BlockSpec(memory_space=pl.ANY)] * len(moved),
+        out_specs=out_specs + [pl.BlockSpec(memory_space=pl.ANY)] * len(moved),
+        out_shape=outs + [jax.ShapeDtypeStruct(a.shape, a.dtype) for a in moved],
+        scratch_shapes=[pltpu.VMEM((4,) + a, BF16) for a in scratch] * 2
+        + [pltpu.VMEM((2,) + a, BF16) for a in scratch]
+        + [pltpu.SemaphoreType.DMA((n, 4))] * 2
+        + [pltpu.SemaphoreType.DMA((len(moved),))]
+        + [pltpu.SemaphoreType.DMA((len(moved), n_blk))] * 2,
+        compiler_params=pltpu.CompilerParams(
+            collective_id=collective_id, has_side_effects=True, vmem_limit_bytes=VMEM_LIMIT
+        ),
+        cost_estimate=pl.CostEstimate(flops=flops, bytes_accessed=flops // 400, transcendentals=0),
+        name="ffn_wgrad",
+    )(*lefts, *rights, *moved)
+    return [tuple(flat[2 * k : 2 * k + 2]) for k in range(n)], list(flat[2 * n :])
+
+
+def swap(values, name, bit):
+    size = lax.axis_size(name)
+    return lax.ppermute(values, name, [(k, k ^ (1 << bit)) for k in range(size)])
 
 
 def partner(name, bit):
@@ -422,37 +602,38 @@
     return mine, (other["dp"], other["blk"])
 
 
-def scatter_kernel(orders, *refs):
+def scatter_kernel(orders, fresh, *refs):
     n_streams, n_stages = len(orders), len(orders[0])
+    source = iter(refs)
     take = lambda n: [next(source) for _ in range(n)]
-    source = iter(refs)
-    grads, outs, works = take(n_streams), take(n_streams), take(n_streams)
+    keeps, others, outs, works = take(n_streams), take(n_streams), take(n_streams), take(n_streams)
     landed = [take(n_stages) for _ in range(n_streams)]
-    local_sem, send_sem, recv_sem = take(3)
-    n_chunks = grads[0].shape[0]
-    blocks = grads[0].shape[1]
+    local_sem, other_sem, send_sem, recv_sem = take(4)
+    n_chunks, held = keeps[0].shape[:2]
+    greeted = sorted({stage for order in orders for stage in order[0 if fresh else 1 :]})
 
     barrier = pltpu.get_barrier_semaphore()
-    for name, bit in orders[0]:
+    for name, bit in greeted:
         pl.semaphore_signal(barrier, inc=1, device_id=partner(name, bit)[1], device_id_type=MESH)
-    pl.semaphore_wait(barrier, n_stages)
+    pl.semaphore_wait(barrier, len(greeted))
 
     def base_of(k, stage):
         base = 0
         for earlier in range(1, stage):
-            base = base + partner(*orders[k][earlier])[0] * (blocks >> (earlier + 1))
+            base = base + partner(*orders[k][earlier])[0] * (held >> earlier)
         return base
 
     def local(k, c):
-        mine = partner(*orders[k][0])[0]
-        half = blocks // 2
-        return pltpu.make_async_copy(grads[k].at[c, pl.ds(mine * half, half)], works[k].at[c], local_sem.at[k, c])
+        return pltpu.make_async_copy(keeps[k].at[c], works[k].at[c], local_sem.at[k, c])
+
+    def other(k, c):
+        return pltpu.make_async_copy(others[k].at[c], landed[k][0].at[c], other_sem.at[k, c])
 
     def remote(k, stage, c):
         mine, device = partner(*orders[k][stage])
-        half = blocks >> (stage + 1)
+        half = held >> stage
         if stage == 0:
-            sent = grads[k].at[c, pl.ds((1 - mine) * half, half)]
+            sent = others[k].at[c]
         else:
             sent = works[k].at[c, pl.ds(base_of(k, stage) + (1 - mine) * half, half)]
         return pltpu.make_async_remote_copy(
@@ -465,18 +646,16 @@
         )
 
     def add(k, stage, c):
-        count = blocks >> (stage + 1)
         base = base_of(k, stage + 1)
         if stage == n_stages - 1:
             outs[k][c] = works[k][c, base].astype(F32) + landed[k][stage][c, 0].astype(F32)
             return
 
         def one(d, _):
-            kept = works[k][c, base + d].astype(F32) + landed[k][stage][c, d].astype(F32)
-            works[k][c, base + d] = kept.astype(BF16)
+            works[k][c, base + d] = works[k][c, base + d] + landed[k][stage][c, d]
             return 0
 
-        lax.fori_loop(0, count, one, 0)
+        lax.fori_loop(0, held >> stage, one, 0)
 
     def step(t, _):
         for stage in range(n_stages + 1):
@@ -487,12 +666,17 @@
                 for k in range(n_streams):
                     if stage == 0:
                         local(k, c).start()
+                        if not fresh:
+                            other(k, c).start()
                     else:
                         if stage == 1:
                             local(k, c).wait()
-                        remote(k, stage - 1, c).wait_recv()
+                        if stage == 1 and not fresh:
+                            other(k, c).wait()
+                        else:
+                            remote(k, stage - 1, c).wait_recv()
                         add(k, stage - 1, c)
-                    if stage < n_stages:
+                    if stage < n_stages and (fresh or stage > 0):
                         remote(k, stage, c).start()
 
         return 0
@@ -501,39 +685,37 @@
 
     def finish(c, _):
         for k in range(n_streams):
-            for stage in range(n_stages):
+            for stage in range(0 if fresh else 1, n_stages):
                 remote(k, stage, c).wait_send()
         return 0
 
     lax.fori_loop(0, n_chunks, finish, 0)
 
 
-def scatter_sum(grads, orders, collective_id):
-    n_streams, n_stages = len(grads), len(orders[0])
-    n_chunks, blocks = grads[0].shape[:2]
-    size = sum(a.size for a in grads)
+def scatter_sum(pairs, orders, fresh, collective_id):
+    n_streams, n_stages = len(pairs), len(orders[0])
+    keeps, others = [pair[0] for pair in pairs], [pair[1] for pair in pairs]
+    n_chunks, held = keeps[0].shape[:2]
+    size = sum(a.size for a in keeps)
     return pl.pallas_call(
-        functools.partial(scatter_kernel, orders),
-        in_specs=[pl.BlockSpec(memory_space=pl.ANY)] * n_streams,
+        functools.partial(scatter_kernel, orders, fresh),
+        in_specs=[pl.BlockSpec(memory_space=pl.ANY)] * (2 * n_streams),
         out_specs=[pl.BlockSpec(memory_space=pltpu.VMEM)] * n_streams,
-        out_shape=[jax.ShapeDtypeStruct((n_chunks,) + a.shape[2:], F32) for a in grads],
-        scratch_shapes=[pltpu.VMEM((n_chunks, blocks // 2) + a.shape[2:], BF16) for a in grads]
+        out_shape=[jax.ShapeDtypeStruct((n_chunks,) + a.shape[2:], F32) for a in keeps],
+        scratch_shapes=[pltpu.VMEM(a.shape, BF16) for a in keeps]
         + [
-            pltpu.VMEM((n_chunks, blocks >> (stage + 1)) + a.shape[2:], BF16)
-            for a in grads
+            pltpu.VMEM((n_chunks, held >> stage) + a.shape[2:], BF16)
+            for a in keeps
             for stage in range(n_stages)
         ]
-        + [
-            pltpu.SemaphoreType.DMA((n_streams, n_chunks)),
-            pltpu.SemaphoreType.DMA((n_streams, n_stages, n_chunks)),
-            pltpu.SemaphoreType.DMA((n_streams, n_stages, n_chunks)),
-        ],
+        + [pltpu.SemaphoreType.DMA((n_streams, n_chunks))] * 2
+        + [pltpu.SemaphoreType.DMA((n_streams, n_stages, n_chunks))] * 2,
         compiler_params=pltpu.CompilerParams(
             collective_id=collective_id, has_side_effects=True, vmem_limit_bytes=VMEM_LIMIT
         ),
-        cost_estimate=pl.CostEstimate(flops=size, bytes_accessed=8 * size, transcendentals=0),
+        cost_estimate=pl.CostEstimate(flops=10**11, bytes_accessed=16 * size, transcendentals=0),
         name="scatter_sum",
-    )(*grads)
+    )(*keeps, *others)
 
 
 def whole_block(pieces, block_rows, block_cols):
@@ -547,9 +729,9 @@
     take = lambda n: [next(source) for _ in range(n)]
     gathered = take(rows)
     hidden_ref, cot_ref, gain_ref, wo_ref, wg_ref, wu_ref, wd_ref = take(7)
-    low_ref, mid_ref, inner_ref, dgate_ref, dup_ref, out_ref, dres_ref, dbranch_ref, dgain_ref = take(9)
+    lowt_ref, mid_ref, inner_ref, dgate_ref, dup_ref, out_ref, dres_ref, dbranch_ref, dgain_ref = take(9)
     d_attn = take(rows)
-    resid_ref, acc_ref, dmid_ref = take(3)
+    low_ref, resid_ref, acc_ref, dmid_ref = take(4)
     length, width = gathered[0].shape[1:]
     step = pl.program_id(0)
 
@@ -565,6 +747,7 @@
             mid_ref[at, :] = (normed * gain_ref[...]).astype(BF16)
         acc_ref[...] = jnp.zeros_like(acc_ref)
         dmid_ref[...] = jnp.zeros_like(dmid_ref)
+        lowt_ref[...] = low_ref[...].T
 
     for r in range(rows):
         at = pl.ds(r * length, length)
@@ -576,9 +759,9 @@
         inner = (act * up).astype(BF16)
         d_gate = (d_inner * up * (sigma * (1.0 + gate * (1.0 - sigma)))).astype(BF16)
         d_up = (d_inner * act).astype(BF16)
-        inner_ref[at, :] = inner
-        dgate_ref[at, :] = d_gate
-        dup_ref[at, :] = d_up
+        inner_ref[:, at] = inner.T
+        dgate_ref[:, at] = d_gate.T
+        dup_ref[:, at] = d_up.T
         acc_ref[at, :] += dot(inner, wd_ref[...])
         dmid_ref[at, :] += dot_nt(d_gate, wg_ref[...]) + dot_nt(d_up, wu_ref[...])
 
@@ -612,10 +795,10 @@
     once = lambda a: pl.BlockSpec(a.shape, lambda j: (0,) * len(a.shape), pipeline_mode=pl.Buffered(1))
     cols = pl.BlockSpec((model, chunk), lambda j: (0, j))
     shape = jax.ShapeDtypeStruct
-    token_cols = pl.BlockSpec((tokens, chunk), lambda j: (0, j))
+    inner_rows = pl.BlockSpec((chunk, tokens), lambda j: (j, 0))
     outs = (
-        [shape((tokens, model), BF16)] * 2
-        + [shape((tokens, inner), BF16)] * 3
+        [shape((model, tokens), BF16), shape((tokens, model), BF16)]
+        + [shape((inner, tokens), BF16)] * 3
         + [shape((tokens, model), BF16), shape((tokens, model), F32), shape((tokens, model), BF16)]
         + [shape((1, model), F32)]
         + [shape((n_blk, length, width), BF16)] * rows
@@ -625,9 +808,9 @@
         grid=(inner // chunk,),
         in_specs=[once(a) for a in gathered]
         + [once(hidden), once(cot), once(gain), once(w_out), cols, cols, pl.BlockSpec((chunk, model), lambda j: (j, 0))],
-        out_specs=[full(outs[0])] * 2 + [token_cols] * 3 + [full(a) for a in outs[5:]],
+        out_specs=[full(a) for a in outs[:2]] + [inner_rows] * 3 + [full(a) for a in outs[5:]],
         out_shape=outs,
-        scratch_shapes=[pltpu.VMEM((tokens, model), F32)] * 3,
+        scratch_shapes=[pltpu.VMEM((tokens, model), BF16)] + [pltpu.VMEM((tokens, model), F32)] * 3,
         compiler_params=pltpu.CompilerParams(vmem_limit_bytes=VMEM_LIMIT),
         cost_estimate=pl.CostEstimate(
             flops=12 * tokens * model * inner + 4 * tokens * model * model,
@@ -638,15 +821,14 @@
     )(*gathered, hidden, cot, gain, w_out, w_gate, w_up, w_down)
 
 
-def turn_back_kernel(rows, cos_ref, sin_ref, *refs):
-    backs, (low_ref, first_ref) = refs[:rows], refs[rows:]
-    n_blk, _, length, width = backs[0].shape
+def turn_back_kernel(cos_ref, sin_ref, back_ref, low_ref, first_ref):
+    n_blk, rows, _, length, width = back_ref.shape
     which = pl.program_id(0)
     for r in range(rows):
         at = pl.ds(r * length, length)
         for s in range(n_blk):
             cols = slice(s * width, (s + 1) * width)
-            values = backs[r][s, 0].astype(F32)
+            values = back_ref[s, r, 0].astype(F32)
 
             @pl.when(which < 2)
             def _():
@@ -661,15 +843,14 @@
                 low_ref[0, at, cols] = (0.5 * values).astype(BF16)
 
 
-def turn_back(backs, cos, sin):
-    rows = len(backs)
-    n_blk, _, length, width = backs[0].shape
+def turn_back(back, cos, sin):
+    n_blk, rows, _, length, width = back.shape
     tokens, model = rows * length, n_blk * width
     full = lambda a: pl.BlockSpec(a.shape, lambda w: (0, 0))
     return pl.pallas_call(
-        functools.partial(turn_back_kernel, rows),
+        turn_back_kernel,
         grid=(3,),
-        in_specs=[full(cos), full(sin)] + [pl.BlockSpec((n_blk, 1, length, width), lambda w: (0, w, 0, 0))] * rows,
+        in_specs=[full(cos), full(sin), pl.BlockSpec((n_blk, rows, 1, length, width), lambda w: (0, 0, w, 0, 0))],
         out_specs=[
             pl.BlockSpec((1, tokens, model), lambda w: (w, 0, 0)),
             pl.BlockSpec((tokens, model), lambda w: (0, 0)),
@@ -677,7 +858,7 @@
         out_shape=[jax.ShapeDtypeStruct((3, tokens, model), BF16), jax.ShapeDtypeStruct((tokens, model), F32)],
         compiler_params=pltpu.CompilerParams(vmem_limit_bytes=VMEM_LIMIT),
         name="turn_back",
-    )(cos, sin, *backs)
+    )(cos, sin, back)
 
 
 def input_grad_kernel(hidden_ref, dres_ref, gain_ref, low_ref, wq_ref, wk_ref, wv_ref, out_ref, dgain_ref):
@@ -771,33 +952,39 @@
         attended.append(o_f)
         lse.append(lse_r)
         gathered.append(exchange(o_low))
-    attn_low, normed_mid, inner_low, d_gate, d_up, block_out, d_resid_mid, d_branch, d_gain_two, *d_attn = feed_forward(
+    attn_low_t, normed_mid, inner_t, d_gate_t, d_up_t, block_out, d_resid_mid, d_branch, d_gain_two, *d_attn = feed_forward(
         gathered, hidden, cot, row_gain(ffn_gain), w_out, w_gate, w_up, w_down
     )
-    d_own = [exchange(d_attn[r]) for r in range(rows)]
 
     inner = w_gate.shape[1]
     by_blocks = (model // n_dp) % 128 == 0 and width == 128 and (inner // n_blk) % 32 == 0
     early, late = scatter_steps(False), scatter_steps(True)
     if by_blocks:
-        (gate_blocks,) = wgrad([early], d_gate, [normed_mid], False)
-        (up_blocks,) = wgrad([early], d_up, [normed_mid], False)
-        (down_blocks,) = wgrad([late], inner_low, [cot], True)
-        (project_blocks,) = wgrad([early], attn_low, [d_branch], True)
-        ffn_blocks = (gate_blocks, up_blocks, down_blocks, project_blocks)
-
-    back_own = [attn_bwd(lens, qkv[r], d_own[r], attended[r], lse[r], r, n_docs) for r in range(rows)]
+        folded, d_own = ffn_wgrad(
+            (
+                (early, False, d_gate_t, normed_mid),
+                (early, False, d_up_t, normed_mid),
+                (late, True, inner_t, cot),
+                (late, True, attn_low_t, d_branch),
+            ),
+            d_attn,
+            2,
+        )
+        kept = [keep for keep, sent in folded]
+        ffn_got = [swap(sent, *(early[1] if k < 2 else late[1])) for k, (_, sent) in enumerate(folded)]
+        back_own = attn_bwd(lens, qkv, d_own, attended, lse, n_docs)
+        back = exchange(back_own)
+        token, kept = lax.optimization_barrier((back_own, kept))
+        sums_ffn = scatter_sum(list(zip(kept, ffn_got)), (early[1:],) * 2 + (late[1:],) * 2, False, 0)
+        back, sums_ffn = lax.optimization_barrier((back, sums_ffn))
+    else:
+        d_own = [exchange(d_attn[r]) for r in range(rows)]
+        back = exchange(attn_bwd(lens, qkv, d_own, attended, lse, n_docs))
+    low, grad_first = turn_back(back, cos, sin)
+
     if by_blocks:
-        back_own[-1], ffn_blocks = lax.optimization_barrier((back_own[-1], ffn_blocks))
-    back = [exchange(b) for b in back_own]
-    if by_blocks:
-        sums_ffn = scatter_sum(ffn_blocks, (early, early, late, early), 0)
-        back, sums_ffn = lax.optimization_barrier((back, sums_ffn))
-    low, grad_first = turn_back(back, cos, sin)
-
-    if by_blocks:
-        qkv_blocks = wgrad([early, late, early], normed_in, [low[0], low[1], low[2]], True)
-        sums_qkv = scatter_sum(qkv_blocks, (early, late, early), 1)
+        qkv_pairs = wgrad([early, late, early], normed_in, [low[0], low[1], low[2]], True)
+        sums_qkv = scatter_sum(qkv_pairs, (early, late, early), True, 1)
         block = lambda pieces, r, c: whole_block(pieces, r, c)
         grad_gate = block(sums_ffn[0], inner // n_blk, model // n_dp).T
         grad_up = block(sums_ffn[1], inner // n_blk, model // n_dp).T
@@ -807,17 +994,16 @@
     else:
         mid_cf, in_cf = core_first(normed_mid), core_first(normed_in)
         sent = lambda a, b, name, y: scatter(dot_tn(a, b).astype(BF16), name, y).astype(F32)
-        grad_down = sent(inner_low, y_first(cot), "dp", False)
-        grad_gate = sent(d_gate, mid_cf, "blk", False).T
-        grad_up = sent(d_up, mid_cf, "blk", True).T
-        grad_project = sent(d_branch, core_first(attn_low), "blk", True).T
+        grad_down = sent(inner_t.T, y_first(cot), "dp", False)
+        grad_gate = sent(d_gate_t.T, mid_cf, "blk", False).T
+        grad_up = sent(d_up_t.T, mid_cf, "blk", True).T
+        grad_project = sent(d_branch, core_first(attn_low_t.T), "blk", True).T
         grad_query, grad_key, grad_value = [sent(low[k], in_cf, "blk", True).T for k in range(3)]
     grad_input, d_gain_one = input_grad(hidden, d_resid_mid, row_gain(attn_gain), low, w_query, w_key, w_value)
 
     squares = jnp.sum(sums, axis=(0, 2))
-    squares = jnp.concatenate([squares, jnp.zeros((126,), F32)])
-    early_sums = total(jnp.concatenate([d_gain_two.reshape(model), squares]))
-    gain_one = total(d_gain_one.reshape(model))
+    small = jnp.concatenate([d_gain_one.reshape(model), d_gain_two.reshape(model), squares, jnp.zeros((126,), F32)])
+    small = total(small)
     n_entries = n_blk * length * rows * n_dp * model
     return (
         unflat(block_out),
@@ -830,10 +1016,10 @@
         grad_gate,
         grad_up,
         grad_down,
-        gain_one,
-        early_sums[:model],
-        early_sums[model] / n_entries,
-        early_sums[model + 1] / n_entries,
+        small[:model],
+        small[model : 2 * model],
+        small[2 * model] / n_entries,
+        small[2 * model + 1] / n_entries,
     )
 
 

time: 509 us -> 485 us (0.953)
  blocking collectives: 61.5 us -> 44.4 us
  waiting for transfers between devices: 42.7 us -> 58.9 us
  starting transfers between devices: 42.5 us -> 27.6 us
    pallas_call x5 -> x1, Pallas kernels: 36.5 us -> 7.67 us  [wgrad(): pl.pallas_call(functools.partial(wgrad_kernel, orders, n_left, n_right, l...]
    ppermute x0 -> x4, waiting for transfers between devices: none -> 23.3 us  [swap(): return lax.ppermute(values, name, [(k, k ^ 1 << bit) for k in range(size)])]
    pallas_call x5, Pallas kernels: 209 us -> 230 us  [the longest x2 148 us: scatter_sum(): pl.pallas_call(functools.partial(scatter_kernel, orders, fresh), in_specs...]
    all_to_all x2 -> x1, blocking collectives: 61.5 us -> 44.4 us  [exchange(): return lax.all_to_all(values, 'blk', 0, 0, tiled=True)]
    all_to_all x6 -> x4, starting transfers between devices: 28.9 us -> 17.2 us  [exchange(): return lax.all_to_all(values, 'blk', 0, 0, tiled=True)]
    ppermute x10 -> x5, starting transfers between devices: 13.6 us -> 6.21 us  [total(): lax.ppermute(values, name, [(k, k ^ 1 << bit) for k in range(size)])]
    ppermute x10 -> x5, waiting for transfers between devices: 7.88 us -> 1.66 us  [total(): lax.ppermute(values, name, [(k, k ^ 1 << bit) for k in range(size)])]
    all_to_all x6 -> x4, waiting for transfers between devices: 34.8 us -> 34 us  [exchange(): return lax.all_to_all(values, 'blk', 0, 0, tiled=True)]
  transfers between devices with their start and end apart: 16 -> 13, of which waited for: 9 -> 6; matrix products, arithmetic and copies ran while one was open for 3% -> 3% of each run, Pallas kernels for 56% -> 45%
where the time goes in v3:
time: 485 us; the launch traced here: 483 us
  Pallas kernels  319 us (66%)
  waiting for transfers between devices  58.9 us (12%)
  blocking collectives  44.4 us (9%)
  starting transfers between devices  27.6 us (6%)
  local copies, waits for them, and re-layouts  26.2 us (5%)
    pallas_call x2, Pallas kernels, scatter_sum(): pl.pallas_call(functools.partial(scatter_kernel, orders, fresh), in_specs...  148 us
    all_to_all x1, blocking collectives, exchange(): return lax.all_to_all(values, 'blk', 0, 0, tiled=True)  44.4 us
    pallas_call x1, Pallas kernels, ffn_wgrad(): pl.pallas_call(functools.partial(ffn_wgrad_kernel, plans, n_dp, n_blk, le...  41.1 us
    all_to_all x4, waiting for transfers between devices, exchange(): return lax.all_to_all(values, 'blk', 0, 0, tiled=True)  34 us
    pallas_call x1, Pallas kernels, attn_bwd(): pl.pallas_call(functools.partial(attn_bwd_kernel, rows, n_docs, heads), g...  33.6 us
    pallas_call x1, Pallas kernels, feed_forward(): pl.pallas_call(functools.partial(ffn_kernel, rows, n_blk), grid=(inner //...  32.8 us
    pallas_call x2, Pallas kernels, attn_fwd(): pl.pallas_call(functools.partial(attn_fwd_kernel, row, n_docs, heads), gr...  29.5 us
    ppermute x4, waiting for transfers between devices, swap(): return lax.ppermute(values, name, [(k, k ^ 1 << bit) for k in range(size)])  23.3 us
  transfers between devices with their start and end apart: 13, of which 6 were waited for; matrix products, arithmetic and copies ran while one was open for 3% of the time, Pallas kernels for 45%

profile of v3, /device:TPU:0, one launch (start us, length us, event | category | flops | bytes accessed | tf_op | source)
XLA Modules:
  0.0 483.4 jit_solution(4827234971345583094)
XLA Ops:
  1.7 2.5 copy.35
  5.5 1.8 fusion
  7.3 8.5 %qkv.1 = (bf16[8,3,256,128]{3,2,1,0:T(8,128)(2,1)}, bf16[8,3,256,128]{3,2,1,0:T(8,128)(2,1)}, bf16[512,1024]{1,0:T(8,128)(2,1)}, f32[4,2,256]{2,1,0:T(2,128)}) custom-call(bf16[512,1024]{1,0:T(8,128)(2,1)} %bitcast.64, bf16[512,1024]{1,0:T(8,128)(2,1)} %bitcast.80, f32[512,128]{1,0:T(8,128)} %get-tuple-element.136.cos_ref, ...), custom_call_target="tpu_custom_call" | custom-call | flops 3221225472 | bytes 11534336 | tf_op jit(solution)/shard_map/qkv/pallas_call | solution.py:83
  15.8 44.4 %all_to_all.25.qkv_ref.refs_4_ = bf16[8,3,256,128]{3,2,1,0:T(8,128)(2,1)} all-to-all(bf16[8,3,256,128]{3,2,1,0:T(8,128)(2,1)} %get-tuple-element.73), channel_id=1, replica_groups=mesh['dp'=4,'blk'=8] {'blk'}, dimensions={0} | all-to-all | bytes 3145728 | tf_op jit(solution)/shard_map/all_to_all | solution.py:295
  60.2 3.7 all-to-all-start
  64.5 14.5 %attn_fwd.3 = (f32[8,256,128]{2,1,0:T(8,128)}, bf16[8,256,128]{2,1,0:T(8,128)(2,1)}, f32[8,2,256]{2,1,0:T(2,128)}) custom-call(s32[16]{0:T(128)} %reshape.140.lens_ref, bf16[8,3,256,128]{3,2,1,0:T(8,128)(2,1)} %all_to_all.25.qkv_ref.refs_4_), custom_call_target="tpu_custom_call" | custom-call | flops 10000000000 | bytes 3000000 | tf_op jit(solution)/shard_map/attn_fwd/pallas_call | solution.py:185
  79.0 21.6 %all-to-all-done.qkv_ref.refs_0_ = bf16[8,3,256,128]{3,2,1,0:T(8,128)(2,1)S(1)} async-done(((bf16[8,3,256,128]{3,2,1,0:T(8,128)(2,1)}), bf16[8,3,256,128]{3,2,1,0:T(8,128)(2,1)S(1)}, u32[]{:S(2)}, u32[]{:S(2)}) %all-to-all-start) | async-done | bytes 1572896 | tf_op jit(solution)/shard_map/all_to_all | solution.py:295
  100.6 3.6 all-to-all-start.3
  104.2 15.1 %attn_fwd.2 = (f32[8,256,128]{2,1,0:T(8,128)}, bf16[8,256,128]{2,1,0:T(8,128)(2,1)}, f32[8,2,256]{2,1,0:T(2,128)}) custom-call(s32[16]{0:T(128)} %reshape.140.lens_ref, bf16[8,3,256,128]{3,2,1,0:T(8,128)(2,1)} %copy-done.4), custom_call_target="tpu_custom_call" | custom-call | flops 10000000000 | bytes 3000000 | tf_op jit(solution)/shard_map/attn_fwd/pallas_call | solution.py:185
  119.3 6.0 %all-to-all-start.1 = ((bf16[8,256,128]{2,1,0:T(8,128)(2,1)}), bf16[8,256,128]{2,1,0:T(8,128)(2,1)S(1)}, u32[]{:S(2)}, u32[]{:S(2)}) async-start(bf16[8,256,128]{2,1,0:T(8,128)(2,1)} %get-tuple-element.72), calls=%async_computation.1 | async-start | bytes 1048576 | tf_op jit(solution)/shard_map/all_to_all | solution.py:295
  126.6 12.4 %all-to-all-done.1.refs_0_ = bf16[8,256,128]{2,1,0:T(8,128)(2,1)S(1)} async-done(((bf16[8,256,128]{2,1,0:T(8,128)(2,1)}), bf16[8,256,128]{2,1,0:T(8,128)(2,1)S(1)}, u32[]{:S(2)}, u32[]{:S(2)}) %all-to-all-start.1) | async-done | bytes 524320 | tf_op jit(solution)/shard_map/all_to_all | solution.py:295
  139.8 32.8 %ffn.1 = (bf16[1024,512]{1,0:T(8,128)(2,1)}, bf16[512,1024]{1,0:T(8,128)(2,1)}, bf16[2816,512]{1,0:T(8,128)(2,1)}, bf16[2816,512]{1,0:T(8,128)(2,1)}, bf16[2816,...) custom-call(bf16[8,256,128]{2,1,0:T(8,128)(2,1)} %copy-done.8, ...), custom_call_target="tpu_custom_call" | custom-call | flops 19864223744 | bytes 36438016 | tf_op jit(solution)/shard_map/ffn/pallas_call | solution.py:806
  172.6 41.1 %ffn_wgrad.1 = (bf16[4,8,176,128]{3,2,1,0:T(8,128)(2,1)}, bf16[4,8,176,128]{3,2,1,0:T(8,128)(2,1)}, bf16[4,8,176,128]{3,2,1,0:T(8,128)(2,1)}, bf16[4,8,176,128]{...) custom-call(bf16[8,2,176,512]{3,2,1,0:T(8,128)(2,1)} %bitcast.97, ...), custom_call_target="tpu_custom_call" | custom-call | flops 9932111872 | bytes 24830280 | tf_op jit(solution)/shard_map/ffn_wgrad/pallas_call | solution.py:572
  213.7 1.5 collective-permute-start
  216.3 1.5 collective-permute-start.3
  217.9 33.6 %attn_bwd.1 = bf16[8,2,3,256,128]{4,3,2,1,0:T(8,128)(2,1)} custom-call(s32[16]{0:T(128)} %reshape.140.lens_ref, bf16[8,3,256,128]{3,2,1,0:T(8,128)(2,1)} %copy-done.4, bf16[8,256,128]{2,1,0:T(8,128)(2,1)} %get-tuple-element.85.refs_1_, f32[8,256,128]{2,1,0:T(8,128)} %get-tuple-element.86.refs_2_, f32[8,2,256]{2,1,0:T(2,128)} %get-tuple-element.87.refs_3_, ...), custom_call_target="tpu_custom_call" | custom-call | flops 4000000000 | bytes 12000000 | tf_op jit(solution)/shard_map/attn_bwd/pallas_call | solution.py:275
  251.5 3.9 all-to-all-start.4
  255.4 20.9 %collective-permute-done.3.refs_7_ = bf16[4,8,64,128]{3,2,1,0:T(8,128)(2,1)} collective-permute-done((bf16[4,8,64,128]{3,2,1,0:T(8,128)(2,1)}, bf16[4,8,64,128]{3,2,1,0:T(8,128)(2,1)}, u32[]{:S(2)}, u32[]{:S(2)}) %collective-permute-start.3) | collective-permute-done | bytes 524320 | tf_op jit(solution)/shard_map/ppermute | solution.py:594
  276.3 2.4 collective-permute-done.1.refs_5_
  278.6 102.2 %scatter_sum.2 = (f32[4,176,128]{2,1,0:T(8,128)}, f32[4,176,128]{2,1,0:T(8,128)}, f32[4,176,128]{2,1,0:T(8,128)}, f32[4,64,128]{2,1,0:T(8,128)}) custom-call(bf16[4,8,176,128]{3,2,1,0:T(8,128)(2,1)} %get-tuple-element.95.refs_0_, bf16[4,8,176,128]{3,2,1,0:T(8,128)(2,1)} %get-tuple-element.96.refs_1_, bf16[4,8,176,128]{3,2,1,0:T(8,128)(2,1)} %get-tuple-element.97.refs_2_, ...), custom_call_target="tpu_custom_call" | custom-call | flops 99999997952 | bytes 38797312 | tf_op jit(solution)/shard_map/scatter_sum/pallas_call | solution.py:700
  380.9 1.7 copy-done
  382.6 7.8 %turn_back.1 = (bf16[3,512,1024]{2,1,0:T(8,128)(2,1)}, f32[512,1024]{1,0:T(8,128)}) custom-call(f32[512,128]{1,0:T(8,128)} %get-tuple-element.136.cos_ref, f32[512,128]{1,0:T(8,128)} %get-tuple-element.135.sin_ref, bf16[8,2,3,256,128]{4,3,2,1,0:T(8,128)(2,1)} %copy-done), custom_call_target="tpu_custom_call" | custom-call | tf_op jit(solution)/shard_map/turn_back/pallas_call | solution.py:850
  390.4 10.2 %input_grad.1 = (f32[512,1024]{1,0:T(8,128)}, f32[1,1024]{1,0:T(1,128)}) custom-call(bf16[512,1024]{1,0:T(8,128)(2,1)} %bitcast.66, f32[512,1024]{1,0:T(8,128)} %get-tuple-element.76.dres_ref, f32[1,1024]{1,0:T(1,128)} %bitcast.92, bf16[3,512,1024]{2,1,0:T(8,128)(2,1)} %get-tuple-element.108.low_ref, bf16[1024,1024]{1,0:T(8,128)(2,1)} %wq_ref.3, ...), custom_call_target="tpu_custom_call" | custom-call | flops 3221225472 | bytes 14680064 | tf_op jit(solution)/shard_map/input_grad/pallas_call | solution.py:883
  402.6 1.5 collective-permute-start.5
  404.1 3.3 copy.53
  407.3 1.5 collective-permute-start.6
  408.8 1.7 slice_bitcast_fusion
  411.0 2.4 collective-permute-start.7
  413.5 7.7 %wgrad.1 = (bf16[4,16,64,128]{3,2,1,0:T(8,128)(2,1)}, bf16[4,16,64,128]{3,2,1,0:T(8,128)(2,1)}, bf16[4,16,64,128]{3,2,1,0:T(8,128)(2,1)}, bf16[4,16,64,128]{3,2,...) custom-call(bf16[512,1024]{1,0:T(8,128)(2,1)} %get-tuple-element.111.left_ref, ...), custom_call_target="tpu_custom_call" | custom-call | flops 3221225472 | bytes 10485760 | tf_op jit(solution)/shard_map/wgrad/pallas_call | solution.py:420
  422.0 45.4 %scatter_sum.3 = (f32[4,64,128]{2,1,0:T(8,128)}, f32[4,64,128]{2,1,0:T(8,128)}, f32[4,64,128]{2,1,0:T(8,128)}) custom-call(bf16[4,16,64,128]{3,2,1,0:T(8,128)(2,1)} %get-tuple-element.112.refs_0_, bf16[4,16,64,128]{3,2,1,0:T(8,128)(2,1)} %get-tuple-element.113.refs_1_, bf16[4,16,64,128]{3,2,1,0:T(8,128)(2,1)} %get-tuple-element.114.refs_2_, ...), custom_call_target="tpu_custom_call" | custom-call | flops 99999997952 | bytes 25165824 | tf_op jit(solution)/shard_map/scatter_sum/pallas_call | solution.py:700
  469.4 2.9 copy.51
  472.4 2.9 copy.52
  (78 shorter events, 16.0 us)
Async XLA Ops:
  0.6 3.6 copy-start.5
  60.2 3.7 copy-start.18
  60.2 40.4 %all-to-all-start = ((bf16[8,3,256,128]{3,2,1,0:T(8,128)(2,1)}), bf16[8,3,256,128]{3,2,1,0:T(8,128)(2,1)S(1)}, u32[]{:S(2)}, u32[]{:S(2)}) async-start(bf16[8,3,256,128]{3,2,1,0:T(8,128)(2,1)} %get-tuple-element.71), calls=%async_computation | async-start | bytes 3145728 | tf_op jit(solution)/shard_map/all_to_all | solution.py:295
  100.6 3.6 copy-start.4
  100.6 18.7 %all-to-all-start.3 = ((bf16[8,256,128]{2,1,0:T(8,128)(2,1)}), bf16[8,256,128]{2,1,0:T(8,128)(2,1)S(1)}, u32[]{:S(2)}, u32[]{:S(2)}) async-start(bf16[8,256,128]{2,1,0:T(8,128)(2,1)} %get-tuple-element.74), calls=%async_computation.3 | async-start | bytes 1048576 | tf_op jit(solution)/shard_map/all_to_all | solution.py:295
  104.2 21.1 %copy-start.6 = (bf16[256,2,1024]{2,1,0:T(2,128)(2,1)S(1)}, bf16[256,2,1024]{2,1,0:T(2,128)(2,1)}, u32[]{:S(2)}) copy-start(bf16[256,2,1024]{2,1,0:T(2,128)(2,1)} %param.25) | copy-start | bytes 3145732
  119.3 19.7 %copy-start.7 = (bf16[8,256,128]{2,1,0:T(8,128)(2,1)}, bf16[8,256,128]{2,1,0:T(8,128)(2,1)S(1)}, u32[]{:S(2)}) copy-start(bf16[8,256,128]{2,1,0:T(8,128)(2,1)S(1)} %all-to-all-done.3.refs_1_) | copy-start | bytes 1572868
  119.3 19.7 %all-to-all-start.1 = ((bf16[8,256,128]{2,1,0:T(8,128)(2,1)}), bf16[8,256,128]{2,1,0:T(8,128)(2,1)S(1)}, u32[]{:S(2)}, u32[]{:S(2)}) async-start(bf16[8,256,128]{2,1,0:T(8,128)(2,1)} %get-tuple-element.72), calls=%async_computation.1 | async-start | bytes 1048576 | tf_op jit(solution)/shard_map/all_to_all | solution.py:295
  139.0 0.8 copy-start.8
  172.6 45.2 %copy-start.16 = (f32[4,2,256]{2,1,0:T(2,128)S(1)}, f32[4,2,256]{2,1,0:T(2,128)}, u32[]{:S(2)}) copy-start(f32[4,2,256]{2,1,0:T(2,128)} %get-tuple-element.127) | copy-start | bytes 24580
  213.7 62.6 %collective-permute-start = (bf16[4,8,176,128]{3,2,1,0:T(8,128)(2,1)}, bf16[4,8,176,128]{3,2,1,0:T(8,128)(2,1)}, u32[]{:S(2)}, u32[]{:S(2)}) collective-permute-start(bf16[4,8,176,128]{3,2,1,0:T(8,128)(2,1)} %get-tuple-element.99), channel_id=1, source_target_pairs={{0,16},{8,24},{16,0},{24,8},{1,17},{9,25},{17,1},{25,9},{2,18},{10... | collective-permute-start | bytes 4325384 | tf_op jit(solution)/shard_map/ppermute | solution.py:594
  215.2 63.4 %collective-permute-start.1 = (bf16[4,8,176,128]{3,2,1,0:T(8,128)(2,1)}, bf16[4,8,176,128]{3,2,1,0:T(8,128)(2,1)}, u32[]{:S(2)}, u32[]{:S(2)}) collective-permute-start(bf16[4,8,176,128]{3,2,1,0:T(8,128)(2,1)} %get-tuple-element.100), channel_id=1, source_target_pairs={{0,16},{8,24},{16,0},{24,8},{1,17},{9,25},{17,1},{25,9},{2,18},{10... | collective-permute-start | bytes 4325384 | tf_op jit(solution)/shard_map/ppermute | solution.py:594
  215.8 62.9 %collective-permute-start.2 = (bf16[4,8,176,128]{3,2,1,0:T(8,128)(2,1)}, bf16[4,8,176,128]{3,2,1,0:T(8,128)(2,1)}, u32[]{:S(2)}, u32[]{:S(2)}) collective-permute-start(bf16[4,8,176,128]{3,2,1,0:T(8,128)(2,1)} %get-tuple-element.101), channel_id=1, source_target_pairs={{0,1},{1,0},{2,3},{3,2},{4,5},{5,4},{6,7},{7,6},{8,9},{9,8},{10,11... | collective-permute-start | bytes 4325384 | tf_op jit(solution)/shard_map/ppermute | solution.py:594
  216.3 59.9 %collective-permute-start.3 = (bf16[4,8,64,128]{3,2,1,0:T(8,128)(2,1)}, bf16[4,8,64,128]{3,2,1,0:T(8,128)(2,1)}, u32[]{:S(2)}, u32[]{:S(2)}) collective-permute-start(bf16[4,8,64,128]{3,2,1,0:T(8,128)(2,1)} %get-tuple-element.102), channel_id=1, source_target_pairs={{0,1},{1,0},{2,3},{3,2},{4,5},{5,4},{6,7},{7,6},{8,9},{9,8},{10,11... | collective-permute-start | bytes 1572872 | tf_op jit(solution)/shard_map/ppermute | solution.py:594
  251.5 129.4 %all-to-all-start.4 = ((bf16[8,2,3,256,128]{4,3,2,1,0:T(8,128)(2,1)}), bf16[8,2,3,256,128]{4,3,2,1,0:T(8,128)(2,1)S(1)}, u32[]{:S(2)}, u32[]{:S(2)}) async-start(bf16[8,2,3,256,128]{4,3,2,1,0:T(8,128)(2,1)} %attn_bwd.1), calls=%async_computation.4 | async-start | bytes 6291456 | tf_op jit(solution)/shard_map/all_to_all | solution.py:295
  380.9 1.7 copy-start
  390.4 10.2 %copy-start.17 = (f32[1,1024]{1,0:T(1,128)S(1)}, f32[1,1024]{1,0:T(1,128)}, u32[]{:S(2)}) copy-start(f32[1,1024]{1,0:T(1,128)} %get-tuple-element.126) | copy-start | bytes 12292
  390.4 18.4 %copy-start.1 = (bf16[3,512,1024]{2,1,0:T(8,128)(2,1)S(1)}, bf16[3,512,1024]{2,1,0:T(8,128)(2,1)}, u32[]{:S(2)}) copy-start(bf16[3,512,1024]{2,1,0:T(8,128)(2,1)} %get-tuple-element.108.low_ref) | copy-start | bytes 9437188
  401.4 1.2 collective-permute-start.4
  402.6 4.7 collective-permute-start.5
  407.3 3.7 collective-permute-start.6
  411.0 10.1 %collective-permute-start.7 = (f32[2176]{0:T(1024)S(1)}, f32[2176]{0:T(1024)S(1)}, u32[]{:S(2)}, u32[]{:S(2)}) collective-permute-start(f32[2176]{0:T(1024)S(1)} %add.53), channel_id=1, source_target_pairs={{0,2},{1,3},{2,0},{3,1},{4,6},{5,7},{6,4},{7,5},{8,10},{9,11},{10,... | collective-permute-start | bytes 26120 | tf_op jit(solution)/shard_map/ppermute | solution.py:351
  421.2 54.1 %collective-permute-start.8 = (f32[2176]{0:T(1024)S(1)}, f32[2176]{0:T(1024)S(1)}, u32[]{:S(2)}, u32[]{:S(2)}) collective-permute-start(f32[2176]{0:T(1024)S(1)} %add.54), channel_id=1, source_target_pairs={{0,4},{1,5},{2,6},{3,7},{4,0},{5,1},{6,2},{7,3},{8,12},{9,13},{10,... | collective-permute-start | bytes 26120 | tf_op jit(solution)/shard_map/ppermute | solution.py:351
  422.0 45.5 %copy-start.11 = (f32[4,176,128]{2,1,0:T(8,128)S(1)}, f32[4,176,128]{2,1,0:T(8,128)}, u32[]{:S(2)}) copy-start(f32[4,176,128]{2,1,0:T(8,128)} %get-tuple-element.122) | copy-start | bytes 1081348
  422.0 46.4 %copy-start.10 = (f32[4,176,128]{2,1,0:T(8,128)S(1)}, f32[4,176,128]{2,1,0:T(8,128)}, u32[]{:S(2)}) copy-start(f32[4,176,128]{2,1,0:T(8,128)} %get-tuple-element.123) | copy-start | bytes 1081348
  467.4 1.9 copy-start.2
  469.4 2.9 copy-start.3
  472.3 5.5 %copy-start.15 = (f32[4,64,128]{2,1,0:T(8,128)S(1)}, f32[4,64,128]{2,1,0:T(8,128)}, u32[]{:S(2)}) copy-start(f32[4,64,128]{2,1,0:T(8,128)} %get-tuple-element.118) | copy-start | bytes 393220
  472.3 6.1 %copy-start.14 = (f32[4,64,128]{2,1,0:T(8,128)S(1)}, f32[4,64,128]{2,1,0:T(8,128)}, u32[]{:S(2)}) copy-start(f32[4,64,128]{2,1,0:T(8,128)} %get-tuple-element.119) | copy-start | bytes 393220
  472.3 6.8 %copy-start.13 = (f32[4,64,128]{2,1,0:T(8,128)S(1)}, f32[4,64,128]{2,1,0:T(8,128)}, u32[]{:S(2)}) copy-start(f32[4,64,128]{2,1,0:T(8,128)} %get-tuple-element.120) | copy-start | bytes 393220
  472.3 7.4 %copy-start.12 = (f32[4,64,128]{2,1,0:T(8,128)S(1)}, f32[4,64,128]{2,1,0:T(8,128)}, u32[]{:S(2)}) copy-start(f32[4,64,128]{2,1,0:T(8,128)} %get-tuple-element.121) | copy-start | bytes 393220
  472.3 8.1 %copy-start.9 = (f32[4,176,128]{2,1,0:T(8,128)S(1)}, f32[4,176,128]{2,1,0:T(8,128)}, u32[]{:S(2)}) copy-start(f32[4,176,128]{2,1,0:T(8,128)} %get-tuple-element.124) | copy-start | bytes 1081348

commit v4 on v3

--- a/solution.py
+++ b/solution.py
@@ -330,6 +330,14 @@
     return [("dp", 0)] + rest + blk
 
 
+def block_order(y_early):
+    rest = [("dp", b) for b in range(1, bits_of("dp"))]
+    blk = [("blk", b) for b in range(bits_of("blk"))]
+    if y_early:
+        return [("dp", 0)] + blk[:1] + rest + blk[1:]
+    return [("dp", 0)] + rest + blk
+
+
 def scatter(grad, rows_name, y_early):
     n_rows = lax.axis_size(rows_name)
     rows, cols = grad.shape
@@ -362,77 +370,6 @@
     for name, bit in order[1:]:
         place = 2 * place + (((dp if name == "dp" else blk) >> bit) & 1)
     return place
-
-
-def wgrad_kernel(orders, n_left, n_right, left_is_dp, n_out, left_ref, *refs):
-    right_refs, out_refs, turned_ref = refs[:n_out], refs[n_out : 3 * n_out], refs[3 * n_out]
-    left_rows, right_cols = left_ref.shape[1] // n_left, right_refs[0].shape[1] // n_right
-    row_parts, col_parts, size = chunks_of(left_rows, right_cols)
-    q = pl.program_id(0)
-    core = lax.axis_index("dp") % 2
-
-    @pl.when(q == 0)
-    def _():
-        turned_ref[...] = left_ref[...].T
-
-    row_part, col_part = q // col_parts, q % col_parts
-    for half in range(2):
-        side = core if half == 0 else 1 - core
-        left_places = [2 * k + side for k in range(n_left // 2)] if left_is_dp else list(range(n_left))
-        right_places = list(range(n_right)) if left_is_dp else [2 * k + side for k in range(n_right // 2)]
-        left = jnp.concatenate(
-            [
-                turned_ref[pl.ds(pl.multiple_of(k * left_rows + row_part * size, 16), size), :]
-                for k in left_places
-            ],
-            axis=0,
-        )
-        for n, right_ref in enumerate(right_refs):
-            if left_is_dp:
-                right = right_ref[...]
-            else:
-                right = jnp.concatenate(
-                    [
-                        right_ref[:, pl.ds(pl.multiple_of(k * right_cols + col_part * 128, 128), 128)]
-                        for k in right_places
-                    ],
-                    axis=1,
-                )
-            result = dot(left, right).astype(BF16)
-            out_ref = out_refs[2 * n + half]
-            for k in range(len(left_places)):
-                for m in range(len(right_places)):
-                    dp, blk = (2 * k, m) if left_is_dp else (2 * m, k)
-                    out_ref[0, place_of(orders[n], dp, blk)] = result[
-                        k * size : (k + 1) * size, m * 128 : (m + 1) * 128
-                    ]
-
-
-def wgrad(orders, left, rights, left_is_dp):
-    n_dp, n_blk = lax.axis_size("dp"), lax.axis_size("blk")
-    n_left, n_right = (n_dp, n_blk) if left_is_dp else (n_blk, n_dp)
-    tokens, left_cols = left.shape
-    right_cols = rights[0].shape[1]
-    row_parts, col_parts, size = chunks_of(left_cols // n_left, right_cols // n_right)
-    full = lambda a: pl.BlockSpec(a.shape, lambda q: (0, 0))
-    n_out = len(rights)
-    blocks = n_dp * n_blk // 2
-    flat = pl.pallas_call(
-        functools.partial(wgrad_kernel, orders, n_left, n_right, left_is_dp, n_out),
-        grid=(4,),
-        in_specs=[full(left)] + [full(a) for a in rights],
-        out_specs=[pl.BlockSpec((1, blocks, size, 128), lambda q: (q, 0, 0, 0))] * (2 * n_out),
-        out_shape=[jax.ShapeDtypeStruct((4, blocks, size, 128), BF16)] * (2 * n_out),
-        scratch_shapes=[pltpu.VMEM((left_cols, tokens), BF16)],
-        compiler_params=pltpu.CompilerParams(vmem_limit_bytes=VMEM_LIMIT),
-        cost_estimate=pl.CostEstimate(
-            flops=2 * n_out * tokens * left_cols * right_cols,
-            bytes_accessed=2 * tokens * (left_cols + n_out * right_cols) + 2 * n_out * left_cols * right_cols,
-            transcendentals=0,
-        ),
-        name="wgrad",
-    )(left, *rights)
-    return [tuple(flat[2 * n : 2 * n + 2]) for n in range(n_out)]
 
 
 def blocks_dot(left_ref, right_ref, left_is_dp, side, col, order, n_dp, n_blk, out_ref, *at):
@@ -589,6 +526,40 @@
     return [tuple(flat[2 * k : 2 * k + 2]) for k in range(n)], list(flat[2 * n :])
 
 
+def fold_kernel(stages, *refs):
+    n = len(stages)
+    for k, (name, bit) in enumerate(stages):
+        mine, _ = partner(name, bit)
+        keep_ref, got_ref = refs[2 * k], refs[2 * k + 1]
+        half = keep_ref.shape[1] // 2
+        for out_ref, side in ((refs[2 * n + 2 * k], mine), (refs[2 * n + 2 * k + 1], 1 - mine)):
+
+            def one(d, _):
+                at = side * half + d
+                out_ref[0, d] = keep_ref[0, at] + got_ref[0, at]
+                return 0
+
+            lax.fori_loop(0, half, one, 0)
+
+
+def fold(pairs, stages):
+    n = len(pairs)
+    arrays = [a for pair in pairs for a in pair]
+    block = lambda a, parts: pl.BlockSpec((1, a.shape[1] // parts) + a.shape[2:], lambda c: (c, 0, 0, 0))
+    half = lambda a: jax.ShapeDtypeStruct((a.shape[0], a.shape[1] // 2) + a.shape[2:], BF16)
+    flat = pl.pallas_call(
+        functools.partial(fold_kernel, stages),
+        grid=(arrays[0].shape[0],),
+        in_specs=[block(a, 1) for a in arrays],
+        out_specs=[block(a, 2) for a in arrays],
+        out_shape=[half(a) for a in arrays],
+        compiler_params=pltpu.CompilerParams(vmem_limit_bytes=VMEM_LIMIT),
+        cost_estimate=pl.CostEstimate(flops=10**11, bytes_accessed=10**8, transcendentals=0),
+        name="fold",
+    )(*arrays)
+    return [tuple(flat[2 * k : 2 * k + 2]) for k in range(n)]
+
+
 def swap(values, name, bit):
     size = lax.axis_size(name)
     return lax.ppermute(values, name, [(k, k ^ (1 << bit)) for k in range(size)])
@@ -600,122 +571,6 @@
     other = dict(here)
     other[name] = here[name] + (1 - 2 * mine) * (1 << bit)
     return mine, (other["dp"], other["blk"])
-
-
-def scatter_kernel(orders, fresh, *refs):
-    n_streams, n_stages = len(orders), len(orders[0])
-    source = iter(refs)
-    take = lambda n: [next(source) for _ in range(n)]
-    keeps, others, outs, works = take(n_streams), take(n_streams), take(n_streams), take(n_streams)
-    landed = [take(n_stages) for _ in range(n_streams)]
-    local_sem, other_sem, send_sem, recv_sem = take(4)
-    n_chunks, held = keeps[0].shape[:2]
-    greeted = sorted({stage for order in orders for stage in order[0 if fresh else 1 :]})
-
-    barrier = pltpu.get_barrier_semaphore()
-    for name, bit in greeted:
-        pl.semaphore_signal(barrier, inc=1, device_id=partner(name, bit)[1], device_id_type=MESH)
-    pl.semaphore_wait(barrier, len(greeted))
-
-    def base_of(k, stage):
-        base = 0
-        for earlier in range(1, stage):
-            base = base + partner(*orders[k][earlier])[0] * (held >> earlier)
-        return base
-
-    def local(k, c):
-        return pltpu.make_async_copy(keeps[k].at[c], works[k].at[c], local_sem.at[k, c])
-
-    def other(k, c):
-        return pltpu.make_async_copy(others[k].at[c], landed[k][0].at[c], other_sem.at[k, c])
-
-    def remote(k, stage, c):
-        mine, device = partner(*orders[k][stage])
-        half = held >> stage
-        if stage == 0:
-            sent = others[k].at[c]
-        else:
-            sent = works[k].at[c, pl.ds(base_of(k, stage) + (1 - mine) * half, half)]
-        return pltpu.make_async_remote_copy(
-            src_ref=sent,
-            dst_ref=landed[k][stage].at[c],
-            send_sem=send_sem.at[k, stage, c],
-            recv_sem=recv_sem.at[k, stage, c],
-            device_id=device,
-            device_id_type=MESH,
-        )
-
-    def add(k, stage, c):
-        base = base_of(k, stage + 1)
-        if stage == n_stages - 1:
-            outs[k][c] = works[k][c, base].astype(F32) + landed[k][stage][c, 0].astype(F32)
-            return
-
-        def one(d, _):
-            works[k][c, base + d] = works[k][c, base + d] + landed[k][stage][c, d]
-            return 0
-
-        lax.fori_loop(0, held >> stage, one, 0)
-
-    def step(t, _):
-        for stage in range(n_stages + 1):
-            c = t - stage
-
-            @pl.when((c >= 0) & (c < n_chunks))
-            def _():
-                for k in range(n_streams):
-                    if stage == 0:
-                        local(k, c).start()
-                        if not fresh:
-                            other(k, c).start()
-                    else:
-                        if stage == 1:
-                            local(k, c).wait()
-                        if stage == 1 and not fresh:
-                            other(k, c).wait()
-                        else:
-                            remote(k, stage - 1, c).wait_recv()
-                        add(k, stage - 1, c)
-                    if stage < n_stages and (fresh or stage > 0):
-                        remote(k, stage, c).start()
-
-        return 0
-
-    lax.fori_loop(0, n_chunks + n_stages, step, 0)
-
-    def finish(c, _):
-        for k in range(n_streams):
-            for stage in range(0 if fresh else 1, n_stages):
-                remote(k, stage, c).wait_send()
-        return 0
-
-    lax.fori_loop(0, n_chunks, finish, 0)
-
-
-def scatter_sum(pairs, orders, fresh, collective_id):
-    n_streams, n_stages = len(pairs), len(orders[0])
-    keeps, others = [pair[0] for pair in pairs], [pair[1] for pair in pairs]
-    n_chunks, held = keeps[0].shape[:2]
-    size = sum(a.size for a in keeps)
-    return pl.pallas_call(
-        functools.partial(scatter_kernel, orders, fresh),
-        in_specs=[pl.BlockSpec(memory_space=pl.ANY)] * (2 * n_streams),
-        out_specs=[pl.BlockSpec(memory_space=pltpu.VMEM)] * n_streams,
-        out_shape=[jax.ShapeDtypeStruct((n_chunks,) + a.shape[2:], F32) for a in keeps],
-        scratch_shapes=[pltpu.VMEM(a.shape, BF16) for a in keeps]
-        + [
-            pltpu.VMEM((n_chunks, held >> stage) + a.shape[2:], BF16)
-            for a in keeps
-            for stage in range(n_stages)
-        ]
-        + [pltpu.SemaphoreType.DMA((n_streams, n_chunks))] * 2
-        + [pltpu.SemaphoreType.DMA((n_streams, n_stages, n_chunks))] * 2,
-        compiler_params=pltpu.CompilerParams(
-            collective_id=collective_id, has_side_effects=True, vmem_limit_bytes=VMEM_LIMIT
-        ),
-        cost_estimate=pl.CostEstimate(flops=10**11, bytes_accessed=16 * size, transcendentals=0),
-        name="scatter_sum",
-    )(*keeps, *others)
 
 
 def whole_block(pieces, block_rows, block_cols):
@@ -821,6 +676,291 @@
     )(*gathered, hidden, cot, gain, w_out, w_gate, w_up, w_down)
 
 
+class Halving:
+    def __init__(self, order, work, sent, landed, send_sem, recv_sem):
+        self.order, self.work, self.sent, self.landed = order, work, sent, landed
+        self.send_sem, self.recv_sem = send_sem, recv_sem
+        self.held = work.shape[1]
+
+    def base(self, stage):
+        base = 0
+        for earlier in range(1, stage):
+            base = base + partner(*self.order[earlier])[0] * (self.held >> earlier)
+        return base
+
+    def remote(self, stage, c):
+        mine, device = partner(*self.order[stage])
+        half = self.held >> stage
+        if stage == 0:
+            sent = self.sent.at[c]
+        else:
+            sent = self.work.at[c, pl.ds(self.base(stage) + (1 - mine) * half, half)]
+        return pltpu.make_async_remote_copy(
+            src_ref=sent,
+            dst_ref=self.landed[stage].at[c],
+            send_sem=self.send_sem.at[stage, c],
+            recv_sem=self.recv_sem.at[stage, c],
+            device_id=device,
+            device_id_type=MESH,
+        )
+
+    def add(self, stage, c):
+        base = self.base(stage + 1)
+
+        def one(d, _):
+            self.work[c, base + d] = self.work[c, base + d] + self.landed[stage][c, d]
+            return 0
+
+        lax.fori_loop(0, self.held >> stage, one, 0)
+
+    def result(self, c):
+        stage = len(self.order) - 1
+        return self.work[c, self.base(stage + 1)].astype(F32) + self.landed[stage][c, 0].astype(F32)
+
+
+def tail_kernel(ffn_orders, qkv_orders, n_dp, n_blk, *refs):
+    source = iter(refs)
+    take = lambda n: [next(source) for _ in range(n)]
+    n_ffn, n_qkv = len(ffn_orders), 3
+    ffn_stages, qkv_stages = len(ffn_orders[0]), len(qkv_orders[0])
+    cos_ref, sin_ref, gain_ref, small_ref = take(4)
+    loads = take(7)
+    keeps, gots = take(n_ffn), take(n_ffn)
+    ffn_outs, qkv_outs = take(n_ffn), take(n_qkv)
+    first_ref, input_ref, total_ref = take(3)
+    back_ref, turned_ref, hidden_ref, dres_ref, *weights = here = take(7)
+    low_ref, acc_ref, vecs, vec_landed = take(4)
+    load_sem, keep_sem, got_sem, vec_send, vec_recv = take(5)
+    streams = []
+    for k, order in enumerate(ffn_orders):
+        work, *landed = take(1 + ffn_stages)
+        streams.append(Halving(order, work, None, landed, *take(2)))
+    late = []
+    for u in range(n_qkv):
+        late.append([])
+        for order in qkv_orders:
+            work, sent, *landed = take(2 + qkv_stages)
+            late[u].append(Halving(order, work, sent, landed, *take(2)))
+    _, rows, _, length, width = back_ref.shape
+    core, _ = partner("dp", 0)
+    n_chunks = keeps[0].shape[0]
+
+    load = [pltpu.make_async_copy(a, b, load_sem.at[k]) for k, (a, b) in enumerate(zip(loads, here))]
+    keep_copy = lambda k, c: pltpu.make_async_copy(keeps[k].at[c], streams[k].work.at[c], keep_sem.at[k, c])
+    got_copy = lambda k, c: pltpu.make_async_copy(gots[k].at[c], streams[k].landed[0].at[c], got_sem.at[k, c])
+    load[0].start()
+    load[1].start()
+    for c in range(n_chunks):
+        for k in range(n_ffn):
+            keep_copy(k, c).start()
+            got_copy(k, c).start()
+    for copy in load[2:]:
+        copy.start()
+
+    everyone = qkv_orders[0]
+    barrier = pltpu.get_barrier_semaphore()
+    for name, bit in everyone:
+        pl.semaphore_signal(barrier, inc=1, device_id=partner(name, bit)[1], device_id_type=MESH)
+    pl.semaphore_wait(barrier, len(everyone))
+
+    def ffn(c, stage):
+        for k, stream in enumerate(streams):
+            if stage == 1:
+                keep_copy(k, c).wait()
+                got_copy(k, c).wait()
+            else:
+                stream.remote(stage - 1, c).wait_recv()
+            if stage < ffn_stages:
+                stream.add(stage - 1, c)
+                stream.remote(stage, c).start()
+            else:
+                ffn_outs[k][c] = stream.result(c)
+
+    def projections(which):
+        for r in range(rows):
+            at = pl.ds(r * length, length)
+            for s in range(n_blk):
+                cols = slice(s * width, (s + 1) * width)
+                values = back_ref[s, r, which].astype(F32)
+                if which < 2:
+                    turned = values * cos_ref[at, :] - swap_halves(values) * sin_ref[at, :]
+                else:
+                    turned = 0.5 * values
+                    first_ref[at, cols] = turned
+                low_ref[which, at, cols] = turned.astype(BF16)
+        for fresh in range(2):
+            side = 1 - core if fresh == 0 else core
+            left = jnp.concatenate([turned_ref[2 * k + side] for k in range(n_dp // 2)], axis=0)
+            size, half = turned_ref.shape[1], turned_ref.shape[1] // 2
+            result = dot(left, low_ref[which]).astype(BF16)
+            for h, stream in enumerate(late[which]):
+                out_ref = stream.sent if fresh == 0 else stream.work
+                for d in range(n_dp // 2):
+                    for e in range(n_blk):
+                        out_ref[0, place_of(stream.order, 2 * d, e)] = result[
+                            d * size + h * half : d * size + (h + 1) * half, e * width : (e + 1) * width
+                        ]
+                if fresh == 0:
+                    stream.remote(0, 0).start()
+
+    def late_step(which, stage):
+        for h, stream in enumerate(late[which]):
+            stream.remote(stage - 1, 0).wait_recv()
+            if stage < qkv_stages:
+                stream.add(stage - 1, 0)
+                stream.remote(stage, 0).start()
+            else:
+                half = stream.work.shape[2]
+                qkv_outs[which][h * half : (h + 1) * half, :] = stream.result(0)
+
+    def vec_copy(e):
+        return pltpu.make_async_remote_copy(
+            src_ref=vecs.at[e],
+            dst_ref=vec_landed.at[e],
+            send_sem=vec_send.at[e],
+            recv_sem=vec_recv.at[e],
+            device_id=partner(*everyone[e])[1],
+            device_id_type=MESH,
+        )
+
+    model = hidden_ref.shape[1]
+    n_vec = len(everyone)
+
+    def matmul():
+        for k in range(2, 7):
+            load[k].wait()
+        for r in range(rows):
+            at = pl.ds(r * length, length)
+            acc_ref[at, :] = (
+                dot_nt(low_ref[0, at, :], weights[0][...])
+                + dot_nt(low_ref[1, at, :], weights[1][...])
+                + dot_nt(low_ref[2, at, :], weights[2][...])
+            )
+
+    def norm():
+        d_gain = jnp.zeros((1, model), F32)
+        for r in range(rows):
+            at = pl.ds(r * length, length)
+            normed, inverse = rms_parts(hidden_ref[at, :].astype(F32))
+            d_normed = acc_ref[at, :]
+            d_gain = d_gain + jnp.sum(d_normed * normed, axis=0, keepdims=True)
+            input_ref[at, :] = dres_ref[at, :] + norm_back(d_normed * gain_ref[...], normed, inverse)
+        vecs[0, :, :model] = d_gain
+        vecs[0, :, model:] = small_ref[...]
+        vec_copy(0).start()
+
+    def vec(e):
+        vec_copy(e).wait_recv()
+        summed = vecs[e] + vec_landed[e]
+        if e == n_vec - 1:
+            total_ref[...] = summed
+        else:
+            vecs[e + 1] = summed
+            vec_copy(e + 1).start()
+
+    chunks = range(n_chunks)
+    for c in chunks:
+        ffn(c, 1)
+    load[0].wait()
+    load[1].wait()
+    projections(2)
+    projections(1)
+    late_step(2, 1)
+    projections(0)
+    late_step(1, 1)
+    ffn(0, 2)
+    late_step(0, 1)
+    matmul()
+    late_step(2, 2)
+    ffn(1, 2)
+    norm()
+    late_step(1, 2)
+    ffn(2, 2)
+    vecs_left = list(range(n_vec))
+    vec(vecs_left.pop(0))
+    late_step(2, 3)
+    late_step(0, 2)
+    ffn(3, 2)
+    vec(vecs_left.pop(0))
+    late_step(1, 3)
+    late_step(0, 3)
+    for stage in range(4, qkv_stages + 1):
+        vec(vecs_left.pop(0))
+        for which in (2, 1, 0):
+            late_step(which, stage)
+    for c in chunks:
+        for stage in range(3, ffn_stages + 1):
+            ffn(c, stage)
+    for e in vecs_left:
+        vec(e)
+
+    def finish(c, _):
+        for stream in streams:
+            for stage in range(1, ffn_stages):
+                stream.remote(stage, c).wait_send()
+        return 0
+
+    lax.fori_loop(0, n_chunks, finish, 0)
+    for stream in late[0] + late[1] + late[2]:
+        for stage in range(qkv_stages):
+            stream.remote(stage, 0).wait_send()
+    for e in range(n_vec):
+        vec_copy(e).wait_send()
+
+
+def tail(ffn_pairs, ffn_orders, qkv_orders, back, normed_t, hidden, d_resid, weights, cos, sin, gain, small, collective_id):
+    n_dp, n_blk = lax.axis_size("dp"), lax.axis_size("blk")
+    tokens, model = hidden.shape
+    keeps, gots = [pair[0] for pair in ffn_pairs], [pair[1] for pair in ffn_pairs]
+    loads = [back, normed_t.reshape(n_dp, model // n_dp, tokens), hidden, d_resid, *weights]
+    ffn_stages, qkv_stages, n_qkv = len(ffn_orders[0]), len(qkv_orders[0]), 3
+    n_chunks = keeps[0].shape[0]
+    block = (model // n_dp, model // n_blk)
+    held = n_dp * n_blk // 2
+    shape = jax.ShapeDtypeStruct
+    vec = (1, model + small.shape[1])
+    outs = (
+        [shape((n_chunks,) + a.shape[2:], F32) for a in keeps]
+        + [shape(block, F32)] * n_qkv
+        + [shape((tokens, model), F32)] * 2
+        + [shape(vec, F32)]
+    )
+    scratch = [pltpu.VMEM(a.shape, a.dtype) for a in loads]
+    scratch += [
+        pltpu.VMEM((n_qkv, tokens, model), BF16),
+        pltpu.VMEM((tokens, model), F32),
+        pltpu.VMEM((qkv_stages,) + vec, F32),
+        pltpu.VMEM((qkv_stages,) + vec, F32),
+        pltpu.SemaphoreType.DMA((len(loads),)),
+        pltpu.SemaphoreType.DMA((len(keeps), n_chunks)),
+        pltpu.SemaphoreType.DMA((len(keeps), n_chunks)),
+        pltpu.SemaphoreType.DMA((qkv_stages,)),
+        pltpu.SemaphoreType.DMA((qkv_stages,)),
+    ]
+    for a in keeps:
+        scratch.append(pltpu.VMEM(a.shape, BF16))
+        scratch += [pltpu.VMEM((n_chunks, a.shape[1] >> stage) + a.shape[2:], BF16) for stage in range(ffn_stages)]
+        scratch += [pltpu.SemaphoreType.DMA((ffn_stages, n_chunks))] * 2
+    part = (block[0] // len(qkv_orders), block[1])
+    for _ in range(n_qkv * len(qkv_orders)):
+        scratch += [pltpu.VMEM((1, held) + part, BF16)] * 2
+        scratch += [pltpu.VMEM((1, held >> stage) + part, BF16) for stage in range(qkv_stages)]
+        scratch += [pltpu.SemaphoreType.DMA((qkv_stages, 1))] * 2
+    vmem, anywhere = pl.BlockSpec(memory_space=pltpu.VMEM), pl.BlockSpec(memory_space=pl.ANY)
+    return pl.pallas_call(
+        functools.partial(tail_kernel, ffn_orders, qkv_orders, n_dp, n_blk),
+        in_specs=[vmem] * 4 + [anywhere] * (len(loads) + 2 * len(keeps)),
+        out_specs=[vmem] * len(outs),
+        out_shape=outs,
+        scratch_shapes=scratch,
+        compiler_params=pltpu.CompilerParams(
+            collective_id=collective_id, has_side_effects=True, vmem_limit_bytes=60 * 2**20
+        ),
+        cost_estimate=pl.CostEstimate(flops=10**11, bytes_accessed=10**8, transcendentals=0),
+        name="tail",
+    )(cos, sin, gain, small, *loads, *keeps, *gots)
+
+
 def turn_back_kernel(cos_ref, sin_ref, back_ref, low_ref, first_ref):
     n_blk, rows, _, length, width = back_ref.shape
     which = pl.program_id(0)
@@ -958,7 +1098,7 @@
 
     inner = w_gate.shape[1]
     by_blocks = (model // n_dp) % 128 == 0 and width == 128 and (inner // n_blk) % 32 == 0
-    early, late = scatter_steps(False), scatter_steps(True)
+    early, late = block_order(False), block_order(True)
     if by_blocks:
         folded, d_own = ffn_wgrad(
             (
@@ -971,27 +1111,44 @@
             2,
         )
         kept = [keep for keep, sent in folded]
-        ffn_got = [swap(sent, *(early[1] if k < 2 else late[1])) for k, (_, sent) in enumerate(folded)]
+        orders = (early, early, late, late)
+        ffn_got = [swap(sent, *order[1]) for order, (_, sent) in zip(orders, folded)]
         back_own = attn_bwd(lens, qkv, d_own, attended, lse, n_docs)
         back = exchange(back_own)
+        second = [order[2] for order in orders]
         token, kept = lax.optimization_barrier((back_own, kept))
-        sums_ffn = scatter_sum(list(zip(kept, ffn_got)), (early[1:],) * 2 + (late[1:],) * 2, False, 0)
-        back, sums_ffn = lax.optimization_barrier((back, sums_ffn))
+        folded = fold(list(zip(kept, ffn_got)), second)
+        ffn_pairs = [(keep, swap(sent, *stage)) for (keep, sent), stage in zip(folded, second)]
     else:
         d_own = [exchange(d_attn[r]) for r in range(rows)]
         back = exchange(attn_bwd(lens, qkv, d_own, attended, lse, n_docs))
-    low, grad_first = turn_back(back, cos, sin)
-
+
+    squares = jnp.sum(sums, axis=(0, 2)).reshape(1, 2)
+    small = jnp.concatenate([d_gain_two, squares, jnp.zeros((1, 126), F32)], axis=1)
     if by_blocks:
-        qkv_pairs = wgrad([early, late, early], normed_in, [low[0], low[1], low[2]], True)
-        sums_qkv = scatter_sum(qkv_pairs, (early, late, early), True, 1)
-        block = lambda pieces, r, c: whole_block(pieces, r, c)
-        grad_gate = block(sums_ffn[0], inner // n_blk, model // n_dp).T
-        grad_up = block(sums_ffn[1], inner // n_blk, model // n_dp).T
-        grad_down = block(sums_ffn[2], inner // n_dp, model // n_blk)
-        grad_project = block(sums_ffn[3], model // n_dp, model // n_blk)
-        grad_query, grad_key, grad_value = [block(a, model // n_dp, model // n_blk) for a in sums_qkv]
+        *blocks, grad_first, grad_input, small = tail(
+            ffn_pairs,
+            tuple(order[2:] for order in orders),
+            (early, late),
+            back,
+            normed_in.T,
+            hidden,
+            d_resid_mid,
+            (w_query, w_key, w_value),
+            cos,
+            sin,
+            row_gain(attn_gain),
+            small,
+            0,
+        )
+        small = small.reshape(-1)
+        grad_gate = whole_block(blocks[0], inner // n_blk, model // n_dp).T
+        grad_up = whole_block(blocks[1], inner // n_blk, model // n_dp).T
+        grad_down = whole_block(blocks[2], inner // n_dp, model // n_blk)
+        grad_project = whole_block(blocks[3], model // n_dp, model // n_blk)
+        grad_query, grad_key, grad_value = blocks[4:]
     else:
+        low, grad_first = turn_back(back, cos, sin)
         mid_cf, in_cf = core_first(normed_mid), core_first(normed_in)
         sent = lambda a, b, name, y: scatter(dot_tn(a, b).astype(BF16), name, y).astype(F32)
         grad_down = sent(inner_t.T, y_first(cot), "dp", False)
@@ -999,11 +1156,8 @@
         grad_up = sent(d_up_t.T, mid_cf, "blk", True).T
         grad_project = sent(d_branch, core_first(attn_low_t.T), "blk", True).T
         grad_query, grad_key, grad_value = [sent(low[k], in_cf, "blk", True).T for k in range(3)]
-    grad_input, d_gain_one = input_grad(hidden, d_resid_mid, row_gain(attn_gain), low, w_query, w_key, w_value)
-
-    squares = jnp.sum(sums, axis=(0, 2))
-    small = jnp.concatenate([d_gain_one.reshape(model), d_gain_two.reshape(model), squares, jnp.zeros((126,), F32)])
-    small = total(small)
+        grad_input, d_gain_one = input_grad(hidden, d_resid_mid, row_gain(attn_gain), low, w_query, w_key, w_value)
+        small = total(jnp.concatenate([d_gain_one.reshape(model), small.reshape(-1)]))
     n_entries = n_blk * length * rows * n_dp * model
     return (
         unflat(block_out),

time: 485 us -> 418 us (0.86)
  Pallas kernels: 319 us -> 219 us
  waiting for transfers between devices: 58.9 us -> 90 us
    pallas_call x5 -> x2, Pallas kernels: 173 us -> 73.9 us  [the longest x1 67.1 us: tail(): pl.pallas_call(functools.partial(tail_kernel, ffn_orders, qkv_orders, n_d...]
    ppermute x4 -> x8, waiting for transfers between devices: 23.3 us -> 55.9 us  [swap(): return lax.ppermute(values, name, [(k, k ^ 1 << bit) for k in range(size)])]
    ppermute x5 -> x0, starting transfers between devices: 6.21 us -> none  [total(): lax.ppermute(values, name, [(k, k ^ 1 << bit) for k in range(size)])]
  transfers between devices with their start and end apart: 13 -> 12, of which waited for: 6 -> 8; matrix products, arithmetic and copies ran while one was open for 3% -> 2% of each run, Pallas kernels for 45% -> 17%
where the time goes in v4:
time: 418 us; the launch traced here: 416 us
  Pallas kernels  219 us (52%)
  waiting for transfers between devices  90 us (22%)
  blocking collectives  44.4 us (11%)
  local copies, waits for them, and re-layouts  29.8 us (7%)
  starting transfers between devices  25.4 us (6%)
  between operations  4.47 us (1%)
    pallas_call x1, Pallas kernels, tail(): pl.pallas_call(functools.partial(tail_kernel, ffn_orders, qkv_orders, n_d...  67.1 us
    ppermute x8, waiting for transfers between devices, swap(): return lax.ppermute(values, name, [(k, k ^ 1 << bit) for k in range(size)])  55.9 us
    all_to_all x1, blocking collectives, exchange(): return lax.all_to_all(values, 'blk', 0, 0, tiled=True)  44.4 us
    pallas_call x1, Pallas kernels, ffn_wgrad(): pl.pallas_call(functools.partial(ffn_wgrad_kernel, plans, n_dp, n_blk, le...  41.2 us
    all_to_all x4, waiting for transfers between devices, exchange(): return lax.all_to_all(values, 'blk', 0, 0, tiled=True)  34.1 us
    pallas_call x1, Pallas kernels, attn_bwd(): pl.pallas_call(functools.partial(attn_bwd_kernel, rows, n_docs, heads), g...  33.5 us
    pallas_call x1, Pallas kernels, feed_forward(): pl.pallas_call(functools.partial(ffn_kernel, rows, n_blk), grid=(inner //...  32.8 us
    pallas_call x2, Pallas kernels, attn_fwd(): pl.pallas_call(functools.partial(attn_fwd_kernel, row, n_docs, heads), gr...  29.5 us
  transfers between devices with their start and end apart: 12, of which 8 were waited for; matrix products, arithmetic and copies ran while one was open for 2% of the time, Pallas kernels for 17%

profile of v4, /device:TPU:0, one launch (start us, length us, event | category | flops | bytes accessed | tf_op | source)
XLA Modules:
  0.0 416.4 jit_solution(10575074997676067452)
XLA Ops:
  1.7 2.5 copy.36
  5.5 1.8 fusion
  7.3 8.5 %qkv.1 = (bf16[8,3,256,128]{3,2,1,0:T(8,128)(2,1)}, bf16[8,3,256,128]{3,2,1,0:T(8,128)(2,1)}, bf16[512,1024]{1,0:T(8,128)(2,1)}, f32[4,2,256]{2,1,0:T(2,128)}) custom-call(bf16[512,1024]{1,0:T(8,128)(2,1)} %bitcast.67, bf16[512,1024]{1,0:T(8,128)(2,1)} %bitcast.76, f32[512,128]{1,0:T(8,128)} %get-tuple-element.125.cos_ref.refs_0_, ...), custom_call_target="tpu_custom_call" | custom-call | flops 3221225472 | bytes 11534336 | tf_op jit(solution)/shard_map/qkv/pallas_call | solution.py:83
  15.8 44.4 %all_to_all.25.qkv_ref.refs_4_ = bf16[8,3,256,128]{3,2,1,0:T(8,128)(2,1)} all-to-all(bf16[8,3,256,128]{3,2,1,0:T(8,128)(2,1)} %get-tuple-element.69), channel_id=1, replica_groups=mesh['dp'=4,'blk'=8] {'blk'}, dimensions={0} | all-to-all | bytes 3145728 | tf_op jit(solution)/shard_map/all_to_all | solution.py:295
  60.2 3.7 all-to-all-start
  64.5 14.9 %attn_fwd.3 = (f32[8,256,128]{2,1,0:T(8,128)}, bf16[8,256,128]{2,1,0:T(8,128)(2,1)}, f32[8,2,256]{2,1,0:T(2,128)}) custom-call(s32[16]{0:T(128)} %reshape.147.lens_ref, bf16[8,3,256,128]{3,2,1,0:T(8,128)(2,1)} %all_to_all.25.qkv_ref.refs_4_), custom_call_target="tpu_custom_call" | custom-call | flops 10000000000 | bytes 3000000 | tf_op jit(solution)/shard_map/attn_fwd/pallas_call | solution.py:185
  79.4 21.1 %all-to-all-done.qkv_ref.refs_0_ = bf16[8,3,256,128]{3,2,1,0:T(8,128)(2,1)S(1)} async-done(((bf16[8,3,256,128]{3,2,1,0:T(8,128)(2,1)}), bf16[8,3,256,128]{3,2,1,0:T(8,128)(2,1)S(1)}, u32[]{:S(2)}, u32[]{:S(2)}) %all-to-all-start) | async-done | bytes 1572896 | tf_op jit(solution)/shard_map/all_to_all | solution.py:295
  100.6 3.6 all-to-all-start.3
  104.2 14.6 %attn_fwd.2 = (f32[8,256,128]{2,1,0:T(8,128)}, bf16[8,256,128]{2,1,0:T(8,128)(2,1)}, f32[8,2,256]{2,1,0:T(2,128)}) custom-call(s32[16]{0:T(128)} %reshape.147.lens_ref, bf16[8,3,256,128]{3,2,1,0:T(8,128)(2,1)} %copy-done.2), custom_call_target="tpu_custom_call" | custom-call | flops 10000000000 | bytes 3000000 | tf_op jit(solution)/shard_map/attn_fwd/pallas_call | solution.py:185
  118.9 5.9 %all-to-all-start.1 = ((bf16[8,256,128]{2,1,0:T(8,128)(2,1)}), bf16[8,256,128]{2,1,0:T(8,128)(2,1)S(1)}, u32[]{:S(2)}, u32[]{:S(2)}) async-start(bf16[8,256,128]{2,1,0:T(8,128)(2,1)} %get-tuple-element.68), calls=%async_computation.1 | async-start | bytes 1048576 | tf_op jit(solution)/shard_map/all_to_all | solution.py:295
  126.1 12.9 %all-to-all-done.1.refs_0_ = bf16[8,256,128]{2,1,0:T(8,128)(2,1)S(1)} async-done(((bf16[8,256,128]{2,1,0:T(8,128)(2,1)}), bf16[8,256,128]{2,1,0:T(8,128)(2,1)S(1)}, u32[]{:S(2)}, u32[]{:S(2)}) %all-to-all-start.1) | async-done | bytes 524320 | tf_op jit(solution)/shard_map/all_to_all | solution.py:295
  139.7 32.8 %ffn.1 = (bf16[1024,512]{1,0:T(8,128)(2,1)}, bf16[512,1024]{1,0:T(8,128)(2,1)}, bf16[2816,512]{1,0:T(8,128)(2,1)}, bf16[2816,512]{1,0:T(8,128)(2,1)}, bf16[2816,...) custom-call(bf16[8,256,128]{2,1,0:T(8,128)(2,1)} %copy-done.6, ...), custom_call_target="tpu_custom_call" | custom-call | flops 19864223744 | bytes 36438016 | tf_op jit(solution)/shard_map/ffn/pallas_call | solution.py:661
  172.5 41.2 %ffn_wgrad.1 = (bf16[4,8,176,128]{3,2,1,0:T(8,128)(2,1)}, bf16[4,8,176,128]{3,2,1,0:T(8,128)(2,1)}, bf16[4,8,176,128]{3,2,1,0:T(8,128)(2,1)}, bf16[4,8,176,128]{...) custom-call(bf16[8,2,176,512]{3,2,1,0:T(8,128)(2,1)} %bitcast.91, ...), custom_call_target="tpu_custom_call" | custom-call | flops 9932111872 | bytes 24830280 | tf_op jit(solution)/shard_map/ffn_wgrad/pallas_call | solution.py:509
  213.8 2.0 collective-permute-start.1
  216.3 1.5 collective-permute-start.3
  217.8 33.5 %attn_bwd.1 = bf16[8,2,3,256,128]{4,3,2,1,0:T(8,128)(2,1)} custom-call(s32[16]{0:T(128)} %reshape.147.lens_ref, bf16[8,3,256,128]{3,2,1,0:T(8,128)(2,1)} %copy-done.2, bf16[8,256,128]{2,1,0:T(8,128)(2,1)} %get-tuple-element.82.refs_1_, f32[8,256,128]{2,1,0:T(8,128)} %get-tuple-element.83.refs_2_, f32[8,2,256]{2,1,0:T(2,128)} %get-tuple-element.84.refs_3_, ...), custom_call_target="tpu_custom_call" | custom-call | flops 4000000000 | bytes 12000000 | tf_op jit(solution)/shard_map/attn_bwd/pallas_call | solution.py:275
  251.3 3.9 all-to-all-start.4
  255.2 22.1 %collective-permute-done.3.refs_7_ = bf16[4,8,64,128]{3,2,1,0:T(8,128)(2,1)} collective-permute-done((bf16[4,8,64,128]{3,2,1,0:T(8,128)(2,1)}, bf16[4,8,64,128]{3,2,1,0:T(8,128)(2,1)}, u32[]{:S(2)}, u32[]{:S(2)}) %collective-permute-start.3) | collective-permute-done | bytes 524320 | tf_op jit(solution)/shard_map/ppermute | solution.py:565
  277.3 1.3 collective-permute-done.1.refs_3_
  278.7 6.8 %fold.1 = (bf16[4,4,176,128]{3,2,1,0:T(8,128)(2,1)}, bf16[4,4,176,128]{3,2,1,0:T(8,128)(2,1)}, bf16[4,4,176,128]{3,2,1,0:T(8,128)(2,1)}, bf16[4,4,176,128]{3,2,1...) custom-call(bf16[4,8,176,128]{3,2,1,0:T(8,128)(2,1)} %get-tuple-elem, ...), custom_call_target="tpu_custom_call" | custom-call | flops 99999997952 | bytes 100000000 | tf_op jit(solution)/shard_map/fold/pallas_call | solution.py:550
  285.4 1.5 collective-permute-start.4
  287.8 1.7 collective-permute-start.7
  289.5 2.3 copy.40
  292.0 3.3 copy.55
  295.9 14.3 %collective-permute-done.7.refs_18_ = bf16[4,4,64,128]{3,2,1,0:T(8,128)(2,1)S(1)} collective-permute-done((bf16[4,4,64,128]{3,2,1,0:T(8,128)(2,1)}, bf16[4,4,64,128]{3,2,1,0:T(8,128)(2,1)S(1)}, u32[]{:S(2)}, u32[]{:S(2)}) %collective-permute-start.7) | collective-permute-done | bytes 262176 | tf_op jit(solution)/shard_map/ppermute | solution.py:565
  310.2 2.8 collective-permute-done.4.refs_15_
  313.0 15.4 %collective-permute-done.5.refs_16_ = bf16[4,4,176,128]{3,2,1,0:T(8,128)(2,1)} collective-permute-done((bf16[4,4,176,128]{3,2,1,0:T(8,128)(2,1)}, bf16[4,4,176,128]{3,2,1,0:T(8,128)(2,1)}, u32[]{:S(2)}, u32[]{:S(2)}) %collective-permute-start.5) | collective-permute-done | bytes 720928 | tf_op jit(solution)/shard_map/ppermute | solution.py:565
  328.4 1.6 copy-done
  330.0 67.1 %tail.1 = (f32[4,176,128]{2,1,0:T(8,128)}, f32[4,176,128]{2,1,0:T(8,128)}, f32[4,176,128]{2,1,0:T(8,128)}, f32[4,64,128]{2,1,0:T(8,128)}, f32[256,128]{1,0:T(8,1...) custom-call(f32[512,128]{1,0:T(8,128)} %get-tuple-element.125.cos_re, ...), custom_call_target="tpu_custom_call" | custom-call | flops 99999997952 | bytes 100000000 | tf_op jit(solution)/shard_map/tail/pallas_call | solution.py:950
  397.2 1.3 fusion.5
  399.8 4.7 %copy.54 = f32[2,256,1024]{2,0,1:T(2,128)} copy(f32[2,256,1024]{2,1,0:T(8,128)} %bitcast.61) | data formatting | bytes 4194304 | tf_op jit(solution)/shard_map/reshape | solution.py:1077
  404.5 2.9 copy.53
  (66 shorter events, 13.9 us)
Async XLA Ops:
  0.6 3.6 copy-start.3
  60.2 3.7 copy-start.16
  60.2 40.4 %all-to-all-start = ((bf16[8,3,256,128]{3,2,1,0:T(8,128)(2,1)}), bf16[8,3,256,128]{3,2,1,0:T(8,128)(2,1)S(1)}, u32[]{:S(2)}, u32[]{:S(2)}) async-start(bf16[8,3,256,128]{3,2,1,0:T(8,128)(2,1)} %get-tuple-element.67), calls=%async_computation | async-start | bytes 3145728 | tf_op jit(solution)/shard_map/all_to_all | solution.py:295
  100.6 3.6 copy-start.2
  100.6 18.3 %all-to-all-start.3 = ((bf16[8,256,128]{2,1,0:T(8,128)(2,1)}), bf16[8,256,128]{2,1,0:T(8,128)(2,1)S(1)}, u32[]{:S(2)}, u32[]{:S(2)}) async-start(bf16[8,256,128]{2,1,0:T(8,128)(2,1)} %get-tuple-element.70), calls=%async_computation.3 | async-start | bytes 1048576 | tf_op jit(solution)/shard_map/all_to_all | solution.py:295
  104.2 20.6 %copy-start.4 = (bf16[256,2,1024]{2,1,0:T(2,128)(2,1)S(1)}, bf16[256,2,1024]{2,1,0:T(2,128)(2,1)}, u32[]{:S(2)}) copy-start(bf16[256,2,1024]{2,1,0:T(2,128)(2,1)} %param.25) | copy-start | bytes 3145732
  118.9 20.1 %copy-start.5 = (bf16[8,256,128]{2,1,0:T(8,128)(2,1)}, bf16[8,256,128]{2,1,0:T(8,128)(2,1)S(1)}, u32[]{:S(2)}) copy-start(bf16[8,256,128]{2,1,0:T(8,128)(2,1)S(1)} %all-to-all-done.3.refs_1_) | copy-start | bytes 1572868
  118.9 20.1 %all-to-all-start.1 = ((bf16[8,256,128]{2,1,0:T(8,128)(2,1)}), bf16[8,256,128]{2,1,0:T(8,128)(2,1)S(1)}, u32[]{:S(2)}, u32[]{:S(2)}) async-start(bf16[8,256,128]{2,1,0:T(8,128)(2,1)} %get-tuple-element.68), calls=%async_computation.1 | async-start | bytes 1048576 | tf_op jit(solution)/shard_map/all_to_all | solution.py:295
  138.9 0.8 copy-start.6
  213.7 63.6 %collective-permute-start = (bf16[4,8,176,128]{3,2,1,0:T(8,128)(2,1)}, bf16[4,8,176,128]{3,2,1,0:T(8,128)(2,1)}, u32[]{:S(2)}, u32[]{:S(2)}) collective-permute-start(bf16[4,8,176,128]{3,2,1,0:T(8,128)(2,1)} %get-tuple-element.95), channel_id=1, source_target_pairs={{0,16},{8,24},{16,0},{24,8},{1,17},{9,25},{17,1},{25,9},{2,18},{10... | collective-permute-start | bytes 4325384 | tf_op jit(solution)/shard_map/ppermute | solution.py:565
  213.8 64.9 %collective-permute-start.1 = (bf16[4,8,176,128]{3,2,1,0:T(8,128)(2,1)}, bf16[4,8,176,128]{3,2,1,0:T(8,128)(2,1)}, u32[]{:S(2)}, u32[]{:S(2)}) collective-permute-start(bf16[4,8,176,128]{3,2,1,0:T(8,128)(2,1)} %get-tuple-element.97), channel_id=1, source_target_pairs={{0,16},{8,24},{16,0},{24,8},{1,17},{9,25},{17,1},{25,9},{2,18},{10... | collective-permute-start | bytes 4325384 | tf_op jit(solution)/shard_map/ppermute | solution.py:565
  215.8 62.9 %collective-permute-start.2 = (bf16[4,8,176,128]{3,2,1,0:T(8,128)(2,1)}, bf16[4,8,176,128]{3,2,1,0:T(8,128)(2,1)}, u32[]{:S(2)}, u32[]{:S(2)}) collective-permute-start(bf16[4,8,176,128]{3,2,1,0:T(8,128)(2,1)} %get-tuple-element.99), channel_id=1, source_target_pairs={{0,1},{1,0},{2,3},{3,2},{4,5},{5,4},{6,7},{7,6},{8,9},{9,8},{10,11... | collective-permute-start | bytes 4325384 | tf_op jit(solution)/shard_map/ppermute | solution.py:565
  216.3 61.0 %collective-permute-start.3 = (bf16[4,8,64,128]{3,2,1,0:T(8,128)(2,1)}, bf16[4,8,64,128]{3,2,1,0:T(8,128)(2,1)}, u32[]{:S(2)}, u32[]{:S(2)}) collective-permute-start(bf16[4,8,64,128]{3,2,1,0:T(8,128)(2,1)} %get-tuple-element.101), channel_id=1, source_target_pairs={{0,1},{1,0},{2,3},{3,2},{4,5},{5,4},{6,7},{7,6},{8,9},{9,8},{10,11... | collective-permute-start | bytes 1572872 | tf_op jit(solution)/shard_map/ppermute | solution.py:565
  251.3 77.1 %all-to-all-start.4 = ((bf16[8,2,3,256,128]{4,3,2,1,0:T(8,128)(2,1)}), bf16[8,2,3,256,128]{4,3,2,1,0:T(8,128)(2,1)S(1)}, u32[]{:S(2)}, u32[]{:S(2)}) async-start(bf16[8,2,3,256,128]{4,3,2,1,0:T(8,128)(2,1)} %attn_bwd.1), calls=%async_computation.4 | async-start | bytes 6291456 | tf_op jit(solution)/shard_map/all_to_all | solution.py:295
  285.4 6.4 %copy-start.14 = (f32[4,2,256]{2,1,0:T(2,128)S(1)}, f32[4,2,256]{2,1,0:T(2,128)}, u32[]{:S(2)}) copy-start(f32[4,2,256]{2,1,0:T(2,128)} %get-tuple-element.73) | copy-start | bytes 24580
  285.4 27.6 %collective-permute-start.4 = (bf16[4,4,176,128]{3,2,1,0:T(8,128)(2,1)}, bf16[4,4,176,128]{3,2,1,0:T(8,128)(2,1)}, u32[]{:S(2)}, u32[]{:S(2)}) collective-permute-start(bf16[4,4,176,128]{3,2,1,0:T(8,128)(2,1)} %get-tuple-element.106), channel_id=1, source_target_pairs={{0,1},{1,0},{2,3},{3,2},{4,5},{5,4},{6,7},{7,6},{8,9},{9,8},{10,11... | collective-permute-start | bytes 2162696 | tf_op jit(solution)/shard_map/ppermute | solution.py:565
  286.9 41.5 %collective-permute-start.5 = (bf16[4,4,176,128]{3,2,1,0:T(8,128)(2,1)}, bf16[4,4,176,128]{3,2,1,0:T(8,128)(2,1)}, u32[]{:S(2)}, u32[]{:S(2)}) collective-permute-start(bf16[4,4,176,128]{3,2,1,0:T(8,128)(2,1)} %get-tuple-element.107), channel_id=1, source_target_pairs={{0,1},{1,0},{2,3},{3,2},{4,5},{5,4},{6,7},{7,6},{8,9},{9,8},{10,11... | collective-permute-start | bytes 2162696 | tf_op jit(solution)/shard_map/ppermute | solution.py:565
  287.5 40.9 %collective-permute-start.6 = (bf16[4,4,176,128]{3,2,1,0:T(8,128)(2,1)}, bf16[4,4,176,128]{3,2,1,0:T(8,128)(2,1)}, u32[]{:S(2)}, u32[]{:S(2)}) collective-permute-start(bf16[4,4,176,128]{3,2,1,0:T(8,128)(2,1)} %get-tuple-element.108), channel_id=1, source_target_pairs={{0,16},{8,24},{16,0},{24,8},{1,17},{9,25},{17,1},{25,9},{2,18},{10... | collective-permute-start | bytes 2162696 | tf_op jit(solution)/shard_map/ppermute | solution.py:565
  287.8 22.4 %collective-permute-start.7 = (bf16[4,4,64,128]{3,2,1,0:T(8,128)(2,1)}, bf16[4,4,64,128]{3,2,1,0:T(8,128)(2,1)S(1)}, u32[]{:S(2)}, u32[]{:S(2)}) collective-permute-start(bf16[4,4,64,128]{3,2,1,0:T(8,128)(2,1)} %get-tuple-element.109), channel_id=1, source_target_pairs={{0,16},{8,24},{16,0},{24,8},{1,17},{9,25},{17,1},{25,9},{2,18},{10... | collective-permute-start | bytes 786440 | tf_op jit(solution)/shard_map/ppermute | solution.py:565
  289.5 5.7 %copy-start.15 = (f32[1,1024]{1,0:T(1,128)S(1)}, f32[1,1024]{1,0:T(1,128)}, u32[]{:S(2)}) copy-start(f32[1,1024]{1,0:T(1,128)} %get-tuple-element.72) | copy-start | bytes 12292
  310.2 18.2 %copy-start.17 = (bf16[4,4,64,128]{3,2,1,0:T(8,128)(2,1)}, bf16[4,4,64,128]{3,2,1,0:T(8,128)(2,1)S(1)}, u32[]{:S(2)}) copy-start(bf16[4,4,64,128]{3,2,1,0:T(8,128)(2,1)S(1)} %collective-permute-done.7.refs_18_) | copy-start | bytes 786436
  328.4 1.6 copy-start
  399.8 4.7 %copy-start.1 = (f32[512,1024]{1,0:T(8,128)S(1)}, f32[512,1024]{1,0:T(8,128)}, u32[]{:S(2)}) copy-start(f32[512,1024]{1,0:T(8,128)} %get-tuple-element.111) | copy-start | bytes 6291460
  404.5 4.3 %copy-start.9 = (f32[4,176,128]{2,1,0:T(8,128)S(1)}, f32[4,176,128]{2,1,0:T(8,128)}, u32[]{:S(2)}) copy-start(f32[4,176,128]{2,1,0:T(8,128)} %get-tuple-element.116) | copy-start | bytes 1081348
  404.5 5.3 %copy-start.8 = (f32[4,176,128]{2,1,0:T(8,128)S(1)}, f32[4,176,128]{2,1,0:T(8,128)}, u32[]{:S(2)}) copy-start(f32[4,176,128]{2,1,0:T(8,128)} %get-tuple-element.117) | copy-start | bytes 1081348
  407.4 3.3 copy-start.13
  407.4 4.0 copy-start.12
  407.4 4.6 %copy-start.11 = (f32[256,128]{1,0:T(8,128)S(1)}, f32[256,128]{1,0:T(8,128)}, u32[]{:S(2)}) copy-start(f32[256,128]{1,0:T(8,128)} %get-tuple-element.147) | copy-start | bytes 393220
  407.4 5.3 %copy-start.10 = (f32[4,64,128]{2,1,0:T(8,128)S(1)}, f32[4,64,128]{2,1,0:T(8,128)}, u32[]{:S(2)}) copy-start(f32[4,64,128]{2,1,0:T(8,128)} %get-tuple-element.115) | copy-start | bytes 393220
  407.4 5.9 %copy-start.7 = (f32[4,176,128]{2,1,0:T(8,128)S(1)}, f32[4,176,128]{2,1,0:T(8,128)}, u32[]{:S(2)}) copy-start(f32[4,176,128]{2,1,0:T(8,128)} %get-tuple-element.118) | copy-start | bytes 1081348

commit v5 on v4

--- a/solution.py
+++ b/solution.py
@@ -338,6 +338,12 @@
     return [("dp", 0)] + rest + blk
 
 
+def z_order():
+    rest = [("dp", b) for b in range(1, bits_of("dp"))]
+    blk = [("blk", b) for b in range(bits_of("blk"))]
+    return [("dp", 0)] + blk[1:2] + rest + blk[:1] + blk[2:]
+
+
 def scatter(grad, rows_name, y_early):
     n_rows = lax.axis_size(rows_name)
     rows, cols = grad.shape
@@ -372,7 +378,7 @@
     return place
 
 
-def blocks_dot(left_ref, right_ref, left_is_dp, side, col, order, n_dp, n_blk, out_ref, *at):
+def blocks_dot(left_ref, right_ref, left_is_dp, side, col, order, n_dp, n_blk, row, out_ref, *at):
     size = left_ref.shape[2]
     tokens = left_ref.shape[3]
     if left_is_dp:
@@ -392,16 +398,19 @@
     for d in range(n_dp // 2):
         for e in range(n_blk):
             k, m = (d, e) if left_is_dp else (e, d)
-            out_ref[(*at, place_of(order, 2 * d, e))] = result[k * size : (k + 1) * size, m * 128 : (m + 1) * 128]
+            out_ref[(*at, place_of(order, 2 * d, e), slice(row, row + size))] = result[
+                k * size : (k + 1) * size, m * 128 : (m + 1) * 128
+            ]
 
 
 def ffn_wgrad_kernel(plans, n_dp, n_blk, rows, *refs):
     source = iter(refs)
     take = lambda n: [next(source) for _ in range(n)]
-    n = len(plans)
-    lefts, rights, moved, outs, arrived = take(n), take(n), take(rows), take(2 * n), take(rows)
+    n, n_terms = len(plans), sum(len(terms) for _, terms, _ in plans)
+    lefts, rights, moved, outs, arrived = take(n_terms), take(n_terms), take(rows), take(2 * n), take(rows)
     sents, landed, keeps = take(n), take(n), take(n)
-    send_sem, recv_sem, own_sem, out_sem, in_sem = take(5)
+    send_sem, recv_sem = take(2)
+    own_sem, out_sem, in_sem = take(3) if rows else (None, None, None)
     step = pl.program_id(0)
     core, device = partner("dp", 0)
     here = lax.axis_index("blk")
@@ -424,10 +433,10 @@
     def _():
         barrier = pltpu.get_barrier_semaphore()
         pl.semaphore_signal(barrier, inc=1, device_id=device, device_id_type=MESH)
-        for m in range(1, n_blk):
+        for m in range(1, n_blk if rows else 1):
             there = (lax.axis_index("dp"), (here + m) % n_blk)
             pl.semaphore_signal(barrier, inc=1, device_id=there, device_id_type=MESH)
-        pl.semaphore_wait(barrier, n_blk)
+        pl.semaphore_wait(barrier, n_blk if rows else 1)
         for r in range(rows):
             own(r).start()
             for m in range(1, n_blk):
@@ -443,19 +452,22 @@
             device_id_type=MESH,
         )
 
-    for k, (order, left_is_dp, col_parts) in enumerate(plans):
-        c = step - 4 * k
-
-        @pl.when((c >= 0) & (c < 4))
+    first = 0
+    for k, (order, terms, pieces) in enumerate(plans):
+        c = step - first
+        first += pieces
+
+        @pl.when((c >= 0) & (c < pieces))
         def _():
-            make = lambda side, *out: blocks_dot(
-                lefts[k], rights[k], left_is_dp, side, c % col_parts, order, n_dp, n_blk, *out
-            )
+            def make(side, *out):
+                for at, left_is_dp, col_parts, row in terms:
+                    blocks_dot(lefts[at], rights[at], left_is_dp, side, c % col_parts, order, n_dp, n_blk, row, *out)
+
             make(1 - core, sents[k], c)
             remote(k, c).start()
             make(core, keeps[k], c % 2)
 
-        @pl.when((c >= 1) & (c < 5))
+        @pl.when((c >= 1) & (c < pieces + 1))
         def _():
             remote(k, c - 1).wait_recv()
             mine, _ = partner(*order[1])
@@ -469,10 +481,10 @@
 
                 lax.fori_loop(0, half, one, 0)
 
-    @pl.when(step == 4 * n)
+    @pl.when(step == first)
     def _():
         for k in range(n):
-            for c in range(4):
+            for c in range(plans[k][2]):
                 remote(k, c).wait_send()
         for r in range(rows):
             own(r).wait()
@@ -480,47 +492,57 @@
                 across(r, m).wait()
 
 
-def ffn_wgrad(items, moved, collective_id):
+def ffn_wgrad(items, moved, flops, collective_id):
     n_dp, n_blk = lax.axis_size("dp"), lax.axis_size("blk")
     lefts, rights, plans, left_specs, right_specs, out_specs, outs, scratch = [], [], [], [], [], [], [], []
     held = n_dp * n_blk // 2
-    flops = 0
-    for k, (order, left_is_dp, left, right) in enumerate(items):
-        n_left, n_right = (n_dp, n_blk) if left_is_dp else (n_blk, n_dp)
-        cols, tokens = left.shape
-        row_parts, col_parts, size = chunks_of(cols // n_left, right.shape[1] // n_right)
-        lefts.append(left.reshape(n_left, row_parts, size, tokens))
-        rights.append(right)
-        plans.append((order, left_is_dp, col_parts))
-        flops += 2 * left.size * right.shape[1]
-        left_specs.append(
+    steps = 0
+    for order, wanted, terms in items:
+        count, row, plan = len(wanted), 0, []
+        for left_is_dp, left, right in terms:
+            n_left, n_right = (n_dp, n_blk) if left_is_dp else (n_blk, n_dp)
+            cols, tokens = left.shape
+            row_parts, col_parts, size = chunks_of(cols // n_left, right.shape[1] // n_right)
+            plan.append((len(lefts), left_is_dp, col_parts, row))
+            row += size
+            lefts.append(left.reshape(n_left, row_parts, size, tokens))
+            rights.append(right)
+            left_specs.append(
+                pl.BlockSpec(
+                    (n_left, 1, size, tokens),
+                    lambda p, at=steps, low=wanted[0], count=count, col_parts=col_parts: (
+                        0,
+                        (low + jnp.clip(p - at, 0, count - 1)) // col_parts,
+                        0,
+                        0,
+                    ),
+                )
+            )
+            right_specs.append(pl.BlockSpec(right.shape, lambda p: (0, 0), pipeline_mode=pl.Buffered(1)))
+        plans.append((order, plan, count))
+        out_specs += [
             pl.BlockSpec(
-                (n_left, 1, size, tokens),
-                lambda p, k=k, col_parts=col_parts: (0, jnp.clip(p - 4 * k, 0, 3) // col_parts, 0, 0),
+                (1, held // 2, row, 128), lambda p, at=steps, count=count: (jnp.clip(p - 1 - at, 0, count - 1), 0, 0, 0)
             )
-        )
-        right_specs.append(pl.BlockSpec(right.shape, lambda p: (0, 0), pipeline_mode=pl.Buffered(1)))
-        out_specs += [
-            pl.BlockSpec((1, held // 2, size, 128), lambda p, k=k: (jnp.clip(p - 1 - 4 * k, 0, 3), 0, 0, 0))
         ] * 2
-        outs += [jax.ShapeDtypeStruct((4, held // 2, size, 128), BF16)] * 2
-        scratch.append((held, size, 128))
+        outs += [jax.ShapeDtypeStruct((count, held // 2, row, 128), BF16)] * 2
+        scratch.append((count, held, row, 128))
+        steps += count
     n = len(items)
     flat = pl.pallas_call(
         functools.partial(ffn_wgrad_kernel, plans, n_dp, n_blk, len(moved)),
-        grid=(4 * n + 1,),
+        grid=(steps + 1,),
         in_specs=left_specs + right_specs + [pl.BlockSpec(memory_space=pl.ANY)] * len(moved),
         out_specs=out_specs + [pl.BlockSpec(memory_space=pl.ANY)] * len(moved),
         out_shape=outs + [jax.ShapeDtypeStruct(a.shape, a.dtype) for a in moved],
-        scratch_shapes=[pltpu.VMEM((4,) + a, BF16) for a in scratch] * 2
-        + [pltpu.VMEM((2,) + a, BF16) for a in scratch]
+        scratch_shapes=[pltpu.VMEM(a, BF16) for a in scratch] * 2
+        + [pltpu.VMEM((2,) + a[1:], BF16) for a in scratch]
         + [pltpu.SemaphoreType.DMA((n, 4))] * 2
-        + [pltpu.SemaphoreType.DMA((len(moved),))]
-        + [pltpu.SemaphoreType.DMA((len(moved), n_blk))] * 2,
+        + ([pltpu.SemaphoreType.DMA((len(moved),))] + [pltpu.SemaphoreType.DMA((len(moved), n_blk))] * 2 if moved else []),
         compiler_params=pltpu.CompilerParams(
             collective_id=collective_id, has_side_effects=True, vmem_limit_bytes=VMEM_LIMIT
         ),
-        cost_estimate=pl.CostEstimate(flops=flops, bytes_accessed=flops // 400, transcendentals=0),
+        cost_estimate=pl.CostEstimate(flops=flops, bytes_accessed=10**7, transcendentals=0),
         name="ffn_wgrad",
     )(*lefts, *rights, *moved)
     return [tuple(flat[2 * k : 2 * k + 2]) for k in range(n)], list(flat[2 * n :])
@@ -542,7 +564,7 @@
             lax.fori_loop(0, half, one, 0)
 
 
-def fold(pairs, stages):
+def fold(pairs, stages, flops):
     n = len(pairs)
     arrays = [a for pair in pairs for a in pair]
     block = lambda a, parts: pl.BlockSpec((1, a.shape[1] // parts) + a.shape[2:], lambda c: (c, 0, 0, 0))
@@ -554,7 +576,7 @@
         out_specs=[block(a, 2) for a in arrays],
         out_shape=[half(a) for a in arrays],
         compiler_params=pltpu.CompilerParams(vmem_limit_bytes=VMEM_LIMIT),
-        cost_estimate=pl.CostEstimate(flops=10**11, bytes_accessed=10**8, transcendentals=0),
+        cost_estimate=pl.CostEstimate(flops=flops, bytes_accessed=10**7, transcendentals=0),
         name="fold",
     )(*arrays)
     return [tuple(flat[2 * k : 2 * k + 2]) for k in range(n)]
@@ -743,17 +765,18 @@
             late[u].append(Halving(order, work, sent, landed, *take(2)))
     _, rows, _, length, width = back_ref.shape
     core, _ = partner("dp", 0)
-    n_chunks = keeps[0].shape[0]
+    counts = [a.shape[0] for a in keeps]
 
     load = [pltpu.make_async_copy(a, b, load_sem.at[k]) for k, (a, b) in enumerate(zip(loads, here))]
     keep_copy = lambda k, c: pltpu.make_async_copy(keeps[k].at[c], streams[k].work.at[c], keep_sem.at[k, c])
     got_copy = lambda k, c: pltpu.make_async_copy(gots[k].at[c], streams[k].landed[0].at[c], got_sem.at[k, c])
     load[0].start()
     load[1].start()
-    for c in range(n_chunks):
+    for c in range(max(counts)):
         for k in range(n_ffn):
-            keep_copy(k, c).start()
-            got_copy(k, c).start()
+            if c < counts[k]:
+                keep_copy(k, c).start()
+                got_copy(k, c).start()
     for copy in load[2:]:
         copy.start()
 
@@ -765,6 +788,8 @@
 
     def ffn(c, stage):
         for k, stream in enumerate(streams):
+            if c >= counts[k]:
+                continue
             if stage == 1:
                 keep_copy(k, c).wait()
                 got_copy(k, c).wait()
@@ -858,7 +883,7 @@
             vecs[e + 1] = summed
             vec_copy(e + 1).start()
 
-    chunks = range(n_chunks)
+    chunks = range(max(counts))
     for c in chunks:
         ffn(c, 1)
     load[0].wait()
@@ -894,13 +919,10 @@
     for e in vecs_left:
         vec(e)
 
-    def finish(c, _):
-        for stream in streams:
+    for stream, count in zip(streams, counts):
+        for c in range(count):
             for stage in range(1, ffn_stages):
                 stream.remote(stage, c).wait_send()
-        return 0
-
-    lax.fori_loop(0, n_chunks, finish, 0)
     for stream in late[0] + late[1] + late[2]:
         for stage in range(qkv_stages):
             stream.remote(stage, 0).wait_send()
@@ -914,13 +936,13 @@
     keeps, gots = [pair[0] for pair in ffn_pairs], [pair[1] for pair in ffn_pairs]
     loads = [back, normed_t.reshape(n_dp, model // n_dp, tokens), hidden, d_resid, *weights]
     ffn_stages, qkv_stages, n_qkv = len(ffn_orders[0]), len(qkv_orders[0]), 3
-    n_chunks = keeps[0].shape[0]
+    n_chunks = max(a.shape[0] for a in keeps)
     block = (model // n_dp, model // n_blk)
     held = n_dp * n_blk // 2
     shape = jax.ShapeDtypeStruct
     vec = (1, model + small.shape[1])
     outs = (
-        [shape((n_chunks,) + a.shape[2:], F32) for a in keeps]
+        [shape(a.shape[:1] + a.shape[2:], F32) for a in keeps]
         + [shape(block, F32)] * n_qkv
         + [shape((tokens, model), F32)] * 2
         + [shape(vec, F32)]
@@ -939,8 +961,8 @@
     ]
     for a in keeps:
         scratch.append(pltpu.VMEM(a.shape, BF16))
-        scratch += [pltpu.VMEM((n_chunks, a.shape[1] >> stage) + a.shape[2:], BF16) for stage in range(ffn_stages)]
-        scratch += [pltpu.SemaphoreType.DMA((ffn_stages, n_chunks))] * 2
+        scratch += [pltpu.VMEM((a.shape[0], a.shape[1] >> stage) + a.shape[2:], BF16) for stage in range(ffn_stages)]
+        scratch += [pltpu.SemaphoreType.DMA((ffn_stages, a.shape[0]))] * 2
     part = (block[0] // len(qkv_orders), block[1])
     for _ in range(n_qkv * len(qkv_orders)):
         scratch += [pltpu.VMEM((1, held) + part, BF16)] * 2
@@ -1098,27 +1120,35 @@
 
     inner = w_gate.shape[1]
     by_blocks = (model // n_dp) % 128 == 0 and width == 128 and (inner // n_blk) % 32 == 0
-    early, late = block_order(False), block_order(True)
+    early, late, middle = block_order(False), block_order(True), z_order()
     if by_blocks:
+        orders = (early, late, middle)
+        pieces = (0, 1, 2, 3)
+        exchanged = lambda pairs, stages: [(keep, swap(sent, *stage)) for (keep, sent), stage in zip(pairs, stages)]
         folded, d_own = ffn_wgrad(
             (
-                (early, False, d_gate_t, normed_mid),
-                (early, False, d_up_t, normed_mid),
-                (late, True, inner_t, cot),
-                (late, True, attn_low_t, d_branch),
+                (early, pieces, [(False, d_gate_t, normed_mid)]),
+                (late, pieces, [(False, d_up_t, normed_mid)]),
+                (middle, pieces, [(True, inner_t, cot)]),
             ),
             d_attn,
-            2,
+            10**9,
+            1,
         )
-        kept = [keep for keep, sent in folded]
-        orders = (early, early, late, late)
-        ffn_got = [swap(sent, *order[1]) for order, (_, sent) in zip(orders, folded)]
+        ffn_pairs = exchanged(folded, [order[1] for order in orders])
         back_own = attn_bwd(lens, qkv, d_own, attended, lse, n_docs)
         back = exchange(back_own)
+        kept = [keep for keep, got in ffn_pairs]
+        token, kept = lax.optimization_barrier((back_own, kept))
         second = [order[2] for order in orders]
-        token, kept = lax.optimization_barrier((back_own, kept))
-        folded = fold(list(zip(kept, ffn_got)), second)
-        ffn_pairs = [(keep, swap(sent, *stage)) for (keep, sent), stage in zip(folded, second)]
+        folded = fold([(keep, got) for keep, (_, got) in zip(kept, ffn_pairs)], second, 10**9)
+        ffn_pairs = exchanged(folded, second)
+        folded, attn_low_t = lax.optimization_barrier((folded, attn_low_t))
+        ffn_pairs = [(keep, got) for (keep, _), (_, got) in zip(folded, ffn_pairs)]
+        project, _ = ffn_wgrad(((early, pieces, [(True, attn_low_t, d_branch)]),), [], 10**11, 2)
+        project = exchanged(project, [early[1]])
+        ffn_pairs += exchanged(fold(project, [early[2]], 10**9), [early[2]])
+        orders += (early,)
     else:
         d_own = [exchange(d_attn[r]) for r in range(rows)]
         back = exchange(attn_bwd(lens, qkv, d_own, attended, lse, n_docs))
@@ -1144,8 +1174,8 @@
         small = small.reshape(-1)
         grad_gate = whole_block(blocks[0], inner // n_blk, model // n_dp).T
         grad_up = whole_block(blocks[1], inner // n_blk, model // n_dp).T
-        grad_down = whole_block(blocks[2], inner // n_dp, model // n_blk)
-        grad_project = whole_block(blocks[3], model // n_dp, model // n_blk)
+        grad_down = blocks[2].reshape(inner // n_dp, model // n_blk)
+        grad_project = blocks[3].reshape(model // n_dp, model // n_blk)
         grad_query, grad_key, grad_value = blocks[4:]
     else:
         low, grad_first = turn_back(back, cos, sin)

time: 418 us -> 398 us (0.952)
  Pallas kernels: 219 us -> 206 us
  waiting for transfers between devices: 90 us -> 77.5 us
    ppermute x8, waiting for transfers between devices: 55.9 us -> 27.6 us  [swap(): return lax.ppermute(values, name, [(k, k ^ 1 << bit) for k in range(size)])]
    all_to_all x4, waiting for transfers between devices: 34.1 us -> 49.9 us  [exchange(): return lax.all_to_all(values, 'blk', 0, 0, tiled=True)]
    pallas_call x1, Pallas kernels: 67.1 us -> 58.9 us  [tail(): pl.pallas_call(functools.partial(tail_kernel, ffn_orders, qkv_orders, n_d...]
    pallas_call x1, Pallas kernels: 33.5 us -> 28.1 us  [attn_bwd(): pl.pallas_call(functools.partial(attn_bwd_kernel, rows, n_docs, heads), g...]
    ppermute x8, starting transfers between devices: 8.23 us -> 12.9 us  [swap(): return lax.ppermute(values, name, [(k, k ^ 1 << bit) for k in range(size)])]
    pallas_call x2, Pallas kernels: 29.5 us -> 25.1 us  [attn_fwd(): pl.pallas_call(functools.partial(attn_fwd_kernel, row, n_docs, heads), gr...]
    pallas_call x1 -> x2, Pallas kernels: 6.76 us -> 9.65 us  [fold(): pl.pallas_call(functools.partial(fold_kernel, stages), grid=(arrays[0].sh...]
    pallas_call x1 -> x2, Pallas kernels: 41.2 us -> 42.7 us  [ffn_wgrad(): pl.pallas_call(functools.partial(ffn_wgrad_kernel, plans, n_dp, n_blk, le...]
  transfers between devices with their start and end apart: 12 -> 12, of which waited for: 8 -> 8; matrix products, arithmetic and copies ran while one was open for 2% -> 2% of each run, Pallas kernels for 17% -> 18%
where the time goes in v5:
time: 398 us; the launch traced here: 394 us
  Pallas kernels  206 us (52%)
  waiting for transfers between devices  77.5 us (19%)
  blocking collectives  44.4 us (11%)
  local copies, waits for them, and re-layouts  30.6 us (8%)
  starting transfers between devices  28.7 us (7%)
  between operations  4.45 us (1%)
    pallas_call x1, Pallas kernels, tail(): pl.pallas_call(functools.partial(tail_kernel, ffn_orders, qkv_orders, n_d...  58.9 us
    all_to_all x4, waiting for transfers between devices, exchange(): return lax.all_to_all(values, 'blk', 0, 0, tiled=True)  49.9 us
    all_to_all x1, blocking collectives, exchange(): return lax.all_to_all(values, 'blk', 0, 0, tiled=True)  44.4 us
    pallas_call x2, Pallas kernels, ffn_wgrad(): pl.pallas_call(functools.partial(ffn_wgrad_kernel, plans, n_dp, n_blk, le...  42.7 us
    pallas_call x1, Pallas kernels, feed_forward(): pl.pallas_call(functools.partial(ffn_kernel, rows, n_blk), grid=(inner //...  32.8 us
    pallas_call x1, Pallas kernels, attn_bwd(): pl.pallas_call(functools.partial(attn_bwd_kernel, rows, n_docs, heads), g...  28.1 us
    ppermute x8, waiting for transfers between devices, swap(): return lax.ppermute(values, name, [(k, k ^ 1 << bit) for k in range(size)])  27.6 us
    pallas_call x2, Pallas kernels, attn_fwd(): pl.pallas_call(functools.partial(attn_fwd_kernel, row, n_docs, heads), gr...  25.1 us
  transfers between devices with their start and end apart: 12, of which 8 were waited for; matrix products, arithmetic and copies ran while one was open for 2% of the time, Pallas kernels for 18%

profile of v5, /device:TPU:0, one launch (start us, length us, event | category | flops | bytes accessed | tf_op | source)
XLA Modules:
  0.0 394.3 jit_solution(4375497864984740291)
XLA Ops:
  1.7 2.5 copy.36
  5.5 1.8 fusion
  7.3 8.5 %qkv.1 = (bf16[8,3,256,128]{3,2,1,0:T(8,128)(2,1)}, bf16[8,3,256,128]{3,2,1,0:T(8,128)(2,1)}, bf16[512,1024]{1,0:T(8,128)(2,1)}, f32[4,2,256]{2,1,0:T(2,128)}) custom-call(bf16[512,1024]{1,0:T(8,128)(2,1)} %bitcast.72, bf16[512,1024]{1,0:T(8,128)(2,1)} %bitcast.79, f32[512,128]{1,0:T(8,128)} %get-tuple-element.131.cos_ref.refs_0_, ...), custom_call_target="tpu_custom_call" | custom-call | flops 3221225472 | bytes 11534336 | tf_op jit(solution)/shard_map/qkv/pallas_call | solution.py:83
  15.8 44.4 %all_to_all.25.qkv_ref.refs_4_ = bf16[8,3,256,128]{3,2,1,0:T(8,128)(2,1)} all-to-all(bf16[8,3,256,128]{3,2,1,0:T(8,128)(2,1)} %get-tuple-element.72), channel_id=1, replica_groups=mesh['dp'=4,'blk'=8] {'blk'}, dimensions={0} | all-to-all | bytes 3145728 | tf_op jit(solution)/shard_map/all_to_all | solution.py:295
  60.2 3.7 all-to-all-start
  64.5 12.5 %attn_fwd.3 = (f32[8,256,128]{2,1,0:T(8,128)}, bf16[8,256,128]{2,1,0:T(8,128)(2,1)}, f32[8,2,256]{2,1,0:T(2,128)}) custom-call(s32[16]{0:T(128)} %reshape.153.lens_ref, bf16[8,3,256,128]{3,2,1,0:T(8,128)(2,1)} %all_to_all.25.qkv_ref.refs_4_), custom_call_target="tpu_custom_call" | custom-call | flops 10000000000 | bytes 3000000 | tf_op jit(solution)/shard_map/attn_fwd/pallas_call | solution.py:185
  77.0 23.6 %all-to-all-done.qkv_ref.refs_0_ = bf16[8,3,256,128]{3,2,1,0:T(8,128)(2,1)S(1)} async-done(((bf16[8,3,256,128]{3,2,1,0:T(8,128)(2,1)}), bf16[8,3,256,128]{3,2,1,0:T(8,128)(2,1)S(1)}, u32[]{:S(2)}, u32[]{:S(2)}) %all-to-all-start) | async-done | bytes 1572896 | tf_op jit(solution)/shard_map/all_to_all | solution.py:295
  100.6 3.6 all-to-all-start.3
  104.2 12.6 %attn_fwd.2 = (f32[8,256,128]{2,1,0:T(8,128)}, bf16[8,256,128]{2,1,0:T(8,128)(2,1)}, f32[8,2,256]{2,1,0:T(2,128)}) custom-call(s32[16]{0:T(128)} %reshape.153.lens_ref, bf16[8,3,256,128]{3,2,1,0:T(8,128)(2,1)} %copy-done.2), custom_call_target="tpu_custom_call" | custom-call | flops 10000000000 | bytes 3000000 | tf_op jit(solution)/shard_map/attn_fwd/pallas_call | solution.py:185
  116.8 2.0 all-to-all-done.3.refs_1_
  118.9 4.0 %all-to-all-start.1 = ((bf16[8,256,128]{2,1,0:T(8,128)(2,1)}), bf16[8,256,128]{2,1,0:T(8,128)(2,1)S(1)}, u32[]{:S(2)}, u32[]{:S(2)}) async-start(bf16[8,256,128]{2,1,0:T(8,128)(2,1)} %get-tuple-element.71), calls=%async_computation.1 | async-start | bytes 1048576 | tf_op jit(solution)/shard_map/all_to_all | solution.py:295
  124.1 13.1 %all-to-all-done.1.refs_0_ = bf16[8,256,128]{2,1,0:T(8,128)(2,1)S(1)} async-done(((bf16[8,256,128]{2,1,0:T(8,128)(2,1)}), bf16[8,256,128]{2,1,0:T(8,128)(2,1)S(1)}, u32[]{:S(2)}, u32[]{:S(2)}) %all-to-all-start.1) | async-done | bytes 524320 | tf_op jit(solution)/shard_map/all_to_all | solution.py:295
  138.0 32.8 %ffn.1 = (bf16[1024,512]{1,0:T(8,128)(2,1)}, bf16[512,1024]{1,0:T(8,128)(2,1)}, bf16[2816,512]{1,0:T(8,128)(2,1)}, bf16[2816,512]{1,0:T(8,128)(2,1)}, bf16[2816,...) custom-call(bf16[8,256,128]{2,1,0:T(8,128)(2,1)} %copy-done.6, ...), custom_call_target="tpu_custom_call" | custom-call | flops 19864223744 | bytes 36438016 | tf_op jit(solution)/shard_map/ffn/pallas_call | solution.py:683
  170.8 34.7 %ffn_wgrad.2 = (bf16[4,8,176,128]{3,2,1,0:T(8,128)(2,1)}, bf16[4,8,176,128]{3,2,1,0:T(8,128)(2,1)}, bf16[4,8,176,128]{3,2,1,0:T(8,128)(2,1)}, bf16[4,8,176,128]{...) custom-call(bf16[8,2,176,512]{3,2,1,0:T(8,128)(2,1)} %bitcast.61, ...), custom_call_target="tpu_custom_call" | custom-call | flops 1000000000 | bytes 10000000 | tf_op jit(solution)/shard_map/ffn_wgrad/pallas_call | solution.py:532
  205.5 3.3 collective-permute-start
  210.0 28.1 %attn_bwd.1 = bf16[8,2,3,256,128]{4,3,2,1,0:T(8,128)(2,1)} custom-call(s32[16]{0:T(128)} %reshape.153.lens_ref, bf16[8,3,256,128]{3,2,1,0:T(8,128)(2,1)} %copy-done.2, bf16[8,256,128]{2,1,0:T(8,128)(2,1)} %get-tuple-element.83.refs_1_, f32[8,256,128]{2,1,0:T(8,128)} %get-tuple-element.84.refs_2_, f32[8,2,256]{2,1,0:T(2,128)} %get-tuple-element.85.refs_3_, ...), custom_call_target="tpu_custom_call" | custom-call | flops 4000000000 | bytes 12000000 | tf_op jit(solution)/shard_map/attn_bwd/pallas_call | solution.py:275
  238.1 4.5 %all-to-all-start.4 = ((bf16[8,2,3,256,128]{4,3,2,1,0:T(8,128)(2,1)}), bf16[8,2,3,256,128]{4,3,2,1,0:T(8,128)(2,1)S(1)}, u32[]{:S(2)}, u32[]{:S(2)}) async-start(bf16[8,2,3,256,128]{4,3,2,1,0:T(8,128)(2,1)} %attn_bwd.1), calls=%async_computation.4 | async-start | bytes 6291456 | tf_op jit(solution)/shard_map/all_to_all | solution.py:295
  242.9 6.3 %fold.2 = (bf16[4,4,176,128]{3,2,1,0:T(8,128)(2,1)}, bf16[4,4,176,128]{3,2,1,0:T(8,128)(2,1)}, bf16[4,4,176,128]{3,2,1,0:T(8,128)(2,1)}, bf16[4,4,176,128]{3,2,1...) custom-call(bf16[4,8,176,128]{3,2,1,0:T(8,128)(2,1)} %get-tuple-element.94.refs_0_, ...), custom_call_target="tpu_custom_call" | custom-call | flops 1000000000 | bytes 10000000 | tf_op jit(solution)/shard_map/fold/pallas_call | solution.py:572
  249.2 8.0 %ffn_wgrad.3 = (bf16[4,8,64,128]{3,2,1,0:T(8,128)(2,1)}, bf16[4,8,64,128]{3,2,1,0:T(8,128)(2,1)}) custom-call(bf16[4,4,64,512]{3,2,1,0:T(8,128)(2,1)} %bitcast.93, bf16[512,1024]{1,0:T(8,128)(2,1)} %get-tuple-element.111.refs_1_), custom_call_target="tpu_custom_call" | custom-call | flops 99999997952 | bytes 10000000 | tf_op jit(solution)/shard_map/ffn_wgrad/pallas_call | solution.py:532
  257.2 2.9 collective-permute-start.3
  261.9 1.9 collective-permute-start.6
  263.8 9.2 %collective-permute-done.3.refs_1_ = bf16[4,8,64,128]{3,2,1,0:T(8,128)(2,1)S(1)} collective-permute-done((bf16[4,8,64,128]{3,2,1,0:T(8,128)(2,1)}, bf16[4,8,64,128]{3,2,1,0:T(8,128)(2,1)S(1)}, u32[]{:S(2)}, u32[]{:S(2)}) %collective-permute-start.3) | collective-permute-done | bytes 524320 | tf_op jit(solution)/shard_map/ppermute | solution.py:587
  273.8 3.4 fold.3
  277.1 1.7 collective-permute-start.7
  278.9 2.3 copy.40
  281.3 3.3 copy.55
  285.3 11.3 %collective-permute-done.4.refs_15_ = bf16[4,4,176,128]{3,2,1,0:T(8,128)(2,1)} collective-permute-done((bf16[4,4,176,128]{3,2,1,0:T(8,128)(2,1)}, bf16[4,4,176,128]{3,2,1,0:T(8,128)(2,1)}, u32[]{:S(2)}, u32[]{:S(2)}) %collective-permute-start.4) | collective-permute-done | bytes 720928 | tf_op jit(solution)/shard_map/ppermute | solution.py:587
  296.6 6.8 %collective-permute-done.6.refs_17_ = bf16[4,4,176,128]{3,2,1,0:T(8,128)(2,1)} collective-permute-done((bf16[4,4,176,128]{3,2,1,0:T(8,128)(2,1)}, bf16[4,4,176,128]{3,2,1,0:T(8,128)(2,1)}, u32[]{:S(2)}, u32[]{:S(2)}) %collective-permute-start.6) | collective-permute-done | bytes 720928 | tf_op jit(solution)/shard_map/ppermute | solution.py:587
  303.4 11.2 %all-to-all-done.4.refs_4_ = bf16[8,2,3,256,128]{4,3,2,1,0:T(8,128)(2,1)S(1)} async-done(((bf16[8,2,3,256,128]{4,3,2,1,0:T(8,128)(2,1)}), bf16[8,2,3,256,128]{4,3,2,1,0:T(8,128)(2,1)S(1)}, u32[]{:S(2)}, u32[]{:S(2)}) %all-to-all-start.4) | async-done | bytes 3145760 | tf_op jit(solution)/shard_map/all_to_all | solution.py:295
  316.3 58.9 %tail.1 = (f32[4,176,128]{2,1,0:T(8,128)}, f32[4,176,128]{2,1,0:T(8,128)}, f32[4,176,128]{2,1,0:T(8,128)}, f32[4,64,128]{2,1,0:T(8,128)}, f32[256,128]{1,0:T(8,1...) custom-call(f32[512,128]{1,0:T(8,128)} %get-tuple-element.131.cos_re, ...), custom_call_target="tpu_custom_call" | custom-call | flops 99999997952 | bytes 100000000 | tf_op jit(solution)/shard_map/tail/pallas_call | solution.py:972
  377.7 4.7 %copy.54 = f32[2,256,1024]{2,0,1:T(2,128)} copy(f32[2,256,1024]{2,1,0:T(8,128)} %bitcast.66) | data formatting | bytes 4194304 | tf_op jit(solution)/shard_map/reshape | solution.py:1099
  382.4 2.9 copy.53
  (70 shorter events, 19.4 us)
Async XLA Ops:
  0.6 3.6 copy-start.3
  60.2 3.7 copy-start.16
  60.2 40.4 %all-to-all-start = ((bf16[8,3,256,128]{3,2,1,0:T(8,128)(2,1)}), bf16[8,3,256,128]{3,2,1,0:T(8,128)(2,1)S(1)}, u32[]{:S(2)}, u32[]{:S(2)}) async-start(bf16[8,3,256,128]{3,2,1,0:T(8,128)(2,1)} %get-tuple-element.70), calls=%async_computation | async-start | bytes 3145728 | tf_op jit(solution)/shard_map/all_to_all | solution.py:295
  100.6 3.6 copy-start.2
  100.6 18.3 %all-to-all-start.3 = ((bf16[8,256,128]{2,1,0:T(8,128)(2,1)}), bf16[8,256,128]{2,1,0:T(8,128)(2,1)S(1)}, u32[]{:S(2)}, u32[]{:S(2)}) async-start(bf16[8,256,128]{2,1,0:T(8,128)(2,1)} %get-tuple-element.73), calls=%async_computation.3 | async-start | bytes 1048576 | tf_op jit(solution)/shard_map/all_to_all | solution.py:295
  104.2 18.6 %copy-start.4 = (bf16[256,2,1024]{2,1,0:T(2,128)(2,1)S(1)}, bf16[256,2,1024]{2,1,0:T(2,128)(2,1)}, u32[]{:S(2)}) copy-start(bf16[256,2,1024]{2,1,0:T(2,128)(2,1)} %param.25) | copy-start | bytes 3145732
  118.9 18.3 %copy-start.5 = (bf16[8,256,128]{2,1,0:T(8,128)(2,1)}, bf16[8,256,128]{2,1,0:T(8,128)(2,1)S(1)}, u32[]{:S(2)}) copy-start(bf16[8,256,128]{2,1,0:T(8,128)(2,1)S(1)} %all-to-all-done.3.refs_1_) | copy-start | bytes 1572868
  118.9 18.3 %all-to-all-start.1 = ((bf16[8,256,128]{2,1,0:T(8,128)(2,1)}), bf16[8,256,128]{2,1,0:T(8,128)(2,1)S(1)}, u32[]{:S(2)}, u32[]{:S(2)}) async-start(bf16[8,256,128]{2,1,0:T(8,128)(2,1)} %get-tuple-element.71), calls=%async_computation.1 | async-start | bytes 1048576 | tf_op jit(solution)/shard_map/all_to_all | solution.py:295
  137.2 0.8 copy-start.6
  205.5 37.1 %collective-permute-start = (bf16[4,8,176,128]{3,2,1,0:T(8,128)(2,1)}, bf16[4,8,176,128]{3,2,1,0:T(8,128)(2,1)}, u32[]{:S(2)}, u32[]{:S(2)}) collective-permute-start(bf16[4,8,176,128]{3,2,1,0:T(8,128)(2,1)} %get-tuple-element.95), channel_id=1, source_target_pairs={{0,16},{8,24},{16,0},{24,8},{1,17},{9,25},{17,1},{25,9},{2,18},{10... | collective-permute-start | bytes 4325384 | tf_op jit(solution)/shard_map/ppermute | solution.py:587
  208.8 33.8 %collective-permute-start.1 = (bf16[4,8,176,128]{3,2,1,0:T(8,128)(2,1)}, bf16[4,8,176,128]{3,2,1,0:T(8,128)(2,1)}, u32[]{:S(2)}, u32[]{:S(2)}) collective-permute-start(bf16[4,8,176,128]{3,2,1,0:T(8,128)(2,1)} %get-tuple-element.97), channel_id=1, source_target_pairs={{0,1},{1,0},{2,3},{3,2},{4,5},{5,4},{6,7},{7,6},{8,9},{9,8},{10,11... | collective-permute-start | bytes 4325384 | tf_op jit(solution)/shard_map/ppermute | solution.py:587
  209.4 33.5 %collective-permute-start.2 = (bf16[4,8,176,128]{3,2,1,0:T(8,128)(2,1)}, bf16[4,8,176,128]{3,2,1,0:T(8,128)(2,1)}, u32[]{:S(2)}, u32[]{:S(2)}) collective-permute-start(bf16[4,8,176,128]{3,2,1,0:T(8,128)(2,1)} %get-tuple-element.99), channel_id=1, source_target_pairs={{0,2},{1,3},{2,0},{3,1},{4,6},{5,7},{6,4},{7,5},{8,10},{9,11},{10,... | collective-permute-start | bytes 4325384 | tf_op jit(solution)/shard_map/ppermute | solution.py:587
  238.1 76.6 %all-to-all-start.4 = ((bf16[8,2,3,256,128]{4,3,2,1,0:T(8,128)(2,1)}), bf16[8,2,3,256,128]{4,3,2,1,0:T(8,128)(2,1)S(1)}, u32[]{:S(2)}, u32[]{:S(2)}) async-start(bf16[8,2,3,256,128]{4,3,2,1,0:T(8,128)(2,1)} %attn_bwd.1), calls=%async_computation.4 | async-start | bytes 6291456 | tf_op jit(solution)/shard_map/all_to_all | solution.py:295
  257.2 15.8 %collective-permute-start.3 = (bf16[4,8,64,128]{3,2,1,0:T(8,128)(2,1)}, bf16[4,8,64,128]{3,2,1,0:T(8,128)(2,1)S(1)}, u32[]{:S(2)}, u32[]{:S(2)}) collective-permute-start(bf16[4,8,64,128]{3,2,1,0:T(8,128)(2,1)} %get-tuple-element.113), channel_id=1, source_target_pairs={{0,16},{8,24},{16,0},{24,8},{1,17},{9,25},{17,1},{25,9},{2,18},{10... | collective-permute-start | bytes 1572872 | tf_op jit(solution)/shard_map/ppermute | solution.py:587
  260.0 36.6 %collective-permute-start.4 = (bf16[4,4,176,128]{3,2,1,0:T(8,128)(2,1)}, bf16[4,4,176,128]{3,2,1,0:T(8,128)(2,1)}, u32[]{:S(2)}, u32[]{:S(2)}) collective-permute-start(bf16[4,4,176,128]{3,2,1,0:T(8,128)(2,1)} %get-tuple-element.101), channel_id=1, source_target_pairs={{0,1},{1,0},{2,3},{3,2},{4,5},{5,4},{6,7},{7,6},{8,9},{9,8},{10,11... | collective-permute-start | bytes 2162696 | tf_op jit(solution)/shard_map/ppermute | solution.py:587
  261.8 34.8 %collective-permute-start.5 = (bf16[4,4,176,128]{3,2,1,0:T(8,128)(2,1)}, bf16[4,4,176,128]{3,2,1,0:T(8,128)(2,1)}, u32[]{:S(2)}, u32[]{:S(2)}) collective-permute-start(bf16[4,4,176,128]{3,2,1,0:T(8,128)(2,1)} %get-tuple-element.103), channel_id=1, source_target_pairs={{0,16},{8,24},{16,0},{24,8},{1,17},{9,25},{17,1},{25,9},{2,18},{10... | collective-permute-start | bytes 2162696 | tf_op jit(solution)/shard_map/ppermute | solution.py:587
  261.9 41.5 %collective-permute-start.6 = (bf16[4,4,176,128]{3,2,1,0:T(8,128)(2,1)}, bf16[4,4,176,128]{3,2,1,0:T(8,128)(2,1)}, u32[]{:S(2)}, u32[]{:S(2)}) collective-permute-start(bf16[4,4,176,128]{3,2,1,0:T(8,128)(2,1)} %get-tuple-element.105), channel_id=1, source_target_pairs={{0,16},{8,24},{16,0},{24,8},{1,17},{9,25},{17,1},{25,9},{2,18},{10... | collective-permute-start | bytes 2162696 | tf_op jit(solution)/shard_map/ppermute | solution.py:587
  273.0 0.8 copy-start.17
  273.8 7.4 %copy-start.14 = (f32[4,2,256]{2,1,0:T(2,128)S(1)}, f32[4,2,256]{2,1,0:T(2,128)}, u32[]{:S(2)}) copy-start(f32[4,2,256]{2,1,0:T(2,128)} %get-tuple-element.76) | copy-start | bytes 24580
  277.1 26.2 %collective-permute-start.7 = (bf16[4,4,64,128]{3,2,1,0:T(8,128)(2,1)}, bf16[4,4,64,128]{3,2,1,0:T(8,128)(2,1)S(1)}, u32[]{:S(2)}, u32[]{:S(2)}) collective-permute-start(bf16[4,4,64,128]{3,2,1,0:T(8,128)(2,1)} %get-tuple-element.115), channel_id=1, source_target_pairs={{0,1},{1,0},{2,3},{3,2},{4,5},{5,4},{6,7},{7,6},{8,9},{9,8},{10,11... | collective-permute-start | bytes 786440 | tf_op jit(solution)/shard_map/ppermute | solution.py:587
  278.9 5.7 %copy-start.15 = (f32[1,1024]{1,0:T(1,128)S(1)}, f32[1,1024]{1,0:T(1,128)}, u32[]{:S(2)}) copy-start(f32[1,1024]{1,0:T(1,128)} %get-tuple-element.75) | copy-start | bytes 12292
  303.4 11.3 %copy-start.18 = (bf16[4,4,64,128]{3,2,1,0:T(8,128)(2,1)}, bf16[4,4,64,128]{3,2,1,0:T(8,128)(2,1)S(1)}, u32[]{:S(2)}) copy-start(bf16[4,4,64,128]{3,2,1,0:T(8,128)(2,1)S(1)} %collective-permute-done.7.refs_18_) | copy-start | bytes 786436
  314.6 1.6 copy-start
  377.7 4.7 %copy-start.1 = (f32[512,1024]{1,0:T(8,128)S(1)}, f32[512,1024]{1,0:T(8,128)}, u32[]{:S(2)}) copy-start(f32[512,1024]{1,0:T(8,128)} %get-tuple-element.117) | copy-start | bytes 6291460
  382.4 4.3 %copy-start.9 = (f32[4,176,128]{2,1,0:T(8,128)S(1)}, f32[4,176,128]{2,1,0:T(8,128)}, u32[]{:S(2)}) copy-start(f32[4,176,128]{2,1,0:T(8,128)} %get-tuple-element.122) | copy-start | bytes 1081348
  382.4 5.3 %copy-start.8 = (f32[4,176,128]{2,1,0:T(8,128)S(1)}, f32[4,176,128]{2,1,0:T(8,128)}, u32[]{:S(2)}) copy-start(f32[4,176,128]{2,1,0:T(8,128)} %get-tuple-element.123) | copy-start | bytes 1081348
  385.4 3.3 copy-start.13
  385.4 4.0 %copy-start.12 = (f32[256,128]{1,0:T(8,128)S(1)}, f32[256,128]{1,0:T(8,128)}, u32[]{:S(2)}) copy-start(f32[256,128]{1,0:T(8,128)} %get-tuple-element.152) | copy-start | bytes 393220
  385.4 4.6 %copy-start.11 = (f32[256,128]{1,0:T(8,128)S(1)}, f32[256,128]{1,0:T(8,128)}, u32[]{:S(2)}) copy-start(f32[256,128]{1,0:T(8,128)} %get-tuple-element.153) | copy-start | bytes 393220
  385.4 5.3 %copy-start.10 = (f32[4,64,128]{2,1,0:T(8,128)S(1)}, f32[4,64,128]{2,1,0:T(8,128)}, u32[]{:S(2)}) copy-start(f32[4,64,128]{2,1,0:T(8,128)} %get-tuple-element.121) | copy-start | bytes 393220
  385.4 5.9 %copy-start.7 = (f32[4,176,128]{2,1,0:T(8,128)S(1)}, f32[4,176,128]{2,1,0:T(8,128)}, u32[]{:S(2)}) copy-start(f32[4,176,128]{2,1,0:T(8,128)} %get-tuple-element.124) | copy-start | bytes 1081348

commit v6 on v5

--- a/solution.py
+++ b/solution.py
@@ -595,107 +595,94 @@
     return mine, (other["dp"], other["blk"])
 
 
-def whole_block(pieces, block_rows, block_cols):
-    row_parts, col_parts, size = chunks_of(block_rows, block_cols)
-    shaped = pieces.reshape(row_parts, col_parts, size, 128)
-    return jnp.transpose(shaped, (0, 2, 1, 3)).reshape(block_rows, block_cols)
-
-
-def ffn_kernel(rows, n_blk, *refs):
-    source = iter(refs)
-    take = lambda n: [next(source) for _ in range(n)]
-    gathered = take(rows)
-    hidden_ref, cot_ref, gain_ref, wo_ref, wg_ref, wu_ref, wd_ref = take(7)
-    lowt_ref, mid_ref, inner_ref, dgate_ref, dup_ref, out_ref, dres_ref, dbranch_ref, dgain_ref = take(9)
-    d_attn = take(rows)
-    low_ref, resid_ref, acc_ref, dmid_ref = take(4)
-    length, width = gathered[0].shape[1:]
+def ffn_kernel(gathered_ref, hidden_ref, cot_ref, gain_ref, wo_ref, wg_ref, wu_ref, wd_ref, *refs):
+    out_refs, (low_ref, resid_ref, acc_ref, dmid_ref) = refs[-14:-4], refs[-4:]
+    lowt_ref, mid_ref, inner_ref, dgate_ref, dup_ref, out_ref, dres_ref, dbranch_ref, dgain_ref, dattn_ref = out_refs
+    n_blk, length, width = gathered_ref.shape
     step = pl.program_id(0)
 
     @pl.when(step == 0)
     def _():
-        for r in range(rows):
-            at = pl.ds(r * length, length)
-            for s in range(n_blk):
-                low_ref[at, s * width : (s + 1) * width] = gathered[r][s]
-            resid = hidden_ref[at, :].astype(F32) + dot(low_ref[at, :], wo_ref[...])
-            resid_ref[at, :] = resid
-            normed, _ = rms_parts(resid)
-            mid_ref[at, :] = (normed * gain_ref[...]).astype(BF16)
+        for s in range(n_blk):
+            low_ref[:, s * width : (s + 1) * width] = gathered_ref[s]
+        resid = hidden_ref[...].astype(F32) + dot(low_ref[...], wo_ref[...])
+        resid_ref[...] = resid
+        normed, _ = rms_parts(resid)
+        mid_ref[...] = (normed * gain_ref[...]).astype(BF16)
         acc_ref[...] = jnp.zeros_like(acc_ref)
         dmid_ref[...] = jnp.zeros_like(dmid_ref)
         lowt_ref[...] = low_ref[...].T
 
-    for r in range(rows):
-        at = pl.ds(r * length, length)
-        gate = dot(mid_ref[at, :], wg_ref[...])
-        up = dot(mid_ref[at, :], wu_ref[...])
-        d_inner = dot_nt(cot_ref[at, :], wd_ref[...])
-        sigma = 1.0 / (1.0 + jnp.exp(-gate))
-        act = gate * sigma
-        inner = (act * up).astype(BF16)
-        d_gate = (d_inner * up * (sigma * (1.0 + gate * (1.0 - sigma)))).astype(BF16)
-        d_up = (d_inner * act).astype(BF16)
-        inner_ref[:, at] = inner.T
-        dgate_ref[:, at] = d_gate.T
-        dup_ref[:, at] = d_up.T
-        acc_ref[at, :] += dot(inner, wd_ref[...])
-        dmid_ref[at, :] += dot_nt(d_gate, wg_ref[...]) + dot_nt(d_up, wu_ref[...])
+    gate = dot(mid_ref[...], wg_ref[...])
+    up = dot(mid_ref[...], wu_ref[...])
+    d_inner = dot_nt(cot_ref[...], wd_ref[...])
+    sigma = 1.0 / (1.0 + jnp.exp(-gate))
+    act = gate * sigma
+    inner = (act * up).astype(BF16)
+    d_gate = (d_inner * up * (sigma * (1.0 + gate * (1.0 - sigma)))).astype(BF16)
+    d_up = (d_inner * act).astype(BF16)
+    inner_ref[...] = inner.T
+    dgate_ref[...] = d_gate.T
+    dup_ref[...] = d_up.T
+    acc_ref[...] += dot(inner, wd_ref[...])
+    dmid_ref[...] += dot_nt(d_gate, wg_ref[...]) + dot_nt(d_up, wu_ref[...])
 
     @pl.when(step == pl.num_programs(0) - 1)
     def _():
-        d_gain = jnp.zeros(dgain_ref.shape, F32)
-        for r in range(rows):
-            at = pl.ds(r * length, length)
-            resid = resid_ref[at, :]
-            out_ref[at, :] = (resid + acc_ref[at, :]).astype(BF16)
-            normed, inverse = rms_parts(resid)
-            d_mid = dmid_ref[at, :]
-            d_gain = d_gain + jnp.sum(d_mid * normed, axis=0, keepdims=True)
-            d_resid = cot_ref[at, :].astype(F32) + norm_back(d_mid * gain_ref[...], normed, inverse)
-            dres_ref[at, :] = d_resid
-            d_branch = d_resid.astype(BF16)
-            dbranch_ref[at, :] = d_branch
-            back = dot_nt(d_branch, wo_ref[...]).astype(BF16)
-            for s in range(n_blk):
-                d_attn[r][s] = back[:, s * width : (s + 1) * width]
-        dgain_ref[...] = d_gain
-
-
-def feed_forward(gathered, hidden, cot, gain, w_out, w_gate, w_up, w_down):
-    rows = len(gathered)
-    n_blk, length, width = gathered[0].shape
+        resid = resid_ref[...]
+        out_ref[...] = (resid + acc_ref[...]).astype(BF16)
+        normed, inverse = rms_parts(resid)
+        d_mid = dmid_ref[...]
+        dgain_ref[...] = jnp.sum(d_mid * normed, axis=0, keepdims=True)
+        d_resid = cot_ref[...].astype(F32) + norm_back(d_mid * gain_ref[...], normed, inverse)
+        dres_ref[...] = d_resid
+        d_branch = d_resid.astype(BF16)
+        dbranch_ref[...] = d_branch
+        back = dot_nt(d_branch, wo_ref[...]).astype(BF16)
+        for s in range(n_blk):
+            dattn_ref[s] = back[:, s * width : (s + 1) * width]
+
+
+def feed_forward(row, before, gathered, hidden, cot, gain, w_out, w_gate, w_up, w_down):
+    n_blk, length, width = gathered.shape
     tokens, model = hidden.shape
     inner = w_gate.shape[1]
     chunk = 256
-    full = lambda a: pl.BlockSpec(a.shape, lambda j: (0,) * len(a.shape))
     once = lambda a: pl.BlockSpec(a.shape, lambda j: (0,) * len(a.shape), pipeline_mode=pl.Buffered(1))
+    whole = lambda a: pl.BlockSpec(a.shape, lambda j: (0,) * len(a.shape))
     cols = pl.BlockSpec((model, chunk), lambda j: (0, j))
+    own = pl.BlockSpec((length, model), lambda j: (row, 0), pipeline_mode=pl.Buffered(1))
+    mine = pl.BlockSpec((length, model), lambda j: (row, 0))
+    turned = pl.BlockSpec((chunk, length), lambda j: (j, row))
     shape = jax.ShapeDtypeStruct
-    inner_rows = pl.BlockSpec((chunk, tokens), lambda j: (j, 0))
-    outs = (
+    shared = (
         [shape((model, tokens), BF16), shape((tokens, model), BF16)]
         + [shape((inner, tokens), BF16)] * 3
         + [shape((tokens, model), BF16), shape((tokens, model), F32), shape((tokens, model), BF16)]
-        + [shape((1, model), F32)]
-        + [shape((n_blk, length, width), BF16)] * rows
     )
+    outs = shared + [shape((1, model), F32), shape((n_blk, length, width), BF16)]
+    before = list(before or [])
     return pl.pallas_call(
-        functools.partial(ffn_kernel, rows, n_blk),
+        ffn_kernel,
         grid=(inner // chunk,),
-        in_specs=[once(a) for a in gathered]
-        + [once(hidden), once(cot), once(gain), once(w_out), cols, cols, pl.BlockSpec((chunk, model), lambda j: (j, 0))],
-        out_specs=[full(a) for a in outs[:2]] + [inner_rows] * 3 + [full(a) for a in outs[5:]],
+        in_specs=[once(gathered), own, own, once(gain), once(w_out)]
+        + [cols, cols, pl.BlockSpec((chunk, model), lambda j: (j, 0))]
+        + [pl.BlockSpec(memory_space=pl.ANY)] * len(before),
+        out_specs=[pl.BlockSpec((model, length), lambda j: (0, row)), mine]
+        + [turned] * 3
+        + [mine] * 3
+        + [whole(a) for a in outs[8:]],
         out_shape=outs,
-        scratch_shapes=[pltpu.VMEM((tokens, model), BF16)] + [pltpu.VMEM((tokens, model), F32)] * 3,
+        scratch_shapes=[pltpu.VMEM((length, model), BF16)] + [pltpu.VMEM((length, model), F32)] * 3,
+        input_output_aliases={8 + k: k for k in range(len(before))},
         compiler_params=pltpu.CompilerParams(vmem_limit_bytes=VMEM_LIMIT),
         cost_estimate=pl.CostEstimate(
-            flops=12 * tokens * model * inner + 4 * tokens * model * model,
-            bytes_accessed=6 * model * inner + 6 * tokens * inner + 20 * tokens * model,
-            transcendentals=tokens * inner,
+            flops=12 * length * model * inner + 4 * length * model * model,
+            bytes_accessed=6 * model * inner + 6 * length * inner + 20 * length * model,
+            transcendentals=length * inner,
         ),
         name="ffn",
-    )(*gathered, hidden, cot, gain, w_out, w_gate, w_up, w_down)
+    )(gathered, hidden, cot, gain, w_out, w_gate, w_up, w_down, *before)
 
 
 class Halving:
@@ -738,6 +725,16 @@
     def result(self, c):
         stage = len(self.order) - 1
         return self.work[c, self.base(stage + 1)].astype(F32) + self.landed[stage][c, 0].astype(F32)
+
+
+def store_piece(out_ref, c, piece):
+    size = piece.shape[0]
+    if out_ref.shape[1] == 128:
+        out_ref[c * size : (c + 1) * size, :] = piece
+    else:
+        cols = out_ref.shape[0] // 128
+        row, col = c // cols, c % cols
+        out_ref[col * 128 : (col + 1) * 128, row * size : (row + 1) * size] = piece.T
 
 
 def tail_kernel(ffn_orders, qkv_orders, n_dp, n_blk, *refs):
@@ -799,7 +796,7 @@
                 stream.add(stage - 1, c)
                 stream.remote(stage, c).start()
             else:
-                ffn_outs[k][c] = stream.result(c)
+                store_piece(ffn_outs[k], c, stream.result(c))
 
     def projections(which):
         for r in range(rows):
@@ -811,7 +808,7 @@
                     turned = values * cos_ref[at, :] - swap_halves(values) * sin_ref[at, :]
                 else:
                     turned = 0.5 * values
-                    first_ref[at, cols] = turned
+                    first_ref[:, r, cols] = turned
                 low_ref[which, at, cols] = turned.astype(BF16)
         for fresh in range(2):
             side = 1 - core if fresh == 0 else core
@@ -869,7 +866,7 @@
             normed, inverse = rms_parts(hidden_ref[at, :].astype(F32))
             d_normed = acc_ref[at, :]
             d_gain = d_gain + jnp.sum(d_normed * normed, axis=0, keepdims=True)
-            input_ref[at, :] = dres_ref[at, :] + norm_back(d_normed * gain_ref[...], normed, inverse)
+            input_ref[:, r, :] = dres_ref[at, :] + norm_back(d_normed * gain_ref[...], normed, inverse)
         vecs[0, :, :model] = d_gain
         vecs[0, :, model:] = small_ref[...]
         vec_copy(0).start()
@@ -930,9 +927,10 @@
         vec_copy(e).wait_send()
 
 
-def tail(ffn_pairs, ffn_orders, qkv_orders, back, normed_t, hidden, d_resid, weights, cos, sin, gain, small, collective_id):
+def tail(ffn_pairs, ffn_blocks, ffn_orders, qkv_orders, back, normed_t, hidden, d_resid, weights, cos, sin, gain, small, collective_id):
     n_dp, n_blk = lax.axis_size("dp"), lax.axis_size("blk")
     tokens, model = hidden.shape
+    rows, length = back.shape[1], back.shape[3]
     keeps, gots = [pair[0] for pair in ffn_pairs], [pair[1] for pair in ffn_pairs]
     loads = [back, normed_t.reshape(n_dp, model // n_dp, tokens), hidden, d_resid, *weights]
     ffn_stages, qkv_stages, n_qkv = len(ffn_orders[0]), len(qkv_orders[0]), 3
@@ -942,9 +940,9 @@
     shape = jax.ShapeDtypeStruct
     vec = (1, model + small.shape[1])
     outs = (
-        [shape(a.shape[:1] + a.shape[2:], F32) for a in keeps]
+        [shape(a, F32) for a in ffn_blocks]
         + [shape(block, F32)] * n_qkv
-        + [shape((tokens, model), F32)] * 2
+        + [shape((length, rows, model), F32)] * 2
         + [shape(vec, F32)]
     )
     scratch = [pltpu.VMEM(a.shape, a.dtype) for a in loads]
@@ -1114,9 +1112,15 @@
         attended.append(o_f)
         lse.append(lse_r)
         gathered.append(exchange(o_low))
-    attn_low_t, normed_mid, inner_t, d_gate_t, d_up_t, block_out, d_resid_mid, d_branch, d_gain_two, *d_attn = feed_forward(
-        gathered, hidden, cot, row_gain(ffn_gain), w_out, w_gate, w_up, w_down
-    )
+    shared, d_gains, d_attn = None, [], []
+    for r in range(rows):
+        *shared, d_gain, d_attn_r = feed_forward(
+            r, shared, gathered[r], hidden, cot, row_gain(ffn_gain), w_out, w_gate, w_up, w_down
+        )
+        d_gains.append(d_gain)
+        d_attn.append(d_attn_r)
+    attn_low_t, normed_mid, inner_t, d_gate_t, d_up_t, block_out, d_resid_mid, d_branch = shared
+    d_gain_two = sum(d_gains)
 
     inner = w_gate.shape[1]
     by_blocks = (model // n_dp) % 128 == 0 and width == 128 and (inner // n_blk) % 32 == 0
@@ -1158,6 +1162,7 @@
     if by_blocks:
         *blocks, grad_first, grad_input, small = tail(
             ffn_pairs,
+            ((model // n_dp, inner // n_blk),) * 2 + ((inner // n_dp, model // n_blk), (model // n_dp, model // n_blk)),
             tuple(order[2:] for order in orders),
             (early, late),
             back,
@@ -1172,10 +1177,7 @@
             0,
         )
         small = small.reshape(-1)
-        grad_gate = whole_block(blocks[0], inner // n_blk, model // n_dp).T
-        grad_up = whole_block(blocks[1], inner // n_blk, model // n_dp).T
-        grad_down = blocks[2].reshape(inner // n_dp, model // n_blk)
-        grad_project = blocks[3].reshape(model // n_dp, model // n_blk)
+        grad_gate, grad_up, grad_down, grad_project = blocks[:4]
         grad_query, grad_key, grad_value = blocks[4:]
     else:
         low, grad_first = turn_back(back, cos, sin)
@@ -1186,13 +1188,15 @@
         grad_up = sent(d_up_t.T, mid_cf, "blk", True).T
         grad_project = sent(d_branch, core_first(attn_low_t.T), "blk", True).T
         grad_query, grad_key, grad_value = [sent(low[k], in_cf, "blk", True).T for k in range(3)]
+        grad_first = unflat(grad_first)
         grad_input, d_gain_one = input_grad(hidden, d_resid_mid, row_gain(attn_gain), low, w_query, w_key, w_value)
+        grad_input = unflat(grad_input)
         small = total(jnp.concatenate([d_gain_one.reshape(model), small.reshape(-1)]))
     n_entries = n_blk * length * rows * n_dp * model
     return (
         unflat(block_out),
-        unflat(grad_input),
-        unflat(grad_first),
+        grad_input,
+        grad_first,
         grad_query,
         grad_key,
         grad_value,

time: 398 us -> 394 us (0.990)
  Pallas kernels: 206 us -> 225 us
  waiting for transfers between devices: 77.5 us -> 59.2 us
    all_to_all x4, waiting for transfers between devices: 49.9 us -> 28.1 us  [exchange(): return lax.all_to_all(values, 'blk', 0, 0, tiled=True)]
    pallas_call x1 -> x2, Pallas kernels: 32.8 us -> 42.5 us  [feed_forward(): pl.pallas_call(ffn_kernel, grid=(inner // chunk,), in_specs=[once(gathere...]
    reshape x3 -> x1, local copies, waits for them, and re-layouts: 10.9 us -> 2.05 us  [body(): unflat = lambda a: jnp.transpose(a.reshape(rows, length, model), (1, 0, 2))]
    unnamed x46 -> x54, local copies, waits for them, and re-layouts: 8.14 us -> 15.5 us
    pallas_call x1, Pallas kernels: 28.1 us -> 32.9 us  [attn_bwd(): pl.pallas_call(functools.partial(attn_bwd_kernel, rows, n_docs, heads), g...]
    ppermute x8, starting transfers between devices: 12.9 us -> 8.67 us  [swap(): return lax.ppermute(values, name, [(k, k ^ 1 << bit) for k in range(size)])]
  transfers between devices with their start and end apart: 12 -> 12, of which waited for: 8 -> 6; matrix products, arithmetic and copies ran while one was open for 2% -> 2% of each run, Pallas kernels for 18% -> 26%
where the time goes in v6:
time: 394 us; the launch traced here: 391 us
  Pallas kernels  225 us (57%)
  waiting for transfers between devices  59.2 us (15%)
  blocking collectives  44.4 us (11%)
  local copies, waits for them, and re-layouts  27.8 us (7%)
  starting transfers between devices  26.5 us (7%)
  between operations  4.44 us (1%)
    pallas_call x1, Pallas kernels, tail(): pl.pallas_call(functools.partial(tail_kernel, ffn_orders, qkv_orders, n_d...  58.5 us
    all_to_all x1, blocking collectives, exchange(): return lax.all_to_all(values, 'blk', 0, 0, tiled=True)  44.4 us
    pallas_call x2, Pallas kernels, ffn_wgrad(): pl.pallas_call(functools.partial(ffn_wgrad_kernel, plans, n_dp, n_blk, le...  44.1 us
    pallas_call x2, Pallas kernels, feed_forward(): pl.pallas_call(ffn_kernel, grid=(inner // chunk,), in_specs=[once(gathere...  42.5 us
    pallas_call x1, Pallas kernels, attn_bwd(): pl.pallas_call(functools.partial(attn_bwd_kernel, rows, n_docs, heads), g...  32.9 us
    ppermute x8, waiting for transfers between devices, swap(): return lax.ppermute(values, name, [(k, k ^ 1 << bit) for k in range(size)])  31.1 us
    pallas_call x2, Pallas kernels, attn_fwd(): pl.pallas_call(functools.partial(attn_fwd_kernel, row, n_docs, heads), gr...  28.9 us
    all_to_all x4, waiting for transfers between devices, exchange(): return lax.all_to_all(values, 'blk', 0, 0, tiled=True)  28.1 us
  transfers between devices with their start and end apart: 12, of which 6 were waited for; matrix products, arithmetic and copies ran while one was open for 2% of the time, Pallas kernels for 26%

profile of v6, /device:TPU:0, one launch (start us, length us, event | category | flops | bytes accessed | tf_op | source)
XLA Modules:
  0.0 390.5 jit_solution(14426986270472118360)
XLA Ops:
  1.7 2.5 copy.42
  5.5 1.8 fusion
  7.3 8.5 %qkv.1 = (bf16[8,3,256,128]{3,2,1,0:T(8,128)(2,1)}, bf16[8,3,256,128]{3,2,1,0:T(8,128)(2,1)}, bf16[512,1024]{1,0:T(8,128)(2,1)}, f32[4,2,256]{2,1,0:T(2,128)}) custom-call(bf16[512,1024]{1,0:T(8,128)(2,1)} %bitcast.32, bf16[512,1024]{1,0:T(8,128)(2,1)} %bitcast.44, f32[512,128]{1,0:T(8,128)} %get-tuple-element.177.cos_ref.refs_0_, ...), custom_call_target="tpu_custom_call" | custom-call | flops 3221225472 | bytes 11534336 | tf_op jit(solution)/shard_map/qkv/pallas_call | solution.py:83
  15.8 44.4 %all_to_all.25.qkv_ref.refs_0_ = bf16[8,3,256,128]{3,2,1,0:T(8,128)(2,1)} all-to-all(bf16[8,3,256,128]{3,2,1,0:T(8,128)(2,1)} %get-tuple-element.81), channel_id=1, replica_groups=mesh['dp'=4,'blk'=8] {'blk'}, dimensions={0} | all-to-all | bytes 3145728 | tf_op jit(solution)/shard_map/all_to_all | solution.py:295
  60.2 3.7 all-to-all-start
  65.8 14.4 %attn_fwd.3 = (f32[8,256,128]{2,1,0:T(8,128)}, bf16[8,256,128]{2,1,0:T(8,128)(2,1)}, f32[8,2,256]{2,1,0:T(2,128)}) custom-call(s32[16]{0:T(128)} %reshape.130.lens_ref, bf16[8,3,256,128]{3,2,1,0:T(8,128)(2,1)} %all_to_all.25.qkv_ref.refs_0_), custom_call_target="tpu_custom_call" | custom-call | flops 10000000000 | bytes 3000000 | tf_op jit(solution)/shard_map/attn_fwd/pallas_call | solution.py:185
  80.2 20.4 %all-to-all-done.qkv_ref.refs_4_ = bf16[8,3,256,128]{3,2,1,0:T(8,128)(2,1)S(1)} async-done(((bf16[8,3,256,128]{3,2,1,0:T(8,128)(2,1)}), bf16[8,3,256,128]{3,2,1,0:T(8,128)(2,1)S(1)}, u32[]{:S(2)}, u32[]{:S(2)}) %all-to-all-start) | async-done | bytes 1572896 | tf_op jit(solution)/shard_map/all_to_all | solution.py:295
  100.6 3.6 all-to-all-start.3
  104.2 14.4 %attn_fwd.2 = (f32[8,256,128]{2,1,0:T(8,128)}, bf16[8,256,128]{2,1,0:T(8,128)(2,1)}, f32[8,2,256]{2,1,0:T(2,128)}) custom-call(s32[16]{0:T(128)} %reshape.130.lens_ref, bf16[8,3,256,128]{3,2,1,0:T(8,128)(2,1)} %copy-done.3), custom_call_target="tpu_custom_call" | custom-call | flops 10000000000 | bytes 3000000 | tf_op jit(solution)/shard_map/attn_fwd/pallas_call | solution.py:185
  118.9 5.8 %all-to-all-start.1 = ((bf16[8,256,128]{2,1,0:T(8,128)(2,1)}), bf16[8,256,128]{2,1,0:T(8,128)(2,1)S(1)}, u32[]{:S(2)}, u32[]{:S(2)}) async-start(bf16[8,256,128]{2,1,0:T(8,128)(2,1)} %get-tuple-element.80), calls=%async_computation.1 | async-start | bytes 1048576 | tf_op jit(solution)/shard_map/all_to_all | solution.py:295
  124.7 21.3 %ffn.2 = (bf16[1024,512]{1,0:T(8,128)(2,1)}, bf16[512,1024]{1,0:T(8,128)(2,1)}, bf16[2816,512]{1,0:T(8,128)(2,1)}, bf16[2816,512]{1,0:T(8,128)(2,1)}, bf16[2816,...) custom-call(bf16[8,256,128]{2,1,0:T(8,128)(2,1)} %copy-done.9, ...), custom_call_target="tpu_custom_call" | custom-call | flops 9932111872 | bytes 26869760 | tf_op jit(solution)/shard_map/ffn/pallas_call | solution.py:665
  146.8 21.3 %ffn.3 = (bf16[1024,512]{1,0:T(8,128)(2,1)}, bf16[512,1024]{1,0:T(8,128)(2,1)}, bf16[2816,512]{1,0:T(8,128)(2,1)}, bf16[2816,512]{1,0:T(8,128)(2,1)}, bf16[2816,...) custom-call(bf16[8,256,128]{2,1,0:T(8,128)(2,1)} %copy-done.1, ...), custom_call_target="tpu_custom_call", output_to_operand_aliasing={{0}: (8, {}), {1}: (9, {}), {2}: (10, {}), {3}: (11, {}), {... | custom-call | flops 9932111872 | bytes 26869760 | tf_op jit(solution)/shard_map/ffn/pallas_call | solution.py:665
  168.0 37.3 %ffn_wgrad.2 = (bf16[4,8,176,128]{3,2,1,0:T(8,128)(2,1)}, bf16[4,8,176,128]{3,2,1,0:T(8,128)(2,1)}, bf16[4,8,176,128]{3,2,1,0:T(8,128)(2,1)}, bf16[4,8,176,128]{...) custom-call(bf16[8,2,176,512]{3,2,1,0:T(8,128)(2,1)} %bitcast.27, ...), custom_call_target="tpu_custom_call" | custom-call | flops 1000000000 | bytes 10000000 | tf_op jit(solution)/shard_map/ffn_wgrad/pallas_call | solution.py:532
  205.3 1.5 collective-permute-start
  208.0 32.9 %attn_bwd.1 = bf16[8,2,3,256,128]{4,3,2,1,0:T(8,128)(2,1)} custom-call(s32[16]{0:T(128)} %reshape.130.lens_ref, bf16[8,3,256,128]{3,2,1,0:T(8,128)(2,1)} %all_to_all.25.qkv_ref.refs_0_, bf16[8,256,128]{2,1,0:T(8,128)(2,1)} %get-tuple-element.101.refs_1_, f32[8,256,128]{2,1,0:T(8,128)} %get-tuple-element.102.refs_2_, ...), custom_call_target="tpu_custom_call" | custom-call | flops 4000000000 | bytes 12000000 | tf_op jit(solution)/shard_map/attn_bwd/pallas_call | solution.py:275
  241.0 4.7 %all-to-all-start.4 = ((bf16[8,2,3,256,128]{4,3,2,1,0:T(8,128)(2,1)}), bf16[8,2,3,256,128]{4,3,2,1,0:T(8,128)(2,1)}, u32[]{:S(2)}, u32[]{:S(2)}) async-start(bf16[8,2,3,256,128]{4,3,2,1,0:T(8,128)(2,1)} %attn_bwd.1), calls=%async_computation.4 | async-start | bytes 6291456 | tf_op jit(solution)/shard_map/all_to_all | solution.py:295
  247.3 6.3 %fold.2 = (bf16[4,4,176,128]{3,2,1,0:T(8,128)(2,1)}, bf16[4,4,176,128]{3,2,1,0:T(8,128)(2,1)}, bf16[4,4,176,128]{3,2,1,0:T(8,128)(2,1)}, bf16[4,4,176,128]{3,2,1...) custom-call(bf16[4,8,176,128]{3,2,1,0:T(8,128)(2,1)} %get-tuple-element.112.refs_0_, ...), custom_call_target="tpu_custom_call" | custom-call | flops 1000000000 | bytes 10000000 | tf_op jit(solution)/shard_map/fold/pallas_call | solution.py:572
  253.6 6.8 %ffn_wgrad.3 = (bf16[4,8,64,128]{3,2,1,0:T(8,128)(2,1)}, bf16[4,8,64,128]{3,2,1,0:T(8,128)(2,1)}) custom-call(bf16[4,4,64,512]{3,2,1,0:T(8,128)(2,1)} %bitcast.37, bf16[512,1024]{1,0:T(8,128)(2,1)} %get-tuple-element.129.refs_1_), custom_call_target="tpu_custom_call" | custom-call | flops 99999997952 | bytes 10000000 | tf_op jit(solution)/shard_map/ffn_wgrad/pallas_call | solution.py:532
  261.1 1.7 collective-permute-start.4
  262.7 1.4 collective-permute-start.5
  264.8 10.7 %collective-permute-done.3.refs_1_ = bf16[4,8,64,128]{3,2,1,0:T(8,128)(2,1)S(1)} collective-permute-done((bf16[4,8,64,128]{3,2,1,0:T(8,128)(2,1)}, bf16[4,8,64,128]{3,2,1,0:T(8,128)(2,1)S(1)}, u32[]{:S(2)}, u32[]{:S(2)}) %collective-permute-start.3) | collective-permute-done | bytes 524320 | tf_op jit(solution)/shard_map/ppermute | solution.py:587
  276.2 3.5 fold.3
  279.7 1.7 collective-permute-start.7
  282.8 2.0 copy.51
  285.6 10.6 %collective-permute-done.4.refs_15_ = bf16[4,4,176,128]{3,2,1,0:T(8,128)(2,1)S(1)} collective-permute-done((bf16[4,4,176,128]{3,2,1,0:T(8,128)(2,1)}, bf16[4,4,176,128]{3,2,1,0:T(8,128)(2,1)S(1)}, u32[]{:S(2)}, u32[]{:S(2)}) %collective-permute-start.4) | collective-permute-done | bytes 720928 | tf_op jit(solution)/shard_map/ppermute | solution.py:587
  296.2 9.9 %collective-permute-done.6.refs_17_ = bf16[4,4,176,128]{3,2,1,0:T(8,128)(2,1)} collective-permute-done((bf16[4,4,176,128]{3,2,1,0:T(8,128)(2,1)}, bf16[4,4,176,128]{3,2,1,0:T(8,128)(2,1)}, u32[]{:S(2)}, u32[]{:S(2)}) %collective-permute-start.6) | collective-permute-done | bytes 720928 | tf_op jit(solution)/shard_map/ppermute | solution.py:587
  306.0 7.5 %all-to-all-done.4.refs_4_ = bf16[8,2,3,256,128]{4,3,2,1,0:T(8,128)(2,1)} async-done(((bf16[8,2,3,256,128]{4,3,2,1,0:T(8,128)(2,1)}), bf16[8,2,3,256,128]{4,3,2,1,0:T(8,128)(2,1)}, u32[]{:S(2)}, u32[]{:S(2)}) %all-to-all-start.4) | async-done | bytes 3145760 | tf_op jit(solution)/shard_map/all_to_all | solution.py:295
  313.6 58.5 %tail.1 = (f32[256,352]{1,0:T(8,128)}, f32[256,352]{1,0:T(8,128)}, f32[704,128]{1,0:T(8,128)}, f32[256,128]{1,0:T(8,128)}, f32[256,128]{1,0:T(8,128)}, /*index=5...) custom-call(f32[512,128]{1,0:T(8,128)} %get-tuple-element.177.cos_re, ...), custom_call_target="tpu_custom_call" | custom-call | flops 99999997952 | bytes 100000000 | tf_op jit(solution)/shard_map/tail/pallas_call | solution.py:970
  376.0 1.9 copy.47
  377.9 1.9 copy.48
  379.7 3.8 copy.67
  383.6 1.3 copy.68
  (76 shorter events, 18.1 us)
Async XLA Ops:
  0.6 3.6 copy-start.6
  60.2 3.7 copy-start.18
  60.2 4.3 %copy-start.7 = (bf16[256,2,1024]{2,1,0:T(2,128)(2,1)S(1)}, bf16[256,2,1024]{2,1,0:T(2,128)(2,1)}, u32[]{:S(2)}) copy-start(bf16[256,2,1024]{2,1,0:T(2,128)(2,1)} %param.25) | copy-start | bytes 3145732
  60.2 40.4 %all-to-all-start = ((bf16[8,3,256,128]{3,2,1,0:T(8,128)(2,1)}), bf16[8,3,256,128]{3,2,1,0:T(8,128)(2,1)S(1)}, u32[]{:S(2)}, u32[]{:S(2)}) async-start(bf16[8,3,256,128]{3,2,1,0:T(8,128)(2,1)} %get-tuple-element.79), calls=%async_computation | async-start | bytes 3145728 | tf_op jit(solution)/shard_map/all_to_all | solution.py:295
  100.6 3.6 copy-start.3
  100.6 18.3 %all-to-all-start.3 = ((bf16[8,256,128]{2,1,0:T(8,128)(2,1)}), bf16[8,256,128]{2,1,0:T(8,128)(2,1)S(1)}, u32[]{:S(2)}, u32[]{:S(2)}) async-start(bf16[8,256,128]{2,1,0:T(8,128)(2,1)} %get-tuple-element.82), calls=%async_computation.3 | async-start | bytes 1048576 | tf_op jit(solution)/shard_map/all_to_all | solution.py:295
  118.9 5.8 %copy-start.9 = (bf16[8,256,128]{2,1,0:T(8,128)(2,1)}, bf16[8,256,128]{2,1,0:T(8,128)(2,1)S(1)}, u32[]{:S(2)}) copy-start(bf16[8,256,128]{2,1,0:T(8,128)(2,1)S(1)} %all-to-all-done.3.gathered_ref) | copy-start | bytes 1572868
  118.9 27.1 %all-to-all-start.1 = ((bf16[8,256,128]{2,1,0:T(8,128)(2,1)}), bf16[8,256,128]{2,1,0:T(8,128)(2,1)S(1)}, u32[]{:S(2)}, u32[]{:S(2)}) async-start(bf16[8,256,128]{2,1,0:T(8,128)(2,1)} %get-tuple-element.80), calls=%async_computation.1 | async-start | bytes 1048576 | tf_op jit(solution)/shard_map/all_to_all | solution.py:295
  205.3 40.3 %collective-permute-start = (bf16[4,8,176,128]{3,2,1,0:T(8,128)(2,1)}, bf16[4,8,176,128]{3,2,1,0:T(8,128)(2,1)S(1)}, u32[]{:S(2)}, u32[]{:S(2)}) collective-permute-start(bf16[4,8,176,128]{3,2,1,0:T(8,128)(2,1)} %get-tuple-element.113), channel_id=1, source_target_pairs={{0,16},{8,24},{16,0},{24,8},{1,17},{9,25},{17,1},{25,9},{2,18},{10... | collective-permute-start | bytes 4325384 | tf_op jit(solution)/shard_map/ppermute | solution.py:587
  206.9 38.8 %collective-permute-start.1 = (bf16[4,8,176,128]{3,2,1,0:T(8,128)(2,1)}, bf16[4,8,176,128]{3,2,1,0:T(8,128)(2,1)S(1)}, u32[]{:S(2)}, u32[]{:S(2)}) collective-permute-start(bf16[4,8,176,128]{3,2,1,0:T(8,128)(2,1)} %get-tuple-element.115), channel_id=1, source_target_pairs={{0,1},{1,0},{2,3},{3,2},{4,5},{5,4},{6,7},{7,6},{8,9},{9,8},{10,11... | collective-permute-start | bytes 4325384 | tf_op jit(solution)/shard_map/ppermute | solution.py:587
  207.5 38.2 %collective-permute-start.2 = (bf16[4,8,176,128]{3,2,1,0:T(8,128)(2,1)}, bf16[4,8,176,128]{3,2,1,0:T(8,128)(2,1)}, u32[]{:S(2)}, u32[]{:S(2)}) collective-permute-start(bf16[4,8,176,128]{3,2,1,0:T(8,128)(2,1)} %get-tuple-element.117), channel_id=1, source_target_pairs={{0,2},{1,3},{2,0},{3,1},{4,6},{5,7},{6,4},{7,5},{8,10},{9,11},{10,... | collective-permute-start | bytes 4325384 | tf_op jit(solution)/shard_map/ppermute | solution.py:587
  241.0 72.6 %all-to-all-start.4 = ((bf16[8,2,3,256,128]{4,3,2,1,0:T(8,128)(2,1)}), bf16[8,2,3,256,128]{4,3,2,1,0:T(8,128)(2,1)}, u32[]{:S(2)}, u32[]{:S(2)}) async-start(bf16[8,2,3,256,128]{4,3,2,1,0:T(8,128)(2,1)} %attn_bwd.1), calls=%async_computation.4 | async-start | bytes 6291456 | tf_op jit(solution)/shard_map/all_to_all | solution.py:295
  245.6 1.1 copy-start.4
  245.7 1.7 copy-start.5
  260.4 21.0 %copy-start.8 = (bf16[512,1024]{1,0:T(8,128)(2,1)S(1)}, bf16[512,1024]{1,0:T(8,128)(2,1)}, u32[]{:S(2)}) copy-start(bf16[512,1024]{1,0:T(8,128)(2,1)} %get-tuple-element.107) | copy-start | bytes 3145732
  260.4 15.0 %collective-permute-start.3 = (bf16[4,8,64,128]{3,2,1,0:T(8,128)(2,1)}, bf16[4,8,64,128]{3,2,1,0:T(8,128)(2,1)S(1)}, u32[]{:S(2)}, u32[]{:S(2)}) collective-permute-start(bf16[4,8,64,128]{3,2,1,0:T(8,128)(2,1)} %get-tuple-element.131), channel_id=1, source_target_pairs={{0,16},{8,24},{16,0},{24,8},{1,17},{9,25},{17,1},{25,9},{2,18},{10... | collective-permute-start | bytes 1572872 | tf_op jit(solution)/shard_map/ppermute | solution.py:587
  261.1 35.1 %collective-permute-start.4 = (bf16[4,4,176,128]{3,2,1,0:T(8,128)(2,1)}, bf16[4,4,176,128]{3,2,1,0:T(8,128)(2,1)S(1)}, u32[]{:S(2)}, u32[]{:S(2)}) collective-permute-start(bf16[4,4,176,128]{3,2,1,0:T(8,128)(2,1)} %get-tuple-element.119), channel_id=1, source_target_pairs={{0,1},{1,0},{2,3},{3,2},{4,5},{5,4},{6,7},{7,6},{8,9},{9,8},{10,11... | collective-permute-start | bytes 2162696 | tf_op jit(solution)/shard_map/ppermute | solution.py:587
  262.7 33.4 %collective-permute-start.5 = (bf16[4,4,176,128]{3,2,1,0:T(8,128)(2,1)}, bf16[4,4,176,128]{3,2,1,0:T(8,128)(2,1)S(1)}, u32[]{:S(2)}, u32[]{:S(2)}) collective-permute-start(bf16[4,4,176,128]{3,2,1,0:T(8,128)(2,1)} %get-tuple-element.121), channel_id=1, source_target_pairs={{0,16},{8,24},{16,0},{24,8},{1,17},{9,25},{17,1},{25,9},{2,18},{10... | collective-permute-start | bytes 2162696 | tf_op jit(solution)/shard_map/ppermute | solution.py:587
  264.2 41.8 %collective-permute-start.6 = (bf16[4,4,176,128]{3,2,1,0:T(8,128)(2,1)}, bf16[4,4,176,128]{3,2,1,0:T(8,128)(2,1)}, u32[]{:S(2)}, u32[]{:S(2)}) collective-permute-start(bf16[4,4,176,128]{3,2,1,0:T(8,128)(2,1)} %get-tuple-element.123), channel_id=1, source_target_pairs={{0,16},{8,24},{16,0},{24,8},{1,17},{9,25},{17,1},{25,9},{2,18},{10... | collective-permute-start | bytes 2162696 | tf_op jit(solution)/shard_map/ppermute | solution.py:587
  276.2 6.5 %copy-start.15 = (f32[4,2,256]{2,1,0:T(2,128)S(1)}, f32[4,2,256]{2,1,0:T(2,128)}, u32[]{:S(2)}) copy-start(f32[4,2,256]{2,1,0:T(2,128)} %get-tuple-element.94) | copy-start | bytes 24580
  276.2 6.6 %copy-start = (bf16[512,1024]{1,0:T(8,128)(2,1)S(1)}, bf16[512,1024]{1,0:T(8,128)(2,1)}, u32[]{:S(2)}) copy-start(bf16[512,1024]{1,0:T(8,128)(2,1)} %get-tuple-element.91) | copy-start | bytes 3145732
  279.7 26.3 %collective-permute-start.7 = (bf16[4,4,64,128]{3,2,1,0:T(8,128)(2,1)}, bf16[4,4,64,128]{3,2,1,0:T(8,128)(2,1)}, u32[]{:S(2)}, u32[]{:S(2)}) collective-permute-start(bf16[4,4,64,128]{3,2,1,0:T(8,128)(2,1)} %get-tuple-element.133), channel_id=1, source_target_pairs={{0,1},{1,0},{2,3},{3,2},{4,5},{5,4},{6,7},{7,6},{8,9},{9,8},{10,11... | collective-permute-start | bytes 786440 | tf_op jit(solution)/shard_map/ppermute | solution.py:587
  281.4 3.5 copy-start.16
  281.4 3.5 copy-start.17
  296.2 17.4 %copy-start.19 = (bf16[4,4,176,128]{3,2,1,0:T(8,128)(2,1)}, bf16[4,4,176,128]{3,2,1,0:T(8,128)(2,1)S(1)}, u32[]{:S(2)}) copy-start(bf16[4,4,176,128]{3,2,1,0:T(8,128)(2,1)S(1)} %collective-permute-done.4.refs_15_) | copy-start | bytes 2162692
  296.2 17.4 %copy-start.20 = (bf16[4,4,176,128]{3,2,1,0:T(8,128)(2,1)}, bf16[4,4,176,128]{3,2,1,0:T(8,128)(2,1)S(1)}, u32[]{:S(2)}) copy-start(bf16[4,4,176,128]{3,2,1,0:T(8,128)(2,1)S(1)} %collective-permute-done.5.refs_16_) | copy-start | bytes 2162692
  379.7 3.8 copy-start.2
  383.5 1.4 copy-start.14
  383.5 2.0 copy-start.13
  383.5 2.7 copy-start.12
  383.5 3.3 copy-start.11
  383.5 4.0 %copy-start.10 = (f32[704,128]{1,0:T(8,128)S(1)}, f32[704,128]{1,0:T(8,128)}, u32[]{:S(2)}) copy-start(f32[704,128]{1,0:T(8,128)} %get-tuple-element.203) | copy-start | bytes 1081348
  (2 other events, 1.6 us)

commit v7 on v6

--- a/solution.py
+++ b/solution.py
@@ -14,6 +14,7 @@
 F32 = jnp.float32
 BF16 = jnp.bfloat16
 VMEM_LIMIT = 56 * 2**20
+LAST_FLOPS = 6 * 10**10
 MESH = pl.DeviceIdType.MESH
 
 
@@ -202,13 +203,13 @@
     )(lens, qkv)
 
 
-def attn_bwd_kernel(rows, n_docs, heads, lens_ref, *refs):
+def attn_bwd_kernel(rows, first_row, n_docs, heads, lens_ref, *refs):
     scratch = refs[4 * rows :]
     for row in range(rows):
 
         @pl.when(pl.program_id(0) == row)
         def _():
-            attn_bwd_row(row, n_docs, heads, lens_ref, *refs[4 * row : 4 * row + 4], *scratch)
+            attn_bwd_row(first_row + row, n_docs, heads, lens_ref, *refs[4 * row : 4 * row + 4], *scratch)
 
 
 def attn_bwd_row(row, n_docs, heads, lens_ref, qkv_ref, do_ref, o_ref, lse_ref, out_ref, dq_ref, delta_ref):
@@ -266,14 +267,14 @@
     out_ref[0, 0, 2] = d_value.astype(BF16)
 
 
-def attn_bwd(lens, qkv, d_out, attended, lse, n_docs):
+def attn_bwd(lens, qkv, d_out, attended, lse, first_row, n_docs):
     rows = len(qkv)
     n_blk, _, length, width = qkv[0].shape
     heads = width // HEAD_DIM
     whole = lambda a: pl.BlockSpec(a.shape, lambda r, j, lens: (0,) * a.ndim)
     arrays = [a for per_row in zip(qkv, d_out, attended, lse) for a in per_row]
     return pl.pallas_call(
-        functools.partial(attn_bwd_kernel, rows, n_docs, heads),
+        functools.partial(attn_bwd_kernel, rows, first_row, n_docs, heads),
         grid_spec=pltpu.PrefetchScalarGridSpec(
             num_scalar_prefetch=1,
             grid=(rows, n_blk),
@@ -728,53 +729,56 @@
 
 
 def store_piece(out_ref, c, piece):
-    size = piece.shape[0]
-    if out_ref.shape[1] == 128:
-        out_ref[c * size : (c + 1) * size, :] = piece
-    else:
-        cols = out_ref.shape[0] // 128
-        row, col = c // cols, c % cols
-        out_ref[col * 128 : (col + 1) * 128, row * size : (row + 1) * size] = piece.T
-
-
-def tail_kernel(ffn_orders, qkv_orders, n_dp, n_blk, *refs):
+    size, cols = piece.shape[0], out_ref.shape[1] // 128
+    row, col = c // cols, c % cols
+    out_ref[row * size : (row + 1) * size, col * 128 : (col + 1) * 128] = piece
+
+
+def tail_kernel(ffn_orders, own_order, qkv_orders, n_dp, n_blk, rows, *refs):
     source = iter(refs)
     take = lambda n: [next(source) for _ in range(n)]
     n_ffn, n_qkv = len(ffn_orders), 3
     ffn_stages, qkv_stages = len(ffn_orders[0]), len(qkv_orders[0])
     cos_ref, sin_ref, gain_ref, small_ref = take(4)
-    loads = take(7)
+    loads = take(6 + rows)
     keeps, gots = take(n_ffn), take(n_ffn)
-    ffn_outs, qkv_outs = take(n_ffn), take(n_qkv)
+    own_keep, own_sent = take(2)
+    ffn_outs, (own_out,), qkv_outs = take(n_ffn), take(1), take(n_qkv)
     first_ref, input_ref, total_ref = take(3)
-    back_ref, turned_ref, hidden_ref, dres_ref, *weights = here = take(7)
+    here = take(6 + rows)
+    back_refs, (turned_ref, hidden_ref, dres_ref, *weights) = here[:rows], here[rows:]
     low_ref, acc_ref, vecs, vec_landed = take(4)
     load_sem, keep_sem, got_sem, vec_send, vec_recv = take(5)
     streams = []
     for k, order in enumerate(ffn_orders):
         work, *landed = take(1 + ffn_stages)
         streams.append(Halving(order, work, None, landed, *take(2)))
+    work, *landed = take(1 + len(own_order))
+    own = Halving(own_order, work, own_sent, landed, *take(2))
+    (own_sem,) = take(1)
+    own_copy = pltpu.make_async_copy(own_keep, own.work, own_sem)
     late = []
     for u in range(n_qkv):
         late.append([])
         for order in qkv_orders:
             work, sent, *landed = take(2 + qkv_stages)
             late[u].append(Halving(order, work, sent, landed, *take(2)))
-    _, rows, _, length, width = back_ref.shape
+    length, width = back_refs[0].shape[3:]
     core, _ = partner("dp", 0)
     counts = [a.shape[0] for a in keeps]
 
     load = [pltpu.make_async_copy(a, b, load_sem.at[k]) for k, (a, b) in enumerate(zip(loads, here))]
     keep_copy = lambda k, c: pltpu.make_async_copy(keeps[k].at[c], streams[k].work.at[c], keep_sem.at[k, c])
     got_copy = lambda k, c: pltpu.make_async_copy(gots[k].at[c], streams[k].landed[0].at[c], got_sem.at[k, c])
-    load[0].start()
-    load[1].start()
+    for copy in load[: rows + 1]:
+        copy.start()
     for c in range(max(counts)):
         for k in range(n_ffn):
             if c < counts[k]:
                 keep_copy(k, c).start()
                 got_copy(k, c).start()
-    for copy in load[2:]:
+    own_copy.start()
+    for copy in load[rows + 1 :]:
         copy.start()
 
     everyone = qkv_orders[0]
@@ -803,7 +807,7 @@
             at = pl.ds(r * length, length)
             for s in range(n_blk):
                 cols = slice(s * width, (s + 1) * width)
-                values = back_ref[s, r, which].astype(F32)
+                values = back_refs[r][s, 0, which].astype(F32)
                 if which < 2:
                     turned = values * cos_ref[at, :] - swap_halves(values) * sin_ref[at, :]
                 else:
@@ -825,6 +829,17 @@
                 if fresh == 0:
                     stream.remote(0, 0).start()
 
+    def own_step(stage):
+        if stage == 1:
+            own_copy.wait()
+        for c in range(own.work.shape[0]):
+            own.remote(stage - 1, c).wait_recv()
+            if stage < len(own.order):
+                own.add(stage - 1, c)
+                own.remote(stage, c).start()
+            else:
+                store_piece(own_out, c, own.result(c))
+
     def late_step(which, stage):
         for h, stream in enumerate(late[which]):
             stream.remote(stage - 1, 0).wait_recv()
@@ -849,8 +864,8 @@
     n_vec = len(everyone)
 
     def matmul():
-        for k in range(2, 7):
-            load[k].wait()
+        for copy in load[rows + 1 :]:
+            copy.wait()
         for r in range(rows):
             at = pl.ds(r * length, length)
             acc_ref[at, :] = (
@@ -881,25 +896,31 @@
             vec_copy(e + 1).start()
 
     chunks = range(max(counts))
+    for c in range(own.work.shape[0]):
+        own.remote(0, c).start()
     for c in chunks:
         ffn(c, 1)
-    load[0].wait()
-    load[1].wait()
+    for copy in load[: rows + 1]:
+        copy.wait()
     projections(2)
     projections(1)
     late_step(2, 1)
+    own_step(1)
     projections(0)
     late_step(1, 1)
     ffn(0, 2)
     late_step(0, 1)
     matmul()
+    own_step(2)
     late_step(2, 2)
     ffn(1, 2)
     norm()
+    own_step(3)
     late_step(1, 2)
     ffn(2, 2)
     vecs_left = list(range(n_vec))
     vec(vecs_left.pop(0))
+    own_step(4)
     late_step(2, 3)
     late_step(0, 2)
     ffn(3, 2)
@@ -920,6 +941,9 @@
         for c in range(count):
             for stage in range(1, ffn_stages):
                 stream.remote(stage, c).wait_send()
+    for c in range(own.work.shape[0]):
+        for stage in range(len(own.order)):
+            own.remote(stage, c).wait_send()
     for stream in late[0] + late[1] + late[2]:
         for stage in range(qkv_stages):
             stream.remote(stage, 0).wait_send()
@@ -927,12 +951,12 @@
         vec_copy(e).wait_send()
 
 
-def tail(ffn_pairs, ffn_blocks, ffn_orders, qkv_orders, back, normed_t, hidden, d_resid, weights, cos, sin, gain, small, collective_id):
+def tail(ffn_pairs, ffn_blocks, ffn_orders, own_pair, own_order, qkv_orders, backs, normed_t, hidden, d_resid, weights, cos, sin, gain, small, collective_id):
     n_dp, n_blk = lax.axis_size("dp"), lax.axis_size("blk")
     tokens, model = hidden.shape
-    rows, length = back.shape[1], back.shape[3]
+    rows, length = len(backs), backs[0].shape[3]
     keeps, gots = [pair[0] for pair in ffn_pairs], [pair[1] for pair in ffn_pairs]
-    loads = [back, normed_t.reshape(n_dp, model // n_dp, tokens), hidden, d_resid, *weights]
+    loads = [*backs, normed_t.reshape(n_dp, model // n_dp, tokens), hidden, d_resid, *weights]
     ffn_stages, qkv_stages, n_qkv = len(ffn_orders[0]), len(qkv_orders[0]), 3
     n_chunks = max(a.shape[0] for a in keeps)
     block = (model // n_dp, model // n_blk)
@@ -962,14 +986,18 @@
         scratch += [pltpu.VMEM((a.shape[0], a.shape[1] >> stage) + a.shape[2:], BF16) for stage in range(ffn_stages)]
         scratch += [pltpu.SemaphoreType.DMA((ffn_stages, a.shape[0]))] * 2
     part = (block[0] // len(qkv_orders), block[1])
+    keep = own_pair[0]
+    scratch.append(pltpu.VMEM(keep.shape, BF16))
+    scratch += [pltpu.VMEM((keep.shape[0], keep.shape[1] >> stage) + keep.shape[2:], BF16) for stage in range(len(own_order))]
+    scratch += [pltpu.SemaphoreType.DMA((len(own_order), keep.shape[0]))] * 2 + [pltpu.SemaphoreType.DMA]
     for _ in range(n_qkv * len(qkv_orders)):
         scratch += [pltpu.VMEM((1, held) + part, BF16)] * 2
         scratch += [pltpu.VMEM((1, held >> stage) + part, BF16) for stage in range(qkv_stages)]
         scratch += [pltpu.SemaphoreType.DMA((qkv_stages, 1))] * 2
     vmem, anywhere = pl.BlockSpec(memory_space=pltpu.VMEM), pl.BlockSpec(memory_space=pl.ANY)
     return pl.pallas_call(
-        functools.partial(tail_kernel, ffn_orders, qkv_orders, n_dp, n_blk),
-        in_specs=[vmem] * 4 + [anywhere] * (len(loads) + 2 * len(keeps)),
+        functools.partial(tail_kernel, ffn_orders, own_order, qkv_orders, n_dp, n_blk, rows),
+        in_specs=[vmem] * 4 + [anywhere] * (len(loads) + 2 * len(keeps) + 2),
         out_specs=[vmem] * len(outs),
         out_shape=outs,
         scratch_shapes=scratch,
@@ -978,7 +1006,7 @@
         ),
         cost_estimate=pl.CostEstimate(flops=10**11, bytes_accessed=10**8, transcendentals=0),
         name="tail",
-    )(cos, sin, gain, small, *loads, *keeps, *gots)
+    )(cos, sin, gain, small, *loads, *keeps, *gots, *own_pair)
 
 
 def turn_back_kernel(cos_ref, sin_ref, back_ref, low_ref, first_ref):
@@ -1140,8 +1168,11 @@
             1,
         )
         ffn_pairs = exchanged(folded, [order[1] for order in orders])
-        back_own = attn_bwd(lens, qkv, d_own, attended, lse, n_docs)
-        back = exchange(back_own)
+        back_own = [
+            attn_bwd(lens, qkv[r : r + 1], d_own[r : r + 1], attended[r : r + 1], lse[r : r + 1], r, n_docs)
+            for r in range(rows)
+        ]
+        backs = [exchange(b) for b in back_own[:-1]]
         kept = [keep for keep, got in ffn_pairs]
         token, kept = lax.optimization_barrier((back_own, kept))
         second = [order[2] for order in orders]
@@ -1149,23 +1180,25 @@
         ffn_pairs = exchanged(folded, second)
         folded, attn_low_t = lax.optimization_barrier((folded, attn_low_t))
         ffn_pairs = [(keep, got) for (keep, _), (_, got) in zip(folded, ffn_pairs)]
-        project, _ = ffn_wgrad(((early, pieces, [(True, attn_low_t, d_branch)]),), [], 10**11, 2)
-        project = exchanged(project, [early[1]])
-        ffn_pairs += exchanged(fold(project, [early[2]], 10**9), [early[2]])
-        orders += (early,)
+        project, back_last = ffn_wgrad(
+            ((early, pieces, [(True, attn_low_t, d_branch)]),), back_own[-1:], LAST_FLOPS, 2
+        )
+        backs += back_last
     else:
         d_own = [exchange(d_attn[r]) for r in range(rows)]
-        back = exchange(attn_bwd(lens, qkv, d_own, attended, lse, n_docs))
+        back = exchange(attn_bwd(lens, qkv, d_own, attended, lse, 0, n_docs))
 
     squares = jnp.sum(sums, axis=(0, 2)).reshape(1, 2)
     small = jnp.concatenate([d_gain_two, squares, jnp.zeros((1, 126), F32)], axis=1)
     if by_blocks:
         *blocks, grad_first, grad_input, small = tail(
             ffn_pairs,
-            ((model // n_dp, inner // n_blk),) * 2 + ((inner // n_dp, model // n_blk), (model // n_dp, model // n_blk)),
+            ((inner // n_blk, model // n_dp),) * 2 + ((inner // n_dp, model // n_blk), (model // n_dp, model // n_blk)),
             tuple(order[2:] for order in orders),
+            project[0],
+            early[1:],
             (early, late),
-            back,
+            backs,
             normed_in.T,
             hidden,
             d_resid_mid,
@@ -1177,7 +1210,8 @@
             0,
         )
         small = small.reshape(-1)
-        grad_gate, grad_up, grad_down, grad_project = blocks[:4]
+        grad_gate, grad_up = blocks[0].T, blocks[1].T
+        grad_down, grad_project = blocks[2:4]
         grad_query, grad_key, grad_value = blocks[4:]
     else:
         low, grad_first = turn_back(back, cos, sin)

time: 394 us -> 385 us (0.977)
  waiting for transfers between devices: 59.2 us -> 22.5 us
  Pallas kernels: 225 us -> 260 us
  starting transfers between devices: 26.5 us -> 21.6 us
    ppermute x8 -> x6, waiting for transfers between devices: 31.1 us -> 0.02 us  [swap(): return lax.ppermute(values, name, [(k, k ^ 1 << bit) for k in range(size)])]
    pallas_call x2, Pallas kernels: 44.1 us -> 73.5 us  [ffn_wgrad(): pl.pallas_call(functools.partial(ffn_wgrad_kernel, plans, n_dp, n_blk, le...]
    pallas_call x2 -> x3, Pallas kernels: 91.4 us -> 102 us  [the longest x1 69.5 us: tail(): pl.pallas_call(functools.partial(tail_kernel, ffn_orders, own_order, qkv_...]
    all_to_all x4, waiting for transfers between devices: 28.1 us -> 22.5 us  [exchange(): return lax.all_to_all(values, 'blk', 0, 0, tiled=True)]
    pallas_call x2 -> x1, Pallas kernels: 9.79 us -> 6.31 us  [fold(): pl.pallas_call(functools.partial(fold_kernel, stages), grid=(arrays[0].sh...]
    ppermute x8 -> x6, starting transfers between devices: 8.67 us -> 6.64 us  [swap(): return lax.ppermute(values, name, [(k, k ^ 1 << bit) for k in range(size)])]
  transfers between devices with their start and end apart: 12 -> 10, of which waited for: 6 -> 2; matrix products, arithmetic and copies ran while one was open for 2% -> 2% of each run, Pallas kernels for 26% -> 32%
where the time goes in v7:
time: 385 us; the launch traced here: 382 us
  Pallas kernels  260 us (68%)
  blocking collectives  44.4 us (12%)
  local copies, waits for them, and re-layouts  26.5 us (7%)
  waiting for transfers between devices  22.5 us (6%)
  starting transfers between devices  21.6 us (6%)
  between operations  4.5 us (1%)
    pallas_call x2, Pallas kernels, ffn_wgrad(): pl.pallas_call(functools.partial(ffn_wgrad_kernel, plans, n_dp, n_blk, le...  73.5 us
    pallas_call x1, Pallas kernels, tail(): pl.pallas_call(functools.partial(tail_kernel, ffn_orders, own_order, qkv_...  69.5 us
    all_to_all x1, blocking collectives, exchange(): return lax.all_to_all(values, 'blk', 0, 0, tiled=True)  44.4 us
    pallas_call x2, Pallas kernels, feed_forward(): pl.pallas_call(ffn_kernel, grid=(inner // chunk,), in_specs=[once(gathere...  42.5 us
    pallas_call x2, Pallas kernels, attn_bwd(): pl.pallas_call(functools.partial(attn_bwd_kernel, rows, first_row, n_docs...  32.6 us
    pallas_call x2, Pallas kernels, attn_fwd(): pl.pallas_call(functools.partial(attn_fwd_kernel, row, n_docs, heads), gr...  26.9 us
    all_to_all x4, waiting for transfers between devices, exchange(): return lax.all_to_all(values, 'blk', 0, 0, tiled=True)  22.5 us
    all_to_all x4, starting transfers between devices, exchange(): return lax.all_to_all(values, 'blk', 0, 0, tiled=True)  15 us
  transfers between devices with their start and end apart: 10, of which 2 were waited for; matrix products, arithmetic and copies ran while one was open for 2% of the time, Pallas kernels for 32%

profile of v7, /device:TPU:0, one launch (start us, length us, event | category | flops | bytes accessed | tf_op | source)
XLA Modules:
  0.0 382.5 jit_solution(211050236248700692)
XLA Ops:
  1.7 2.5 copy.40
  4.2 1.2 copy.41
  5.5 1.8 fusion
  7.3 8.5 %qkv.1 = (bf16[8,3,256,128]{3,2,1,0:T(8,128)(2,1)}, bf16[8,3,256,128]{3,2,1,0:T(8,128)(2,1)}, bf16[512,1024]{1,0:T(8,128)(2,1)}, f32[4,2,256]{2,1,0:T(2,128)}) custom-call(bf16[512,1024]{1,0:T(8,128)(2,1)} %bitcast.34, bf16[512,1024]{1,0:T(8,128)(2,1)} %bitcast.46, f32[512,128]{1,0:T(8,128)} %get-tuple-element.147.cos_ref.refs_0_, ...), custom_call_target="tpu_custom_call" | custom-call | flops 3221225472 | bytes 11534336 | tf_op jit(solution)/shard_map/qkv/pallas_call | solution.py:84
  15.8 44.4 %all_to_all.25.qkv_ref.refs_0_ = bf16[8,3,256,128]{3,2,1,0:T(8,128)(2,1)} all-to-all(bf16[8,3,256,128]{3,2,1,0:T(8,128)(2,1)} %get-tuple-element.80), channel_id=1, replica_groups=mesh['dp'=4,'blk'=8] {'blk'}, dimensions={0} | all-to-all | bytes 3145728 | tf_op jit(solution)/shard_map/all_to_all | solution.py:296
  60.2 3.7 all-to-all-start
  64.5 1.2 copy.42
  65.8 14.5 %attn_fwd.3 = (f32[8,256,128]{2,1,0:T(8,128)}, bf16[8,256,128]{2,1,0:T(8,128)(2,1)}, f32[8,2,256]{2,1,0:T(2,128)}) custom-call(s32[16]{0:T(128)} %reshape.130.lens_ref, bf16[8,3,256,128]{3,2,1,0:T(8,128)(2,1)} %all_to_all.25.qkv_ref.refs_0_), custom_call_target="tpu_custom_call" | custom-call | flops 10000000000 | bytes 3000000 | tf_op jit(solution)/shard_map/attn_fwd/pallas_call | solution.py:186
  80.2 20.3 %all-to-all-done.qkv_ref.refs_0_ = bf16[8,3,256,128]{3,2,1,0:T(8,128)(2,1)S(1)} async-done(((bf16[8,3,256,128]{3,2,1,0:T(8,128)(2,1)}), bf16[8,3,256,128]{3,2,1,0:T(8,128)(2,1)S(1)}, u32[]{:S(2)}, u32[]{:S(2)}) %all-to-all-start) | async-done | bytes 1572896 | tf_op jit(solution)/shard_map/all_to_all | solution.py:296
  100.6 3.6 all-to-all-start.3
  104.2 12.5 %attn_fwd.2 = (f32[8,256,128]{2,1,0:T(8,128)}, bf16[8,256,128]{2,1,0:T(8,128)(2,1)}, f32[8,2,256]{2,1,0:T(2,128)}) custom-call(s32[16]{0:T(128)} %reshape.130.lens_ref, bf16[8,3,256,128]{3,2,1,0:T(8,128)(2,1)} %copy-done.3), custom_call_target="tpu_custom_call" | custom-call | flops 10000000000 | bytes 3000000 | tf_op jit(solution)/shard_map/attn_fwd/pallas_call | solution.py:186
  116.7 2.2 all-to-all-done.3.gathered_ref
  118.9 3.8 %all-to-all-start.1 = ((bf16[8,256,128]{2,1,0:T(8,128)(2,1)}), bf16[8,256,128]{2,1,0:T(8,128)(2,1)S(1)}, u32[]{:S(2)}, u32[]{:S(2)}) async-start(bf16[8,256,128]{2,1,0:T(8,128)(2,1)} %get-tuple-element.79), calls=%async_computation.1 | async-start | bytes 1048576 | tf_op jit(solution)/shard_map/all_to_all | solution.py:296
  122.7 21.3 %ffn.2 = (bf16[1024,512]{1,0:T(8,128)(2,1)}, bf16[512,1024]{1,0:T(8,128)(2,1)}, bf16[2816,512]{1,0:T(8,128)(2,1)}, bf16[2816,512]{1,0:T(8,128)(2,1)}, bf16[2816,...) custom-call(bf16[8,256,128]{2,1,0:T(8,128)(2,1)} %copy-done.8, ...), custom_call_target="tpu_custom_call" | custom-call | flops 9932111872 | bytes 26869760 | tf_op jit(solution)/shard_map/ffn/pallas_call | solution.py:666
  144.8 21.3 %ffn.3 = (bf16[1024,512]{1,0:T(8,128)(2,1)}, bf16[512,1024]{1,0:T(8,128)(2,1)}, bf16[2816,512]{1,0:T(8,128)(2,1)}, bf16[2816,512]{1,0:T(8,128)(2,1)}, bf16[2816,...) custom-call(bf16[8,256,128]{2,1,0:T(8,128)(2,1)} %copy-done.1, ...), custom_call_target="tpu_custom_call", output_to_operand_aliasing={{0}: (8, {}), {1}: (9, {}), {2}: (10, {}), {3}: (11, {}), {... | custom-call | flops 9932111872 | bytes 26869760 | tf_op jit(solution)/shard_map/ffn/pallas_call | solution.py:666
  166.1 37.4 %ffn_wgrad.2 = (bf16[4,8,176,128]{3,2,1,0:T(8,128)(2,1)}, bf16[4,8,176,128]{3,2,1,0:T(8,128)(2,1)}, bf16[4,8,176,128]{3,2,1,0:T(8,128)(2,1)}, bf16[4,8,176,128]{...) custom-call(bf16[8,2,176,512]{3,2,1,0:T(8,128)(2,1)} %bitcast.29, ...), custom_call_target="tpu_custom_call" | custom-call | flops 1000000000 | bytes 10000000 | tf_op jit(solution)/shard_map/ffn_wgrad/pallas_call | solution.py:533
  203.5 1.6 collective-permute-start
  206.2 2.3 copy.44
  208.6 2.0 copy.47
  210.7 17.5 %attn_bwd.2 = bf16[8,1,3,256,128]{4,3,2,1,0:T(8,128)(2,1)} custom-call(s32[16]{0:T(128)} %reshape.130.lens_ref, bf16[8,3,256,128]{3,2,1,0:T(8,128)(2,1)} %all_to_all.25.qkv_ref.refs_0_, bf16[8,256,128]{2,1,0:T(8,128)(2,1)} %get-tuple-element.100.refs_1_, f32[8,256,128]{2,1,0:T(8,128)} %get-tuple-element.101.refs_2_, f32[8,2,256]{2,1,0:T(2,128)} %get-tuple-element.102.refs_3_), custom_call_target="tpu_custom_call" | custom-call | flops 4000000000 | bytes 12000000 | tf_op jit(solution)/shard_map/attn_bwd/pallas_call | solution.py:276
  228.1 3.8 all-to-all-start.4
  231.9 15.2 %attn_bwd.3.refs_2_ = bf16[8,1,3,256,128]{4,3,2,1,0:T(8,128)(2,1)} custom-call(s32[16]{0:T(128)} %reshape.130.lens_ref, bf16[8,3,256,128]{3,2,1,0:T(8,128)(2,1)} %copy-done.3, bf16[8,256,128]{2,1,0:T(8,128)(2,1)} %get-tuple-element.103.refs_1_, f32[8,256,128]{2,1,0:T(8,128)} %get-tuple-element.104.refs_2_, f32[8,2,256]{2,1,0:T(2,128)} %get-tuple-element.105.refs_3_), custom_call_target="tpu_custom_call" | custom-call | flops 4000000000 | bytes 12000000 | tf_op jit(solution)/shard_map/attn_bwd/pallas_call | solution.py:276
  247.8 1.1 copy-done.5
  248.9 6.3 %fold.1 = (bf16[4,4,176,128]{3,2,1,0:T(8,128)(2,1)}, bf16[4,4,176,128]{3,2,1,0:T(8,128)(2,1)}, bf16[4,4,176,128]{3,2,1,0:T(8,128)(2,1)}, bf16[4,4,176,128]{3,2,1...) custom-call(bf16[4,8,176,128]{3,2,1,0:T(8,128)(2,1)} %get-tuple-element.109.refs_0_, ...), custom_call_target="tpu_custom_call" | custom-call | flops 1000000000 | bytes 10000000 | tf_op jit(solution)/shard_map/fold/pallas_call | solution.py:573
  255.2 1.9 collective-permute-start.3
  257.6 1.5 collective-permute-start.5
  259.1 36.1 %ffn_wgrad.3 = (bf16[4,8,64,128]{3,2,1,0:T(8,128)(2,1)}, bf16[4,8,64,128]{3,2,1,0:T(8,128)(2,1)}, bf16[8,1,3,256,128]{4,3,2,1,0:T(8,128)(2,1)}) custom-call(bf16[4,4,64,512]{3,2,1,0:T(8,128)(2,1)} %bitcast.39, bf16[512,1024]{1,0:T(8,128)(2,1)} %get-tuple-element.123.refs_1_, bf16[8,1,3,256,128]{4,3,2,1,0:T(8,128)(2,1)} %attn_bwd.3.refs_2_), custom_call_target="tpu_custom_call" | custom-call | flops 60000002048 | bytes 10000000 | tf_op jit(solution)/shard_map/ffn_wgrad/pallas_call | solution.py:533
  296.9 69.5 %tail.1 = (f32[352,256]{1,0:T(8,128)}, f32[352,256]{1,0:T(8,128)}, f32[704,128]{1,0:T(8,128)}, f32[256,128]{1,0:T(8,128)}, f32[256,128]{1,0:T(8,128)}, /*index=5...) custom-call(f32[512,128]{1,0:T(8,128)} %get-tuple-element.147.cos_re, ...), custom_call_target="tpu_custom_call" | custom-call | flops 99999997952 | bytes 100000000 | tf_op jit(solution)/shard_map/tail/pallas_call | solution.py:998
  366.4 1.3 fusion.5
  367.6 1.3 fusion.6
  370.2 3.8 copy.65
  374.0 1.3 copy.66
  (72 shorter events, 11.4 us)
Async XLA Ops:
  0.6 3.6 copy-start.6
  60.2 3.7 copy-start.19
  60.2 4.3 %copy-start.7 = (bf16[256,2,1024]{2,1,0:T(2,128)(2,1)S(1)}, bf16[256,2,1024]{2,1,0:T(2,128)(2,1)}, u32[]{:S(2)}) copy-start(bf16[256,2,1024]{2,1,0:T(2,128)(2,1)} %param.25) | copy-start | bytes 3145732
  60.2 40.4 %all-to-all-start = ((bf16[8,3,256,128]{3,2,1,0:T(8,128)(2,1)}), bf16[8,3,256,128]{3,2,1,0:T(8,128)(2,1)S(1)}, u32[]{:S(2)}, u32[]{:S(2)}) async-start(bf16[8,3,256,128]{3,2,1,0:T(8,128)(2,1)} %get-tuple-element.78), calls=%async_computation | async-start | bytes 3145728 | tf_op jit(solution)/shard_map/all_to_all | solution.py:296
  100.6 3.6 copy-start.3
  100.6 18.3 %all-to-all-start.3 = ((bf16[8,256,128]{2,1,0:T(8,128)(2,1)}), bf16[8,256,128]{2,1,0:T(8,128)(2,1)S(1)}, u32[]{:S(2)}, u32[]{:S(2)}) async-start(bf16[8,256,128]{2,1,0:T(8,128)(2,1)} %get-tuple-element.81), calls=%async_computation.3 | async-start | bytes 1048576 | tf_op jit(solution)/shard_map/all_to_all | solution.py:296
  118.9 3.9 %copy-start.8 = (bf16[8,256,128]{2,1,0:T(8,128)(2,1)}, bf16[8,256,128]{2,1,0:T(8,128)(2,1)S(1)}, u32[]{:S(2)}) copy-start(bf16[8,256,128]{2,1,0:T(8,128)(2,1)S(1)} %all-to-all-done.3.gathered_ref) | copy-start | bytes 1572868
  118.9 25.1 %all-to-all-start.1 = ((bf16[8,256,128]{2,1,0:T(8,128)(2,1)}), bf16[8,256,128]{2,1,0:T(8,128)(2,1)S(1)}, u32[]{:S(2)}, u32[]{:S(2)}) async-start(bf16[8,256,128]{2,1,0:T(8,128)(2,1)} %get-tuple-element.79), calls=%async_computation.1 | async-start | bytes 1048576 | tf_op jit(solution)/shard_map/all_to_all | solution.py:296
  144.0 0.8 copy-start.1
  203.5 5.0 %copy-start.16 = (f32[4,2,256]{2,1,0:T(2,128)S(1)}, f32[4,2,256]{2,1,0:T(2,128)}, u32[]{:S(2)}) copy-start(f32[4,2,256]{2,1,0:T(2,128)} %get-tuple-element.93) | copy-start | bytes 24580
  203.5 5.1 %copy-start = (bf16[512,1024]{1,0:T(8,128)(2,1)S(1)}, bf16[512,1024]{1,0:T(8,128)(2,1)}, u32[]{:S(2)}) copy-start(bf16[512,1024]{1,0:T(8,128)(2,1)} %get-tuple-element.90) | copy-start | bytes 3145732
  203.5 44.3 %collective-permute-start = (bf16[4,8,176,128]{3,2,1,0:T(8,128)(2,1)}, bf16[4,8,176,128]{3,2,1,0:T(8,128)(2,1)S(1)}, u32[]{:S(2)}, u32[]{:S(2)}) collective-permute-start(bf16[4,8,176,128]{3,2,1,0:T(8,128)(2,1)} %get-tuple-element.110), channel_id=1, source_target_pairs={{0,16},{8,24},{16,0},{24,8},{1,17},{9,25},{17,1},{25,9},{2,18},{10... | collective-permute-start | bytes 4325384 | tf_op jit(solution)/shard_map/ppermute | solution.py:588
  205.1 42.7 %collective-permute-start.1 = (bf16[4,8,176,128]{3,2,1,0:T(8,128)(2,1)}, bf16[4,8,176,128]{3,2,1,0:T(8,128)(2,1)}, u32[]{:S(2)}, u32[]{:S(2)}) collective-permute-start(bf16[4,8,176,128]{3,2,1,0:T(8,128)(2,1)} %get-tuple-element.112), channel_id=1, source_target_pairs={{0,1},{1,0},{2,3},{3,2},{4,5},{5,4},{6,7},{7,6},{8,9},{9,8},{10,11... | collective-permute-start | bytes 4325384 | tf_op jit(solution)/shard_map/ppermute | solution.py:588
  205.6 42.2 %collective-permute-start.2 = (bf16[4,8,176,128]{3,2,1,0:T(8,128)(2,1)}, bf16[4,8,176,128]{3,2,1,0:T(8,128)(2,1)}, u32[]{:S(2)}, u32[]{:S(2)}) collective-permute-start(bf16[4,8,176,128]{3,2,1,0:T(8,128)(2,1)} %get-tuple-element.114), channel_id=1, source_target_pairs={{0,2},{1,3},{2,0},{3,1},{4,6},{5,7},{6,4},{7,5},{8,10},{9,11},{10,... | collective-permute-start | bytes 4325384 | tf_op jit(solution)/shard_map/ppermute | solution.py:588
  228.1 67.2 %all-to-all-start.4 = ((bf16[8,1,3,256,128]{4,3,2,1,0:T(8,128)(2,1)}), bf16[8,1,3,256,128]{4,3,2,1,0:T(8,128)(2,1)S(1)}, u32[]{:S(2)}, u32[]{:S(2)}) async-start(bf16[8,1,3,256,128]{4,3,2,1,0:T(8,128)(2,1)} %attn_bwd.2), calls=%async_computation.4 | async-start | bytes 3145728 | tf_op jit(solution)/shard_map/all_to_all | solution.py:296
  231.9 15.2 %copy-start.17 = (f32[1,1024]{1,0:T(1,128)S(1)}, f32[1,1024]{1,0:T(1,128)}, u32[]{:S(2)}) copy-start(f32[1,1024]{1,0:T(1,128)} %get-tuple-element.91) | copy-start | bytes 12292
  231.9 15.2 %copy-start.18 = (f32[1,1024]{1,0:T(1,128)S(1)}, f32[1,1024]{1,0:T(1,128)}, u32[]{:S(2)}) copy-start(f32[1,1024]{1,0:T(1,128)} %get-tuple-element.92) | copy-start | bytes 12292
  247.8 1.1 copy-start.5
  255.2 40.0 %collective-permute-start.3 = (bf16[4,4,176,128]{3,2,1,0:T(8,128)(2,1)}, bf16[4,4,176,128]{3,2,1,0:T(8,128)(2,1)S(1)}, u32[]{:S(2)}, u32[]{:S(2)}) collective-permute-start(bf16[4,4,176,128]{3,2,1,0:T(8,128)(2,1)} %get-tuple-element.116), channel_id=1, source_target_pairs={{0,1},{1,0},{2,3},{3,2},{4,5},{5,4},{6,7},{7,6},{8,9},{9,8},{10,11... | collective-permute-start | bytes 2162696 | tf_op jit(solution)/shard_map/ppermute | solution.py:588
  257.1 38.2 %collective-permute-start.4 = (bf16[4,4,176,128]{3,2,1,0:T(8,128)(2,1)}, bf16[4,4,176,128]{3,2,1,0:T(8,128)(2,1)S(1)}, u32[]{:S(2)}, u32[]{:S(2)}) collective-permute-start(bf16[4,4,176,128]{3,2,1,0:T(8,128)(2,1)} %get-tuple-element.118), channel_id=1, source_target_pairs={{0,16},{8,24},{16,0},{24,8},{1,17},{9,25},{17,1},{25,9},{2,18},{10... | collective-permute-start | bytes 2162696 | tf_op jit(solution)/shard_map/ppermute | solution.py:588
  257.6 37.7 %collective-permute-start.5 = (bf16[4,4,176,128]{3,2,1,0:T(8,128)(2,1)}, bf16[4,4,176,128]{3,2,1,0:T(8,128)(2,1)}, u32[]{:S(2)}, u32[]{:S(2)}) collective-permute-start(bf16[4,4,176,128]{3,2,1,0:T(8,128)(2,1)} %get-tuple-element.120), channel_id=1, source_target_pairs={{0,16},{8,24},{16,0},{24,8},{1,17},{9,25},{17,1},{25,9},{2,18},{10... | collective-permute-start | bytes 2162696 | tf_op jit(solution)/shard_map/ppermute | solution.py:588
  295.3 0.9 copy-start.20
  295.3 1.1 copy-start.21
  295.3 1.6 copy-start.4
  370.2 3.8 copy-start.2
  374.0 1.4 copy-start.15
  374.0 2.0 copy-start.14
  374.0 2.7 copy-start.13
  374.0 3.3 copy-start.12
  374.0 4.0 %copy-start.11 = (f32[352,256]{1,0:T(8,128)S(1)}, f32[352,256]{1,0:T(8,128)}, u32[]{:S(2)}) copy-start(f32[352,256]{1,0:T(8,128)} %get-tuple-element.138) | copy-start | bytes 1081348
  374.0 4.7 %copy-start.10 = (f32[352,256]{1,0:T(8,128)S(1)}, f32[352,256]{1,0:T(8,128)}, u32[]{:S(2)}) copy-start(f32[352,256]{1,0:T(8,128)} %get-tuple-element.139) | copy-start | bytes 1081348
  375.3 4.1 %copy-start.9 = (f32[704,128]{1,0:T(8,128)S(1)}, f32[704,128]{1,0:T(8,128)}, u32[]{:S(2)}) copy-start(f32[704,128]{1,0:T(8,128)} %get-tuple-element.173) | copy-start | bytes 1081348

commit v8 on v7

--- a/solution.py
+++ b/solution.py
@@ -143,24 +143,29 @@
     masks = head_masks(heads, width)
     queries = by_head(qkv_ref[i, 0] * jnp.asarray(HEAD_DIM**-0.5, BF16), masks)
 
-    def tile(step, carry):
+    def pair(step, carry):
         run_max, run_sum = carry
-        j = i - step
-        scores = dot_nt(qkv_ref[j, 1], queries)
-        key = j * length + lax.broadcasted_iota(jnp.int32, scores.shape, 0)
-        scores = jnp.where((key <= place) & (key >= start), scores, NEG)
-        new_max = jnp.maximum(run_max, jnp.max(scores, axis=0, keepdims=True))
-        weights = jnp.exp(scores - new_max)
+        tiles = [i - 2 * step, i - 2 * step - 1]
+        at = [tiles[0], jnp.maximum(tiles[1], 0)]
+        scores = []
+        for j, source in zip(tiles, at):
+            raw = dot_nt(qkv_ref[source, 1], queries)
+            key = j * length + lax.broadcasted_iota(jnp.int32, raw.shape, 0)
+            scores.append(jnp.where((key <= place) & (key >= start), raw, NEG))
+        highest = jnp.max(jnp.maximum(scores[0], scores[1]), axis=0, keepdims=True)
+        new_max = jnp.maximum(run_max, highest)
+        weights = [jnp.exp(one - new_max) for one in scores]
         factor = jnp.exp(run_max - new_max)
-        run_sum = run_sum * factor + jnp.sum(weights, axis=0, keepdims=True)
-        acc_ref[...] = acc_ref[...] * factor + dot_tn(qkv_ref[j, 2], weights.astype(BF16))
+        run_sum = run_sum * factor + jnp.sum(weights[0] + weights[1], axis=0, keepdims=True)
+        added = dot_tn(qkv_ref[at[0], 2], weights[0].astype(BF16)) + dot_tn(qkv_ref[at[1], 2], weights[1].astype(BF16))
+        acc_ref[...] = acc_ref[...] * factor + added
         return new_max, run_sum
 
     acc_ref[...] = jnp.zeros_like(acc_ref)
     run_max, run_sum = lax.fori_loop(
         0,
-        i - lowest + 1,
-        tile,
+        (i - lowest + 2) // 2,
+        pair,
         (jnp.full((1, heads * length), NEG, F32), jnp.zeros((1, heads * length), F32)),
     )
     result = acc_ref[...] / run_sum
@@ -240,9 +245,14 @@
     keys, values = qkv_ref[j, 1], qkv_ref[j, 2]
     key_heads = [keys * mask for mask in masks]
 
-    def tile(i, carry):
+    def tile(step, carry):
+        first = j + 2 * step
+        carry = one_tile(first, first, carry)
+        return one_tile(first + 1, jnp.minimum(first + 1, n_blk - 1), carry)
+
+    def one_tile(index, i, carry):
         d_key, d_value = carry
-        start, place = start_rows(ends, i, length, heads)
+        start, place = start_rows(ends, index, length, heads)
         queries = by_head(qkv_ref[i, 0] * jnp.asarray(scale, BF16), masks)
         d_out = by_head(do_ref[i], masks)
         lse = jnp.concatenate([lse_ref[i, h : h + 1, :] for h in range(heads)], axis=1)
@@ -261,7 +271,7 @@
         return d_key, d_value
 
     zero = jnp.zeros((length, width), F32)
-    d_key, d_value = lax.fori_loop(j, highest + 1, tile, (zero, zero))
+    d_key, d_value = lax.fori_loop(0, (highest - j + 2) // 2, tile, (zero, zero))
     out_ref[0, 0, 0] = (dq_ref[j] * scale).astype(BF16)
     out_ref[0, 0, 1] = d_key.astype(BF16)
     out_ref[0, 0, 2] = d_value.astype(BF16)

time: 385 us -> 383 us (level)
  Pallas kernels: 260 us -> 255 us
where the time goes in v8:
time: 383 us; the launch traced here: 381 us
  Pallas kernels  255 us (67%)
  blocking collectives  44.4 us (12%)
  local copies, waits for them, and re-layouts  26.5 us (7%)
  waiting for transfers between devices  26.1 us (7%)
  starting transfers between devices  21.4 us (6%)
  between operations  4.5 us (1%)
    pallas_call x2, Pallas kernels, ffn_wgrad(): pl.pallas_call(functools.partial(ffn_wgrad_kernel, plans, n_dp, n_blk, le...  75.6 us
    pallas_call x1, Pallas kernels, tail(): pl.pallas_call(functools.partial(tail_kernel, ffn_orders, own_order, qkv_...  67.6 us
    all_to_all x1, blocking collectives, exchange(): return lax.all_to_all(values, 'blk', 0, 0, tiled=True)  44.4 us
    pallas_call x2, Pallas kernels, feed_forward(): pl.pallas_call(ffn_kernel, grid=(inner // chunk,), in_specs=[once(gathere...  42.5 us
    pallas_call x2, Pallas kernels, attn_bwd(): pl.pallas_call(functools.partial(attn_bwd_kernel, rows, first_row, n_docs...  31.2 us
    all_to_all x4, waiting for transfers between devices, exchange(): return lax.all_to_all(values, 'blk', 0, 0, tiled=True)  26 us
    pallas_call x2, Pallas kernels, attn_fwd(): pl.pallas_call(functools.partial(attn_fwd_kernel, row, n_docs, heads), gr...  23.4 us
    all_to_all x4, starting transfers between devices, exchange(): return lax.all_to_all(values, 'blk', 0, 0, tiled=True)  14.9 us
  transfers between devices with their start and end apart: 10, of which 2 were waited for; matrix products, arithmetic and copies ran while one was open for 2% of the time, Pallas kernels for 32%

profile of v8, /device:TPU:0, one launch (start us, length us, event | category | flops | bytes accessed | tf_op | source)
XLA Modules:
  0.0 381.0 jit_solution(17793096721896911541)
XLA Ops:
  1.7 2.5 copy.40
  4.2 1.2 copy.41
  5.5 1.8 fusion
  7.3 8.5 %qkv.1 = (bf16[8,3,256,128]{3,2,1,0:T(8,128)(2,1)}, bf16[8,3,256,128]{3,2,1,0:T(8,128)(2,1)}, bf16[512,1024]{1,0:T(8,128)(2,1)}, f32[4,2,256]{2,1,0:T(2,128)}) custom-call(bf16[512,1024]{1,0:T(8,128)(2,1)} %bitcast.34, bf16[512,1024]{1,0:T(8,128)(2,1)} %bitcast.46, f32[512,128]{1,0:T(8,128)} %get-tuple-element.147.cos_ref.refs_0_, ...), custom_call_target="tpu_custom_call" | custom-call | flops 3221225472 | bytes 11534336 | tf_op jit(solution)/shard_map/qkv/pallas_call | solution.py:84
  15.8 44.4 %all_to_all.25.qkv_ref.refs_0_ = bf16[8,3,256,128]{3,2,1,0:T(8,128)(2,1)} all-to-all(bf16[8,3,256,128]{3,2,1,0:T(8,128)(2,1)} %get-tuple-element.80), channel_id=1, replica_groups=mesh['dp'=4,'blk'=8] {'blk'}, dimensions={0} | all-to-all | bytes 3145728 | tf_op jit(solution)/shard_map/all_to_all | solution.py:306
  60.2 3.7 all-to-all-start
  64.5 1.2 copy.42
  65.8 11.0 %attn_fwd.3 = (f32[8,256,128]{2,1,0:T(8,128)}, bf16[8,256,128]{2,1,0:T(8,128)(2,1)}, f32[8,2,256]{2,1,0:T(2,128)}) custom-call(s32[16]{0:T(128)} %reshape.130.lens_ref, bf16[8,3,256,128]{3,2,1,0:T(8,128)(2,1)} %all_to_all.25.qkv_ref.refs_0_), custom_call_target="tpu_custom_call" | custom-call | flops 10000000000 | bytes 3000000 | tf_op jit(solution)/shard_map/attn_fwd/pallas_call | solution.py:191
  76.8 23.8 %all-to-all-done.qkv_ref.refs_0_ = bf16[8,3,256,128]{3,2,1,0:T(8,128)(2,1)S(1)} async-done(((bf16[8,3,256,128]{3,2,1,0:T(8,128)(2,1)}), bf16[8,3,256,128]{3,2,1,0:T(8,128)(2,1)S(1)}, u32[]{:S(2)}, u32[]{:S(2)}) %all-to-all-start) | async-done | bytes 1572896 | tf_op jit(solution)/shard_map/all_to_all | solution.py:306
  100.6 3.6 all-to-all-start.3
  104.2 12.4 %attn_fwd.2 = (f32[8,256,128]{2,1,0:T(8,128)}, bf16[8,256,128]{2,1,0:T(8,128)(2,1)}, f32[8,2,256]{2,1,0:T(2,128)}) custom-call(s32[16]{0:T(128)} %reshape.130.lens_ref, bf16[8,3,256,128]{3,2,1,0:T(8,128)(2,1)} %copy-done.3), custom_call_target="tpu_custom_call" | custom-call | flops 10000000000 | bytes 3000000 | tf_op jit(solution)/shard_map/attn_fwd/pallas_call | solution.py:191
  116.6 2.3 all-to-all-done.3.gathered_ref
  118.9 3.8 all-to-all-start.1
  122.6 21.3 %ffn.2 = (bf16[1024,512]{1,0:T(8,128)(2,1)}, bf16[512,1024]{1,0:T(8,128)(2,1)}, bf16[2816,512]{1,0:T(8,128)(2,1)}, bf16[2816,512]{1,0:T(8,128)(2,1)}, bf16[2816,...) custom-call(bf16[8,256,128]{2,1,0:T(8,128)(2,1)} %copy-done.8, ...), custom_call_target="tpu_custom_call" | custom-call | flops 9932111872 | bytes 26869760 | tf_op jit(solution)/shard_map/ffn/pallas_call | solution.py:676
  144.7 21.3 %ffn.3 = (bf16[1024,512]{1,0:T(8,128)(2,1)}, bf16[512,1024]{1,0:T(8,128)(2,1)}, bf16[2816,512]{1,0:T(8,128)(2,1)}, bf16[2816,512]{1,0:T(8,128)(2,1)}, bf16[2816,...) custom-call(bf16[8,256,128]{2,1,0:T(8,128)(2,1)} %copy-done.1, ...), custom_call_target="tpu_custom_call", output_to_operand_aliasing={{0}: (8, {}), {1}: (9, {}), {2}: (10, {}), {3}: (11, {}), {... | custom-call | flops 9932111872 | bytes 26869760 | tf_op jit(solution)/shard_map/ffn/pallas_call | solution.py:676
  166.0 37.1 %ffn_wgrad.2 = (bf16[4,8,176,128]{3,2,1,0:T(8,128)(2,1)}, bf16[4,8,176,128]{3,2,1,0:T(8,128)(2,1)}, bf16[4,8,176,128]{3,2,1,0:T(8,128)(2,1)}, bf16[4,8,176,128]{...) custom-call(bf16[8,2,176,512]{3,2,1,0:T(8,128)(2,1)} %bitcast.29, ...), custom_call_target="tpu_custom_call" | custom-call | flops 1000000000 | bytes 10000000 | tf_op jit(solution)/shard_map/ffn_wgrad/pallas_call | solution.py:543
  203.1 1.4 collective-permute-start
  205.7 2.3 copy.44
  208.1 2.0 copy.47
  210.1 14.6 %attn_bwd.2 = bf16[8,1,3,256,128]{4,3,2,1,0:T(8,128)(2,1)} custom-call(s32[16]{0:T(128)} %reshape.130.lens_ref, bf16[8,3,256,128]{3,2,1,0:T(8,128)(2,1)} %all_to_all.25.qkv_ref.refs_0_, bf16[8,256,128]{2,1,0:T(8,128)(2,1)} %get-tuple-element.100.refs_1_, f32[8,256,128]{2,1,0:T(8,128)} %get-tuple-element.101.refs_2_, f32[8,2,256]{2,1,0:T(2,128)} %get-tuple-element.102.refs_3_), custom_call_target="tpu_custom_call" | custom-call | flops 4000000000 | bytes 12000000 | tf_op jit(solution)/shard_map/attn_bwd/pallas_call | solution.py:286
  224.7 3.8 all-to-all-start.4
  228.5 16.6 %attn_bwd.3.refs_2_ = bf16[8,1,3,256,128]{4,3,2,1,0:T(8,128)(2,1)} custom-call(s32[16]{0:T(128)} %reshape.130.lens_ref, bf16[8,3,256,128]{3,2,1,0:T(8,128)(2,1)} %copy-done.3, bf16[8,256,128]{2,1,0:T(8,128)(2,1)} %get-tuple-element.103.refs_1_, f32[8,256,128]{2,1,0:T(8,128)} %get-tuple-element.104.refs_2_, f32[8,2,256]{2,1,0:T(2,128)} %get-tuple-element.105.refs_3_), custom_call_target="tpu_custom_call" | custom-call | flops 4000000000 | bytes 12000000 | tf_op jit(solution)/shard_map/attn_bwd/pallas_call | solution.py:286
  245.9 1.1 copy-done.5
  247.0 6.3 %fold.1 = (bf16[4,4,176,128]{3,2,1,0:T(8,128)(2,1)}, bf16[4,4,176,128]{3,2,1,0:T(8,128)(2,1)}, bf16[4,4,176,128]{3,2,1,0:T(8,128)(2,1)}, bf16[4,4,176,128]{3,2,1...) custom-call(bf16[4,8,176,128]{3,2,1,0:T(8,128)(2,1)} %get-tuple-element.109.refs_0_, ...), custom_call_target="tpu_custom_call" | custom-call | flops 1000000000 | bytes 10000000 | tf_op jit(solution)/shard_map/fold/pallas_call | solution.py:583
  253.3 1.9 collective-permute-start.3
  255.8 1.4 collective-permute-start.5
  257.2 38.5 %ffn_wgrad.3 = (bf16[4,8,64,128]{3,2,1,0:T(8,128)(2,1)}, bf16[4,8,64,128]{3,2,1,0:T(8,128)(2,1)}, bf16[8,1,3,256,128]{4,3,2,1,0:T(8,128)(2,1)}) custom-call(bf16[4,4,64,512]{3,2,1,0:T(8,128)(2,1)} %bitcast.39, bf16[512,1024]{1,0:T(8,128)(2,1)} %get-tuple-element.123.refs_1_, bf16[8,1,3,256,128]{4,3,2,1,0:T(8,128)(2,1)} %attn_bwd.3.refs_2_), custom_call_target="tpu_custom_call" | custom-call | flops 60000002048 | bytes 10000000 | tf_op jit(solution)/shard_map/ffn_wgrad/pallas_call | solution.py:543
  297.3 67.6 %tail.1 = (f32[352,256]{1,0:T(8,128)}, f32[352,256]{1,0:T(8,128)}, f32[704,128]{1,0:T(8,128)}, f32[256,128]{1,0:T(8,128)}, f32[256,128]{1,0:T(8,128)}, /*index=5...) custom-call(f32[512,128]{1,0:T(8,128)} %get-tuple-element.147.cos_re, ...), custom_call_target="tpu_custom_call" | custom-call | flops 99999997952 | bytes 100000000 | tf_op jit(solution)/shard_map/tail/pallas_call | solution.py:1008
  364.9 1.3 fusion.5
  366.2 1.3 fusion.6
  368.8 3.8 copy.65
  372.6 1.3 copy.66
  (72 shorter events, 11.5 us)
Async XLA Ops:
  0.6 3.6 copy-start.6
  60.2 3.7 copy-start.19
  60.2 4.3 %copy-start.7 = (bf16[256,2,1024]{2,1,0:T(2,128)(2,1)S(1)}, bf16[256,2,1024]{2,1,0:T(2,128)(2,1)}, u32[]{:S(2)}) copy-start(bf16[256,2,1024]{2,1,0:T(2,128)(2,1)} %param.25) | copy-start | bytes 3145732
  60.2 40.4 %all-to-all-start = ((bf16[8,3,256,128]{3,2,1,0:T(8,128)(2,1)}), bf16[8,3,256,128]{3,2,1,0:T(8,128)(2,1)S(1)}, u32[]{:S(2)}, u32[]{:S(2)}) async-start(bf16[8,3,256,128]{3,2,1,0:T(8,128)(2,1)} %get-tuple-element.78), calls=%async_computation | async-start | bytes 3145728 | tf_op jit(solution)/shard_map/all_to_all | solution.py:306
  100.6 3.6 copy-start.3
  100.6 18.3 %all-to-all-start.3 = ((bf16[8,256,128]{2,1,0:T(8,128)(2,1)}), bf16[8,256,128]{2,1,0:T(8,128)(2,1)S(1)}, u32[]{:S(2)}, u32[]{:S(2)}) async-start(bf16[8,256,128]{2,1,0:T(8,128)(2,1)} %get-tuple-element.81), calls=%async_computation.3 | async-start | bytes 1048576 | tf_op jit(solution)/shard_map/all_to_all | solution.py:306
  118.9 3.8 copy-start.8
  118.9 25.0 %all-to-all-start.1 = ((bf16[8,256,128]{2,1,0:T(8,128)(2,1)}), bf16[8,256,128]{2,1,0:T(8,128)(2,1)S(1)}, u32[]{:S(2)}, u32[]{:S(2)}) async-start(bf16[8,256,128]{2,1,0:T(8,128)(2,1)} %get-tuple-element.79), calls=%async_computation.1 | async-start | bytes 1048576 | tf_op jit(solution)/shard_map/all_to_all | solution.py:306
  143.9 0.8 copy-start.1
  203.1 4.9 %copy-start.16 = (f32[4,2,256]{2,1,0:T(2,128)S(1)}, f32[4,2,256]{2,1,0:T(2,128)}, u32[]{:S(2)}) copy-start(f32[4,2,256]{2,1,0:T(2,128)} %get-tuple-element.93) | copy-start | bytes 24580
  203.1 5.0 %copy-start = (bf16[512,1024]{1,0:T(8,128)(2,1)S(1)}, bf16[512,1024]{1,0:T(8,128)(2,1)}, u32[]{:S(2)}) copy-start(bf16[512,1024]{1,0:T(8,128)(2,1)} %get-tuple-element.90) | copy-start | bytes 3145732
  203.1 42.8 %collective-permute-start = (bf16[4,8,176,128]{3,2,1,0:T(8,128)(2,1)}, bf16[4,8,176,128]{3,2,1,0:T(8,128)(2,1)S(1)}, u32[]{:S(2)}, u32[]{:S(2)}) collective-permute-start(bf16[4,8,176,128]{3,2,1,0:T(8,128)(2,1)} %get-tuple-element.110), channel_id=1, source_target_pairs={{0,16},{8,24},{16,0},{24,8},{1,17},{9,25},{17,1},{25,9},{2,18},{10... | collective-permute-start | bytes 4325384 | tf_op jit(solution)/shard_map/ppermute | solution.py:598
  204.6 41.3 %collective-permute-start.1 = (bf16[4,8,176,128]{3,2,1,0:T(8,128)(2,1)}, bf16[4,8,176,128]{3,2,1,0:T(8,128)(2,1)}, u32[]{:S(2)}, u32[]{:S(2)}) collective-permute-start(bf16[4,8,176,128]{3,2,1,0:T(8,128)(2,1)} %get-tuple-element.112), channel_id=1, source_target_pairs={{0,1},{1,0},{2,3},{3,2},{4,5},{5,4},{6,7},{7,6},{8,9},{9,8},{10,11... | collective-permute-start | bytes 4325384 | tf_op jit(solution)/shard_map/ppermute | solution.py:598
  205.1 40.8 %collective-permute-start.2 = (bf16[4,8,176,128]{3,2,1,0:T(8,128)(2,1)}, bf16[4,8,176,128]{3,2,1,0:T(8,128)(2,1)}, u32[]{:S(2)}, u32[]{:S(2)}) collective-permute-start(bf16[4,8,176,128]{3,2,1,0:T(8,128)(2,1)} %get-tuple-element.114), channel_id=1, source_target_pairs={{0,2},{1,3},{2,0},{3,1},{4,6},{5,7},{6,4},{7,5},{8,10},{9,11},{10,... | collective-permute-start | bytes 4325384 | tf_op jit(solution)/shard_map/ppermute | solution.py:598
  224.7 71.0 %all-to-all-start.4 = ((bf16[8,1,3,256,128]{4,3,2,1,0:T(8,128)(2,1)}), bf16[8,1,3,256,128]{4,3,2,1,0:T(8,128)(2,1)S(1)}, u32[]{:S(2)}, u32[]{:S(2)}) async-start(bf16[8,1,3,256,128]{4,3,2,1,0:T(8,128)(2,1)} %attn_bwd.2), calls=%async_computation.4 | async-start | bytes 3145728 | tf_op jit(solution)/shard_map/all_to_all | solution.py:306
  228.5 16.7 %copy-start.17 = (f32[1,1024]{1,0:T(1,128)S(1)}, f32[1,1024]{1,0:T(1,128)}, u32[]{:S(2)}) copy-start(f32[1,1024]{1,0:T(1,128)} %get-tuple-element.91) | copy-start | bytes 12292
  228.5 16.6 %copy-start.18 = (f32[1,1024]{1,0:T(1,128)S(1)}, f32[1,1024]{1,0:T(1,128)}, u32[]{:S(2)}) copy-start(f32[1,1024]{1,0:T(1,128)} %get-tuple-element.92) | copy-start | bytes 12292
  245.9 1.1 copy-start.5
  253.3 42.4 %collective-permute-start.3 = (bf16[4,4,176,128]{3,2,1,0:T(8,128)(2,1)}, bf16[4,4,176,128]{3,2,1,0:T(8,128)(2,1)S(1)}, u32[]{:S(2)}, u32[]{:S(2)}) collective-permute-start(bf16[4,4,176,128]{3,2,1,0:T(8,128)(2,1)} %get-tuple-element.116), channel_id=1, source_target_pairs={{0,1},{1,0},{2,3},{3,2},{4,5},{5,4},{6,7},{7,6},{8,9},{9,8},{10,11... | collective-permute-start | bytes 2162696 | tf_op jit(solution)/shard_map/ppermute | solution.py:598
  255.2 40.5 %collective-permute-start.4 = (bf16[4,4,176,128]{3,2,1,0:T(8,128)(2,1)}, bf16[4,4,176,128]{3,2,1,0:T(8,128)(2,1)S(1)}, u32[]{:S(2)}, u32[]{:S(2)}) collective-permute-start(bf16[4,4,176,128]{3,2,1,0:T(8,128)(2,1)} %get-tuple-element.118), channel_id=1, source_target_pairs={{0,16},{8,24},{16,0},{24,8},{1,17},{9,25},{17,1},{25,9},{2,18},{10... | collective-permute-start | bytes 2162696 | tf_op jit(solution)/shard_map/ppermute | solution.py:598
  255.8 39.9 %collective-permute-start.5 = (bf16[4,4,176,128]{3,2,1,0:T(8,128)(2,1)}, bf16[4,4,176,128]{3,2,1,0:T(8,128)(2,1)}, u32[]{:S(2)}, u32[]{:S(2)}) collective-permute-start(bf16[4,4,176,128]{3,2,1,0:T(8,128)(2,1)} %get-tuple-element.120), channel_id=1, source_target_pairs={{0,16},{8,24},{16,0},{24,8},{1,17},{9,25},{17,1},{25,9},{2,18},{10... | collective-permute-start | bytes 2162696 | tf_op jit(solution)/shard_map/ppermute | solution.py:598
  295.7 0.9 copy-start.20
  295.7 1.1 copy-start.21
  295.7 1.6 copy-start.4
  368.8 3.8 copy-start.2
  372.5 1.4 copy-start.15
  372.6 2.0 copy-start.14
  372.6 2.7 copy-start.13
  372.6 3.3 copy-start.12
  372.6 4.0 %copy-start.11 = (f32[352,256]{1,0:T(8,128)S(1)}, f32[352,256]{1,0:T(8,128)}, u32[]{:S(2)}) copy-start(f32[352,256]{1,0:T(8,128)} %get-tuple-element.138) | copy-start | bytes 1081348
  372.6 4.7 %copy-start.10 = (f32[352,256]{1,0:T(8,128)S(1)}, f32[352,256]{1,0:T(8,128)}, u32[]{:S(2)}) copy-start(f32[352,256]{1,0:T(8,128)} %get-tuple-element.139) | copy-start | bytes 1081348
  373.9 4.1 %copy-start.9 = (f32[704,128]{1,0:T(8,128)S(1)}, f32[704,128]{1,0:T(8,128)}, u32[]{:S(2)}) copy-start(f32[704,128]{1,0:T(8,128)} %get-tuple-element.173) | copy-start | bytes 1081348

commit v9 on v8

--- a/solution.py
+++ b/solution.py
@@ -52,19 +52,20 @@
 
     first_sum = jnp.zeros((1, chunk), F32)
     mixed_sum = jnp.zeros((1, chunk), F32)
+    raws = [dot(normed_ref[...], w_ref[...]) for w_ref in (wq_ref, wk_ref, wv_ref)]
     for r in range(rows):
         at = pl.ds(r * length, length)
-        normed = normed_ref[at, :]
+        own = slice(r * length, (r + 1) * length)
         cos, sin = cos_ref[at, :], sin_ref[at, :]
-        for which, w_ref in ((0, wq_ref), (1, wk_ref)):
-            raw = dot(normed, w_ref[...])
+        for which in range(2):
+            raw = raws[which][own]
             for c in range(chunk // 128):
                 part = raw[:, c * 128 : (c + 1) * 128]
                 turned = (part * cos + swap_halves(part) * sin).astype(BF16)
                 for s in range(128 // width):
                     out_refs[r][c * (128 // width) + s, which] = turned[:, s * width : (s + 1) * width]
         first = first_ref[at, :].astype(F32)
-        mixed = 0.5 * dot(normed, wv_ref[...]) + 0.5 * first
+        mixed = 0.5 * raws[2][own] + 0.5 * first
         first_sum = first_sum + jnp.sum(first * first, axis=0, keepdims=True)
         mixed_sum = mixed_sum + jnp.sum(mixed * mixed, axis=0, keepdims=True)
         low = mixed.astype(BF16)

time: 383 us -> 384 us (level)
  no operation moved by 1% of the time
where the time goes in v9:
time: 384 us; the launch traced here: 381 us
  Pallas kernels  258 us (67%)
  blocking collectives  44.4 us (12%)
  local copies, waits for them, and re-layouts  26.5 us (7%)
  waiting for transfers between devices  24 us (6%)
  starting transfers between devices  21.5 us (6%)
  between operations  4.5 us (1%)
    pallas_call x2, Pallas kernels, ffn_wgrad(): pl.pallas_call(functools.partial(ffn_wgrad_kernel, plans, n_dp, n_blk, le...  71.9 us
    pallas_call x1, Pallas kernels, tail(): pl.pallas_call(functools.partial(tail_kernel, ffn_orders, own_order, qkv_...  68.7 us
    all_to_all x1, blocking collectives, exchange(): return lax.all_to_all(values, 'blk', 0, 0, tiled=True)  44.4 us
    pallas_call x2, Pallas kernels, feed_forward(): pl.pallas_call(ffn_kernel, grid=(inner // chunk,), in_specs=[once(gathere...  42.5 us
    pallas_call x2, Pallas kernels, attn_bwd(): pl.pallas_call(functools.partial(attn_bwd_kernel, rows, first_row, n_docs...  34.1 us
    pallas_call x2, Pallas kernels, attn_fwd(): pl.pallas_call(functools.partial(attn_fwd_kernel, row, n_docs, heads), gr...  25.5 us
    all_to_all x4, waiting for transfers between devices, exchange(): return lax.all_to_all(values, 'blk', 0, 0, tiled=True)  24 us
    all_to_all x4, starting transfers between devices, exchange(): return lax.all_to_all(values, 'blk', 0, 0, tiled=True)  14.9 us
  transfers between devices with their start and end apart: 10, of which 2 were waited for; matrix products, arithmetic and copies ran while one was open for 2% of the time, Pallas kernels for 32%

profile of v9, /device:TPU:0, one launch (start us, length us, event | category | flops | bytes accessed | tf_op | source)
XLA Modules:
  0.0 381.4 jit_solution(14497734122015663805)
XLA Ops:
  1.7 2.5 copy.40
  4.2 1.2 copy.41
  5.5 1.8 fusion
  7.3 8.6 %qkv.1 = (bf16[8,3,256,128]{3,2,1,0:T(8,128)(2,1)}, bf16[8,3,256,128]{3,2,1,0:T(8,128)(2,1)}, bf16[512,1024]{1,0:T(8,128)(2,1)}, f32[4,2,256]{2,1,0:T(2,128)}) custom-call(bf16[512,1024]{1,0:T(8,128)(2,1)} %bitcast.34, bf16[512,1024]{1,0:T(8,128)(2,1)} %bitcast.46, f32[512,128]{1,0:T(8,128)} %get-tuple-element.147.cos_ref.refs_0_, ...), custom_call_target="tpu_custom_call" | custom-call | flops 3221225472 | bytes 11534336 | tf_op jit(solution)/shard_map/qkv/pallas_call | solution.py:85
  15.8 44.4 %all_to_all.25.qkv_ref.refs_0_ = bf16[8,3,256,128]{3,2,1,0:T(8,128)(2,1)} all-to-all(bf16[8,3,256,128]{3,2,1,0:T(8,128)(2,1)} %get-tuple-element.80), channel_id=1, replica_groups=mesh['dp'=4,'blk'=8] {'blk'}, dimensions={0} | all-to-all | bytes 3145728 | tf_op jit(solution)/shard_map/all_to_all | solution.py:307
  60.2 3.7 all-to-all-start
  64.6 1.2 copy.42
  65.8 13.1 %attn_fwd.3 = (f32[8,256,128]{2,1,0:T(8,128)}, bf16[8,256,128]{2,1,0:T(8,128)(2,1)}, f32[8,2,256]{2,1,0:T(2,128)}) custom-call(s32[16]{0:T(128)} %reshape.130.lens_ref, bf16[8,3,256,128]{3,2,1,0:T(8,128)(2,1)} %all_to_all.25.qkv_ref.refs_0_), custom_call_target="tpu_custom_call" | custom-call | flops 10000000000 | bytes 3000000 | tf_op jit(solution)/shard_map/attn_fwd/pallas_call | solution.py:192
  78.9 21.7 %all-to-all-done.qkv_ref.refs_0_ = bf16[8,3,256,128]{3,2,1,0:T(8,128)(2,1)S(1)} async-done(((bf16[8,3,256,128]{3,2,1,0:T(8,128)(2,1)}), bf16[8,3,256,128]{3,2,1,0:T(8,128)(2,1)S(1)}, u32[]{:S(2)}, u32[]{:S(2)}) %all-to-all-start) | async-done | bytes 1572896 | tf_op jit(solution)/shard_map/all_to_all | solution.py:307
  100.6 3.6 all-to-all-start.3
  104.3 12.4 %attn_fwd.2 = (f32[8,256,128]{2,1,0:T(8,128)}, bf16[8,256,128]{2,1,0:T(8,128)(2,1)}, f32[8,2,256]{2,1,0:T(2,128)}) custom-call(s32[16]{0:T(128)} %reshape.130.lens_ref, bf16[8,3,256,128]{3,2,1,0:T(8,128)(2,1)} %copy-done.3), custom_call_target="tpu_custom_call" | custom-call | flops 10000000000 | bytes 3000000 | tf_op jit(solution)/shard_map/attn_fwd/pallas_call | solution.py:192
  116.7 2.2 all-to-all-done.3.gathered_ref
  118.9 3.8 all-to-all-start.1
  122.7 21.3 %ffn.2 = (bf16[1024,512]{1,0:T(8,128)(2,1)}, bf16[512,1024]{1,0:T(8,128)(2,1)}, bf16[2816,512]{1,0:T(8,128)(2,1)}, bf16[2816,512]{1,0:T(8,128)(2,1)}, bf16[2816,...) custom-call(bf16[8,256,128]{2,1,0:T(8,128)(2,1)} %copy-done.8, ...), custom_call_target="tpu_custom_call" | custom-call | flops 9932111872 | bytes 26869760 | tf_op jit(solution)/shard_map/ffn/pallas_call | solution.py:677
  144.8 21.3 %ffn.3 = (bf16[1024,512]{1,0:T(8,128)(2,1)}, bf16[512,1024]{1,0:T(8,128)(2,1)}, bf16[2816,512]{1,0:T(8,128)(2,1)}, bf16[2816,512]{1,0:T(8,128)(2,1)}, bf16[2816,...) custom-call(bf16[8,256,128]{2,1,0:T(8,128)(2,1)} %copy-done.1, ...), custom_call_target="tpu_custom_call", output_to_operand_aliasing={{0}: (8, {}), {1}: (9, {}), {2}: (10, {}), {3}: (11, {}), {... | custom-call | flops 9932111872 | bytes 26869760 | tf_op jit(solution)/shard_map/ffn/pallas_call | solution.py:677
  166.0 37.1 %ffn_wgrad.2 = (bf16[4,8,176,128]{3,2,1,0:T(8,128)(2,1)}, bf16[4,8,176,128]{3,2,1,0:T(8,128)(2,1)}, bf16[4,8,176,128]{3,2,1,0:T(8,128)(2,1)}, bf16[4,8,176,128]{...) custom-call(bf16[8,2,176,512]{3,2,1,0:T(8,128)(2,1)} %bitcast.29, ...), custom_call_target="tpu_custom_call" | custom-call | flops 1000000000 | bytes 10000000 | tf_op jit(solution)/shard_map/ffn_wgrad/pallas_call | solution.py:544
  203.2 1.6 collective-permute-start
  205.9 2.3 copy.44
  208.3 2.0 copy.47
  210.3 17.5 %attn_bwd.2 = bf16[8,1,3,256,128]{4,3,2,1,0:T(8,128)(2,1)} custom-call(s32[16]{0:T(128)} %reshape.130.lens_ref, bf16[8,3,256,128]{3,2,1,0:T(8,128)(2,1)} %all_to_all.25.qkv_ref.refs_0_, bf16[8,256,128]{2,1,0:T(8,128)(2,1)} %get-tuple-element.100.refs_1_, f32[8,256,128]{2,1,0:T(8,128)} %get-tuple-element.101.refs_2_, f32[8,2,256]{2,1,0:T(2,128)} %get-tuple-element.102.refs_3_), custom_call_target="tpu_custom_call" | custom-call | flops 4000000000 | bytes 12000000 | tf_op jit(solution)/shard_map/attn_bwd/pallas_call | solution.py:287
  227.8 3.8 all-to-all-start.4
  231.6 16.6 %attn_bwd.3.refs_2_ = bf16[8,1,3,256,128]{4,3,2,1,0:T(8,128)(2,1)} custom-call(s32[16]{0:T(128)} %reshape.130.lens_ref, bf16[8,3,256,128]{3,2,1,0:T(8,128)(2,1)} %copy-done.3, bf16[8,256,128]{2,1,0:T(8,128)(2,1)} %get-tuple-element.103.refs_1_, f32[8,256,128]{2,1,0:T(8,128)} %get-tuple-element.104.refs_2_, f32[8,2,256]{2,1,0:T(2,128)} %get-tuple-element.105.refs_3_), custom_call_target="tpu_custom_call" | custom-call | flops 4000000000 | bytes 12000000 | tf_op jit(solution)/shard_map/attn_bwd/pallas_call | solution.py:287
  249.0 1.1 copy-done.5
  250.1 6.3 %fold.1 = (bf16[4,4,176,128]{3,2,1,0:T(8,128)(2,1)}, bf16[4,4,176,128]{3,2,1,0:T(8,128)(2,1)}, bf16[4,4,176,128]{3,2,1,0:T(8,128)(2,1)}, bf16[4,4,176,128]{3,2,1...) custom-call(bf16[4,8,176,128]{3,2,1,0:T(8,128)(2,1)} %get-tuple-element.109.refs_0_, ...), custom_call_target="tpu_custom_call" | custom-call | flops 1000000000 | bytes 10000000 | tf_op jit(solution)/shard_map/fold/pallas_call | solution.py:584
  256.4 1.9 collective-permute-start.3
  258.3 2.0 collective-permute-start.5
  260.3 34.7 %ffn_wgrad.3 = (bf16[4,8,64,128]{3,2,1,0:T(8,128)(2,1)}, bf16[4,8,64,128]{3,2,1,0:T(8,128)(2,1)}, bf16[8,1,3,256,128]{4,3,2,1,0:T(8,128)(2,1)}) custom-call(bf16[4,4,64,512]{3,2,1,0:T(8,128)(2,1)} %bitcast.39, bf16[512,1024]{1,0:T(8,128)(2,1)} %get-tuple-element.123.refs_1_, bf16[8,1,3,256,128]{4,3,2,1,0:T(8,128)(2,1)} %attn_bwd.3.refs_2_), custom_call_target="tpu_custom_call" | custom-call | flops 60000002048 | bytes 10000000 | tf_op jit(solution)/shard_map/ffn_wgrad/pallas_call | solution.py:544
  296.7 68.7 %tail.1 = (f32[352,256]{1,0:T(8,128)}, f32[352,256]{1,0:T(8,128)}, f32[704,128]{1,0:T(8,128)}, f32[256,128]{1,0:T(8,128)}, f32[256,128]{1,0:T(8,128)}, /*index=5...) custom-call(f32[512,128]{1,0:T(8,128)} %get-tuple-element.147.cos_re, ...), custom_call_target="tpu_custom_call" | custom-call | flops 99999997952 | bytes 100000000 | tf_op jit(solution)/shard_map/tail/pallas_call | solution.py:1009
  365.3 1.3 fusion.5
  366.6 1.3 fusion.6
  369.2 3.8 copy.65
  373.0 1.3 copy.66
  (72 shorter events, 10.9 us)
Async XLA Ops:
  0.6 3.6 copy-start.6
  60.2 3.7 copy-start.19
  60.2 4.3 %copy-start.7 = (bf16[256,2,1024]{2,1,0:T(2,128)(2,1)S(1)}, bf16[256,2,1024]{2,1,0:T(2,128)(2,1)}, u32[]{:S(2)}) copy-start(bf16[256,2,1024]{2,1,0:T(2,128)(2,1)} %param.25) | copy-start | bytes 3145732
  60.2 40.4 %all-to-all-start = ((bf16[8,3,256,128]{3,2,1,0:T(8,128)(2,1)}), bf16[8,3,256,128]{3,2,1,0:T(8,128)(2,1)S(1)}, u32[]{:S(2)}, u32[]{:S(2)}) async-start(bf16[8,3,256,128]{3,2,1,0:T(8,128)(2,1)} %get-tuple-element.78), calls=%async_computation | async-start | bytes 3145728 | tf_op jit(solution)/shard_map/all_to_all | solution.py:307
  100.6 3.6 copy-start.3
  100.6 18.3 %all-to-all-start.3 = ((bf16[8,256,128]{2,1,0:T(8,128)(2,1)}), bf16[8,256,128]{2,1,0:T(8,128)(2,1)S(1)}, u32[]{:S(2)}, u32[]{:S(2)}) async-start(bf16[8,256,128]{2,1,0:T(8,128)(2,1)} %get-tuple-element.81), calls=%async_computation.3 | async-start | bytes 1048576 | tf_op jit(solution)/shard_map/all_to_all | solution.py:307
  118.9 3.8 copy-start.8
  118.9 25.0 %all-to-all-start.1 = ((bf16[8,256,128]{2,1,0:T(8,128)(2,1)}), bf16[8,256,128]{2,1,0:T(8,128)(2,1)S(1)}, u32[]{:S(2)}, u32[]{:S(2)}) async-start(bf16[8,256,128]{2,1,0:T(8,128)(2,1)} %get-tuple-element.79), calls=%async_computation.1 | async-start | bytes 1048576 | tf_op jit(solution)/shard_map/all_to_all | solution.py:307
  144.0 0.8 copy-start.1
  203.2 5.0 %copy-start.16 = (f32[4,2,256]{2,1,0:T(2,128)S(1)}, f32[4,2,256]{2,1,0:T(2,128)}, u32[]{:S(2)}) copy-start(f32[4,2,256]{2,1,0:T(2,128)} %get-tuple-element.93) | copy-start | bytes 24580
  203.2 5.1 %copy-start = (bf16[512,1024]{1,0:T(8,128)(2,1)S(1)}, bf16[512,1024]{1,0:T(8,128)(2,1)}, u32[]{:S(2)}) copy-start(bf16[512,1024]{1,0:T(8,128)(2,1)} %get-tuple-element.90) | copy-start | bytes 3145732
  203.2 45.8 %collective-permute-start = (bf16[4,8,176,128]{3,2,1,0:T(8,128)(2,1)}, bf16[4,8,176,128]{3,2,1,0:T(8,128)(2,1)S(1)}, u32[]{:S(2)}, u32[]{:S(2)}) collective-permute-start(bf16[4,8,176,128]{3,2,1,0:T(8,128)(2,1)} %get-tuple-element.110), channel_id=1, source_target_pairs={{0,16},{8,24},{16,0},{24,8},{1,17},{9,25},{17,1},{25,9},{2,18},{10... | collective-permute-start | bytes 4325384 | tf_op jit(solution)/shard_map/ppermute | solution.py:599
  204.7 44.2 %collective-permute-start.1 = (bf16[4,8,176,128]{3,2,1,0:T(8,128)(2,1)}, bf16[4,8,176,128]{3,2,1,0:T(8,128)(2,1)}, u32[]{:S(2)}, u32[]{:S(2)}) collective-permute-start(bf16[4,8,176,128]{3,2,1,0:T(8,128)(2,1)} %get-tuple-element.112), channel_id=1, source_target_pairs={{0,1},{1,0},{2,3},{3,2},{4,5},{5,4},{6,7},{7,6},{8,9},{9,8},{10,11... | collective-permute-start | bytes 4325384 | tf_op jit(solution)/shard_map/ppermute | solution.py:599
  205.3 43.7 %collective-permute-start.2 = (bf16[4,8,176,128]{3,2,1,0:T(8,128)(2,1)}, bf16[4,8,176,128]{3,2,1,0:T(8,128)(2,1)}, u32[]{:S(2)}, u32[]{:S(2)}) collective-permute-start(bf16[4,8,176,128]{3,2,1,0:T(8,128)(2,1)} %get-tuple-element.114), channel_id=1, source_target_pairs={{0,2},{1,3},{2,0},{3,1},{4,6},{5,7},{6,4},{7,5},{8,10},{9,11},{10,... | collective-permute-start | bytes 4325384 | tf_op jit(solution)/shard_map/ppermute | solution.py:599
  227.8 67.3 %all-to-all-start.4 = ((bf16[8,1,3,256,128]{4,3,2,1,0:T(8,128)(2,1)}), bf16[8,1,3,256,128]{4,3,2,1,0:T(8,128)(2,1)S(1)}, u32[]{:S(2)}, u32[]{:S(2)}) async-start(bf16[8,1,3,256,128]{4,3,2,1,0:T(8,128)(2,1)} %attn_bwd.2), calls=%async_computation.4 | async-start | bytes 3145728 | tf_op jit(solution)/shard_map/all_to_all | solution.py:307
  231.6 16.6 %copy-start.17 = (f32[1,1024]{1,0:T(1,128)S(1)}, f32[1,1024]{1,0:T(1,128)}, u32[]{:S(2)}) copy-start(f32[1,1024]{1,0:T(1,128)} %get-tuple-element.91) | copy-start | bytes 12292
  231.6 16.6 %copy-start.18 = (f32[1,1024]{1,0:T(1,128)S(1)}, f32[1,1024]{1,0:T(1,128)}, u32[]{:S(2)}) copy-start(f32[1,1024]{1,0:T(1,128)} %get-tuple-element.92) | copy-start | bytes 12292
  249.0 1.1 copy-start.5
  256.4 38.7 %collective-permute-start.3 = (bf16[4,4,176,128]{3,2,1,0:T(8,128)(2,1)}, bf16[4,4,176,128]{3,2,1,0:T(8,128)(2,1)S(1)}, u32[]{:S(2)}, u32[]{:S(2)}) collective-permute-start(bf16[4,4,176,128]{3,2,1,0:T(8,128)(2,1)} %get-tuple-element.116), channel_id=1, source_target_pairs={{0,1},{1,0},{2,3},{3,2},{4,5},{5,4},{6,7},{7,6},{8,9},{9,8},{10,11... | collective-permute-start | bytes 2162696 | tf_op jit(solution)/shard_map/ppermute | solution.py:599
  258.3 36.8 %collective-permute-start.4 = (bf16[4,4,176,128]{3,2,1,0:T(8,128)(2,1)}, bf16[4,4,176,128]{3,2,1,0:T(8,128)(2,1)S(1)}, u32[]{:S(2)}, u32[]{:S(2)}) collective-permute-start(bf16[4,4,176,128]{3,2,1,0:T(8,128)(2,1)} %get-tuple-element.118), channel_id=1, source_target_pairs={{0,16},{8,24},{16,0},{24,8},{1,17},{9,25},{17,1},{25,9},{2,18},{10... | collective-permute-start | bytes 2162696 | tf_op jit(solution)/shard_map/ppermute | solution.py:599
  258.3 36.8 %collective-permute-start.5 = (bf16[4,4,176,128]{3,2,1,0:T(8,128)(2,1)}, bf16[4,4,176,128]{3,2,1,0:T(8,128)(2,1)}, u32[]{:S(2)}, u32[]{:S(2)}) collective-permute-start(bf16[4,4,176,128]{3,2,1,0:T(8,128)(2,1)} %get-tuple-element.120), channel_id=1, source_target_pairs={{0,16},{8,24},{16,0},{24,8},{1,17},{9,25},{17,1},{25,9},{2,18},{10... | collective-permute-start | bytes 2162696 | tf_op jit(solution)/shard_map/ppermute | solution.py:599
  295.0 0.9 copy-start.20
  295.1 1.1 copy-start.21
  295.1 1.6 copy-start.4
  369.2 3.8 copy-start.2
  373.0 1.4 copy-start.15
  373.0 2.0 copy-start.14
  373.0 2.7 copy-start.13
  373.0 3.3 copy-start.12
  373.0 4.0 %copy-start.11 = (f32[352,256]{1,0:T(8,128)S(1)}, f32[352,256]{1,0:T(8,128)}, u32[]{:S(2)}) copy-start(f32[352,256]{1,0:T(8,128)} %get-tuple-element.138) | copy-start | bytes 1081348
  373.0 4.7 %copy-start.10 = (f32[352,256]{1,0:T(8,128)S(1)}, f32[352,256]{1,0:T(8,128)}, u32[]{:S(2)}) copy-start(f32[352,256]{1,0:T(8,128)} %get-tuple-element.139) | copy-start | bytes 1081348
  374.3 4.1 %copy-start.9 = (f32[704,128]{1,0:T(8,128)S(1)}, f32[704,128]{1,0:T(8,128)}, u32[]{:S(2)}) copy-start(f32[704,128]{1,0:T(8,128)} %get-tuple-element.173) | copy-start | bytes 1081348
